TPU v7x, 32 devices: a whole 2x2x4 slice. The times are simulated.
32 devices in a mesh: cuts: 4 (over z), rcv: 8 (over y, x, core).
Axes of the slice: x: 2, y: 2, z: 4, core: 2. Of those that a mesh axis runs over, the one named last changes fastest.
Arguments:
- down_spectra: float32 [8, 2048, 2560], P('cuts', 'rcv'), parts along dimension 0, may hold values from -0.07905694 to 0.07905694, as said below
- up_sources: float32 [8, 128, 2560], P('cuts', 'rcv'), parts along dimension 0, may hold values from -6 to 6
Outputs:
- solution: float32 [8, 2048, 128], P('cuts', 'rcv'), parts along dimension 0
- residual: float32 [8, 2048, 128], P('cuts', 'rcv'), parts along dimension 0
There are 4 independent parts, one for each index of `cuts`. A program takes and returns all parts, laid end to end along the dimension named above; each array names one. Nothing has to cross between parts.
Inputs may be any that keep to these rules, and one draw needn't show every extreme that they name: `down_spectra`: real-valued entries.
All inputs are finite; a program needn't handle non-finite values.
Results may differ from a plain program's by a relative error of at most 0.00021.
Values sent between devices are 32-bit elements; how exact they have to be, the bound alone decides.
No kernel may reach another device: no remote copies, remote signals or barrier semaphores. Data moves between devices by JAX's collectives and lax.ppermute only.
A program may use at most 64 MiB of HBM per device.

v0:
```python
import jax
import jax.numpy as jnp
from jax import lax
from jax.experimental import pallas as pl
from jax.experimental.pallas import tpu as pltpu
from jax.sharding import PartitionSpec as P

damping_ratio = 0.1
LANES = 128
f32 = jnp.float32
bf16 = jnp.bfloat16


def dot(left, right, right_dim):
    return lax.dot_general(left, right, (((1,), (right_dim,)), ((), ())), preferred_element_type=f32)


def parts_of(value):
    high = value.astype(bf16)
    return high, (value - high.astype(f32)).astype(bf16)


def call(kernel, outs, args, scratch=()):
    spec = pl.BlockSpec(memory_space=pltpu.VMEM)
    return pl.pallas_call(
        kernel,
        out_shape=[jax.ShapeDtypeStruct(shape, dtype) for shape, dtype in outs],
        in_specs=[spec] * len(args),
        out_specs=[spec] * len(outs),
        scratch_shapes=[pltpu.VMEM(shape, dtype) for shape, dtype in scratch],
        compiler_params=pltpu.CompilerParams(vmem_limit_bytes=40 << 20),
    )(*args)


def split_kernel(down_ref, high_ref, low_ref, energy_ref):
    rows, shots = down_ref.shape[1:]
    energy_ref[...] = jnp.zeros_like(energy_ref)

    def step(index, carry):
        at = pl.ds(pl.multiple_of(index * 16, 16), 16)
        for part in range(2):
            value = down_ref[part, at, :]
            high, low = parts_of(value)
            high_ref[part, at, :] = high
            low_ref[part, at, :] = low
            square = value * value
            energy_ref[...] += square[:8] + square[8:]
        return carry

    lax.fori_loop(0, rows // 16, step, 0)


def stage(value_ref, first_ref, second_ref, sign):
    half = value_ref.shape[0] // 2
    real = value_ref[:half, :]
    imag = value_ref[half:, :]
    for at, (a, b) in enumerate(zip(parts_of(real), parts_of(imag))):
        base = 2 * half * at
        first_ref[base : base + half, :] = a
        first_ref[base + half : base + 2 * half, :] = b
        second_ref[base : base + half, :] = b if sign > 0 else -b
        second_ref[base + half : base + 2 * half, :] = a if sign < 0 else -a


def apply_down(first, second, high_ref, low_ref, columns):
    count = first.shape[0] // 2
    total = dot(first, high_ref[0, :, columns], 1) + dot(second, high_ref[1, :, columns], 1)
    low = dot(first[:count], low_ref[0, :, columns], 1) + dot(second[:count], low_ref[1, :, columns], 1)
    return total[:count] + total[count:] + low


def apply_adjoint(first, second, high_ref, low_ref, columns):
    count = first.shape[0] // 2
    total = dot(first, high_ref[0, :, columns], 0) + dot(second, high_ref[1, :, columns], 0)
    low = dot(first[:count], low_ref[0, :, columns], 0) + dot(second[:count], low_ref[1, :, columns], 0)
    return total[:count] + total[count:] + low


def project(value_ref, first_ref, second_ref, blocks, columns):
    stage(value_ref, first_ref, second_ref, 1)
    rows = blocks[0][0].shape[1]
    total = 0.0
    for at, (high, low) in enumerate(blocks):
        own = slice(at * rows, (at + 1) * rows)
        total = total + apply_adjoint(first_ref[:, own], second_ref[:, own], high, low, columns)
    return total


def row_squares(value):
    return jnp.sum(value * value, axis=1, keepdims=True)


def both(value):
    half = value.shape[0] // 2
    total = value[:half] + value[half:]
    return jnp.concatenate([total, total], axis=0)


def tail(*columns):
    lane = lax.broadcasted_iota(jnp.int32, (columns[0].shape[0], LANES), 1)
    out = jnp.zeros(lane.shape, f32)
    for at, column in enumerate(columns):
        out = jnp.where(lane == at, column, out)
    return out


def rhs_kernel(sources, *refs):
    (real_ref, imag_ref, ha, la, ea, hb, lb, eb, rhs_ref, out_ref, x_ref, first_ref, second_ref, third_ref, fourth_ref) = refs
    half, shots = real_ref.shape
    x_ref[:half, :] = real_ref[...]
    x_ref[half:, :] = -imag_ref[...]
    stage(x_ref, first_ref, second_ref, -1)
    rows = ha.shape[1]
    every = slice(0, shots)
    for at, (high, low) in enumerate(((ha, la), (hb, lb))):
        rhs_ref[:, at * rows : (at + 1) * rows] = apply_down(first_ref[...], second_ref[...], high, low, every)
    front = out_ref.shape[1] - LANES
    out_ref[:, :front] = project(rhs_ref, third_ref, fourth_ref, ((ha, la), (hb, lb)), slice(0, front))
    energy = jnp.sum(ea[...] + eb[...])
    out_ref[:, front:] = tail(row_squares(rhs_ref[...]), jnp.full((2 * half, 1), energy, f32))


def back_kernel(*refs):
    (value_ref, ha, la, hb, lb, out_ref, first_ref, second_ref) = refs
    shots = ha.shape[2]
    out_ref[...] = project(value_ref, first_ref, second_ref, ((ha, la), (hb, lb)), slice(shots - out_ref.shape[1], shots))


def image_of(x_ref, first_ref, second_ref, blocks, image_ref, columns):
    stage(x_ref, first_ref, second_ref, -1)
    rows = blocks[0][0].shape[1]
    for at, (high, low) in enumerate(blocks):
        image_ref[:, at * rows : (at + 1) * rows] = apply_down(first_ref[...], second_ref[...], high, low, columns)


def first_kernel(receivers, *refs):
    (p0, p1, q0, q1, rhs_ref, ha, la, hb, lb) = refs[:9]
    (x_ref, scalar_ref, image_ref, residual_ref, out_ref, first_ref, second_ref, third_ref, fourth_ref) = refs[9:]
    front = p0.shape[1] - LANES
    x_ref[:, :front] = p0[:, :front] + p1[:, :front]
    x_ref[:, front:] = q0[...] + q1[...]
    ends = p0[:, front:] + p1[:, front:]
    norm = both(ends[:, 0:1])
    damping = damping_ratio * ends[:, 1:2] / receivers
    blocks = ((ha, la), (hb, lb))
    image_of(x_ref, first_ref, second_ref, blocks, image_ref, slice(0, x_ref.shape[1]))
    image = image_ref[...] + damping * rhs_ref[...]
    image_ref[...] = image
    alpha = norm / (both(row_squares(x_ref[...])) + damping * norm)
    residual = rhs_ref[...] - alpha * image
    residual_ref[...] = residual
    scalar_ref[...] = tail(norm, damping, alpha)
    out_ref[:, :front] = project(residual_ref, third_ref, fourth_ref, blocks, slice(0, front))
    out_ref[:, front:] = tail(row_squares(residual))


def last_kernel(*refs):
    (p0, p1, q0, q1, rhs_ref, before_ref, scalar_ref, image_ref, residual_ref, ha, la, hb, lb) = refs[:13]
    (keep_ref, give_ref, x_ref, y_ref, first_ref, second_ref) = refs[13:]
    front = p0.shape[1] - LANES
    x_ref[:, :front] = p0[:, :front] + p1[:, :front]
    x_ref[:, front:] = q0[...] + q1[...]
    following = both(p0[:, front : front + 1] + p1[:, front : front + 1])
    norm = scalar_ref[:, 0:1]
    damping = scalar_ref[:, 1:2]
    alpha = scalar_ref[:, 2:3]
    beta = following / norm
    image_of(x_ref, first_ref, second_ref, ((ha, la), (hb, lb)), y_ref, slice(0, x_ref.shape[1]))
    residual = residual_ref[...]
    image = y_ref[...] + beta * image_ref[...] + damping * residual
    curvature = both(row_squares(x_ref[...] + beta * before_ref[...])) + damping * (following + beta * following)
    alpha_next = following / curvature
    rhs = rhs_ref[...]
    found = alpha * rhs + alpha_next * (residual + beta * rhs)
    left = residual - alpha_next * image
    rows = ha.shape[1]
    keep_ref[0] = found[:, :rows]
    keep_ref[1] = left[:, :rows]
    give_ref[0] = found[:, rows:]
    give_ref[1] = left[:, rows:]


def swap(value, bit, count):
    return lax.ppermute(value, "rcv", [(at, at ^ (1 << bit)) for at in range(count)])


def body(down_spectra, up_sources, *, count, receivers):
    me = lax.axis_index("rcv")
    bits = count.bit_length() - 1
    chip_bits = list(range(1, bits))
    rows, shots = down_spectra.shape[1:]
    own = up_sources.shape[1]
    other_down = swap(down_spectra, 0, count)

    def gather(block, order):
        block = block.reshape((1,) * len(chip_bits) + block.shape)
        for bit in order:
            axis = len(chip_bits) - bit
            other = swap(block, bit, count)
            upper = ((me >> bit) & 1) == 1
            block = jnp.concatenate([jnp.where(upper, other, block), jnp.where(upper, block, other)], axis=axis)
        return block.reshape((-1, shots))

    real = gather(up_sources[0], chip_bits)
    imag = gather(up_sources[1], chip_bits[::-1])
    ha, la, ea = split(down_spectra)
    hb, lb, eb = split(other_down)
    columns = real.shape[0]
    packed = 2 * columns
    front = shots // 2
    wide = [((2 * packed, shots), bf16)] * 2
    short = [((2 * packed, 2 * rows), bf16)] * 2
    rhs, p = call(
        lambda *refs: rhs_kernel(None, *refs),
        [((packed, 2 * rows), f32), ((packed, front + LANES), f32)],
        (real, imag, ha, la, ea, hb, lb, eb),
        [((packed, shots), f32)] + wide + short,
    )
    (q,) = call(back_kernel, [((packed, shots - front), f32)], (rhs, ha, la, hb, lb), short)

    def exchange(p, q):
        for step in range(len(chip_bits) - 1):
            p = p + swap(p, chip_bits[step], count)
            q = q + swap(q, chip_bits[-1 - step], count)
        return p, swap(p, chip_bits[-1], count), q, swap(q, chip_bits[0], count)

    before, scalars, image, residual, p = call(
        lambda *refs: first_kernel(receivers, *refs),
        [
            ((packed, shots), f32),
            ((packed, LANES), f32),
            ((packed, 2 * rows), f32),
            ((packed, 2 * rows), f32),
            ((packed, front + LANES), f32),
        ],
        (*exchange(p, q), rhs, ha, la, hb, lb),
        wide + short,
    )
    (q,) = call(back_kernel, [((packed, shots - front), f32)], (residual, ha, la, hb, lb), short)
    keep, give = call(
        last_kernel,
        [((2, packed, rows), f32)] * 2,
        (*exchange(p, q), rhs, before, scalars, image, residual, ha, la, hb, lb),
        [((packed, shots), f32), ((packed, 2 * rows), f32)] + wide,
    )
    other = swap(give, 0, count)
    upper = (me & 1) == 1
    chips = count // 2

    def order(first, second):
        pair = jnp.stack([first.reshape(2, 2, chips, own, rows), second.reshape(2, 2, chips, own, rows)], axis=3)
        return pair.reshape(2, 2, chips * 2 * own, rows).transpose(0, 1, 3, 2)

    both_cores = order(jnp.where(upper, other, keep), jnp.where(upper, keep, other))
    return both_cores[0], both_cores[1]


def split(value):
    _, rows, shots = value.shape
    return call(
        split_kernel,
        [(value.shape, bf16), (value.shape, bf16), ((8, shots), f32)],
        (value,),
    )


def solution(mesh):
    count = mesh.shape["rcv"]

    def run(down_spectra, up_sources):
        return body(down_spectra, up_sources, count=count, receivers=down_spectra.shape[1] * count)

    specs = (P("cuts", "rcv", None), P("cuts", "rcv", None))
    return jax.shard_map(run, mesh=mesh, in_specs=specs, out_specs=specs, check_vma=False)
```

profile of v0, /device:TPU:0, one launch (start us, length us, event | category | flops | bytes accessed | tf_op | source)
XLA Modules:
  0.0 109.6 jit_solution(13503497343790566859)
XLA Ops:
  0.6 0.5 collective-permute-start.4
  1.1 1.7 %slice_bitcast_fusion.2 = (f32[1,1,16,2560]{3,2,1,0:T(8,128)}, f32[1,1,16,2560]{3,2,1,0:T(8,128)S(1)}) fusion(f32[2,16,2560]{2,1,0:T(8,128)} %param.3), kind=kLoop, calls=%fused_computation.7 | loop fusion | bytes 655360 | tf_op jit(solution)/shard_map/reshape;squeeze | solution.py:196
  2.8 2.5 %collective-permute-start.2 = (f32[1,1,16,2560]{3,2,1,0:T(8,128)}, f32[1,1,16,2560]{3,2,1,0:T(8,128)S(1)}, u32[]{:S(2)}, u32[]{:S(2)}) collective-permute-start(f32[1,1,16,2560]{3,2,1,0:T(8,128)} %get-tuple-element.48), channel_id=1, source_target_pairs={{0,4},{1,5},{2,6},{3,7},{4,0},{5,1},{6,2},{7,3},{8,12},{9,13},{10,... | collective-permute-start | bytes 491528 | tf_op jit(solution)/shard_map/ppermute | solution.py:184
  5.4 1.5 %collective-permute-start = (f32[1,1,16,2560]{3,2,1,0:T(8,128)S(1)}, f32[1,1,16,2560]{3,2,1,0:T(8,128)S(1)}, u32[]{:S(2)}, u32[]{:S(2)}) collective-permute-start(f32[1,1,16,2560]{3,2,1,0:T(8,128)S(1)} %get-tuple-element.49), channel_id=1, source_target_pairs={{0,2},{1,3},{2,0},{3,1},{4,6},{5,7},{6,4},{7,5},{8,10},{9,11},{10,... | collective-permute-start | bytes 491528 | tf_op jit(solution)/shard_map/ppermute | solution.py:184
  6.9 0.0 copy-start.4
  6.9 2.5 %copy-done.4 = f32[2,256,2560]{2,1,0:T(8,128)S(1)} copy-done((f32[2,256,2560]{2,1,0:T(8,128)S(1)}, f32[2,256,2560]{2,1,0:T(8,128)}, u32[]{:S(2)}) %copy-start.4) | copy-done | bytes 5242904
  9.3 0.0 copy-start.5
  9.3 1.3 %shard_map.41 = (bf16[2,256,2560]{2,1,0:T(8,128)(2,1)S(1)}, bf16[2,256,2560]{2,1,0:T(8,128)(2,1)S(1)}, f32[8,2560]{1,0:T(8,128)S(1)}) custom-call(f32[2,256,2560]{2,1,0:T(8,128)S(1)} %copy-done.4), custom_call_target="tpu_custom_call" | custom-call | tf_op jit(solution)/shard_map/pallas_call | solution.py:25
  10.7 0.0 copy-start
  10.7 1.5 %copy-done = bf16[2,256,2560]{2,1,0:T(8,128)(2,1)} copy-done((bf16[2,256,2560]{2,1,0:T(8,128)(2,1)}, bf16[2,256,2560]{2,1,0:T(8,128)(2,1)S(1)}, u32[]{:S(2)}) %copy-start) | copy-done | bytes 2621464
  12.2 0.0 collective-permute-done.2
  12.2 0.0 collective-permute-done
  12.2 0.0 copy-done.5
  12.3 0.6 collective-permute-start.1
  12.9 1.0 collective-permute-start.3
  13.9 8.0 %collective-permute-done.1 = f32[1,2,16,2560]{3,2,1,0:T(8,128)S(1)} collective-permute-done((f32[1,2,16,2560]{3,2,1,0:T(8,128)S(1)}, f32[1,2,16,2560]{3,2,1,0:T(8,128)S(1)}, u32[]{:S(2)}, u32[]{:S(2)}) %collective-permute-start.1) | collective-permute-done | bytes 327712 | tf_op jit(solution)/shard_map/ppermute | solution.py:184
  22.0 0.2 collective-permute-done.3
  22.3 0.0 copy-start.1
  22.3 0.0 collective-permute-done.4.down_ref
  22.3 4.0 %shard_map.42 = (bf16[2,256,2560]{2,1,0:T(8,128)(2,1)S(1)}, bf16[2,256,2560]{2,1,0:T(8,128)(2,1)S(1)}, f32[8,2560]{1,0:T(8,128)S(1)}) custom-call(f32[2,256,2560]{2,1,0:T(8,128)} %collective-permute-done.4.down_ref), custom_call_target="tpu_custom_call" | custom-call | tf_op jit(solution)/shard_map/pallas_call | solution.py:25
  26.3 0.0 copy-start.2
  26.3 0.0 copy-done.1
  26.3 4.2 %shard_map.43 = (f32[128,512]{1,0:T(8,128)S(1)}, f32[128,1408]{1,0:T(8,128)S(1)}) custom-call(f32[64,2560]{1,0:T(8,128)S(1)} %bitcast.27, f32[64,2560]{1,0:T(8,128)S(1)} %bitcast.28, bf16[2,256,2560]{2,1,0:T(8,128)(2,1)S(1)} %get-tuple-element.17.refs_2_.refs_1_.refs_5_.refs_9_, bf16[2,256,2560]{2,1,0:T(8,128)(2,1)S(1)} %copy-done.1, ...), custom_call_target="tpu_custom_call" | custom-call | tf_op jit(solution)/shard_map/pallas_call | solution.py:25
  30.5 0.8 collective-permute-start.5
  31.4 0.0 copy-done.2
  31.4 1.2 %shard_map.44 = f32[128,1280]{1,0:T(8,128)S(1)} custom-call(f32[128,512]{1,0:T(8,128)S(1)} %get-tuple-element.24.refs_0_.refs_4_, bf16[2,256,2560]{2,1,0:T(8,128)(2,1)S(1)} %get-tuple-element.17.refs_2_.refs_1_.refs_5_.refs_9_, bf16[2,256,2560]{2,1,0:T(8,128)(2,1)S(1)} %copy-done.1, ...), custom_call_target="tpu_custom_call" | custom-call | tf_op jit(solution)/shard_map/pallas_call | solution.py:25
  32.5 1.4 %collective-permute-start.7 = (f32[128,1280]{1,0:T(8,128)S(1)}, f32[128,1280]{1,0:T(8,128)S(1)}, u32[]{:S(2)}, u32[]{:S(2)}) collective-permute-start(f32[128,1280]{1,0:T(8,128)S(1)} %shard_map.44), channel_id=1, source_target_pairs={{0,4},{1,5},{2,6},{3,7},{4,0},{5,1},{6,2},{7,3},{8,12},{9,13},{10,... | collective-permute-start | bytes 1966088 | tf_op jit(solution)/shard_map/ppermute | solution.py:184
  33.9 13.6 %collective-permute-done.5 = f32[128,1408]{1,0:T(8,128)S(1)} collective-permute-done((f32[128,1408]{1,0:T(8,128)S(1)}, f32[128,1408]{1,0:T(8,128)S(1)}, u32[]{:S(2)}, u32[]{:S(2)}) %collective-permute-start.5) | collective-permute-done | bytes 720928 | tf_op jit(solution)/shard_map/ppermute | solution.py:184
  47.5 0.1 add.12.refs_0_
  47.6 1.5 %collective-permute-start.6 = (f32[128,1408]{1,0:T(8,128)S(1)}, f32[128,1408]{1,0:T(8,128)S(1)}, u32[]{:S(2)}, u32[]{:S(2)}) collective-permute-start(f32[128,1408]{1,0:T(8,128)S(1)} %add.12.refs_0_), channel_id=1, source_target_pairs={{0,4},{1,5},{2,6},{3,7},{4,0},{5,1},{6,2},{7,3},{8,12},{9,13},{10,... | collective-permute-start | bytes 2162696 | tf_op jit(solution)/shard_map/ppermute | solution.py:184
  49.1 0.0 collective-permute-done.7
  49.1 0.1 add.13.refs_2_
  49.1 0.0 copy-start.3
  49.1 1.0 collective-permute-start.8
  50.1 13.3 %collective-permute-done.8.refs_3_ = f32[128,1280]{1,0:T(8,128)S(1)} collective-permute-done((f32[128,1280]{1,0:T(8,128)S(1)}, f32[128,1280]{1,0:T(8,128)S(1)}, u32[]{:S(2)}, u32[]{:S(2)}) %collective-permute-start.8) | collective-permute-done | bytes 655392 | tf_op jit(solution)/shard_map/ppermute | solution.py:184
  63.4 0.3 collective-permute-done.6.refs_1_
  63.6 6.0 %shard_map.45 = (f32[128,2560]{1,0:T(8,128)S(1)}, f32[128,128]{1,0:T(8,128)S(1)}, f32[128,512]{1,0:T(8,128)S(1)}, f32[128,512]{1,0:T(8,128)S(1)}, f32[128,1408]{1,0:T(8,128)S(1)}) custom-call(f32[128,1408]{1,0:T(8,128)S(1)} %add.12.refs_0_, f32[128,1408]{1,0:T(8,128)S(1)} %collective-permute-done.6.refs_1_, f32[128,1280]{1,0:T(8,128)S(1)} %add.13.refs_2_, ...), custom_call_target="tpu_custom_call" | custom-call | tf_op jit(solution)/shard_map/pallas_call | solution.py:25
  69.7 1.0 collective-permute-start.9
  70.7 0.0 copy-done.3
  70.7 1.2 %shard_map.46 = f32[128,1280]{1,0:T(8,128)S(1)} custom-call(f32[128,512]{1,0:T(8,128)S(1)} %get-tuple-element.26.refs_0_.refs_8_, bf16[2,256,2560]{2,1,0:T(8,128)(2,1)S(1)} %get-tuple-element.17.refs_2_.refs_1_.refs_5_.refs_9_, bf16[2,256,2560]{2,1,0:T(8,128)(2,1)S(1)} %copy-done.1, ...), custom_call_target="tpu_custom_call" | custom-call | tf_op jit(solution)/shard_map/pallas_call | solution.py:25
  71.9 1.5 %collective-permute-start.11 = (f32[128,1280]{1,0:T(8,128)S(1)}, f32[128,1280]{1,0:T(8,128)S(1)}, u32[]{:S(2)}, u32[]{:S(2)}) collective-permute-start(f32[128,1280]{1,0:T(8,128)S(1)} %shard_map.46), channel_id=1, source_target_pairs={{0,4},{1,5},{2,6},{3,7},{4,0},{5,1},{6,2},{7,3},{8,12},{9,13},{10,... | collective-permute-start | bytes 1966088 | tf_op jit(solution)/shard_map/ppermute | solution.py:184
  73.3 11.5 %collective-permute-done.9 = f32[128,1408]{1,0:T(8,128)S(1)} collective-permute-done((f32[128,1408]{1,0:T(8,128)S(1)}, f32[128,1408]{1,0:T(8,128)S(1)}, u32[]{:S(2)}, u32[]{:S(2)}) %collective-permute-start.9) | collective-permute-done | bytes 720928 | tf_op jit(solution)/shard_map/ppermute | solution.py:184
  84.8 0.1 add.14.refs_0_
  84.9 1.3 %collective-permute-start.10 = (f32[128,1408]{1,0:T(8,128)S(1)}, f32[128,1408]{1,0:T(8,128)S(1)}, u32[]{:S(2)}, u32[]{:S(2)}) collective-permute-start(f32[128,1408]{1,0:T(8,128)S(1)} %add.14.refs_0_), channel_id=1, source_target_pairs={{0,4},{1,5},{2,6},{3,7},{4,0},{5,1},{6,2},{7,3},{8,12},{9,13},{10,... | collective-permute-start | bytes 2162696 | tf_op jit(solution)/shard_map/ppermute | solution.py:184
  86.2 1.8 %collective-permute-done.11 = f32[128,1280]{1,0:T(8,128)S(1)} collective-permute-done((f32[128,1280]{1,0:T(8,128)S(1)}, f32[128,1280]{1,0:T(8,128)S(1)}, u32[]{:S(2)}, u32[]{:S(2)}) %collective-permute-start.11) | collective-permute-done | bytes 655392 | tf_op jit(solution)/shard_map/ppermute | solution.py:184
  88.0 0.1 add.15.refs_2_
  88.0 0.2 collective-permute-start.12
  88.3 11.1 %collective-permute-done.12.refs_3_ = f32[128,1280]{1,0:T(8,128)S(1)} collective-permute-done((f32[128,1280]{1,0:T(8,128)S(1)}, f32[128,1280]{1,0:T(8,128)S(1)}, u32[]{:S(2)}, u32[]{:S(2)}) %collective-permute-start.12) | collective-permute-done | bytes 655392 | tf_op jit(solution)/shard_map/ppermute | solution.py:184
  99.4 1.9 %collective-permute-done.10.refs_1_ = f32[128,1408]{1,0:T(8,128)S(1)} collective-permute-done((f32[128,1408]{1,0:T(8,128)S(1)}, f32[128,1408]{1,0:T(8,128)S(1)}, u32[]{:S(2)}, u32[]{:S(2)}) %collective-permute-start.10) | collective-permute-done | bytes 720928 | tf_op jit(solution)/shard_map/ppermute | solution.py:184
  101.3 5.0 %shard_map.47 = (f32[2,128,256]{2,1,0:T(8,128)S(1)}, f32[2,128,256]{2,1,0:T(8,128)S(1)}) custom-call(f32[128,1408]{1,0:T(8,128)S(1)} %add.14.refs_0_, f32[128,1408]{1,0:T(8,128)S(1)} %collective-permute-done.10.refs_1_, f32[128,1280]{1,0:T(8,128)S(1)} %add.15.refs_2_, f32[128,1280]{1,0:T(8,128)S(1)} %collective-permute-done.12.refs_3_, ...), custom_call_target="tpu_custom_call" | custom-call | tf_op jit(solution)/shard_map/pallas_call | solution.py:25
  106.2 0.1 collective-permute-start.13
  106.3 1.5 %collective-permute-done.13 = f32[2,128,256]{2,1,0:T(8,128)S(1)} collective-permute-done((f32[2,128,256]{2,1,0:T(8,128)S(1)}, f32[2,128,256]{2,1,0:T(8,128)S(1)}, u32[]{:S(2)}, u32[]{:S(2)}) %collective-permute-start.13) | collective-permute-done | bytes 262176 | tf_op jit(solution)/shard_map/ppermute | solution.py:184
  108.0 0.8 copy.8
  108.8 0.8 copy.7
  (10 shorter events, 0.4 us)
Async XLA Ops:
  0.6 21.7 %collective-permute-start.4 = (f32[2,256,2560]{2,1,0:T(8,128)}, f32[2,256,2560]{2,1,0:T(8,128)}, u32[]{:S(2)}, u32[]{:S(2)}) collective-permute-start(f32[2,256,2560]{2,1,0:T(8,128)} %down_ref.1), channel_id=1, source_target_pairs={{0,1},{1,0},{2,3},{3,2},{4,5},{5,4},{6,7},{7,6},{8,9},{9,8},{10,11... | collective-permute-start | bytes 15728648 | tf_op jit(solution)/shard_map/ppermute | solution.py:184
  2.8 9.3 %collective-permute-start.2 = (f32[1,1,16,2560]{3,2,1,0:T(8,128)}, f32[1,1,16,2560]{3,2,1,0:T(8,128)S(1)}, u32[]{:S(2)}, u32[]{:S(2)}) collective-permute-start(f32[1,1,16,2560]{3,2,1,0:T(8,128)} %get-tuple-element.48), channel_id=1, source_target_pairs={{0,4},{1,5},{2,6},{3,7},{4,0},{5,1},{6,2},{7,3},{8,12},{9,13},{10,... | collective-permute-start | bytes 491528 | tf_op jit(solution)/shard_map/ppermute | solution.py:184
  5.4 6.8 %collective-permute-start = (f32[1,1,16,2560]{3,2,1,0:T(8,128)S(1)}, f32[1,1,16,2560]{3,2,1,0:T(8,128)S(1)}, u32[]{:S(2)}, u32[]{:S(2)}) collective-permute-start(f32[1,1,16,2560]{3,2,1,0:T(8,128)S(1)} %get-tuple-element.49), channel_id=1, source_target_pairs={{0,2},{1,3},{2,0},{3,1},{4,6},{5,7},{6,4},{7,5},{8,10},{9,11},{10,... | collective-permute-start | bytes 491528 | tf_op jit(solution)/shard_map/ppermute | solution.py:184
  6.9 2.5 %copy-start.4 = (f32[2,256,2560]{2,1,0:T(8,128)S(1)}, f32[2,256,2560]{2,1,0:T(8,128)}, u32[]{:S(2)}) copy-start(f32[2,256,2560]{2,1,0:T(8,128)} %down_ref.1) | copy-start | bytes 15728644
  9.3 2.8 %copy-start.5 = (f32[2,16,2560]{2,1,0:T(8,128)S(1)}, f32[2,16,2560]{2,1,0:T(8,128)}, u32[]{:S(2)}) copy-start(f32[2,16,2560]{2,1,0:T(8,128)} %param.3) | copy-start | bytes 983044
  10.7 1.5 %copy-start = (bf16[2,256,2560]{2,1,0:T(8,128)(2,1)}, bf16[2,256,2560]{2,1,0:T(8,128)(2,1)S(1)}, u32[]{:S(2)}) copy-start(bf16[2,256,2560]{2,1,0:T(8,128)(2,1)S(1)} %get-tuple-element.18.refs_3_.refs_2_.refs_6_.refs_10_) | copy-start | bytes 7864324
  12.3 9.6 %collective-permute-start.1 = (f32[1,2,16,2560]{3,2,1,0:T(8,128)S(1)}, f32[1,2,16,2560]{3,2,1,0:T(8,128)S(1)}, u32[]{:S(2)}, u32[]{:S(2)}) collective-permute-start(f32[1,2,16,2560]{3,2,1,0:T(8,128)S(1)} %pad_maximum_fusion.3), channel_id=1, source_target_pairs={{0,4},{1,5},{2,6},{3,7},{4,0},{5,1},{6,2},{7,3},{8,12},{9,13},{10,... | collective-permute-start | bytes 983048 | tf_op jit(solution)/shard_map/ppermute | solution.py:184
  12.9 9.3 %collective-permute-start.3 = (f32[2,1,16,2560]{3,2,1,0:T(8,128)S(1)}, f32[2,1,16,2560]{3,2,1,0:T(8,128)S(1)}, u32[]{:S(2)}, u32[]{:S(2)}) collective-permute-start(f32[2,1,16,2560]{3,2,1,0:T(8,128)S(1)} %pad_maximum_fusion.4), channel_id=1, source_target_pairs={{0,2},{1,3},{2,0},{3,1},{4,6},{5,7},{6,4},{7,5},{8,10},{9,11},{10,... | collective-permute-start | bytes 983048 | tf_op jit(solution)/shard_map/ppermute | solution.py:184
  22.3 4.0 %copy-start.1 = (bf16[2,256,2560]{2,1,0:T(8,128)(2,1)S(1)}, bf16[2,256,2560]{2,1,0:T(8,128)(2,1)}, u32[]{:S(2)}) copy-start(bf16[2,256,2560]{2,1,0:T(8,128)(2,1)} %copy-done) | copy-start | bytes 7864324
  26.3 5.1 %copy-start.2 = (bf16[2,256,2560]{2,1,0:T(8,128)(2,1)}, bf16[2,256,2560]{2,1,0:T(8,128)(2,1)S(1)}, u32[]{:S(2)}) copy-start(bf16[2,256,2560]{2,1,0:T(8,128)(2,1)S(1)} %get-tuple-element.21.refs_6_.refs_4_.refs_8_.refs_12_) | copy-start | bytes 7864324
  30.5 17.0 %collective-permute-start.5 = (f32[128,1408]{1,0:T(8,128)S(1)}, f32[128,1408]{1,0:T(8,128)S(1)}, u32[]{:S(2)}, u32[]{:S(2)}) collective-permute-start(f32[128,1408]{1,0:T(8,128)S(1)} %get-tuple-element.23), channel_id=1, source_target_pairs={{0,2},{1,3},{2,0},{3,1},{4,6},{5,7},{6,4},{7,5},{8,10},{9,11},{10,... | collective-permute-start | bytes 2162696 | tf_op jit(solution)/shard_map/ppermute | solution.py:184
  32.5 16.5 %collective-permute-start.7 = (f32[128,1280]{1,0:T(8,128)S(1)}, f32[128,1280]{1,0:T(8,128)S(1)}, u32[]{:S(2)}, u32[]{:S(2)}) collective-permute-start(f32[128,1280]{1,0:T(8,128)S(1)} %shard_map.44), channel_id=1, source_target_pairs={{0,4},{1,5},{2,6},{3,7},{4,0},{5,1},{6,2},{7,3},{8,12},{9,13},{10,... | collective-permute-start | bytes 1966088 | tf_op jit(solution)/shard_map/ppermute | solution.py:184
  47.6 16.1 %collective-permute-start.6 = (f32[128,1408]{1,0:T(8,128)S(1)}, f32[128,1408]{1,0:T(8,128)S(1)}, u32[]{:S(2)}, u32[]{:S(2)}) collective-permute-start(f32[128,1408]{1,0:T(8,128)S(1)} %add.12.refs_0_), channel_id=1, source_target_pairs={{0,4},{1,5},{2,6},{3,7},{4,0},{5,1},{6,2},{7,3},{8,12},{9,13},{10,... | collective-permute-start | bytes 2162696 | tf_op jit(solution)/shard_map/ppermute | solution.py:184
  49.1 21.5 %copy-start.3 = (bf16[2,256,2560]{2,1,0:T(8,128)(2,1)S(1)}, bf16[2,256,2560]{2,1,0:T(8,128)(2,1)}, u32[]{:S(2)}) copy-start(bf16[2,256,2560]{2,1,0:T(8,128)(2,1)} %copy-done.2) | copy-start | bytes 7864324
  49.1 14.2 %collective-permute-start.8 = (f32[128,1280]{1,0:T(8,128)S(1)}, f32[128,1280]{1,0:T(8,128)S(1)}, u32[]{:S(2)}, u32[]{:S(2)}) collective-permute-start(f32[128,1280]{1,0:T(8,128)S(1)} %add.13.refs_2_), channel_id=1, source_target_pairs={{0,2},{1,3},{2,0},{3,1},{4,6},{5,7},{6,4},{7,5},{8,10},{9,11},{10,... | collective-permute-start | bytes 1966088 | tf_op jit(solution)/shard_map/ppermute | solution.py:184
  69.7 15.1 %collective-permute-start.9 = (f32[128,1408]{1,0:T(8,128)S(1)}, f32[128,1408]{1,0:T(8,128)S(1)}, u32[]{:S(2)}, u32[]{:S(2)}) collective-permute-start(f32[128,1408]{1,0:T(8,128)S(1)} %get-tuple-element.25), channel_id=1, source_target_pairs={{0,2},{1,3},{2,0},{3,1},{4,6},{5,7},{6,4},{7,5},{8,10},{9,11},{10,... | collective-permute-start | bytes 2162696 | tf_op jit(solution)/shard_map/ppermute | solution.py:184
  71.9 16.1 %collective-permute-start.11 = (f32[128,1280]{1,0:T(8,128)S(1)}, f32[128,1280]{1,0:T(8,128)S(1)}, u32[]{:S(2)}, u32[]{:S(2)}) collective-permute-start(f32[128,1280]{1,0:T(8,128)S(1)} %shard_map.46), channel_id=1, source_target_pairs={{0,4},{1,5},{2,6},{3,7},{4,0},{5,1},{6,2},{7,3},{8,12},{9,13},{10,... | collective-permute-start | bytes 1966088 | tf_op jit(solution)/shard_map/ppermute | solution.py:184
  84.9 16.4 %collective-permute-start.10 = (f32[128,1408]{1,0:T(8,128)S(1)}, f32[128,1408]{1,0:T(8,128)S(1)}, u32[]{:S(2)}, u32[]{:S(2)}) collective-permute-start(f32[128,1408]{1,0:T(8,128)S(1)} %add.14.refs_0_), channel_id=1, source_target_pairs={{0,4},{1,5},{2,6},{3,7},{4,0},{5,1},{6,2},{7,3},{8,12},{9,13},{10,... | collective-permute-start | bytes 2162696 | tf_op jit(solution)/shard_map/ppermute | solution.py:184
  88.0 11.4 %collective-permute-start.12 = (f32[128,1280]{1,0:T(8,128)S(1)}, f32[128,1280]{1,0:T(8,128)S(1)}, u32[]{:S(2)}, u32[]{:S(2)}) collective-permute-start(f32[128,1280]{1,0:T(8,128)S(1)} %add.15.refs_2_), channel_id=1, source_target_pairs={{0,2},{1,3},{2,0},{3,1},{4,6},{5,7},{6,4},{7,5},{8,10},{9,11},{10,... | collective-permute-start | bytes 1966088 | tf_op jit(solution)/shard_map/ppermute | solution.py:184
  106.2 1.6 %collective-permute-start.13 = (f32[2,128,256]{2,1,0:T(8,128)S(1)}, f32[2,128,256]{2,1,0:T(8,128)S(1)}, u32[]{:S(2)}, u32[]{:S(2)}) collective-permute-start(f32[2,128,256]{2,1,0:T(8,128)S(1)} %get-tuple-element.30), channel_id=1, source_target_pairs={{0,1},{1,0},{2,3},{3,2},{4,5},{5,4},{6,7},{7,6},{8,9},{9,8},{10,11... | collective-permute-start | bytes 786440 | tf_op jit(solution)/shard_map/ppermute | solution.py:184
where the time goes:
time: 110 us
  waiting for transfers between devices  63.1 us (57%)
  Pallas kernels  22.8 us (21%)
  starting transfers between devices  14.8 us (13%)
  local copies, waits for them, and re-layouts  7.39 us (7%)
    ppermute x14, waiting for transfers between devices, swap(): lax.ppermute(value, 'rcv', [(at, at ^ 1 << bit) for at in range(count)])  63.1 us
    pallas_call x7, Pallas kernels, call(): pl.pallas_call(kernel, out_shape=[jax.ShapeDtypeStruct(shape, dtype) for...  22.8 us
    ppermute x14, starting transfers between devices, swap(): lax.ppermute(value, 'rcv', [(at, at ^ 1 << bit) for at in range(count)])  14.8 us
    unnamed x14, local copies, waits for them, and re-layouts  5.67 us
  transfers between devices with their start and end apart: 14, of which 10 were waited for; matrix products, arithmetic and copies ran while one was open for 2% of the time, Pallas kernels for 3%

commit v1 on v0

v1 whole, which is shorter than its diff:
```python
import functools
import jax
import jax.numpy as jnp
from jax import lax
from jax.experimental import pallas as pl
from jax.experimental.pallas import tpu as pltpu
from jax.sharding import PartitionSpec as P

damping_ratio = 0.1
LANES = 128
GROUPS = 2
f32 = jnp.float32
bf16 = jnp.bfloat16


def dot(left, right):
    return lax.dot_general(left, right, (((1,), (0,)), ((), ())), preferred_element_type=f32)


def parts_of(value):
    high = value.astype(bf16)
    return high, (value - high.astype(f32)).astype(bf16)


def call(kernel, outs, args, scratch=()):
    spec = pl.BlockSpec(memory_space=pltpu.VMEM)
    return pl.pallas_call(
        kernel,
        out_shape=[jax.ShapeDtypeStruct(shape, dtype) for shape, dtype in outs],
        in_specs=[spec] * len(args),
        out_specs=[spec] * len(outs),
        scratch_shapes=[pltpu.VMEM(shape, dtype) for shape, dtype in scratch],
        compiler_params=pltpu.CompilerParams(vmem_limit_bytes=16 << 20),
    )(*args)


def split_kernel(down_ref, high_ref, low_ref, turned_high_ref, turned_low_ref, energy_ref):
    rows, shots = down_ref.shape[1:]
    width = 2 * LANES
    energy_ref[...] = jnp.zeros_like(energy_ref)

    def step(index, carry):
        at = pl.ds(pl.multiple_of(index * width, width), width)
        for part in range(2):
            value = down_ref[part, :, at]
            high, low = parts_of(value)
            high_ref[part, :, at] = high
            low_ref[part, :, at] = low
            turned_high_ref[part, at, :] = high.T
            turned_low_ref[part, at, :] = low.T
            energy_ref[...] += jnp.sum((value * value).reshape(rows // 8, 8, width), axis=0)
        return carry

    lax.fori_loop(0, shots // width, step, 0)


def split(value):
    _, rows, shots = value.shape
    plain, turned = ((2, rows, shots), bf16), ((2, shots, rows), bf16)
    high, low, turned_high, turned_low, energy = call(
        split_kernel, [plain, plain, turned, turned, ((8, 2 * LANES), f32)], (value,)
    )
    return (high, low), (turned_high, turned_low), energy


def stage(value_ref, first_ref, second_ref, sign):
    half = value_ref.shape[0] // 2
    real = value_ref[:half, :]
    imag = value_ref[half:, :]
    for at, (a, b) in enumerate(zip(parts_of(real), parts_of(imag))):
        base = 2 * half * at
        first_ref[base : base + half, :] = a
        first_ref[base + half : base + 2 * half, :] = b
        second_ref[base : base + half, :] = b if sign > 0 else -b
        second_ref[base + half : base + 2 * half, :] = a if sign < 0 else -a


def times(first, second, high_ref, low_ref, columns=slice(None)):
    count = first.shape[0] // 2
    total = dot(first, high_ref[0, :, columns]) + dot(second, high_ref[1, :, columns])
    low = dot(first[:count], low_ref[0, :, columns]) + dot(second[:count], low_ref[1, :, columns])
    return total[:count] + total[count:] + low


def row_squares(value):
    return jnp.sum(value * value, axis=1, keepdims=True)


def both(value):
    half = value.shape[0] // 2
    total = value[:half] + value[half:]
    return jnp.concatenate([total, total], axis=0)


def tail(*columns):
    lane = lax.broadcasted_iota(jnp.int32, (columns[0].shape[0], LANES), 1)
    out = jnp.zeros(lane.shape, f32)
    for at, column in enumerate(columns):
        out = jnp.where(lane == at, column, out)
    return out


def apply_down(x_ref, first_ref, second_ref, turned, image_ref):
    stage(x_ref, first_ref, second_ref, -1)
    rows = turned[0][0].shape[2]
    for at, (high, low) in enumerate(turned):
        image_ref[:, at * rows : (at + 1) * rows] = times(first_ref[...], second_ref[...], high, low)


def device_bit(bit):
    return (lax.axis_index("rcv") >> bit) & 1


def project(value_ref, first_ref, second_ref, plain, extra, outs, bits):
    stage(value_ref, first_ref, second_ref, 1)
    rows = plain[0][0].shape[1]
    shots = plain[0][0].shape[2]
    half = value_ref.shape[0] // 2
    for at, bit in enumerate(bits):
        columns = slice(at * shots // 2, (at + 1) * shots // 2)
        total = 0.0
        for block, (high, low) in enumerate(plain):
            own = slice(block * rows, (block + 1) * rows)
            total = total + times(first_ref[:, own], second_ref[:, own], high, low, columns)
        pieces = [(slice(0, shots // 2), total)]
        if at == 0:
            pieces.append((slice(shots // 2, shots // 2 + LANES), extra))
        keep_ref, give_ref = outs[2 * at : 2 * at + 2]
        upper = device_bit(bit) == 1
        for place, piece in pieces:
            keep_ref[:, place] = jnp.where(upper, piece[half:], piece[:half])
            give_ref[:, place] = jnp.where(upper, piece[:half], piece[half:])


def collect(pieces, x_ref, ends_ref, bits):
    front = x_ref.shape[1] // 2
    for at, bit in enumerate(bits):
        upper = device_bit(bit)
        for which, piece in enumerate(pieces[2 * at : 2 * at + 2]):
            half = piece.shape[0]
            place = pl.ds(pl.multiple_of((upper ^ which) * half, half), half)
            x_ref[place, at * front : (at + 1) * front] = piece[:, :front]
            if at == 0:
                ends_ref[place, :] = piece[:, front:]


def rhs_kernel(bits, *refs):
    real_ref, imag_ref, *refs = refs
    down, refs = refs[:8], refs[8:]
    (ea, eb), (rhs_ref, *outs), (x_ref, f0, s0, f1, s1) = refs[:2], refs[2:7], refs[7:]
    half = real_ref.shape[0]
    x_ref[:half, :] = real_ref[...]
    x_ref[half:, :] = -imag_ref[...]
    apply_down(x_ref, f0, s0, ((down[4], down[5]), (down[6], down[7])), rhs_ref)
    energy = jnp.full((2 * half, 1), jnp.sum(ea[...] + eb[...]), f32)
    extra = tail(row_squares(rhs_ref[...]), energy)
    project(rhs_ref, f1, s1, ((down[0], down[1]), (down[2], down[3])), extra, outs, bits)


def first_kernel(bits, receivers, *refs):
    pieces, (rhs_ref, *refs) = refs[:4], refs[4:]
    down, refs = refs[:8], refs[8:]
    (x_ref, scalar_ref, image_ref, residual_ref, *outs), (ends_ref, f0, s0, f1, s1) = refs[:8], refs[8:]
    collect(pieces, x_ref, ends_ref, bits)
    norm = both(ends_ref[:, 0:1])
    damping = damping_ratio * ends_ref[:, 1:2] / receivers
    apply_down(x_ref, f0, s0, ((down[4], down[5]), (down[6], down[7])), image_ref)
    image = image_ref[...] + damping * rhs_ref[...]
    image_ref[...] = image
    alpha = norm / (both(row_squares(x_ref[...])) + damping * norm)
    residual = rhs_ref[...] - alpha * image
    residual_ref[...] = residual
    scalar_ref[...] = tail(norm, damping, alpha)
    project(residual_ref, f1, s1, ((down[0], down[1]), (down[2], down[3])), tail(row_squares(residual)), outs, bits)


def last_kernel(bits, *refs):
    pieces, (rhs_ref, before_ref, scalar_ref, image_ref, residual_ref, *turned), refs = refs[:4], refs[4:13], refs[13:]
    keep_ref, give_ref, x_ref, ends_ref, y_ref, f0, s0 = refs
    collect(pieces, x_ref, ends_ref, bits)
    following = both(ends_ref[:, 0:1])
    norm = scalar_ref[:, 0:1]
    damping = scalar_ref[:, 1:2]
    alpha = scalar_ref[:, 2:3]
    beta = following / norm
    apply_down(x_ref, f0, s0, (turned[0:2], turned[2:4]), y_ref)
    residual = residual_ref[...]
    image = y_ref[...] + beta * image_ref[...] + damping * residual
    curvature = both(row_squares(x_ref[...] + beta * before_ref[...])) + damping * (following + beta * following)
    alpha_next = following / curvature
    rhs = rhs_ref[...]
    found = alpha * rhs + alpha_next * (residual + beta * rhs)
    left = residual - alpha_next * image
    rows = turned[0].shape[2]
    keep_ref[0] = found[:, :rows]
    keep_ref[1] = left[:, :rows]
    give_ref[0] = found[:, rows:]
    give_ref[1] = left[:, rows:]


def body(down_spectra, up_sources, *, count, receivers):
    me = lax.axis_index("rcv")
    chip_bits = list(range(1, count.bit_length() - 1))
    orders = (chip_bits, chip_bits[::-1])
    ends = (chip_bits[0], chip_bits[-1])
    rows, shots = down_spectra.shape[1:]
    own = up_sources.shape[1] // GROUPS
    chips = count // 2
    packed = 2 * chips * own
    front = shots // 2

    def swap(value, bit):
        return lax.ppermute(value, "rcv", [(at, at ^ (1 << bit)) for at in range(count)])

    def gather(block, order):
        block = block.reshape((1,) * len(chip_bits) + block.shape)
        for bit in order:
            axis = len(chip_bits) - bit
            other = swap(block, bit)
            upper = ((me >> bit) & 1) == 1
            block = jnp.concatenate([jnp.where(upper, other, block), jnp.where(upper, block, other)], axis=axis)
        return block.reshape((-1, shots))

    def exchange(outs):
        pieces = []
        for order, (keep, give) in zip(orders, (outs[0:2], outs[2:4])):
            keep = keep + swap(give, order[0])
            for bit in order[1:]:
                keep = keep + swap(keep, bit)
            pieces += [keep, swap(keep, order[0])]
        return pieces

    other_down = swap(down_spectra, 0)
    sources = []
    for group in range(GROUPS):
        part = up_sources[:, group * own : (group + 1) * own]
        sources.append((gather(part[0], orders[0]), gather(part[1], orders[1])))
    plain_a, turned_a, energy_a = split(down_spectra)
    plain_b, turned_b, energy_b = split(other_down)
    turned = (*turned_a, *turned_b)
    down = (*plain_a, *plain_b, *turned)

    wide = [((2 * packed, shots), bf16)] * 2
    short = [((2 * packed, 2 * rows), bf16)] * 2
    lines = ((packed, 2 * rows), f32)
    every = ((packed, shots), f32)
    small = ((packed, LANES), f32)
    halves = [((packed // 2, front + LANES), f32)] * 2 + [((packed // 2, front), f32)] * 2

    outs = [
        call(functools.partial(rhs_kernel, ends), [lines] + halves, (*pair, *down, energy_a, energy_b), [every] + wide + short)
        for pair in sources
    ]
    rhs = [out[0] for out in outs]
    sums = [exchange(out[1:]) for out in outs]
    outs = [
        call(
            functools.partial(first_kernel, ends, receivers),
            [every, small, lines, lines] + halves,
            (*sums[group], rhs[group], *down),
            [small] + wide + short,
        )
        for group in range(GROUPS)
    ]
    sums = [exchange(out[4:]) for out in outs]
    results = []
    for group in range(GROUPS):
        keep, give = call(
            functools.partial(last_kernel, ends),
            [((2, packed, rows), f32)] * 2,
            (*sums[group], rhs[group], *outs[group][:4], *turned),
            [every, small, lines] + wide,
        )
        results.append((keep, swap(give, 0)))

    upper = (me & 1) == 1

    def order(first, second):
        parts = [jnp.stack([value.reshape(2, 2, chips, own, rows) for value in pair], axis=3) for pair in zip(first, second)]
        return jnp.stack(parts, axis=4).reshape(2, 2, -1, rows).transpose(0, 1, 3, 2)

    found = order(
        [jnp.where(upper, other, keep) for keep, other in results],
        [jnp.where(upper, keep, other) for keep, other in results],
    )
    return found[0], found[1]


def solution(mesh):
    count = mesh.shape["rcv"]

    def run(down_spectra, up_sources):
        return body(down_spectra, up_sources, count=count, receivers=down_spectra.shape[1] * count)

    specs = (P("cuts", "rcv", None), P("cuts", "rcv", None))
    return jax.shard_map(run, mesh=mesh, in_specs=specs, out_specs=specs, check_vma=False)
```

time: 110 us -> 108 us (0.982)
  waiting for transfers between devices: 63.1 us -> 20 us
  starting transfers between devices: 14.8 us -> 36.8 us
  local copies, waits for them, and re-layouts: 7.39 us -> 19.2 us
  Pallas kernels: 22.8 us -> 28.4 us
  other arithmetic: 0.63 us -> 2.3 us
    ppermute x14 -> x35, waiting for transfers between devices: 63.1 us -> 20 us  [swap(): lax.ppermute(value, 'rcv', [(at, at ^ 1 << bit) for at in range(count)])]
    ppermute x14 -> x35, starting transfers between devices: 14.8 us -> 36.8 us  [swap(): lax.ppermute(value, 'rcv', [(at, at ^ 1 << bit) for at in range(count)])]
    unnamed x14 -> x44, local copies, waits for them, and re-layouts: 5.67 us -> 17.5 us
    pallas_call x7 -> x8, Pallas kernels: 22.8 us -> 28.4 us  [call(): pl.pallas_call(kernel, out_shape=[jax.ShapeDtypeStruct(shape, dtype) for...]
  transfers between devices with their start and end apart: 14 -> 35, of which waited for: 10 -> 13; matrix products, arithmetic and copies ran while one was open for 2% -> 4% of each run, Pallas kernels for 3% -> 18%
where the time goes in v1:
time: 108 us
  starting transfers between devices  36.8 us (34%)
  Pallas kernels  28.4 us (26%)
  waiting for transfers between devices  20 us (19%)
  local copies, waits for them, and re-layouts  19.2 us (18%)
  other arithmetic  2.3 us (2%)
    ppermute x35, starting transfers between devices, swap(): lax.ppermute(value, 'rcv', [(at, at ^ 1 << bit) for at in range(count)])  36.8 us
    pallas_call x8, Pallas kernels, call(): pl.pallas_call(kernel, out_shape=[jax.ShapeDtypeStruct(shape, dtype) for...  28.4 us
    ppermute x35, waiting for transfers between devices, swap(): lax.ppermute(value, 'rcv', [(at, at ^ 1 << bit) for at in range(count)])  20 us
    unnamed x44, local copies, waits for them, and re-layouts  17.5 us
  transfers between devices with their start and end apart: 35, of which 13 were waited for; matrix products, arithmetic and copies ran while one was open for 4% of the time, Pallas kernels for 18%

profile of v1, /device:TPU:0, one launch (start us, length us, event | category | flops | bytes accessed | tf_op | source)
XLA Modules:
  0.0 107.7 jit_solution(17312686236355879194)
XLA Ops:
  0.6 0.5 collective-permute-start.4
  1.1 1.7 %slice_bitcast_fusion.4 = (f32[1,1,8,2560]{3,2,1,0:T(8,128)S(1)}, f32[1,1,8,2560]{3,2,1,0:T(8,128)}, f32[1,1,8,2560]{3,2,1,0:T(8,128)S(1)}, f32[1,1,8,2560]{3,2,1,0:T(8,128)S(1)}) fusion(f32[2,16,2560]{2,1,0:T(8,128)} %param.3), kind=kLoop, calls=%fused_computation.15 | loop fusion | bytes 655360 | tf_op jit(solution)/shard_map/reshape;squeeze | solution.py:216
  2.8 2.5 %collective-permute-start = (f32[1,1,8,2560]{3,2,1,0:T(8,128)}, f32[1,1,8,2560]{3,2,1,0:T(8,128)S(1)}, u32[]{:S(2)}, u32[]{:S(2)}) collective-permute-start(f32[1,1,8,2560]{3,2,1,0:T(8,128)} %get-tuple-element.103), channel_id=1, source_target_pairs={{0,2},{1,3},{2,0},{3,1},{4,6},{5,7},{6,4},{7,5},{8,10},{9,11},{10,... | collective-permute-start | bytes 245768 | tf_op jit(solution)/shard_map/ppermute | solution.py:213
  5.3 2.0 %collective-permute-start.2 = (f32[1,1,8,2560]{3,2,1,0:T(8,128)S(1)}, f32[1,1,8,2560]{3,2,1,0:T(8,128)S(1)}, u32[]{:S(2)}, u32[]{:S(2)}) collective-permute-start(f32[1,1,8,2560]{3,2,1,0:T(8,128)S(1)} %get-tuple-element.102), channel_id=1, source_target_pairs={{0,4},{1,5},{2,6},{3,7},{4,0},{5,1},{6,2},{7,3},{8,12},{9,13},{10,... | collective-permute-start | bytes 245768 | tf_op jit(solution)/shard_map/ppermute | solution.py:213
  7.4 2.5 %copy-done.11 = f32[2,256,2560]{2,1,0:T(8,128)S(1)} copy-done((f32[2,256,2560]{2,1,0:T(8,128)S(1)}, f32[2,256,2560]{2,1,0:T(8,128)}, u32[]{:S(2)}) %copy-start.11) | copy-done | bytes 5242904
  9.9 2.0 %shard_map.41 = (bf16[2,256,2560]{2,1,0:T(8,128)(2,1)S(1)}, bf16[2,256,2560]{2,1,0:T(8,128)(2,1)S(1)}, bf16[2,2560,256]{2,1,0:T(8,128)(2,1)S(1)}, bf16[2,2560,256]{2,1,0:T(8,128)(2,1)S(1)}, f32[8,256]{1,0:T(8,128)S(1)}) custom-call(f32[2,256,2560]{2,1,0:T(8,128)S(1)} %copy-done.11), custom_call_target="tpu_custom_call" | custom-call | tf_op jit(solution)/shard_map/pallas_call | solution.py:27
  11.9 1.5 %copy-done = bf16[2,2560,256]{2,1,0:T(8,128)(2,1)} copy-done((bf16[2,2560,256]{2,1,0:T(8,128)(2,1)}, bf16[2,2560,256]{2,1,0:T(8,128)(2,1)S(1)}, u32[]{:S(2)}) %copy-start) | copy-done | bytes 2621464
  13.5 1.6 %copy-done.7 = bf16[2,256,2560]{2,1,0:T(8,128)(2,1)} copy-done((bf16[2,256,2560]{2,1,0:T(8,128)(2,1)}, bf16[2,256,2560]{2,1,0:T(8,128)(2,1)S(1)}, u32[]{:S(2)}) %copy-start.7) | copy-done | bytes 2621464
  15.0 1.6 %copy-done.9 = bf16[2,256,2560]{2,1,0:T(8,128)(2,1)} copy-done((bf16[2,256,2560]{2,1,0:T(8,128)(2,1)}, bf16[2,256,2560]{2,1,0:T(8,128)(2,1)S(1)}, u32[]{:S(2)}) %copy-start.9) | copy-done | bytes 2621464
  16.7 2.0 %collective-permute-start.21 = (f32[2,1,8,2560]{3,2,1,0:T(8,128)S(1)}, f32[2,1,8,2560]{3,2,1,0:T(8,128)S(1)}, u32[]{:S(2)}, u32[]{:S(2)}) collective-permute-start(f32[2,1,8,2560]{3,2,1,0:T(8,128)S(1)} %pad_maximum_fusion.8), channel_id=1, source_target_pairs={{0,2},{1,3},{2,0},{3,1},{4,6},{5,7},{6,4},{7,5},{8,10},{9,11},{10,... | collective-permute-start | bytes 491528 | tf_op jit(solution)/shard_map/ppermute | solution.py:213
  18.9 2.1 %collective-permute-start.1 = (f32[1,2,8,2560]{3,2,1,0:T(8,128)S(1)}, f32[1,2,8,2560]{3,2,1,0:T(8,128)S(1)}, u32[]{:S(2)}, u32[]{:S(2)}) collective-permute-start(f32[1,2,8,2560]{3,2,1,0:T(8,128)S(1)} %pad_maximum_fusion.5), channel_id=1, source_target_pairs={{0,4},{1,5},{2,6},{3,7},{4,0},{5,1},{6,2},{7,3},{8,12},{9,13},{10,... | collective-permute-start | bytes 491528 | tf_op jit(solution)/shard_map/ppermute | solution.py:213
  21.1 2.8 %collective-permute-done.21 = f32[2,1,8,2560]{3,2,1,0:T(8,128)S(1)} collective-permute-done((f32[2,1,8,2560]{3,2,1,0:T(8,128)S(1)}, f32[2,1,8,2560]{3,2,1,0:T(8,128)S(1)}, u32[]{:S(2)}, u32[]{:S(2)}) %collective-permute-start.21) | collective-permute-done | bytes 163872 | tf_op jit(solution)/shard_map/ppermute | solution.py:213
  23.9 2.1 %collective-permute-done.3 = f32[2,1,8,2560]{3,2,1,0:T(8,128)S(1)} collective-permute-done((f32[2,1,8,2560]{3,2,1,0:T(8,128)S(1)}, f32[2,1,8,2560]{3,2,1,0:T(8,128)S(1)}, u32[]{:S(2)}, u32[]{:S(2)}) %collective-permute-start.3) | collective-permute-done | bytes 163872 | tf_op jit(solution)/shard_map/ppermute | solution.py:213
  26.2 1.5 %collective-permute-done.19 = f32[1,2,8,2560]{3,2,1,0:T(8,128)S(1)} collective-permute-done((f32[1,2,8,2560]{3,2,1,0:T(8,128)S(1)}, f32[1,2,8,2560]{3,2,1,0:T(8,128)S(1)}, u32[]{:S(2)}, u32[]{:S(2)}) %collective-permute-start.19) | collective-permute-done | bytes 163872 | tf_op jit(solution)/shard_map/ppermute | solution.py:213
  27.8 4.7 %shard_map.42 = (bf16[2,256,2560]{2,1,0:T(8,128)(2,1)S(1)}, bf16[2,256,2560]{2,1,0:T(8,128)(2,1)S(1)}, bf16[2,2560,256]{2,1,0:T(8,128)(2,1)S(1)}, bf16[2,2560,256]{2,1,0:T(8,128)(2,1)S(1)}, f32[8,256]{1,0:T(8,128)S(1)}) custom-call(f32[2,256,2560]{2,1,0:T(8,128)} %collective-permute-done.4.down_ref), custom_call_target="tpu_custom_call" | custom-call | tf_op jit(solution)/shard_map/pallas_call | solution.py:27
  32.6 4.1 %shard_map.43 = (f32[64,512]{1,0:T(8,128)S(1)}, f32[32,1408]{1,0:T(8,128)S(1)}, f32[32,1408]{1,0:T(8,128)S(1)}, f32[32,1280]{1,0:T(8,128)S(1)}, f32[32,1280]{1,0:T(8,128)S(1)}) custom-call(f32[32,2560]{1,0:T(8,128)S(1)} %bitcast.53, f32[32,2560]{1,0:T(8,128)S(1)} %bitcast.51, bf16[2,256,2560]{2,1,0:T(8,128)(2,1)S(1)} %copy-done.8, ...), custom_call_target="tpu_custom_call" | custom-call | tf_op jit(solution)/shard_map/pallas_call | solution.py:27
  36.7 1.8 %collective-permute-start.8 = (f32[32,1280]{1,0:T(8,128)S(1)}, f32[32,1280]{1,0:T(8,128)S(1)}, u32[]{:S(2)}, u32[]{:S(2)}) collective-permute-start(f32[32,1280]{1,0:T(8,128)S(1)} %get-tuple-element.55), channel_id=1, source_target_pairs={{0,4},{1,5},{2,6},{3,7},{4,0},{5,1},{6,2},{7,3},{8,12},{9,13},{10,... | collective-permute-start | bytes 491528 | tf_op jit(solution)/shard_map/ppermute | solution.py:213
  38.5 1.5 %collective-permute-start.5 = (f32[32,1408]{1,0:T(8,128)S(1)}, f32[32,1408]{1,0:T(8,128)S(1)}, u32[]{:S(2)}, u32[]{:S(2)}) collective-permute-start(f32[32,1408]{1,0:T(8,128)S(1)} %get-tuple-element.53), channel_id=1, source_target_pairs={{0,2},{1,3},{2,0},{3,1},{4,6},{5,7},{6,4},{7,5},{8,10},{9,11},{10,... | collective-permute-start | bytes 540680 | tf_op jit(solution)/shard_map/ppermute | solution.py:213
  40.0 4.1 %shard_map.46 = (f32[64,512]{1,0:T(8,128)S(1)}, f32[32,1408]{1,0:T(8,128)S(1)}, f32[32,1408]{1,0:T(8,128)S(1)}, f32[32,1280]{1,0:T(8,128)S(1)}, f32[32,1280]{1,0:T(8,128)S(1)}) custom-call(f32[32,2560]{1,0:T(8,128)S(1)} %bitcast.54, f32[32,2560]{1,0:T(8,128)S(1)} %bitcast.52, bf16[2,256,2560]{2,1,0:T(8,128)(2,1)S(1)} %copy-done.8, ...), custom_call_target="tpu_custom_call" | custom-call | tf_op jit(solution)/shard_map/pallas_call | solution.py:27
  44.1 0.6 collective-permute-start.22
  44.7 0.3 collective-permute-start.25
  45.1 1.7 %collective-permute-start.6 = (f32[32,1408]{1,0:T(8,128)S(1)}, f32[32,1408]{1,0:T(8,128)S(1)}, u32[]{:S(2)}, u32[]{:S(2)}) collective-permute-start(f32[32,1408]{1,0:T(8,128)S(1)} %add.48), channel_id=1, source_target_pairs={{0,4},{1,5},{2,6},{3,7},{4,0},{5,1},{6,2},{7,3},{8,12},{9,13},{10,... | collective-permute-start | bytes 540680 | tf_op jit(solution)/shard_map/ppermute | solution.py:213
  46.8 1.6 %collective-permute-start.9 = (f32[32,1280]{1,0:T(8,128)S(1)}, f32[32,1280]{1,0:T(8,128)S(1)}, u32[]{:S(2)}, u32[]{:S(2)}) collective-permute-start(f32[32,1280]{1,0:T(8,128)S(1)} %add.50), channel_id=1, source_target_pairs={{0,2},{1,3},{2,0},{3,1},{4,6},{5,7},{6,4},{7,5},{8,10},{9,11},{10,... | collective-permute-start | bytes 491528 | tf_op jit(solution)/shard_map/ppermute | solution.py:213
  48.4 2.2 %collective-permute-done.22 = f32[32,1408]{1,0:T(8,128)S(1)} collective-permute-done((f32[32,1408]{1,0:T(8,128)S(1)}, f32[32,1408]{1,0:T(8,128)S(1)}, u32[]{:S(2)}, u32[]{:S(2)}) %collective-permute-start.22) | collective-permute-done | bytes 180256 | tf_op jit(solution)/shard_map/ppermute | solution.py:213
  50.6 0.8 collective-permute-done.25
  51.5 1.7 %collective-permute-start.26 = (f32[32,1280]{1,0:T(8,128)S(1)}, f32[32,1280]{1,0:T(8,128)S(1)}, u32[]{:S(2)}, u32[]{:S(2)}) collective-permute-start(f32[32,1280]{1,0:T(8,128)S(1)} %add.58), channel_id=1, source_target_pairs={{0,2},{1,3},{2,0},{3,1},{4,6},{5,7},{6,4},{7,5},{8,10},{9,11},{10,... | collective-permute-start | bytes 491528 | tf_op jit(solution)/shard_map/ppermute | solution.py:213
  53.2 2.1 %collective-permute-done.6 = f32[32,1408]{1,0:T(8,128)S(1)} collective-permute-done((f32[32,1408]{1,0:T(8,128)S(1)}, f32[32,1408]{1,0:T(8,128)S(1)}, u32[]{:S(2)}, u32[]{:S(2)}) %collective-permute-start.6) | collective-permute-done | bytes 180256 | tf_op jit(solution)/shard_map/ppermute | solution.py:213
  55.4 1.7 %collective-permute-start.7 = (f32[32,1408]{1,0:T(8,128)S(1)}, f32[32,1408]{1,0:T(8,128)S(1)}, u32[]{:S(2)}, u32[]{:S(2)}) collective-permute-start(f32[32,1408]{1,0:T(8,128)S(1)} %add.49.refs_0_), channel_id=1, source_target_pairs={{0,2},{1,3},{2,0},{3,1},{4,6},{5,7},{6,4},{7,5},{8,10},{9,11},{10,... | collective-permute-start | bytes 540680 | tf_op jit(solution)/shard_map/ppermute | solution.py:213
  57.1 0.6 collective-permute-start.10
  57.7 1.0 collective-permute-done.23
  58.7 2.2 %collective-permute-start.24 = (f32[32,1408]{1,0:T(8,128)S(1)}, f32[32,1408]{1,0:T(8,128)S(1)}, u32[]{:S(2)}, u32[]{:S(2)}) collective-permute-start(f32[32,1408]{1,0:T(8,128)S(1)} %add.57.refs_0_), channel_id=1, source_target_pairs={{0,2},{1,3},{2,0},{3,1},{4,6},{5,7},{6,4},{7,5},{8,10},{9,11},{10,... | collective-permute-start | bytes 540680 | tf_op jit(solution)/shard_map/ppermute | solution.py:213
  60.9 0.6 collective-permute-start.27
  61.5 1.0 collective-permute-done.10.refs_3_
  62.5 4.0 %shard_map.44 = (f32[64,2560]{1,0:T(8,128)S(1)}, f32[64,128]{1,0:T(8,128)S(1)}, f32[64,512]{1,0:T(8,128)S(1)}, f32[64,512]{1,0:T(8,128)S(1)}, f32[32,1408]{1,0:T...) custom-call(f32[32,1408]{1,0:T(8,128)S(1)} %add.49.refs_0_, ...), custom_call_target="tpu_custom_call" | custom-call | tf_op jit(solution)/shard_map/pallas_call | solution.py:27
  66.5 0.5 collective-permute-start.11
  67.0 0.3 collective-permute-start.14
  67.3 4.2 %shard_map.47 = (f32[64,2560]{1,0:T(8,128)S(1)}, f32[64,128]{1,0:T(8,128)S(1)}, f32[64,512]{1,0:T(8,128)S(1)}, f32[64,512]{1,0:T(8,128)S(1)}, f32[32,1408]{1,0:T...) custom-call(f32[32,1408]{1,0:T(8,128)S(1)} %add.57.refs_0_, ...), custom_call_target="tpu_custom_call" | custom-call | tf_op jit(solution)/shard_map/pallas_call | solution.py:27
  71.5 1.9 %collective-permute-start.28 = (f32[32,1408]{1,0:T(8,128)S(1)}, f32[32,1408]{1,0:T(8,128)S(1)}, u32[]{:S(2)}, u32[]{:S(2)}) collective-permute-start(f32[32,1408]{1,0:T(8,128)S(1)} %get-tuple-element.73), channel_id=1, source_target_pairs={{0,2},{1,3},{2,0},{3,1},{4,6},{5,7},{6,4},{7,5},{8,10},{9,11},{10,... | collective-permute-start | bytes 540680 | tf_op jit(solution)/shard_map/ppermute | solution.py:213
  73.5 1.5 %collective-permute-start.31 = (f32[32,1280]{1,0:T(8,128)S(1)}, f32[32,1280]{1,0:T(8,128)S(1)}, u32[]{:S(2)}, u32[]{:S(2)}) collective-permute-start(f32[32,1280]{1,0:T(8,128)S(1)} %get-tuple-element.75), channel_id=1, source_target_pairs={{0,4},{1,5},{2,6},{3,7},{4,0},{5,1},{6,2},{7,3},{8,12},{9,13},{10,... | collective-permute-start | bytes 491528 | tf_op jit(solution)/shard_map/ppermute | solution.py:213
  75.0 0.6 collective-permute-start.12
  75.8 2.8 %collective-permute-done.28 = f32[32,1408]{1,0:T(8,128)S(1)} collective-permute-done((f32[32,1408]{1,0:T(8,128)S(1)}, f32[32,1408]{1,0:T(8,128)S(1)}, u32[]{:S(2)}, u32[]{:S(2)}) %collective-permute-start.28) | collective-permute-done | bytes 180256 | tf_op jit(solution)/shard_map/ppermute | solution.py:213
  78.7 2.1 %collective-permute-start.29 = (f32[32,1408]{1,0:T(8,128)S(1)}, f32[32,1408]{1,0:T(8,128)S(1)}, u32[]{:S(2)}, u32[]{:S(2)}) collective-permute-start(f32[32,1408]{1,0:T(8,128)S(1)} %add.60), channel_id=1, source_target_pairs={{0,4},{1,5},{2,6},{3,7},{4,0},{5,1},{6,2},{7,3},{8,12},{9,13},{10,... | collective-permute-start | bytes 540680 | tf_op jit(solution)/shard_map/ppermute | solution.py:213
  80.8 1.2 %collective-permute-start.32 = (f32[32,1280]{1,0:T(8,128)S(1)}, f32[32,1280]{1,0:T(8,128)S(1)}, u32[]{:S(2)}, u32[]{:S(2)}) collective-permute-start(f32[32,1280]{1,0:T(8,128)S(1)} %add.62), channel_id=1, source_target_pairs={{0,2},{1,3},{2,0},{3,1},{4,6},{5,7},{6,4},{7,5},{8,10},{9,11},{10,... | collective-permute-start | bytes 491528 | tf_op jit(solution)/shard_map/ppermute | solution.py:213
  82.0 0.5 collective-permute-done.12
  82.6 0.4 collective-permute-start.13
  83.0 2.2 %collective-permute-start.16 = (f32[32,1280]{1,0:T(8,128)S(1)}, f32[32,1280]{1,0:T(8,128)S(1)}, u32[]{:S(2)}, u32[]{:S(2)}) collective-permute-start(f32[32,1280]{1,0:T(8,128)S(1)} %add.55.refs_2_), channel_id=1, source_target_pairs={{0,4},{1,5},{2,6},{3,7},{4,0},{5,1},{6,2},{7,3},{8,12},{9,13},{10,... | collective-permute-start | bytes 491528 | tf_op jit(solution)/shard_map/ppermute | solution.py:213
  85.3 0.9 collective-permute-done.29
  86.2 1.2 %collective-permute-start.30 = (f32[32,1408]{1,0:T(8,128)S(1)}, f32[32,1408]{1,0:T(8,128)}, u32[]{:S(2)}, u32[]{:S(2)}) collective-permute-start(f32[32,1408]{1,0:T(8,128)S(1)} %add.61.refs_0_), channel_id=1, source_target_pairs={{0,2},{1,3},{2,0},{3,1},{4,6},{5,7},{6,4},{7,5},{8,10},{9,11},{10,... | collective-permute-start | bytes 540680 | tf_op jit(solution)/shard_map/ppermute | solution.py:213
  87.4 0.7 add.63.refs_2_
  88.0 0.8 collective-permute-start.33
  88.9 2.4 %shard_map.45 = (f32[2,64,256]{2,1,0:T(8,128)S(1)}, f32[2,64,256]{2,1,0:T(8,128)}) custom-call(f32[32,1408]{1,0:T(8,128)S(1)} %add.53.refs_0_, f32[32,1408]{1,0:T(8,128)S(1)} %collective-permute-done.13.refs_1_, f32[32,1280]{1,0:T(8,128)S(1)} %add.55.refs_2_, f32[32,1280]{1,0:T(8,128)S(1)} %collective-permute-done.16.refs_3_, ...), custom_call_target="tpu_custom_call" | custom-call | tf_op jit(solution)/shard_map/pallas_call | solution.py:27
  91.3 0.6 copy-done.18
  92.0 1.7 %collective-permute-done.33.refs_3_ = f32[32,1280]{1,0:T(8,128)} collective-permute-done((f32[32,1280]{1,0:T(8,128)}, f32[32,1280]{1,0:T(8,128)}, u32[]{:S(2)}, u32[]{:S(2)}) %collective-permute-start.33) | collective-permute-done | bytes 163872 | tf_op jit(solution)/shard_map/ppermute | solution.py:213
  93.7 1.7 %copy-done.2 = bf16[2,2560,256]{2,1,0:T(8,128)(2,1)S(1)} copy-done((bf16[2,2560,256]{2,1,0:T(8,128)(2,1)S(1)}, bf16[2,2560,256]{2,1,0:T(8,128)(2,1)}, u32[]{:S(2)}) %copy-start.2) | copy-done | bytes 2621464
  95.4 1.7 %copy-done.4 = bf16[2,2560,256]{2,1,0:T(8,128)(2,1)S(1)} copy-done((bf16[2,2560,256]{2,1,0:T(8,128)(2,1)S(1)}, bf16[2,2560,256]{2,1,0:T(8,128)(2,1)}, u32[]{:S(2)}) %copy-start.4) | copy-done | bytes 2621464
  97.2 1.7 %copy-done.6 = bf16[2,2560,256]{2,1,0:T(8,128)(2,1)S(1)} copy-done((bf16[2,2560,256]{2,1,0:T(8,128)(2,1)S(1)}, bf16[2,2560,256]{2,1,0:T(8,128)(2,1)}, u32[]{:S(2)}) %copy-start.6) | copy-done | bytes 2621464
  98.9 0.9 copy-done.13
  99.8 0.9 copy-done.15
  100.7 0.9 copy-done.17
  101.6 2.9 %shard_map.48 = (f32[2,64,256]{2,1,0:T(8,128)S(1)}, f32[2,64,256]{2,1,0:T(8,128)S(1)}) custom-call(f32[32,1408]{1,0:T(8,128)S(1)} %add.61.refs_0_, f32[32,1408]{1,0:T(8,128)} %collective-permute-done.30.refs_1_, f32[32,1280]{1,0:T(8,128)} %add.63.refs_2_, f32[32,1280]{1,0:T(8,128)} %collective-permute-done.33.refs_3_, f32[64,512]{1,0:T(8,128)S(1)} %copy-done.13, ...), custom_call_target="tpu_custom_call" | custom-call | tf_op jit(solution)/shard_map/pallas_call | solution.py:27
  104.6 0.9 broadcast_select_fusion.11
  105.6 0.4 collective-permute-done.34
  106.1 0.8 copy.10
  106.9 0.8 copy.9
  (92 shorter events, 1.6 us)
Async XLA Ops:
  0.6 27.2 %collective-permute-start.4 = (f32[2,256,2560]{2,1,0:T(8,128)}, f32[2,256,2560]{2,1,0:T(8,128)}, u32[]{:S(2)}, u32[]{:S(2)}) collective-permute-start(f32[2,256,2560]{2,1,0:T(8,128)} %down_ref.1), channel_id=1, source_target_pairs={{0,1},{1,0},{2,3},{3,2},{4,5},{5,4},{6,7},{7,6},{8,9},{9,8},{10,11... | collective-permute-start | bytes 15728648 | tf_op jit(solution)/shard_map/ppermute | solution.py:213
  2.8 13.8 %collective-permute-start = (f32[1,1,8,2560]{3,2,1,0:T(8,128)}, f32[1,1,8,2560]{3,2,1,0:T(8,128)S(1)}, u32[]{:S(2)}, u32[]{:S(2)}) collective-permute-start(f32[1,1,8,2560]{3,2,1,0:T(8,128)} %get-tuple-element.103), channel_id=1, source_target_pairs={{0,2},{1,3},{2,0},{3,1},{4,6},{5,7},{6,4},{7,5},{8,10},{9,11},{10,... | collective-permute-start | bytes 245768 | tf_op jit(solution)/shard_map/ppermute | solution.py:213
  5.3 11.3 %collective-permute-start.18 = (f32[1,1,8,2560]{3,2,1,0:T(8,128)S(1)}, f32[1,1,8,2560]{3,2,1,0:T(8,128)S(1)}, u32[]{:S(2)}, u32[]{:S(2)}) collective-permute-start(f32[1,1,8,2560]{3,2,1,0:T(8,128)S(1)} %get-tuple-element.105), channel_id=1, source_target_pairs={{0,2},{1,3},{2,0},{3,1},{4,6},{5,7},{6,4},{7,5},{8,10},{9,11},{10,... | collective-permute-start | bytes 245768 | tf_op jit(solution)/shard_map/ppermute | solution.py:213
  5.3 11.3 %collective-permute-start.2 = (f32[1,1,8,2560]{3,2,1,0:T(8,128)S(1)}, f32[1,1,8,2560]{3,2,1,0:T(8,128)S(1)}, u32[]{:S(2)}, u32[]{:S(2)}) collective-permute-start(f32[1,1,8,2560]{3,2,1,0:T(8,128)S(1)} %get-tuple-element.102), channel_id=1, source_target_pairs={{0,4},{1,5},{2,6},{3,7},{4,0},{5,1},{6,2},{7,3},{8,12},{9,13},{10,... | collective-permute-start | bytes 245768 | tf_op jit(solution)/shard_map/ppermute | solution.py:213
  7.4 9.3 %collective-permute-start.20 = (f32[1,1,8,2560]{3,2,1,0:T(8,128)S(1)}, f32[1,1,8,2560]{3,2,1,0:T(8,128)S(1)}, u32[]{:S(2)}, u32[]{:S(2)}) collective-permute-start(f32[1,1,8,2560]{3,2,1,0:T(8,128)S(1)} %get-tuple-element.104), channel_id=1, source_target_pairs={{0,4},{1,5},{2,6},{3,7},{4,0},{5,1},{6,2},{7,3},{8,12},{9,13},{10,... | collective-permute-start | bytes 245768 | tf_op jit(solution)/shard_map/ppermute | solution.py:213
  7.4 2.5 %copy-start.11 = (f32[2,256,2560]{2,1,0:T(8,128)S(1)}, f32[2,256,2560]{2,1,0:T(8,128)}, u32[]{:S(2)}) copy-start(f32[2,256,2560]{2,1,0:T(8,128)} %down_ref.1) | copy-start | bytes 15728644
  9.9 6.7 %copy-start.20 = (f32[2,16,2560]{2,1,0:T(8,128)S(1)}, f32[2,16,2560]{2,1,0:T(8,128)}, u32[]{:S(2)}) copy-start(f32[2,16,2560]{2,1,0:T(8,128)} %param.3) | copy-start | bytes 983044
  11.9 1.6 %copy-start = (bf16[2,2560,256]{2,1,0:T(8,128)(2,1)}, bf16[2,2560,256]{2,1,0:T(8,128)(2,1)S(1)}, u32[]{:S(2)}) copy-start(bf16[2,2560,256]{2,1,0:T(8,128)(2,1)S(1)} %get-tuple-element.47.refs_7_.refs_10_) | copy-start | bytes 7864324
  13.5 1.6 %copy-start.7 = (bf16[2,256,2560]{2,1,0:T(8,128)(2,1)}, bf16[2,256,2560]{2,1,0:T(8,128)(2,1)S(1)}, u32[]{:S(2)}) copy-start(bf16[2,256,2560]{2,1,0:T(8,128)(2,1)S(1)} %get-tuple-element.42.refs_2_.refs_5_) | copy-start | bytes 7864324
  15.0 1.6 %copy-start.9 = (bf16[2,256,2560]{2,1,0:T(8,128)(2,1)}, bf16[2,256,2560]{2,1,0:T(8,128)(2,1)S(1)}, u32[]{:S(2)}) copy-start(bf16[2,256,2560]{2,1,0:T(8,128)(2,1)S(1)} %get-tuple-element.43.refs_3_.refs_6_) | copy-start | bytes 7864324
  16.7 7.2 %collective-permute-start.21 = (f32[2,1,8,2560]{3,2,1,0:T(8,128)S(1)}, f32[2,1,8,2560]{3,2,1,0:T(8,128)S(1)}, u32[]{:S(2)}, u32[]{:S(2)}) collective-permute-start(f32[2,1,8,2560]{3,2,1,0:T(8,128)S(1)} %pad_maximum_fusion.8), channel_id=1, source_target_pairs={{0,2},{1,3},{2,0},{3,1},{4,6},{5,7},{6,4},{7,5},{8,10},{9,11},{10,... | collective-permute-start | bytes 491528 | tf_op jit(solution)/shard_map/ppermute | solution.py:213
  18.8 7.3 %collective-permute-start.3 = (f32[2,1,8,2560]{3,2,1,0:T(8,128)S(1)}, f32[2,1,8,2560]{3,2,1,0:T(8,128)S(1)}, u32[]{:S(2)}, u32[]{:S(2)}) collective-permute-start(f32[2,1,8,2560]{3,2,1,0:T(8,128)S(1)} %pad_maximum_fusion.6), channel_id=1, source_target_pairs={{0,2},{1,3},{2,0},{3,1},{4,6},{5,7},{6,4},{7,5},{8,10},{9,11},{10,... | collective-permute-start | bytes 491528 | tf_op jit(solution)/shard_map/ppermute | solution.py:213
  18.9 7.2 %collective-permute-start.1 = (f32[1,2,8,2560]{3,2,1,0:T(8,128)S(1)}, f32[1,2,8,2560]{3,2,1,0:T(8,128)S(1)}, u32[]{:S(2)}, u32[]{:S(2)}) collective-permute-start(f32[1,2,8,2560]{3,2,1,0:T(8,128)S(1)} %pad_maximum_fusion.5), channel_id=1, source_target_pairs={{0,4},{1,5},{2,6},{3,7},{4,0},{5,1},{6,2},{7,3},{8,12},{9,13},{10,... | collective-permute-start | bytes 491528 | tf_op jit(solution)/shard_map/ppermute | solution.py:213
  21.0 6.7 %collective-permute-start.19 = (f32[1,2,8,2560]{3,2,1,0:T(8,128)S(1)}, f32[1,2,8,2560]{3,2,1,0:T(8,128)S(1)}, u32[]{:S(2)}, u32[]{:S(2)}) collective-permute-start(f32[1,2,8,2560]{3,2,1,0:T(8,128)S(1)} %pad_maximum_fusion.7), channel_id=1, source_target_pairs={{0,4},{1,5},{2,6},{3,7},{4,0},{5,1},{6,2},{7,3},{8,12},{9,13},{10,... | collective-permute-start | bytes 491528 | tf_op jit(solution)/shard_map/ppermute | solution.py:213
  27.7 4.8 %copy-start.10 = (bf16[2,256,2560]{2,1,0:T(8,128)(2,1)S(1)}, bf16[2,256,2560]{2,1,0:T(8,128)(2,1)}, u32[]{:S(2)}) copy-start(bf16[2,256,2560]{2,1,0:T(8,128)(2,1)} %copy-done.9) | copy-start | bytes 7864324
  27.8 4.7 %copy-start.1 = (bf16[2,2560,256]{2,1,0:T(8,128)(2,1)S(1)}, bf16[2,2560,256]{2,1,0:T(8,128)(2,1)}, u32[]{:S(2)}) copy-start(bf16[2,2560,256]{2,1,0:T(8,128)(2,1)} %copy-done) | copy-start | bytes 7864324
  27.8 4.8 %copy-start.8 = (bf16[2,256,2560]{2,1,0:T(8,128)(2,1)S(1)}, bf16[2,256,2560]{2,1,0:T(8,128)(2,1)}, u32[]{:S(2)}) copy-start(bf16[2,256,2560]{2,1,0:T(8,128)(2,1)} %copy-done.7) | copy-start | bytes 7864324
  32.5 56.4 %copy-start.3 = (bf16[2,2560,256]{2,1,0:T(8,128)(2,1)}, bf16[2,2560,256]{2,1,0:T(8,128)(2,1)S(1)}, u32[]{:S(2)}) copy-start(bf16[2,2560,256]{2,1,0:T(8,128)(2,1)S(1)} %get-tuple-element.48.refs_8_.refs_11_) | copy-start | bytes 7864324
  32.5 56.4 %copy-start.5 = (bf16[2,2560,256]{2,1,0:T(8,128)(2,1)}, bf16[2,2560,256]{2,1,0:T(8,128)(2,1)S(1)}, u32[]{:S(2)}) copy-start(bf16[2,2560,256]{2,1,0:T(8,128)(2,1)S(1)} %get-tuple-element.49.refs_9_.refs_12_) | copy-start | bytes 7864324
  36.7 10.1 %collective-permute-start.8 = (f32[32,1280]{1,0:T(8,128)S(1)}, f32[32,1280]{1,0:T(8,128)S(1)}, u32[]{:S(2)}, u32[]{:S(2)}) collective-permute-start(f32[32,1280]{1,0:T(8,128)S(1)} %get-tuple-element.55), channel_id=1, source_target_pairs={{0,4},{1,5},{2,6},{3,7},{4,0},{5,1},{6,2},{7,3},{8,12},{9,13},{10,... | collective-permute-start | bytes 491528 | tf_op jit(solution)/shard_map/ppermute | solution.py:213
  38.5 6.6 %collective-permute-start.5 = (f32[32,1408]{1,0:T(8,128)S(1)}, f32[32,1408]{1,0:T(8,128)S(1)}, u32[]{:S(2)}, u32[]{:S(2)}) collective-permute-start(f32[32,1408]{1,0:T(8,128)S(1)} %get-tuple-element.53), channel_id=1, source_target_pairs={{0,2},{1,3},{2,0},{3,1},{4,6},{5,7},{6,4},{7,5},{8,10},{9,11},{10,... | collective-permute-start | bytes 540680 | tf_op jit(solution)/shard_map/ppermute | solution.py:213
  44.1 23.2 %copy-start.12 = (f32[64,512]{1,0:T(8,128)}, f32[64,512]{1,0:T(8,128)S(1)}, u32[]{:S(2)}) copy-start(f32[64,512]{1,0:T(8,128)S(1)} %get-tuple-element.71.refs_4_) | copy-start | bytes 393220
  44.1 6.5 %collective-permute-start.22 = (f32[32,1408]{1,0:T(8,128)S(1)}, f32[32,1408]{1,0:T(8,128)S(1)}, u32[]{:S(2)}, u32[]{:S(2)}) collective-permute-start(f32[32,1408]{1,0:T(8,128)S(1)} %get-tuple-element.68), channel_id=1, source_target_pairs={{0,2},{1,3},{2,0},{3,1},{4,6},{5,7},{6,4},{7,5},{8,10},{9,11},{10,... | collective-permute-start | bytes 540680 | tf_op jit(solution)/shard_map/ppermute | solution.py:213
  44.7 6.8 %collective-permute-start.25 = (f32[32,1280]{1,0:T(8,128)S(1)}, f32[32,1280]{1,0:T(8,128)S(1)}, u32[]{:S(2)}, u32[]{:S(2)}) collective-permute-start(f32[32,1280]{1,0:T(8,128)S(1)} %get-tuple-element.70), channel_id=1, source_target_pairs={{0,4},{1,5},{2,6},{3,7},{4,0},{5,1},{6,2},{7,3},{8,12},{9,13},{10,... | collective-permute-start | bytes 491528 | tf_op jit(solution)/shard_map/ppermute | solution.py:213
  45.1 10.3 %collective-permute-start.6 = (f32[32,1408]{1,0:T(8,128)S(1)}, f32[32,1408]{1,0:T(8,128)S(1)}, u32[]{:S(2)}, u32[]{:S(2)}) collective-permute-start(f32[32,1408]{1,0:T(8,128)S(1)} %add.48), channel_id=1, source_target_pairs={{0,4},{1,5},{2,6},{3,7},{4,0},{5,1},{6,2},{7,3},{8,12},{9,13},{10,... | collective-permute-start | bytes 540680 | tf_op jit(solution)/shard_map/ppermute | solution.py:213
  46.8 10.2 %collective-permute-start.9 = (f32[32,1280]{1,0:T(8,128)S(1)}, f32[32,1280]{1,0:T(8,128)S(1)}, u32[]{:S(2)}, u32[]{:S(2)}) collective-permute-start(f32[32,1280]{1,0:T(8,128)S(1)} %add.50), channel_id=1, source_target_pairs={{0,2},{1,3},{2,0},{3,1},{4,6},{5,7},{6,4},{7,5},{8,10},{9,11},{10,... | collective-permute-start | bytes 491528 | tf_op jit(solution)/shard_map/ppermute | solution.py:213
  50.6 8.1 %collective-permute-start.23 = (f32[32,1408]{1,0:T(8,128)S(1)}, f32[32,1408]{1,0:T(8,128)S(1)}, u32[]{:S(2)}, u32[]{:S(2)}) collective-permute-start(f32[32,1408]{1,0:T(8,128)S(1)} %add.56), channel_id=1, source_target_pairs={{0,4},{1,5},{2,6},{3,7},{4,0},{5,1},{6,2},{7,3},{8,12},{9,13},{10,... | collective-permute-start | bytes 540680 | tf_op jit(solution)/shard_map/ppermute | solution.py:213
  51.5 9.4 %collective-permute-start.26 = (f32[32,1280]{1,0:T(8,128)S(1)}, f32[32,1280]{1,0:T(8,128)S(1)}, u32[]{:S(2)}, u32[]{:S(2)}) collective-permute-start(f32[32,1280]{1,0:T(8,128)S(1)} %add.58), channel_id=1, source_target_pairs={{0,2},{1,3},{2,0},{3,1},{4,6},{5,7},{6,4},{7,5},{8,10},{9,11},{10,... | collective-permute-start | bytes 491528 | tf_op jit(solution)/shard_map/ppermute | solution.py:213
  55.4 7.1 %collective-permute-start.7 = (f32[32,1408]{1,0:T(8,128)S(1)}, f32[32,1408]{1,0:T(8,128)S(1)}, u32[]{:S(2)}, u32[]{:S(2)}) collective-permute-start(f32[32,1408]{1,0:T(8,128)S(1)} %add.49.refs_0_), channel_id=1, source_target_pairs={{0,2},{1,3},{2,0},{3,1},{4,6},{5,7},{6,4},{7,5},{8,10},{9,11},{10,... | collective-permute-start | bytes 540680 | tf_op jit(solution)/shard_map/ppermute | solution.py:213
  57.1 5.4 %collective-permute-start.10 = (f32[32,1280]{1,0:T(8,128)S(1)}, f32[32,1280]{1,0:T(8,128)S(1)}, u32[]{:S(2)}, u32[]{:S(2)}) collective-permute-start(f32[32,1280]{1,0:T(8,128)S(1)} %add.51.refs_2_), channel_id=1, source_target_pairs={{0,4},{1,5},{2,6},{3,7},{4,0},{5,1},{6,2},{7,3},{8,12},{9,13},{10,... | collective-permute-start | bytes 491528 | tf_op jit(solution)/shard_map/ppermute | solution.py:213
  58.7 8.6 %collective-permute-start.24 = (f32[32,1408]{1,0:T(8,128)S(1)}, f32[32,1408]{1,0:T(8,128)S(1)}, u32[]{:S(2)}, u32[]{:S(2)}) collective-permute-start(f32[32,1408]{1,0:T(8,128)S(1)} %add.57.refs_0_), channel_id=1, source_target_pairs={{0,2},{1,3},{2,0},{3,1},{4,6},{5,7},{6,4},{7,5},{8,10},{9,11},{10,... | collective-permute-start | bytes 540680 | tf_op jit(solution)/shard_map/ppermute | solution.py:213
  60.9 6.4 %collective-permute-start.27 = (f32[32,1280]{1,0:T(8,128)S(1)}, f32[32,1280]{1,0:T(8,128)S(1)}, u32[]{:S(2)}, u32[]{:S(2)}) collective-permute-start(f32[32,1280]{1,0:T(8,128)S(1)} %add.59.refs_2_), channel_id=1, source_target_pairs={{0,4},{1,5},{2,6},{3,7},{4,0},{5,1},{6,2},{7,3},{8,12},{9,13},{10,... | collective-permute-start | bytes 491528 | tf_op jit(solution)/shard_map/ppermute | solution.py:213
  66.5 8.4 %collective-permute-start.11 = (f32[32,1408]{1,0:T(8,128)S(1)}, f32[32,1408]{1,0:T(8,128)S(1)}, u32[]{:S(2)}, u32[]{:S(2)}) collective-permute-start(f32[32,1408]{1,0:T(8,128)S(1)} %get-tuple-element.58), channel_id=1, source_target_pairs={{0,2},{1,3},{2,0},{3,1},{4,6},{5,7},{6,4},{7,5},{8,10},{9,11},{10,... | collective-permute-start | bytes 540680 | tf_op jit(solution)/shard_map/ppermute | solution.py:213
  67.0 8.6 %collective-permute-start.14 = (f32[32,1280]{1,0:T(8,128)S(1)}, f32[32,1280]{1,0:T(8,128)S(1)}, u32[]{:S(2)}, u32[]{:S(2)}) collective-permute-start(f32[32,1280]{1,0:T(8,128)S(1)} %get-tuple-element.60), channel_id=1, source_target_pairs={{0,4},{1,5},{2,6},{3,7},{4,0},{5,1},{6,2},{7,3},{8,12},{9,13},{10,... | collective-permute-start | bytes 491528 | tf_op jit(solution)/shard_map/ppermute | solution.py:213
  71.5 11.5 %copy-start.16 = (f32[64,512]{1,0:T(8,128)}, f32[64,512]{1,0:T(8,128)S(1)}, u32[]{:S(2)}) copy-start(f32[64,512]{1,0:T(8,128)S(1)} %get-tuple-element.79.refs_8_) | copy-start | bytes 393220
  71.5 19.8 %copy-start.14 = (f32[64,512]{1,0:T(8,128)}, f32[64,512]{1,0:T(8,128)S(1)}, u32[]{:S(2)}) copy-start(f32[64,512]{1,0:T(8,128)S(1)} %get-tuple-element.78.refs_7_) | copy-start | bytes 393220
  71.5 7.1 %collective-permute-start.28 = (f32[32,1408]{1,0:T(8,128)S(1)}, f32[32,1408]{1,0:T(8,128)S(1)}, u32[]{:S(2)}, u32[]{:S(2)}) collective-permute-start(f32[32,1408]{1,0:T(8,128)S(1)} %get-tuple-element.73), channel_id=1, source_target_pairs={{0,2},{1,3},{2,0},{3,1},{4,6},{5,7},{6,4},{7,5},{8,10},{9,11},{10,... | collective-permute-start | bytes 540680 | tf_op jit(solution)/shard_map/ppermute | solution.py:213
  73.5 7.4 %collective-permute-start.31 = (f32[32,1280]{1,0:T(8,128)S(1)}, f32[32,1280]{1,0:T(8,128)S(1)}, u32[]{:S(2)}, u32[]{:S(2)}) collective-permute-start(f32[32,1280]{1,0:T(8,128)S(1)} %get-tuple-element.75), channel_id=1, source_target_pairs={{0,4},{1,5},{2,6},{3,7},{4,0},{5,1},{6,2},{7,3},{8,12},{9,13},{10,... | collective-permute-start | bytes 491528 | tf_op jit(solution)/shard_map/ppermute | solution.py:213
  75.0 7.6 %collective-permute-start.12 = (f32[32,1408]{1,0:T(8,128)S(1)}, f32[32,1408]{1,0:T(8,128)S(1)}, u32[]{:S(2)}, u32[]{:S(2)}) collective-permute-start(f32[32,1408]{1,0:T(8,128)S(1)} %add.52), channel_id=1, source_target_pairs={{0,4},{1,5},{2,6},{3,7},{4,0},{5,1},{6,2},{7,3},{8,12},{9,13},{10,... | collective-permute-start | bytes 540680 | tf_op jit(solution)/shard_map/ppermute | solution.py:213
  75.6 7.4 %collective-permute-start.15 = (f32[32,1280]{1,0:T(8,128)S(1)}, f32[32,1280]{1,0:T(8,128)S(1)}, u32[]{:S(2)}, u32[]{:S(2)}) collective-permute-start(f32[32,1280]{1,0:T(8,128)S(1)} %add.54), channel_id=1, source_target_pairs={{0,2},{1,3},{2,0},{3,1},{4,6},{5,7},{6,4},{7,5},{8,10},{9,11},{10,... | collective-permute-start | bytes 491528 | tf_op jit(solution)/shard_map/ppermute | solution.py:213
  78.7 7.5 %collective-permute-start.29 = (f32[32,1408]{1,0:T(8,128)S(1)}, f32[32,1408]{1,0:T(8,128)S(1)}, u32[]{:S(2)}, u32[]{:S(2)}) collective-permute-start(f32[32,1408]{1,0:T(8,128)S(1)} %add.60), channel_id=1, source_target_pairs={{0,4},{1,5},{2,6},{3,7},{4,0},{5,1},{6,2},{7,3},{8,12},{9,13},{10,... | collective-permute-start | bytes 540680 | tf_op jit(solution)/shard_map/ppermute | solution.py:213
  80.8 6.5 %collective-permute-start.32 = (f32[32,1280]{1,0:T(8,128)S(1)}, f32[32,1280]{1,0:T(8,128)S(1)}, u32[]{:S(2)}, u32[]{:S(2)}) collective-permute-start(f32[32,1280]{1,0:T(8,128)S(1)} %add.62), channel_id=1, source_target_pairs={{0,2},{1,3},{2,0},{3,1},{4,6},{5,7},{6,4},{7,5},{8,10},{9,11},{10,... | collective-permute-start | bytes 491528 | tf_op jit(solution)/shard_map/ppermute | solution.py:213
  82.6 6.3 %collective-permute-start.13 = (f32[32,1408]{1,0:T(8,128)S(1)}, f32[32,1408]{1,0:T(8,128)S(1)}, u32[]{:S(2)}, u32[]{:S(2)}) collective-permute-start(f32[32,1408]{1,0:T(8,128)S(1)} %add.53.refs_0_), channel_id=1, source_target_pairs={{0,2},{1,3},{2,0},{3,1},{4,6},{5,7},{6,4},{7,5},{8,10},{9,11},{10,... | collective-permute-start | bytes 540680 | tf_op jit(solution)/shard_map/ppermute | solution.py:213
  83.0 5.8 %collective-permute-start.16 = (f32[32,1280]{1,0:T(8,128)S(1)}, f32[32,1280]{1,0:T(8,128)S(1)}, u32[]{:S(2)}, u32[]{:S(2)}) collective-permute-start(f32[32,1280]{1,0:T(8,128)S(1)} %add.55.refs_2_), channel_id=1, source_target_pairs={{0,4},{1,5},{2,6},{3,7},{4,0},{5,1},{6,2},{7,3},{8,12},{9,13},{10,... | collective-permute-start | bytes 491528 | tf_op jit(solution)/shard_map/ppermute | solution.py:213
  86.2 7.5 %collective-permute-start.30 = (f32[32,1408]{1,0:T(8,128)S(1)}, f32[32,1408]{1,0:T(8,128)}, u32[]{:S(2)}, u32[]{:S(2)}) collective-permute-start(f32[32,1408]{1,0:T(8,128)S(1)} %add.61.refs_0_), channel_id=1, source_target_pairs={{0,2},{1,3},{2,0},{3,1},{4,6},{5,7},{6,4},{7,5},{8,10},{9,11},{10,... | collective-permute-start | bytes 540680 | tf_op jit(solution)/shard_map/ppermute | solution.py:213
  88.0 5.6 %collective-permute-start.33 = (f32[32,1280]{1,0:T(8,128)}, f32[32,1280]{1,0:T(8,128)}, u32[]{:S(2)}, u32[]{:S(2)}) collective-permute-start(f32[32,1280]{1,0:T(8,128)} %add.63.refs_2_), channel_id=1, source_target_pairs={{0,4},{1,5},{2,6},{3,7},{4,0},{5,1},{6,2},{7,3},{8,12},{9,13},{10,... | collective-permute-start | bytes 491528 | tf_op jit(solution)/shard_map/ppermute | solution.py:213
  91.3 0.6 copy-start.18
  92.0 12.6 %collective-permute-start.17 = (f32[2,64,256]{2,1,0:T(8,128)}, f32[2,64,256]{2,1,0:T(8,128)}, u32[]{:S(2)}, u32[]{:S(2)}) collective-permute-start(f32[2,64,256]{2,1,0:T(8,128)} %get-tuple-element.65), channel_id=1, source_target_pairs={{0,1},{1,0},{2,3},{3,2},{4,5},{5,4},{6,7},{7,6},{8,9},{9,8},{10,11... | collective-permute-start | bytes 393224 | tf_op jit(solution)/shard_map/ppermute | solution.py:213
  93.7 1.7 %copy-start.2 = (bf16[2,2560,256]{2,1,0:T(8,128)(2,1)S(1)}, bf16[2,2560,256]{2,1,0:T(8,128)(2,1)}, u32[]{:S(2)}) copy-start(bf16[2,2560,256]{2,1,0:T(8,128)(2,1)} %copy-done) | copy-start | bytes 7864324
  95.4 1.7 %copy-start.4 = (bf16[2,2560,256]{2,1,0:T(8,128)(2,1)S(1)}, bf16[2,2560,256]{2,1,0:T(8,128)(2,1)}, u32[]{:S(2)}) copy-start(bf16[2,2560,256]{2,1,0:T(8,128)(2,1)} %copy-done.3) | copy-start | bytes 7864324
  97.2 1.7 %copy-start.6 = (bf16[2,2560,256]{2,1,0:T(8,128)(2,1)S(1)}, bf16[2,2560,256]{2,1,0:T(8,128)(2,1)}, u32[]{:S(2)}) copy-start(bf16[2,2560,256]{2,1,0:T(8,128)(2,1)} %copy-done.5) | copy-start | bytes 7864324
  98.9 0.9 copy-start.13
  99.8 0.9 copy-start.15
  100.7 0.9 copy-start.17
  101.6 3.0 %copy-start.19 = (f32[2,64,256]{2,1,0:T(8,128)S(1)}, f32[2,64,256]{2,1,0:T(8,128)}, u32[]{:S(2)}) copy-start(f32[2,64,256]{2,1,0:T(8,128)} %copy-done.18) | copy-start | bytes 393220
  104.5 1.4 %collective-permute-start.34 = (f32[2,64,256]{2,1,0:T(8,128)S(1)}, f32[2,64,256]{2,1,0:T(8,128)S(1)}, u32[]{:S(2)}, u32[]{:S(2)}) collective-permute-start(f32[2,64,256]{2,1,0:T(8,128)S(1)} %get-tuple-element.80), channel_id=1, source_target_pairs={{0,1},{1,0},{2,3},{3,2},{4,5},{5,4},{6,7},{7,6},{8,9},{9,8},{10,11... | collective-permute-start | bytes 393224 | tf_op jit(solution)/shard_map/ppermute | solution.py:213

commit v2 on v1

--- a/solution.py
+++ b/solution.py
@@ -22,43 +22,51 @@
     return high, (value - high.astype(f32)).astype(bf16)
 
 
-def call(kernel, outs, args, scratch=()):
+def call(kernel, outs, args, scratch=(), flops=0, grid=(), in_specs=None):
     spec = pl.BlockSpec(memory_space=pltpu.VMEM)
+    moved = sum(value.size * value.dtype.itemsize for value in args)
     return pl.pallas_call(
         kernel,
         out_shape=[jax.ShapeDtypeStruct(shape, dtype) for shape, dtype in outs],
-        in_specs=[spec] * len(args),
+        grid=grid,
+        in_specs=in_specs or [spec] * len(args),
         out_specs=[spec] * len(outs),
         scratch_shapes=[pltpu.VMEM(shape, dtype) for shape, dtype in scratch],
+        cost_estimate=pl.CostEstimate(flops=flops, transcendentals=0, bytes_accessed=moved),
         compiler_params=pltpu.CompilerParams(vmem_limit_bytes=16 << 20),
     )(*args)
 
 
 def split_kernel(down_ref, high_ref, low_ref, turned_high_ref, turned_low_ref, energy_ref):
-    rows, shots = down_ref.shape[1:]
-    width = 2 * LANES
-    energy_ref[...] = jnp.zeros_like(energy_ref)
-
-    def step(index, carry):
-        at = pl.ds(pl.multiple_of(index * width, width), width)
-        for part in range(2):
-            value = down_ref[part, :, at]
-            high, low = parts_of(value)
-            high_ref[part, :, at] = high
-            low_ref[part, :, at] = low
-            turned_high_ref[part, at, :] = high.T
-            turned_low_ref[part, at, :] = low.T
-            energy_ref[...] += jnp.sum((value * value).reshape(rows // 8, 8, width), axis=0)
-        return carry
-
-    lax.fori_loop(0, shots // width, step, 0)
+    rows, width = down_ref.shape[1:]
+    step = pl.program_id(0)
+
+    @pl.when(step == 0)
+    def _():
+        energy_ref[...] = jnp.zeros_like(energy_ref)
+
+    at = pl.ds(pl.multiple_of(step * width, width), width)
+    for part in range(2):
+        value = down_ref[part]
+        high, low = parts_of(value)
+        high_ref[part, :, at] = high
+        low_ref[part, :, at] = low
+        turned_high_ref[part, at, :] = high.T
+        turned_low_ref[part, at, :] = low.T
+        square = jnp.sum((value * value).reshape(rows // 8, 8, width), axis=0)
+        energy_ref[...] += sum(square[:, lane : lane + LANES] for lane in range(0, width, LANES))
 
 
 def split(value):
     _, rows, shots = value.shape
+    width = 4 * LANES
     plain, turned = ((2, rows, shots), bf16), ((2, shots, rows), bf16)
     high, low, turned_high, turned_low, energy = call(
-        split_kernel, [plain, plain, turned, turned, ((8, 2 * LANES), f32)], (value,)
+        split_kernel,
+        [plain, plain, turned, turned, ((8, LANES), f32)],
+        (value,),
+        grid=(shots // width,),
+        in_specs=[pl.BlockSpec((2, rows, width), lambda step: (0, 0, step))],
     )
     return (high, low), (turned_high, turned_low), energy
 
@@ -144,13 +152,23 @@
                 ends_ref[place, :] = piece[:, front:]
 
 
-def rhs_kernel(bits, *refs):
-    real_ref, imag_ref, *refs = refs
+def rhs_kernel(bits, masks, *refs):
+    sources, refs = refs[:4], refs[4:]
     down, refs = refs[:8], refs[8:]
-    (ea, eb), (rhs_ref, *outs), (x_ref, f0, s0, f1, s1) = refs[:2], refs[2:7], refs[7:]
-    half = real_ref.shape[0]
-    x_ref[:half, :] = real_ref[...]
-    x_ref[half:, :] = -imag_ref[...]
+    (ea, eb), (rhs_ref, *outs), (x_ref, f0, s0, f1, s1, *spread) = refs[:2], refs[2:7], refs[7:]
+    half = x_ref.shape[0] // 2
+    own = sources[0].shape[1]
+    chip = lax.axis_index("rcv") >> 1
+    for part in range(2):
+        blocks = [ref[at] for ref in sources[2 * part : 2 * part + 2] for at in range(ref.shape[0])]
+        for mask, block in zip(masks[part], blocks):
+            value = block if part == 0 else -block
+            if spread:
+                spread[0][part * half // own + (chip ^ mask)] = value
+            else:
+                x_ref[pl.ds(pl.multiple_of(part * half + (chip ^ mask) * own, own), own), :] = value
+    for at in range(2 * half // own if spread else 0):
+        x_ref[at * own : (at + 1) * own, :] = spread[0][at]
     apply_down(x_ref, f0, s0, ((down[4], down[5]), (down[6], down[7])), rhs_ref)
     energy = jnp.full((2 * half, 1), jnp.sum(ea[...] + eb[...]), f32)
     extra = tail(row_squares(rhs_ref[...]), energy)
@@ -198,8 +216,25 @@
     give_ref[1] = left[:, rows:]
 
 
+def order_kernel(own, *refs):
+    pieces, (*outs, x_ref) = refs[: 2 * GROUPS], refs[2 * GROUPS :]
+    upper = device_bit(0) == 1
+    chips = pieces[0].shape[1] // (2 * own)
+    for which, out_ref in enumerate(outs):
+        for part in range(2):
+            for chip in range(chips):
+                source = pl.ds((part * chips + chip) * own, own)
+                for group in range(GROUPS):
+                    mine = pieces[2 * group][which, source, :]
+                    other = pieces[2 * group + 1][which, source, :]
+                    base = (2 * chip * GROUPS + group) * own
+                    x_ref[base : base + own, :] = jnp.where(upper, other, mine)
+                    base += GROUPS * own
+                    x_ref[base : base + own, :] = jnp.where(upper, mine, other)
+            out_ref[part] = x_ref[...].T
+
+
 def body(down_spectra, up_sources, *, count, receivers):
-    me = lax.axis_index("rcv")
     chip_bits = list(range(1, count.bit_length() - 1))
     orders = (chip_bits, chip_bits[::-1])
     ends = (chip_bits[0], chip_bits[-1])
@@ -213,13 +248,11 @@
         return lax.ppermute(value, "rcv", [(at, at ^ (1 << bit)) for at in range(count)])
 
     def gather(block, order):
-        block = block.reshape((1,) * len(chip_bits) + block.shape)
-        for bit in order:
-            axis = len(chip_bits) - bit
-            other = swap(block, bit)
-            upper = ((me >> bit) & 1) == 1
-            block = jnp.concatenate([jnp.where(upper, other, block), jnp.where(upper, block, other)], axis=axis)
-        return block.reshape((-1, shots))
+        blocks, masks = block[None], [0]
+        for bit in order[:-1]:
+            blocks = jnp.concatenate([blocks, swap(blocks, bit)], axis=0)
+            masks += [mask | 1 << bit - 1 for mask in masks]
+        return (blocks, swap(blocks, order[-1])), masks + [mask | 1 << order[-1] - 1 for mask in masks]
 
     def exchange(outs):
         pieces = []
@@ -234,7 +267,9 @@
     sources = []
     for group in range(GROUPS):
         part = up_sources[:, group * own : (group + 1) * own]
-        sources.append((gather(part[0], orders[0]), gather(part[1], orders[1])))
+        (real, real_masks), (imag, imag_masks) = gather(part[0], orders[0]), gather(part[1], orders[1])
+        sources.append((*real, *imag))
+    masks = (real_masks, imag_masks)
     plain_a, turned_a, energy_a = split(down_spectra)
     plain_b, turned_b, energy_b = split(other_down)
     turned = (*turned_a, *turned_b)
@@ -245,10 +280,18 @@
     lines = ((packed, 2 * rows), f32)
     every = ((packed, shots), f32)
     small = ((packed, LANES), f32)
+    work = 2 * 2 * 2 * (3 * packed) * 2 * rows * shots
     halves = [((packed // 2, front + LANES), f32)] * 2 + [((packed // 2, front), f32)] * 2
 
+    spread = [((packed // own, own, shots), f32)] if own % 8 else []
     outs = [
-        call(functools.partial(rhs_kernel, ends), [lines] + halves, (*pair, *down, energy_a, energy_b), [every] + wide + short)
+        call(
+            functools.partial(rhs_kernel, ends, masks),
+            [lines] + halves,
+            (*pair, *down, energy_a, energy_b),
+            [every] + wide + short + spread,
+            work,
+        )
         for pair in sources
     ]
     rhs = [out[0] for out in outs]
@@ -259,6 +302,7 @@
             [every, small, lines, lines] + halves,
             (*sums[group], rhs[group], *down),
             [small] + wide + short,
+            work,
         )
         for group in range(GROUPS)
     ]
@@ -270,20 +314,13 @@
             [((2, packed, rows), f32)] * 2,
             (*sums[group], rhs[group], *outs[group][:4], *turned),
             [every, small, lines] + wide,
+            work // 2,
         )
         results.append((keep, swap(give, 0)))
 
-    upper = (me & 1) == 1
-
-    def order(first, second):
-        parts = [jnp.stack([value.reshape(2, 2, chips, own, rows) for value in pair], axis=3) for pair in zip(first, second)]
-        return jnp.stack(parts, axis=4).reshape(2, 2, -1, rows).transpose(0, 1, 3, 2)
-
-    found = order(
-        [jnp.where(upper, other, keep) for keep, other in results],
-        [jnp.where(upper, keep, other) for keep, other in results],
-    )
-    return found[0], found[1]
+    pieces = [piece for pair in results for piece in pair]
+    columns = GROUPS * packed
+    return tuple(call(functools.partial(order_kernel, own), [((2, rows, columns), f32)] * 2, pieces, [((columns, rows), f32)]))
 
 
 def solution(mesh):

time: 108 us -> 86.6 us (0.80)
  local copies, waits for them, and re-layouts: 19.2 us -> 3.51 us
  waiting for transfers between devices: 20 us -> 15.2 us
  starting transfers between devices: 36.8 us -> 41.1 us
  Pallas kernels: 28.4 us -> 25.3 us
  other arithmetic: 2.3 us -> 0.44 us
    unnamed x44 -> x2, local copies, waits for them, and re-layouts: 17.5 us -> 2.49 us
    ppermute x35, waiting for transfers between devices: 20 us -> 15.2 us  [swap(): lax.ppermute(value, 'rcv', [(at, at ^ 1 << bit) for at in range(count)])]
    ppermute x35, starting transfers between devices: 36.8 us -> 41.1 us  [swap(): lax.ppermute(value, 'rcv', [(at, at ^ 1 << bit) for at in range(count)])]
    pallas_call x8 -> x9, Pallas kernels: 28.4 us -> 25.3 us  [call(): pl.pallas_call(kernel, out_shape=[jax.ShapeDtypeStruct(shape, dtype) for...]
    another operation x1 -> x0, local copies, waits for them, and re-layouts: 1.66 us -> none  [gather(): block = block.reshape((1,) * len(chip_bits) + block.shape)]
    select_n x5 -> x0, other arithmetic: 1.1 us -> none  [the longest x2 0.95 us: body(): jnp.where(upper, other, keep)]
  transfers between devices with their start and end apart: 35 -> 35, of which waited for: 13 -> 11; matrix products, arithmetic and copies ran while one was open for 4% -> 2% of each run, Pallas kernels for 18% -> 28%
where the time goes in v2:
time: 86.6 us; the launch traced here: 86.4 us
  starting transfers between devices  41.1 us (47%)
  Pallas kernels  25.3 us (29%)
  waiting for transfers between devices  15.2 us (18%)
  local copies, waits for them, and re-layouts  3.51 us (4%)
    ppermute x35, starting transfers between devices, swap(): lax.ppermute(value, 'rcv', [(at, at ^ 1 << bit) for at in range(count)])  41.1 us
    pallas_call x9, Pallas kernels, call(): pl.pallas_call(kernel, out_shape=[jax.ShapeDtypeStruct(shape, dtype) for...  25.3 us
    ppermute x35, waiting for transfers between devices, swap(): lax.ppermute(value, 'rcv', [(at, at ^ 1 << bit) for at in range(count)])  15.2 us
    unnamed x2, local copies, waits for them, and re-layouts  2.49 us
  transfers between devices with their start and end apart: 35, of which 11 were waited for; matrix products, arithmetic and copies ran while one was open for 2% of the time, Pallas kernels for 28%

profile of v2, /device:TPU:0, one launch (start us, length us, event | category | flops | bytes accessed | tf_op | source)
XLA Modules:
  0.0 86.4 jit_solution(11910142923093688326)
XLA Ops:
  0.6 0.5 collective-permute-start.4
  1.1 1.0 %fusion = (f32[1,8,2560]{2,1,0:T(8,128)S(1)}, f32[1,8,2560]{2,1,0:T(8,128)S(1)}, f32[1,8,2560]{2,1,0:T(8,128)S(1)}, f32[1,8,2560]{2,1,0:T(8,128)S(1)}) fusion(f32[2,16,2560]{2,1,0:T(8,128)} %param.3), kind=kLoop, calls=%fused_computation.4 | loop fusion | bytes 655360 | tf_op jit(solution)/shard_map/slice | solution.py:270
  2.2 2.6 %collective-permute-start.18 = (f32[1,8,2560]{2,1,0:T(8,128)S(1)}, f32[1,8,2560]{2,1,0:T(8,128)S(1)}, u32[]{:S(2)}, u32[]{:S(2)}) collective-permute-start(f32[1,8,2560]{2,1,0:T(8,128)S(1)} %get-tuple-element.85), channel_id=1, source_target_pairs={{0,2},{1,3},{2,0},{3,1},{4,6},{5,7},{6,4},{7,5},{8,10},{9,11},{10,... | collective-permute-start | bytes 245768 | tf_op jit(solution)/shard_map/ppermute | solution.py:248
  4.7 1.5 %collective-permute-start.20 = (f32[1,8,2560]{2,1,0:T(8,128)S(1)}, f32[1,8,2560]{2,1,0:T(8,128)S(1)}, u32[]{:S(2)}, u32[]{:S(2)}) collective-permute-start(f32[1,8,2560]{2,1,0:T(8,128)S(1)} %get-tuple-element.82), channel_id=1, source_target_pairs={{0,4},{1,5},{2,6},{3,7},{4,0},{5,1},{6,2},{7,3},{8,12},{9,13},{10,... | collective-permute-start | bytes 245768 | tf_op jit(solution)/shard_map/ppermute | solution.py:248
  6.3 0.5 collective-permute-start.2
  6.8 0.1 collective-permute-start
  6.9 2.5 %copy-done = f32[2,256,2560]{2,1,0:T(8,128)S(1)} copy-done((f32[2,256,2560]{2,1,0:T(8,128)S(1)}, f32[2,256,2560]{2,1,0:T(8,128)}, u32[]{:S(2)}) %copy-start) | copy-done | bytes 5242904
  9.3 2.2 %shard_map.41 = (bf16[2,256,2560]{2,1,0:T(8,128)(2,1)S(1)}, bf16[2,256,2560]{2,1,0:T(8,128)(2,1)S(1)}, bf16[2,2560,256]{2,1,0:T(8,128)(2,1)S(1)}, bf16[2,2560,256]{2,1,0:T(8,128)(2,1)S(1)}, f32[8,128]{1,0:T(8,128)S(1)}) custom-call(f32[2,256,2560]{2,1,0:T(8,128)S(1)} %copy-done), custom_call_target="tpu_custom_call" | custom-call | bytes 5242880 | tf_op jit(solution)/shard_map/pallas_call | solution.py:28
  11.6 2.0 %collective-permute-start.19 = (f32[2,8,2560]{2,1,0:T(8,128)S(1)}, f32[2,8,2560]{2,1,0:T(8,128)S(1)}, u32[]{:S(2)}, u32[]{:S(2)}) collective-permute-start(f32[2,8,2560]{2,1,0:T(8,128)S(1)} %pad_maximum_fusion.2.refs_0_), channel_id=1, source_target_pairs={{0,4},{1,5},{2,6},{3,7},{4,0},{5,1},{6,2},{7,3},{8,12},{9,13},{10,... | collective-permute-start | bytes 491528 | tf_op jit(solution)/shard_map/ppermute | solution.py:248
  13.6 1.6 %collective-permute-start.21 = (f32[2,8,2560]{2,1,0:T(8,128)S(1)}, f32[2,8,2560]{2,1,0:T(8,128)S(1)}, u32[]{:S(2)}, u32[]{:S(2)}) collective-permute-start(f32[2,8,2560]{2,1,0:T(8,128)S(1)} %pad_maximum_fusion.3.refs_2_), channel_id=1, source_target_pairs={{0,2},{1,3},{2,0},{3,1},{4,6},{5,7},{6,4},{7,5},{8,10},{9,11},{10,... | collective-permute-start | bytes 491528 | tf_op jit(solution)/shard_map/ppermute | solution.py:248
  15.2 0.0 collective-permute-done.2
  15.2 0.6 collective-permute-start.3
  15.9 0.1 collective-permute-start.1
  15.9 2.2 %shard_map.42 = (bf16[2,256,2560]{2,1,0:T(8,128)(2,1)S(1)}, bf16[2,256,2560]{2,1,0:T(8,128)(2,1)S(1)}, bf16[2,2560,256]{2,1,0:T(8,128)(2,1)S(1)}, bf16[2,2560,256]{2,1,0:T(8,128)(2,1)S(1)}, f32[8,128]{1,0:T(8,128)S(1)}) custom-call(f32[2,256,2560]{2,1,0:T(8,128)S(1)} %collective-permute-done.4.down_ref), custom_call_target="tpu_custom_call" | custom-call | bytes 5242880 | tf_op jit(solution)/shard_map/pallas_call | solution.py:28
  18.2 0.1 collective-permute-done.19.refs_1_
  18.3 2.4 %collective-permute-done.21.refs_3_ = f32[2,8,2560]{2,1,0:T(8,128)S(1)} collective-permute-done((f32[2,8,2560]{2,1,0:T(8,128)S(1)}, f32[2,8,2560]{2,1,0:T(8,128)S(1)}, u32[]{:S(2)}, u32[]{:S(2)}) %collective-permute-start.21) | collective-permute-done | bytes 163872 | tf_op jit(solution)/shard_map/ppermute | solution.py:248
  20.6 4.1 %shard_map.46 = (f32[64,512]{1,0:T(8,128)S(1)}, f32[32,1408]{1,0:T(8,128)S(1)}, f32[32,1408]{1,0:T(8,128)S(1)}, f32[32,1280]{1,0:T(8,128)S(1)}, f32[32,1280]{1,0:T(8,128)S(1)}) custom-call(f32[2,8,2560]{2,1,0:T(8,128)S(1)} %pad_maximum_fusion.2.refs_0_, f32[2,8,2560]{2,1,0:T(8,128)S(1)} %collective-permute-done.19.refs_1_, ...), custom_call_target="tpu_custom_call" | custom-call | flops 2013265920 | bytes 21635072 | tf_op jit(solution)/shard_map/pallas_call | solution.py:28
  24.8 0.3 collective-permute-start.25
  25.1 1.8 %collective-permute-start.22 = (f32[32,1408]{1,0:T(8,128)S(1)}, f32[32,1408]{1,0:T(8,128)S(1)}, u32[]{:S(2)}, u32[]{:S(2)}) collective-permute-start(f32[32,1408]{1,0:T(8,128)S(1)} %get-tuple-element.68), channel_id=1, source_target_pairs={{0,2},{1,3},{2,0},{3,1},{4,6},{5,7},{6,4},{7,5},{8,10},{9,11},{10,... | collective-permute-start | bytes 540680 | tf_op jit(solution)/shard_map/ppermute | solution.py:248
  26.8 0.0 collective-permute-done.3.refs_3_
  26.8 4.1 %shard_map.43 = (f32[64,512]{1,0:T(8,128)S(1)}, f32[32,1408]{1,0:T(8,128)S(1)}, f32[32,1408]{1,0:T(8,128)S(1)}, f32[32,1280]{1,0:T(8,128)S(1)}, f32[32,1280]{1,0:T(8,128)S(1)}) custom-call(f32[2,8,2560]{2,1,0:T(8,128)S(1)} %pad_maximum_fusion.refs_0_, f32[2,8,2560]{2,1,0:T(8,128)S(1)} %collective-permute-done.1.refs_1_, ...), custom_call_target="tpu_custom_call" | custom-call | flops 2013265920 | bytes 21635072 | tf_op jit(solution)/shard_map/pallas_call | solution.py:28
  31.0 0.3 collective-permute-start.5
  31.3 0.1 collective-permute-done.22
  31.4 2.2 %collective-permute-start.23 = (f32[32,1408]{1,0:T(8,128)S(1)}, f32[32,1408]{1,0:T(8,128)S(1)}, u32[]{:S(2)}, u32[]{:S(2)}) collective-permute-start(f32[32,1408]{1,0:T(8,128)S(1)} %add.56), channel_id=1, source_target_pairs={{0,4},{1,5},{2,6},{3,7},{4,0},{5,1},{6,2},{7,3},{8,12},{9,13},{10,... | collective-permute-start | bytes 540680 | tf_op jit(solution)/shard_map/ppermute | solution.py:248
  33.6 0.1 collective-permute-start.8
  33.7 0.0 collective-permute-done.25
  33.8 2.3 %collective-permute-start.26 = (f32[32,1280]{1,0:T(8,128)S(1)}, f32[32,1280]{1,0:T(8,128)S(1)}, u32[]{:S(2)}, u32[]{:S(2)}) collective-permute-start(f32[32,1280]{1,0:T(8,128)S(1)} %add.58), channel_id=1, source_target_pairs={{0,2},{1,3},{2,0},{3,1},{4,6},{5,7},{6,4},{7,5},{8,10},{9,11},{10,... | collective-permute-start | bytes 491528 | tf_op jit(solution)/shard_map/ppermute | solution.py:248
  36.1 0.4 collective-permute-done.5
  36.5 2.8 %collective-permute-start.6 = (f32[32,1408]{1,0:T(8,128)S(1)}, f32[32,1408]{1,0:T(8,128)S(1)}, u32[]{:S(2)}, u32[]{:S(2)}) collective-permute-start(f32[32,1408]{1,0:T(8,128)S(1)} %add.48), channel_id=1, source_target_pairs={{0,4},{1,5},{2,6},{3,7},{4,0},{5,1},{6,2},{7,3},{8,12},{9,13},{10,... | collective-permute-start | bytes 540680 | tf_op jit(solution)/shard_map/ppermute | solution.py:248
  39.3 0.0 collective-permute-done.23
  39.3 2.0 %collective-permute-start.24 = (f32[32,1408]{1,0:T(8,128)S(1)}, f32[32,1408]{1,0:T(8,128)S(1)}, u32[]{:S(2)}, u32[]{:S(2)}) collective-permute-start(f32[32,1408]{1,0:T(8,128)S(1)} %add.57.refs_0_), channel_id=1, source_target_pairs={{0,2},{1,3},{2,0},{3,1},{4,6},{5,7},{6,4},{7,5},{8,10},{9,11},{10,... | collective-permute-start | bytes 540680 | tf_op jit(solution)/shard_map/ppermute | solution.py:248
  41.4 1.1 %collective-permute-done.8 = f32[32,1280]{1,0:T(8,128)S(1)} collective-permute-done((f32[32,1280]{1,0:T(8,128)S(1)}, f32[32,1280]{1,0:T(8,128)S(1)}, u32[]{:S(2)}, u32[]{:S(2)}) %collective-permute-start.8) | collective-permute-done | bytes 163872 | tf_op jit(solution)/shard_map/ppermute | solution.py:248
  42.5 1.8 %collective-permute-start.9 = (f32[32,1280]{1,0:T(8,128)S(1)}, f32[32,1280]{1,0:T(8,128)S(1)}, u32[]{:S(2)}, u32[]{:S(2)}) collective-permute-start(f32[32,1280]{1,0:T(8,128)S(1)} %add.50), channel_id=1, source_target_pairs={{0,2},{1,3},{2,0},{3,1},{4,6},{5,7},{6,4},{7,5},{8,10},{9,11},{10,... | collective-permute-start | bytes 491528 | tf_op jit(solution)/shard_map/ppermute | solution.py:248
  44.3 1.5 %collective-permute-start.27 = (f32[32,1280]{1,0:T(8,128)S(1)}, f32[32,1280]{1,0:T(8,128)S(1)}, u32[]{:S(2)}, u32[]{:S(2)}) collective-permute-start(f32[32,1280]{1,0:T(8,128)S(1)} %add.59.refs_2_), channel_id=1, source_target_pairs={{0,4},{1,5},{2,6},{3,7},{4,0},{5,1},{6,2},{7,3},{8,12},{9,13},{10,... | collective-permute-start | bytes 491528 | tf_op jit(solution)/shard_map/ppermute | solution.py:248
  45.7 3.8 %collective-permute-done.9 = f32[32,1280]{1,0:T(8,128)S(1)} collective-permute-done((f32[32,1280]{1,0:T(8,128)S(1)}, f32[32,1280]{1,0:T(8,128)S(1)}, u32[]{:S(2)}, u32[]{:S(2)}) %collective-permute-start.9) | collective-permute-done | bytes 163872 | tf_op jit(solution)/shard_map/ppermute | solution.py:248
  49.6 1.0 %collective-permute-start.10 = (f32[32,1280]{1,0:T(8,128)S(1)}, f32[32,1280]{1,0:T(8,128)S(1)}, u32[]{:S(2)}, u32[]{:S(2)}) collective-permute-start(f32[32,1280]{1,0:T(8,128)S(1)} %add.51.refs_2_), channel_id=1, source_target_pairs={{0,4},{1,5},{2,6},{3,7},{4,0},{5,1},{6,2},{7,3},{8,12},{9,13},{10,... | collective-permute-start | bytes 491528 | tf_op jit(solution)/shard_map/ppermute | solution.py:248
  50.6 0.0 collective-permute-done.6
  50.6 2.1 %collective-permute-start.7 = (f32[32,1408]{1,0:T(8,128)S(1)}, f32[32,1408]{1,0:T(8,128)S(1)}, u32[]{:S(2)}, u32[]{:S(2)}) collective-permute-start(f32[32,1408]{1,0:T(8,128)S(1)} %add.49.refs_0_), channel_id=1, source_target_pairs={{0,2},{1,3},{2,0},{3,1},{4,6},{5,7},{6,4},{7,5},{8,10},{9,11},{10,... | collective-permute-start | bytes 540680 | tf_op jit(solution)/shard_map/ppermute | solution.py:248
  52.7 0.0 collective-permute-done.27.refs_3_
  52.7 0.0 collective-permute-done.24.refs_1_
  52.7 4.0 %shard_map.47 = (f32[64,2560]{1,0:T(8,128)S(1)}, f32[64,128]{1,0:T(8,128)S(1)}, f32[64,512]{1,0:T(8,128)S(1)}, f32[64,512]{1,0:T(8,128)S(1)}, f32[32,1408]{1,0:T...) custom-call(f32[32,1408]{1,0:T(8,128)S(1)} %add.57.refs_0_, ...), custom_call_target="tpu_custom_call" | custom-call | flops 2013265920 | bytes 21790720 | tf_op jit(solution)/shard_map/pallas_call | solution.py:28
  56.8 0.1 collective-permute-start.31
  56.9 1.0 %collective-permute-start.28 = (f32[32,1408]{1,0:T(8,128)S(1)}, f32[32,1408]{1,0:T(8,128)S(1)}, u32[]{:S(2)}, u32[]{:S(2)}) collective-permute-start(f32[32,1408]{1,0:T(8,128)S(1)} %get-tuple-element.73), channel_id=1, source_target_pairs={{0,2},{1,3},{2,0},{3,1},{4,6},{5,7},{6,4},{7,5},{8,10},{9,11},{10,... | collective-permute-start | bytes 540680 | tf_op jit(solution)/shard_map/ppermute | solution.py:248
  57.9 4.2 %shard_map.44 = (f32[64,2560]{1,0:T(8,128)S(1)}, f32[64,128]{1,0:T(8,128)S(1)}, f32[64,512]{1,0:T(8,128)S(1)}, f32[64,512]{1,0:T(8,128)S(1)}, f32[32,1408]{1,0:T...) custom-call(f32[32,1408]{1,0:T(8,128)S(1)} %add.49.refs_0_, ...), custom_call_target="tpu_custom_call" | custom-call | flops 2013265920 | bytes 21790720 | tf_op jit(solution)/shard_map/pallas_call | solution.py:28
  62.1 1.1 %collective-permute-start.11 = (f32[32,1408]{1,0:T(8,128)S(1)}, f32[32,1408]{1,0:T(8,128)S(1)}, u32[]{:S(2)}, u32[]{:S(2)}) collective-permute-start(f32[32,1408]{1,0:T(8,128)S(1)} %get-tuple-element.58), channel_id=1, source_target_pairs={{0,2},{1,3},{2,0},{3,1},{4,6},{5,7},{6,4},{7,5},{8,10},{9,11},{10,... | collective-permute-start | bytes 540680 | tf_op jit(solution)/shard_map/ppermute | solution.py:248
  63.2 1.9 %collective-permute-start.14 = (f32[32,1280]{1,0:T(8,128)S(1)}, f32[32,1280]{1,0:T(8,128)S(1)}, u32[]{:S(2)}, u32[]{:S(2)}) collective-permute-start(f32[32,1280]{1,0:T(8,128)S(1)} %get-tuple-element.60), channel_id=1, source_target_pairs={{0,4},{1,5},{2,6},{3,7},{4,0},{5,1},{6,2},{7,3},{8,12},{9,13},{10,... | collective-permute-start | bytes 491528 | tf_op jit(solution)/shard_map/ppermute | solution.py:248
  65.2 0.7 collective-permute-start.29
  66.0 0.5 collective-permute-start.32
  66.4 3.2 %collective-permute-done.11 = f32[32,1408]{1,0:T(8,128)S(1)} collective-permute-done((f32[32,1408]{1,0:T(8,128)S(1)}, f32[32,1408]{1,0:T(8,128)S(1)}, u32[]{:S(2)}, u32[]{:S(2)}) %collective-permute-start.11) | collective-permute-done | bytes 180256 | tf_op jit(solution)/shard_map/ppermute | solution.py:248
  69.7 0.9 %collective-permute-start.12 = (f32[32,1408]{1,0:T(8,128)S(1)}, f32[32,1408]{1,0:T(8,128)S(1)}, u32[]{:S(2)}, u32[]{:S(2)}) collective-permute-start(f32[32,1408]{1,0:T(8,128)S(1)} %add.52), channel_id=1, source_target_pairs={{0,4},{1,5},{2,6},{3,7},{4,0},{5,1},{6,2},{7,3},{8,12},{9,13},{10,... | collective-permute-start | bytes 540680 | tf_op jit(solution)/shard_map/ppermute | solution.py:248
  70.6 2.2 %collective-permute-start.15 = (f32[32,1280]{1,0:T(8,128)S(1)}, f32[32,1280]{1,0:T(8,128)S(1)}, u32[]{:S(2)}, u32[]{:S(2)}) collective-permute-start(f32[32,1280]{1,0:T(8,128)S(1)} %add.54), channel_id=1, source_target_pairs={{0,2},{1,3},{2,0},{3,1},{4,6},{5,7},{6,4},{7,5},{8,10},{9,11},{10,... | collective-permute-start | bytes 491528 | tf_op jit(solution)/shard_map/ppermute | solution.py:248
  72.8 0.6 collective-permute-done.29
  73.5 0.8 collective-permute-start.30
  74.3 1.8 %collective-permute-start.33 = (f32[32,1280]{1,0:T(8,128)S(1)}, f32[32,1280]{1,0:T(8,128)S(1)}, u32[]{:S(2)}, u32[]{:S(2)}) collective-permute-start(f32[32,1280]{1,0:T(8,128)S(1)} %add.63.refs_2_), channel_id=1, source_target_pairs={{0,4},{1,5},{2,6},{3,7},{4,0},{5,1},{6,2},{7,3},{8,12},{9,13},{10,... | collective-permute-start | bytes 491528 | tf_op jit(solution)/shard_map/ppermute | solution.py:248
  76.2 0.7 collective-permute-start.13
  76.9 1.5 %collective-permute-start.16 = (f32[32,1280]{1,0:T(8,128)S(1)}, f32[32,1280]{1,0:T(8,128)S(1)}, u32[]{:S(2)}, u32[]{:S(2)}) collective-permute-start(f32[32,1280]{1,0:T(8,128)S(1)} %add.55.refs_2_), channel_id=1, source_target_pairs={{0,4},{1,5},{2,6},{3,7},{4,0},{5,1},{6,2},{7,3},{8,12},{9,13},{10,... | collective-permute-start | bytes 491528 | tf_op jit(solution)/shard_map/ppermute | solution.py:248
  78.4 1.3 %collective-permute-done.33.refs_3_ = f32[32,1280]{1,0:T(8,128)S(1)} collective-permute-done((f32[32,1280]{1,0:T(8,128)S(1)}, f32[32,1280]{1,0:T(8,128)S(1)}, u32[]{:S(2)}, u32[]{:S(2)}) %collective-permute-start.33) | collective-permute-done | bytes 163872 | tf_op jit(solution)/shard_map/ppermute | solution.py:248
  79.7 1.8 %shard_map.48 = (f32[2,64,256]{2,1,0:T(8,128)S(1)}, f32[2,64,256]{2,1,0:T(8,128)S(1)}) custom-call(f32[32,1408]{1,0:T(8,128)S(1)} %add.61.refs_0_, f32[32,1408]{1,0:T(8,128)S(1)} %collective-permute-done.30.refs_1_, f32[32,1280]{1,0:T(8,128)S(1)} %add.63.refs_2_, f32[32,1280]{1,0:T(8,128)S(1)} %collective-permute-done.33.refs_3_, ...), custom_call_target="tpu_custom_call" | custom-call | flops 1006632960 | bytes 12255232 | tf_op jit(solution)/shard_map/pallas_call | solution.py:28
  81.5 0.1 collective-permute-start.34
  81.6 0.7 collective-permute-done.16.refs_3_
  82.3 1.8 %shard_map.45 = (f32[2,64,256]{2,1,0:T(8,128)S(1)}, f32[2,64,256]{2,1,0:T(8,128)S(1)}) custom-call(f32[32,1408]{1,0:T(8,128)S(1)} %add.53.refs_0_, f32[32,1408]{1,0:T(8,128)S(1)} %collective-permute-done.13.refs_1_, f32[32,1280]{1,0:T(8,128)S(1)} %add.55.refs_2_, f32[32,1280]{1,0:T(8,128)S(1)} %collective-permute-done.16.refs_3_, ...), custom_call_target="tpu_custom_call" | custom-call | flops 1006632960 | bytes 12255232 | tf_op jit(solution)/shard_map/pallas_call | solution.py:28
  84.1 0.1 collective-permute-start.17
  84.2 1.3 %collective-permute-done.17.refs_1_ = f32[2,64,256]{2,1,0:T(8,128)S(1)} collective-permute-done((f32[2,64,256]{2,1,0:T(8,128)S(1)}, f32[2,64,256]{2,1,0:T(8,128)S(1)}, u32[]{:S(2)}, u32[]{:S(2)}) %collective-permute-start.17) | collective-permute-done | bytes 131104 | tf_op jit(solution)/shard_map/ppermute | solution.py:248
  85.5 0.9 %shard_map.49 = (f32[2,256,128]{2,1,0:T(8,128)}, f32[2,256,128]{2,1,0:T(8,128)}) custom-call(f32[2,64,256]{2,1,0:T(8,128)S(1)} %get-tuple-element.65.refs_0_, f32[2,64,256]{2,1,0:T(8,128)S(1)} %collective-permute-done.17.refs_1_, f32[2,64,256]{2,1,0:T(8,128)S(1)} %get-tuple-element.80.refs_2_, f32[2,64,256]{2,1,0:T(8,128)S(1)} %collective-permute-done.34.refs_3_), custom_call_target="tpu_custom_call" | custom-call | bytes 524288 | tf_op jit(solution)/shard_map/pallas_call | solution.py:28
  (38 shorter events, 0.5 us)
Async XLA Ops:
  0.6 15.3 %collective-permute-start.4 = (f32[2,256,2560]{2,1,0:T(8,128)}, f32[2,256,2560]{2,1,0:T(8,128)S(1)}, u32[]{:S(2)}, u32[]{:S(2)}) collective-permute-start(f32[2,256,2560]{2,1,0:T(8,128)} %down_ref.1), channel_id=1, source_target_pairs={{0,1},{1,0},{2,3},{3,2},{4,5},{5,4},{6,7},{7,6},{8,9},{9,8},{10,11... | collective-permute-start | bytes 15728648 | tf_op jit(solution)/shard_map/ppermute | solution.py:248
  2.2 9.4 %collective-permute-start.18 = (f32[1,8,2560]{2,1,0:T(8,128)S(1)}, f32[1,8,2560]{2,1,0:T(8,128)S(1)}, u32[]{:S(2)}, u32[]{:S(2)}) collective-permute-start(f32[1,8,2560]{2,1,0:T(8,128)S(1)} %get-tuple-element.85), channel_id=1, source_target_pairs={{0,2},{1,3},{2,0},{3,1},{4,6},{5,7},{6,4},{7,5},{8,10},{9,11},{10,... | collective-permute-start | bytes 245768 | tf_op jit(solution)/shard_map/ppermute | solution.py:248
  4.7 8.9 %collective-permute-start.20 = (f32[1,8,2560]{2,1,0:T(8,128)S(1)}, f32[1,8,2560]{2,1,0:T(8,128)S(1)}, u32[]{:S(2)}, u32[]{:S(2)}) collective-permute-start(f32[1,8,2560]{2,1,0:T(8,128)S(1)} %get-tuple-element.82), channel_id=1, source_target_pairs={{0,4},{1,5},{2,6},{3,7},{4,0},{5,1},{6,2},{7,3},{8,12},{9,13},{10,... | collective-permute-start | bytes 245768 | tf_op jit(solution)/shard_map/ppermute | solution.py:248
  6.3 8.9 %collective-permute-start.2 = (f32[1,8,2560]{2,1,0:T(8,128)S(1)}, f32[1,8,2560]{2,1,0:T(8,128)S(1)}, u32[]{:S(2)}, u32[]{:S(2)}) collective-permute-start(f32[1,8,2560]{2,1,0:T(8,128)S(1)} %get-tuple-element.83), channel_id=1, source_target_pairs={{0,4},{1,5},{2,6},{3,7},{4,0},{5,1},{6,2},{7,3},{8,12},{9,13},{10,... | collective-permute-start | bytes 245768 | tf_op jit(solution)/shard_map/ppermute | solution.py:248
  6.8 9.1 %collective-permute-start = (f32[1,8,2560]{2,1,0:T(8,128)S(1)}, f32[1,8,2560]{2,1,0:T(8,128)S(1)}, u32[]{:S(2)}, u32[]{:S(2)}) collective-permute-start(f32[1,8,2560]{2,1,0:T(8,128)S(1)} %get-tuple-element.84), channel_id=1, source_target_pairs={{0,2},{1,3},{2,0},{3,1},{4,6},{5,7},{6,4},{7,5},{8,10},{9,11},{10,... | collective-permute-start | bytes 245768 | tf_op jit(solution)/shard_map/ppermute | solution.py:248
  6.9 2.5 %copy-start = (f32[2,256,2560]{2,1,0:T(8,128)S(1)}, f32[2,256,2560]{2,1,0:T(8,128)}, u32[]{:S(2)}) copy-start(f32[2,256,2560]{2,1,0:T(8,128)} %down_ref.1) | copy-start | bytes 15728644
  11.6 6.7 %collective-permute-start.19 = (f32[2,8,2560]{2,1,0:T(8,128)S(1)}, f32[2,8,2560]{2,1,0:T(8,128)S(1)}, u32[]{:S(2)}, u32[]{:S(2)}) collective-permute-start(f32[2,8,2560]{2,1,0:T(8,128)S(1)} %pad_maximum_fusion.2.refs_0_), channel_id=1, source_target_pairs={{0,4},{1,5},{2,6},{3,7},{4,0},{5,1},{6,2},{7,3},{8,12},{9,13},{10,... | collective-permute-start | bytes 491528 | tf_op jit(solution)/shard_map/ppermute | solution.py:248
  13.6 7.0 %collective-permute-start.21 = (f32[2,8,2560]{2,1,0:T(8,128)S(1)}, f32[2,8,2560]{2,1,0:T(8,128)S(1)}, u32[]{:S(2)}, u32[]{:S(2)}) collective-permute-start(f32[2,8,2560]{2,1,0:T(8,128)S(1)} %pad_maximum_fusion.3.refs_2_), channel_id=1, source_target_pairs={{0,2},{1,3},{2,0},{3,1},{4,6},{5,7},{6,4},{7,5},{8,10},{9,11},{10,... | collective-permute-start | bytes 491528 | tf_op jit(solution)/shard_map/ppermute | solution.py:248
  15.2 11.6 %collective-permute-start.3 = (f32[2,8,2560]{2,1,0:T(8,128)S(1)}, f32[2,8,2560]{2,1,0:T(8,128)S(1)}, u32[]{:S(2)}, u32[]{:S(2)}) collective-permute-start(f32[2,8,2560]{2,1,0:T(8,128)S(1)} %pad_maximum_fusion.1.refs_2_), channel_id=1, source_target_pairs={{0,2},{1,3},{2,0},{3,1},{4,6},{5,7},{6,4},{7,5},{8,10},{9,11},{10,... | collective-permute-start | bytes 491528 | tf_op jit(solution)/shard_map/ppermute | solution.py:248
  15.9 11.0 %collective-permute-start.1 = (f32[2,8,2560]{2,1,0:T(8,128)S(1)}, f32[2,8,2560]{2,1,0:T(8,128)S(1)}, u32[]{:S(2)}, u32[]{:S(2)}) collective-permute-start(f32[2,8,2560]{2,1,0:T(8,128)S(1)} %pad_maximum_fusion.refs_0_), channel_id=1, source_target_pairs={{0,4},{1,5},{2,6},{3,7},{4,0},{5,1},{6,2},{7,3},{8,12},{9,13},{10,... | collective-permute-start | bytes 491528 | tf_op jit(solution)/shard_map/ppermute | solution.py:248
  24.8 9.0 %collective-permute-start.25 = (f32[32,1280]{1,0:T(8,128)S(1)}, f32[32,1280]{1,0:T(8,128)S(1)}, u32[]{:S(2)}, u32[]{:S(2)}) collective-permute-start(f32[32,1280]{1,0:T(8,128)S(1)} %get-tuple-element.70), channel_id=1, source_target_pairs={{0,4},{1,5},{2,6},{3,7},{4,0},{5,1},{6,2},{7,3},{8,12},{9,13},{10,... | collective-permute-start | bytes 491528 | tf_op jit(solution)/shard_map/ppermute | solution.py:248
  25.1 6.3 %collective-permute-start.22 = (f32[32,1408]{1,0:T(8,128)S(1)}, f32[32,1408]{1,0:T(8,128)S(1)}, u32[]{:S(2)}, u32[]{:S(2)}) collective-permute-start(f32[32,1408]{1,0:T(8,128)S(1)} %get-tuple-element.68), channel_id=1, source_target_pairs={{0,2},{1,3},{2,0},{3,1},{4,6},{5,7},{6,4},{7,5},{8,10},{9,11},{10,... | collective-permute-start | bytes 540680 | tf_op jit(solution)/shard_map/ppermute | solution.py:248
  31.0 5.6 %collective-permute-start.5 = (f32[32,1408]{1,0:T(8,128)S(1)}, f32[32,1408]{1,0:T(8,128)S(1)}, u32[]{:S(2)}, u32[]{:S(2)}) collective-permute-start(f32[32,1408]{1,0:T(8,128)S(1)} %get-tuple-element.53), channel_id=1, source_target_pairs={{0,2},{1,3},{2,0},{3,1},{4,6},{5,7},{6,4},{7,5},{8,10},{9,11},{10,... | collective-permute-start | bytes 540680 | tf_op jit(solution)/shard_map/ppermute | solution.py:248
  31.4 7.9 %collective-permute-start.23 = (f32[32,1408]{1,0:T(8,128)S(1)}, f32[32,1408]{1,0:T(8,128)S(1)}, u32[]{:S(2)}, u32[]{:S(2)}) collective-permute-start(f32[32,1408]{1,0:T(8,128)S(1)} %add.56), channel_id=1, source_target_pairs={{0,4},{1,5},{2,6},{3,7},{4,0},{5,1},{6,2},{7,3},{8,12},{9,13},{10,... | collective-permute-start | bytes 540680 | tf_op jit(solution)/shard_map/ppermute | solution.py:248
  33.6 8.8 %collective-permute-start.8 = (f32[32,1280]{1,0:T(8,128)S(1)}, f32[32,1280]{1,0:T(8,128)S(1)}, u32[]{:S(2)}, u32[]{:S(2)}) collective-permute-start(f32[32,1280]{1,0:T(8,128)S(1)} %get-tuple-element.55), channel_id=1, source_target_pairs={{0,4},{1,5},{2,6},{3,7},{4,0},{5,1},{6,2},{7,3},{8,12},{9,13},{10,... | collective-permute-start | bytes 491528 | tf_op jit(solution)/shard_map/ppermute | solution.py:248
  33.8 10.5 %collective-permute-start.26 = (f32[32,1280]{1,0:T(8,128)S(1)}, f32[32,1280]{1,0:T(8,128)S(1)}, u32[]{:S(2)}, u32[]{:S(2)}) collective-permute-start(f32[32,1280]{1,0:T(8,128)S(1)} %add.58), channel_id=1, source_target_pairs={{0,2},{1,3},{2,0},{3,1},{4,6},{5,7},{6,4},{7,5},{8,10},{9,11},{10,... | collective-permute-start | bytes 491528 | tf_op jit(solution)/shard_map/ppermute | solution.py:248
  36.5 14.1 %collective-permute-start.6 = (f32[32,1408]{1,0:T(8,128)S(1)}, f32[32,1408]{1,0:T(8,128)S(1)}, u32[]{:S(2)}, u32[]{:S(2)}) collective-permute-start(f32[32,1408]{1,0:T(8,128)S(1)} %add.48), channel_id=1, source_target_pairs={{0,4},{1,5},{2,6},{3,7},{4,0},{5,1},{6,2},{7,3},{8,12},{9,13},{10,... | collective-permute-start | bytes 540680 | tf_op jit(solution)/shard_map/ppermute | solution.py:248
  39.3 13.4 %collective-permute-start.24 = (f32[32,1408]{1,0:T(8,128)S(1)}, f32[32,1408]{1,0:T(8,128)S(1)}, u32[]{:S(2)}, u32[]{:S(2)}) collective-permute-start(f32[32,1408]{1,0:T(8,128)S(1)} %add.57.refs_0_), channel_id=1, source_target_pairs={{0,2},{1,3},{2,0},{3,1},{4,6},{5,7},{6,4},{7,5},{8,10},{9,11},{10,... | collective-permute-start | bytes 540680 | tf_op jit(solution)/shard_map/ppermute | solution.py:248
  42.5 7.1 %collective-permute-start.9 = (f32[32,1280]{1,0:T(8,128)S(1)}, f32[32,1280]{1,0:T(8,128)S(1)}, u32[]{:S(2)}, u32[]{:S(2)}) collective-permute-start(f32[32,1280]{1,0:T(8,128)S(1)} %add.50), channel_id=1, source_target_pairs={{0,2},{1,3},{2,0},{3,1},{4,6},{5,7},{6,4},{7,5},{8,10},{9,11},{10,... | collective-permute-start | bytes 491528 | tf_op jit(solution)/shard_map/ppermute | solution.py:248
  44.3 8.5 %collective-permute-start.27 = (f32[32,1280]{1,0:T(8,128)S(1)}, f32[32,1280]{1,0:T(8,128)S(1)}, u32[]{:S(2)}, u32[]{:S(2)}) collective-permute-start(f32[32,1280]{1,0:T(8,128)S(1)} %add.59.refs_2_), channel_id=1, source_target_pairs={{0,4},{1,5},{2,6},{3,7},{4,0},{5,1},{6,2},{7,3},{8,12},{9,13},{10,... | collective-permute-start | bytes 491528 | tf_op jit(solution)/shard_map/ppermute | solution.py:248
  49.6 8.3 %collective-permute-start.10 = (f32[32,1280]{1,0:T(8,128)S(1)}, f32[32,1280]{1,0:T(8,128)S(1)}, u32[]{:S(2)}, u32[]{:S(2)}) collective-permute-start(f32[32,1280]{1,0:T(8,128)S(1)} %add.51.refs_2_), channel_id=1, source_target_pairs={{0,4},{1,5},{2,6},{3,7},{4,0},{5,1},{6,2},{7,3},{8,12},{9,13},{10,... | collective-permute-start | bytes 491528 | tf_op jit(solution)/shard_map/ppermute | solution.py:248
  50.6 7.3 %collective-permute-start.7 = (f32[32,1408]{1,0:T(8,128)S(1)}, f32[32,1408]{1,0:T(8,128)S(1)}, u32[]{:S(2)}, u32[]{:S(2)}) collective-permute-start(f32[32,1408]{1,0:T(8,128)S(1)} %add.49.refs_0_), channel_id=1, source_target_pairs={{0,2},{1,3},{2,0},{3,1},{4,6},{5,7},{6,4},{7,5},{8,10},{9,11},{10,... | collective-permute-start | bytes 540680 | tf_op jit(solution)/shard_map/ppermute | solution.py:248
  56.8 9.2 %collective-permute-start.31 = (f32[32,1280]{1,0:T(8,128)S(1)}, f32[32,1280]{1,0:T(8,128)S(1)}, u32[]{:S(2)}, u32[]{:S(2)}) collective-permute-start(f32[32,1280]{1,0:T(8,128)S(1)} %get-tuple-element.75), channel_id=1, source_target_pairs={{0,4},{1,5},{2,6},{3,7},{4,0},{5,1},{6,2},{7,3},{8,12},{9,13},{10,... | collective-permute-start | bytes 491528 | tf_op jit(solution)/shard_map/ppermute | solution.py:248
  56.9 8.3 %collective-permute-start.28 = (f32[32,1408]{1,0:T(8,128)S(1)}, f32[32,1408]{1,0:T(8,128)S(1)}, u32[]{:S(2)}, u32[]{:S(2)}) collective-permute-start(f32[32,1408]{1,0:T(8,128)S(1)} %get-tuple-element.73), channel_id=1, source_target_pairs={{0,2},{1,3},{2,0},{3,1},{4,6},{5,7},{6,4},{7,5},{8,10},{9,11},{10,... | collective-permute-start | bytes 540680 | tf_op jit(solution)/shard_map/ppermute | solution.py:248
  62.1 7.5 %collective-permute-start.11 = (f32[32,1408]{1,0:T(8,128)S(1)}, f32[32,1408]{1,0:T(8,128)S(1)}, u32[]{:S(2)}, u32[]{:S(2)}) collective-permute-start(f32[32,1408]{1,0:T(8,128)S(1)} %get-tuple-element.58), channel_id=1, source_target_pairs={{0,2},{1,3},{2,0},{3,1},{4,6},{5,7},{6,4},{7,5},{8,10},{9,11},{10,... | collective-permute-start | bytes 540680 | tf_op jit(solution)/shard_map/ppermute | solution.py:248
  63.2 7.3 %collective-permute-start.14 = (f32[32,1280]{1,0:T(8,128)S(1)}, f32[32,1280]{1,0:T(8,128)S(1)}, u32[]{:S(2)}, u32[]{:S(2)}) collective-permute-start(f32[32,1280]{1,0:T(8,128)S(1)} %get-tuple-element.60), channel_id=1, source_target_pairs={{0,4},{1,5},{2,6},{3,7},{4,0},{5,1},{6,2},{7,3},{8,12},{9,13},{10,... | collective-permute-start | bytes 491528 | tf_op jit(solution)/shard_map/ppermute | solution.py:248
  65.2 8.2 %collective-permute-start.29 = (f32[32,1408]{1,0:T(8,128)S(1)}, f32[32,1408]{1,0:T(8,128)S(1)}, u32[]{:S(2)}, u32[]{:S(2)}) collective-permute-start(f32[32,1408]{1,0:T(8,128)S(1)} %add.60), channel_id=1, source_target_pairs={{0,4},{1,5},{2,6},{3,7},{4,0},{5,1},{6,2},{7,3},{8,12},{9,13},{10,... | collective-permute-start | bytes 540680 | tf_op jit(solution)/shard_map/ppermute | solution.py:248
  66.0 8.3 %collective-permute-start.32 = (f32[32,1280]{1,0:T(8,128)S(1)}, f32[32,1280]{1,0:T(8,128)S(1)}, u32[]{:S(2)}, u32[]{:S(2)}) collective-permute-start(f32[32,1280]{1,0:T(8,128)S(1)} %add.62), channel_id=1, source_target_pairs={{0,2},{1,3},{2,0},{3,1},{4,6},{5,7},{6,4},{7,5},{8,10},{9,11},{10,... | collective-permute-start | bytes 491528 | tf_op jit(solution)/shard_map/ppermute | solution.py:248
  69.7 6.5 %collective-permute-start.12 = (f32[32,1408]{1,0:T(8,128)S(1)}, f32[32,1408]{1,0:T(8,128)S(1)}, u32[]{:S(2)}, u32[]{:S(2)}) collective-permute-start(f32[32,1408]{1,0:T(8,128)S(1)} %add.52), channel_id=1, source_target_pairs={{0,4},{1,5},{2,6},{3,7},{4,0},{5,1},{6,2},{7,3},{8,12},{9,13},{10,... | collective-permute-start | bytes 540680 | tf_op jit(solution)/shard_map/ppermute | solution.py:248
  70.6 6.3 %collective-permute-start.15 = (f32[32,1280]{1,0:T(8,128)S(1)}, f32[32,1280]{1,0:T(8,128)S(1)}, u32[]{:S(2)}, u32[]{:S(2)}) collective-permute-start(f32[32,1280]{1,0:T(8,128)S(1)} %add.54), channel_id=1, source_target_pairs={{0,2},{1,3},{2,0},{3,1},{4,6},{5,7},{6,4},{7,5},{8,10},{9,11},{10,... | collective-permute-start | bytes 491528 | tf_op jit(solution)/shard_map/ppermute | solution.py:248
  73.5 6.2 %collective-permute-start.30 = (f32[32,1408]{1,0:T(8,128)S(1)}, f32[32,1408]{1,0:T(8,128)S(1)}, u32[]{:S(2)}, u32[]{:S(2)}) collective-permute-start(f32[32,1408]{1,0:T(8,128)S(1)} %add.61.refs_0_), channel_id=1, source_target_pairs={{0,2},{1,3},{2,0},{3,1},{4,6},{5,7},{6,4},{7,5},{8,10},{9,11},{10,... | collective-permute-start | bytes 540680 | tf_op jit(solution)/shard_map/ppermute | solution.py:248
  74.3 5.4 %collective-permute-start.33 = (f32[32,1280]{1,0:T(8,128)S(1)}, f32[32,1280]{1,0:T(8,128)S(1)}, u32[]{:S(2)}, u32[]{:S(2)}) collective-permute-start(f32[32,1280]{1,0:T(8,128)S(1)} %add.63.refs_2_), channel_id=1, source_target_pairs={{0,4},{1,5},{2,6},{3,7},{4,0},{5,1},{6,2},{7,3},{8,12},{9,13},{10,... | collective-permute-start | bytes 491528 | tf_op jit(solution)/shard_map/ppermute | solution.py:248
  76.2 6.1 %collective-permute-start.13 = (f32[32,1408]{1,0:T(8,128)S(1)}, f32[32,1408]{1,0:T(8,128)S(1)}, u32[]{:S(2)}, u32[]{:S(2)}) collective-permute-start(f32[32,1408]{1,0:T(8,128)S(1)} %add.53.refs_0_), channel_id=1, source_target_pairs={{0,2},{1,3},{2,0},{3,1},{4,6},{5,7},{6,4},{7,5},{8,10},{9,11},{10,... | collective-permute-start | bytes 540680 | tf_op jit(solution)/shard_map/ppermute | solution.py:248
  76.9 5.4 %collective-permute-start.16 = (f32[32,1280]{1,0:T(8,128)S(1)}, f32[32,1280]{1,0:T(8,128)S(1)}, u32[]{:S(2)}, u32[]{:S(2)}) collective-permute-start(f32[32,1280]{1,0:T(8,128)S(1)} %add.55.refs_2_), channel_id=1, source_target_pairs={{0,4},{1,5},{2,6},{3,7},{4,0},{5,1},{6,2},{7,3},{8,12},{9,13},{10,... | collective-permute-start | bytes 491528 | tf_op jit(solution)/shard_map/ppermute | solution.py:248
  81.5 2.6 %collective-permute-start.34 = (f32[2,64,256]{2,1,0:T(8,128)S(1)}, f32[2,64,256]{2,1,0:T(8,128)S(1)}, u32[]{:S(2)}, u32[]{:S(2)}) collective-permute-start(f32[2,64,256]{2,1,0:T(8,128)S(1)} %get-tuple-element.81), channel_id=1, source_target_pairs={{0,1},{1,0},{2,3},{3,2},{4,5},{5,4},{6,7},{7,6},{8,9},{9,8},{10,11... | collective-permute-start | bytes 393224 | tf_op jit(solution)/shard_map/ppermute | solution.py:248
  84.1 1.4 %collective-permute-start.17 = (f32[2,64,256]{2,1,0:T(8,128)S(1)}, f32[2,64,256]{2,1,0:T(8,128)S(1)}, u32[]{:S(2)}, u32[]{:S(2)}) collective-permute-start(f32[2,64,256]{2,1,0:T(8,128)S(1)} %get-tuple-element.66), channel_id=1, source_target_pairs={{0,1},{1,0},{2,3},{3,2},{4,5},{5,4},{6,7},{7,6},{8,9},{9,8},{10,11... | collective-permute-start | bytes 393224 | tf_op jit(solution)/shard_map/ppermute | solution.py:248

commit v3 on v2

--- a/solution.py
+++ b/solution.py
@@ -153,16 +153,14 @@
 
 
 def rhs_kernel(bits, masks, *refs):
-    sources, refs = refs[:4], refs[4:]
+    sources, refs = refs[: len(masks)], refs[len(masks) :]
     down, refs = refs[:8], refs[8:]
     (ea, eb), (rhs_ref, *outs), (x_ref, f0, s0, f1, s1, *spread) = refs[:2], refs[2:7], refs[7:]
     half = x_ref.shape[0] // 2
     own = sources[0].shape[1]
     chip = lax.axis_index("rcv") >> 1
-    for part in range(2):
-        blocks = [ref[at] for ref in sources[2 * part : 2 * part + 2] for at in range(ref.shape[0])]
-        for mask, block in zip(masks[part], blocks):
-            value = block if part == 0 else -block
+    for mask, source in zip(masks, sources):
+        for part, value in enumerate((source[0], -source[1])):
             if spread:
                 spread[0][part * half // own + (chip ^ mask)] = value
             else:
@@ -247,13 +245,6 @@
     def swap(value, bit):
         return lax.ppermute(value, "rcv", [(at, at ^ (1 << bit)) for at in range(count)])
 
-    def gather(block, order):
-        blocks, masks = block[None], [0]
-        for bit in order[:-1]:
-            blocks = jnp.concatenate([blocks, swap(blocks, bit)], axis=0)
-            masks += [mask | 1 << bit - 1 for mask in masks]
-        return (blocks, swap(blocks, order[-1])), masks + [mask | 1 << order[-1] - 1 for mask in masks]
-
     def exchange(outs):
         pieces = []
         for order, (keep, give) in zip(orders, (outs[0:2], outs[2:4])):
@@ -263,14 +254,16 @@
             pieces += [keep, swap(keep, order[0])]
         return pieces
 
+    def jump(value, mask):
+        return lax.ppermute(value, "rcv", [(at, at ^ (mask << 1)) for at in range(count)])
+
     other_down = swap(down_spectra, 0)
+    masks = sorted(range(chips), key=lambda mask: mask.bit_count())
     sources = []
     for group in range(GROUPS):
         part = up_sources[:, group * own : (group + 1) * own]
-        (real, real_masks), (imag, imag_masks) = gather(part[0], orders[0]), gather(part[1], orders[1])
-        sources.append((*real, *imag))
-    masks = (real_masks, imag_masks)
-    plain_a, turned_a, energy_a = split(down_spectra)
+        sources.append([jump(part, mask) if mask else part for mask in masks])
+    plain_a, turned_a, energy_a = split(pltpu.with_memory_space_constraint(down_spectra, pltpu.HBM))
     plain_b, turned_b, energy_b = split(other_down)
     turned = (*turned_a, *turned_b)
     down = (*plain_a, *plain_b, *turned)

time: 86.6 us -> 84.5 us (0.976)
  starting transfers between devices: 41.1 us -> 32.7 us
  waiting for transfers between devices: 15.2 us -> 21.4 us
  Pallas kernels: 25.3 us -> 28 us
  local copies, waits for them, and re-layouts: 3.51 us -> 1.02 us
    ppermute x35 -> x27, starting transfers between devices: 41.1 us -> 25 us  [swap(): lax.ppermute(value, 'rcv', [(at, at ^ 1 << bit) for at in range(count)])]
    ppermute x0 -> x6, starting transfers between devices: none -> 7.73 us  [jump(): lax.ppermute(value, 'rcv', [(at, at ^ mask << 1) for at in range(count)])]
    ppermute x35 -> x27, waiting for transfers between devices: 15.2 us -> 21.4 us  [swap(): lax.ppermute(value, 'rcv', [(at, at ^ 1 << bit) for at in range(count)])]
    pallas_call x9, Pallas kernels: 25.3 us -> 28 us  [call(): pl.pallas_call(kernel, out_shape=[jax.ShapeDtypeStruct(shape, dtype) for...]
    unnamed x2 -> x0, local copies, waits for them, and re-layouts: 2.49 us -> none
  transfers between devices with their start and end apart: 35 -> 33, of which waited for: 11 -> 11; matrix products, arithmetic and copies ran while one was open for 2% -> 2% of each run, Pallas kernels for 28% -> 32%
where the time goes in v3:
time: 84.5 us; the launch traced here: 84.3 us
  starting transfers between devices  32.7 us (39%)
  Pallas kernels  28 us (33%)
  waiting for transfers between devices  21.4 us (25%)
  local copies, waits for them, and re-layouts  1.02 us (1%)
    pallas_call x9, Pallas kernels, call(): pl.pallas_call(kernel, out_shape=[jax.ShapeDtypeStruct(shape, dtype) for...  28 us
    ppermute x27, starting transfers between devices, swap(): lax.ppermute(value, 'rcv', [(at, at ^ 1 << bit) for at in range(count)])  25 us
    ppermute x27, waiting for transfers between devices, swap(): lax.ppermute(value, 'rcv', [(at, at ^ 1 << bit) for at in range(count)])  21.4 us
    ppermute x6, starting transfers between devices, jump(): lax.ppermute(value, 'rcv', [(at, at ^ mask << 1) for at in range(count)])  7.73 us
  transfers between devices with their start and end apart: 33, of which 11 were waited for; matrix products, arithmetic and copies ran while one was open for 2% of the time, Pallas kernels for 32%

profile of v3, /device:TPU:0, one launch (start us, length us, event | category | flops | bytes accessed | tf_op | source)
XLA Modules:
  0.0 84.3 jit_solution(16049343682486412905)
XLA Ops:
  0.6 0.5 collective-permute-start.3
  1.1 1.0 %fusion = (f32[2,8,2560]{2,1,0:T(8,128)S(1)}, f32[2,8,2560]{2,1,0:T(8,128)S(1)}) fusion(f32[2,16,2560]{2,1,0:T(8,128)} %param.3), kind=kLoop, calls=%fused_computation | loop fusion | bytes 655360 | tf_op jit(solution)/shard_map/slice | solution.py:264
  2.2 2.6 %collective-permute-start.17 = (f32[2,8,2560]{2,1,0:T(8,128)S(1)}, f32[2,8,2560]{2,1,0:T(8,128)S(1)}, u32[]{:S(2)}, u32[]{:S(2)}) collective-permute-start(f32[2,8,2560]{2,1,0:T(8,128)S(1)} %get-tuple-element.82.refs_0_), channel_id=1, source_target_pairs={{0,2},{1,3},{2,0},{3,1},{4,6},{5,7},{6,4},{7,5},{8,10},{9,11},{10,... | collective-permute-start | bytes 491528 | tf_op jit(solution)/shard_map/ppermute | solution.py:258
  4.7 1.5 %collective-permute-start.18 = (f32[2,8,2560]{2,1,0:T(8,128)S(1)}, f32[2,8,2560]{2,1,0:T(8,128)S(1)}, u32[]{:S(2)}, u32[]{:S(2)}) collective-permute-start(f32[2,8,2560]{2,1,0:T(8,128)S(1)} %get-tuple-element.82.refs_0_), channel_id=1, source_target_pairs={{0,4},{1,5},{2,6},{3,7},{4,0},{5,1},{6,2},{7,3},{8,12},{9,13},{10,... | collective-permute-start | bytes 491528 | tf_op jit(solution)/shard_map/ppermute | solution.py:258
  6.3 0.0 collective-permute-start.19
  6.3 1.9 %collective-permute-start = (f32[2,8,2560]{2,1,0:T(8,128)S(1)}, f32[2,8,2560]{2,1,0:T(8,128)S(1)}, u32[]{:S(2)}, u32[]{:S(2)}) collective-permute-start(f32[2,8,2560]{2,1,0:T(8,128)S(1)} %get-tuple-element.83.refs_0_), channel_id=1, source_target_pairs={{0,2},{1,3},{2,0},{3,1},{4,6},{5,7},{6,4},{7,5},{8,10},{9,11},{10,... | collective-permute-start | bytes 491528 | tf_op jit(solution)/shard_map/ppermute | solution.py:258
  8.2 4.8 %shard_map.41 = (bf16[2,256,2560]{2,1,0:T(8,128)(2,1)S(1)}, bf16[2,256,2560]{2,1,0:T(8,128)(2,1)S(1)}, bf16[2,2560,256]{2,1,0:T(8,128)(2,1)S(1)}, bf16[2,2560,256]{2,1,0:T(8,128)(2,1)S(1)}, f32[8,128]{1,0:T(8,128)S(1)}) custom-call(f32[2,256,2560]{2,1,0:T(8,128)} %down_ref.1), custom_call_target="tpu_custom_call" | custom-call | bytes 5242880 | tf_op jit(solution)/shard_map/pallas_call | solution.py:28
  13.0 0.0 collective-permute-done.3.down_ref
  13.0 1.6 %collective-permute-start.1 = (f32[2,8,2560]{2,1,0:T(8,128)S(1)}, f32[2,8,2560]{2,1,0:T(8,128)S(1)}, u32[]{:S(2)}, u32[]{:S(2)}) collective-permute-start(f32[2,8,2560]{2,1,0:T(8,128)S(1)} %get-tuple-element.83.refs_0_), channel_id=1, source_target_pairs={{0,4},{1,5},{2,6},{3,7},{4,0},{5,1},{6,2},{7,3},{8,12},{9,13},{10,... | collective-permute-start | bytes 491528 | tf_op jit(solution)/shard_map/ppermute | solution.py:258
  14.6 2.2 %shard_map.42 = (bf16[2,256,2560]{2,1,0:T(8,128)(2,1)S(1)}, bf16[2,256,2560]{2,1,0:T(8,128)(2,1)S(1)}, bf16[2,2560,256]{2,1,0:T(8,128)(2,1)S(1)}, bf16[2,2560,256]{2,1,0:T(8,128)(2,1)S(1)}, f32[8,128]{1,0:T(8,128)S(1)}) custom-call(f32[2,256,2560]{2,1,0:T(8,128)S(1)} %collective-permute-done.3.down_ref), custom_call_target="tpu_custom_call" | custom-call | bytes 5242880 | tf_op jit(solution)/shard_map/pallas_call | solution.py:28
  16.8 0.0 collective-permute-done.17.refs_1_
  16.8 0.1 collective-permute-start.2
  16.9 0.0 collective-permute-done.18.refs_2_
  16.9 0.0 collective-permute-done.19.refs_3_
  16.9 4.1 %shard_map.46 = (f32[64,512]{1,0:T(8,128)S(1)}, f32[32,1408]{1,0:T(8,128)S(1)}, f32[32,1408]{1,0:T(8,128)S(1)}, f32[32,1280]{1,0:T(8,128)S(1)}, f32[32,1280]{1,0:T(8,128)S(1)}) custom-call(f32[2,8,2560]{2,1,0:T(8,128)S(1)} %get-tuple-element.82.refs_0_, f32[2,8,2560]{2,1,0:T(8,128)S(1)} %collective-permute-done.17.refs_1_, ...), custom_call_target="tpu_custom_call" | custom-call | flops 2013265920 | bytes 21635072 | tf_op jit(solution)/shard_map/pallas_call | solution.py:28
  21.1 2.0 %collective-permute-start.23 = (f32[32,1280]{1,0:T(8,128)S(1)}, f32[32,1280]{1,0:T(8,128)S(1)}, u32[]{:S(2)}, u32[]{:S(2)}) collective-permute-start(f32[32,1280]{1,0:T(8,128)S(1)} %get-tuple-element.70), channel_id=1, source_target_pairs={{0,4},{1,5},{2,6},{3,7},{4,0},{5,1},{6,2},{7,3},{8,12},{9,13},{10,... | collective-permute-start | bytes 491528 | tf_op jit(solution)/shard_map/ppermute | solution.py:246
  23.1 1.5 %collective-permute-start.20 = (f32[32,1408]{1,0:T(8,128)S(1)}, f32[32,1408]{1,0:T(8,128)S(1)}, u32[]{:S(2)}, u32[]{:S(2)}) collective-permute-start(f32[32,1408]{1,0:T(8,128)S(1)} %get-tuple-element.68), channel_id=1, source_target_pairs={{0,2},{1,3},{2,0},{3,1},{4,6},{5,7},{6,4},{7,5},{8,10},{9,11},{10,... | collective-permute-start | bytes 540680 | tf_op jit(solution)/shard_map/ppermute | solution.py:246
  24.6 4.1 %shard_map.43 = (f32[64,512]{1,0:T(8,128)S(1)}, f32[32,1408]{1,0:T(8,128)S(1)}, f32[32,1408]{1,0:T(8,128)S(1)}, f32[32,1280]{1,0:T(8,128)S(1)}, f32[32,1280]{1,0:T(8,128)S(1)}) custom-call(f32[2,8,2560]{2,1,0:T(8,128)S(1)} %get-tuple-element.83.refs_0_, f32[2,8,2560]{2,1,0:T(8,128)S(1)} %collective-permute-done.refs_1_, ...), custom_call_target="tpu_custom_call" | custom-call | flops 2013265920 | bytes 21635072 | tf_op jit(solution)/shard_map/pallas_call | solution.py:28
  28.7 0.6 collective-permute-start.4
  29.4 0.1 collective-permute-start.21
  29.5 1.9 %collective-permute-start.7 = (f32[32,1280]{1,0:T(8,128)S(1)}, f32[32,1280]{1,0:T(8,128)S(1)}, u32[]{:S(2)}, u32[]{:S(2)}) collective-permute-start(f32[32,1280]{1,0:T(8,128)S(1)} %get-tuple-element.55), channel_id=1, source_target_pairs={{0,4},{1,5},{2,6},{3,7},{4,0},{5,1},{6,2},{7,3},{8,12},{9,13},{10,... | collective-permute-start | bytes 491528 | tf_op jit(solution)/shard_map/ppermute | solution.py:246
  31.5 1.6 %collective-permute-start.24 = (f32[32,1280]{1,0:T(8,128)S(1)}, f32[32,1280]{1,0:T(8,128)S(1)}, u32[]{:S(2)}, u32[]{:S(2)}) collective-permute-start(f32[32,1280]{1,0:T(8,128)S(1)} %add.58), channel_id=1, source_target_pairs={{0,2},{1,3},{2,0},{3,1},{4,6},{5,7},{6,4},{7,5},{8,10},{9,11},{10,... | collective-permute-start | bytes 491528 | tf_op jit(solution)/shard_map/ppermute | solution.py:246
  33.0 2.9 %collective-permute-done.4 = f32[32,1408]{1,0:T(8,128)S(1)} collective-permute-done((f32[32,1408]{1,0:T(8,128)S(1)}, f32[32,1408]{1,0:T(8,128)S(1)}, u32[]{:S(2)}, u32[]{:S(2)}) %collective-permute-start.4) | collective-permute-done | bytes 180256 | tf_op jit(solution)/shard_map/ppermute | solution.py:246
  36.0 0.1 collective-permute-start.5
  36.1 0.8 collective-permute-done.21
  36.9 1.6 %collective-permute-start.22 = (f32[32,1408]{1,0:T(8,128)S(1)}, f32[32,1408]{1,0:T(8,128)S(1)}, u32[]{:S(2)}, u32[]{:S(2)}) collective-permute-start(f32[32,1408]{1,0:T(8,128)S(1)} %add.57.refs_0_), channel_id=1, source_target_pairs={{0,2},{1,3},{2,0},{3,1},{4,6},{5,7},{6,4},{7,5},{8,10},{9,11},{10,... | collective-permute-start | bytes 540680 | tf_op jit(solution)/shard_map/ppermute | solution.py:246
  38.5 1.6 %collective-permute-done.7 = f32[32,1280]{1,0:T(8,128)S(1)} collective-permute-done((f32[32,1280]{1,0:T(8,128)S(1)}, f32[32,1280]{1,0:T(8,128)S(1)}, u32[]{:S(2)}, u32[]{:S(2)}) %collective-permute-start.7) | collective-permute-done | bytes 163872 | tf_op jit(solution)/shard_map/ppermute | solution.py:246
  40.2 1.8 %collective-permute-start.8 = (f32[32,1280]{1,0:T(8,128)S(1)}, f32[32,1280]{1,0:T(8,128)S(1)}, u32[]{:S(2)}, u32[]{:S(2)}) collective-permute-start(f32[32,1280]{1,0:T(8,128)S(1)} %add.50), channel_id=1, source_target_pairs={{0,2},{1,3},{2,0},{3,1},{4,6},{5,7},{6,4},{7,5},{8,10},{9,11},{10,... | collective-permute-start | bytes 491528 | tf_op jit(solution)/shard_map/ppermute | solution.py:246
  42.0 0.6 collective-permute-start.25
  42.6 4.7 %collective-permute-done.8 = f32[32,1280]{1,0:T(8,128)S(1)} collective-permute-done((f32[32,1280]{1,0:T(8,128)S(1)}, f32[32,1280]{1,0:T(8,128)S(1)}, u32[]{:S(2)}, u32[]{:S(2)}) %collective-permute-start.8) | collective-permute-done | bytes 163872 | tf_op jit(solution)/shard_map/ppermute | solution.py:246
  47.3 0.1 collective-permute-start.9
  47.4 1.8 %collective-permute-start.6 = (f32[32,1408]{1,0:T(8,128)S(1)}, f32[32,1408]{1,0:T(8,128)S(1)}, u32[]{:S(2)}, u32[]{:S(2)}) collective-permute-start(f32[32,1408]{1,0:T(8,128)S(1)} %add.49.refs_0_), channel_id=1, source_target_pairs={{0,2},{1,3},{2,0},{3,1},{4,6},{5,7},{6,4},{7,5},{8,10},{9,11},{10,... | collective-permute-start | bytes 540680 | tf_op jit(solution)/shard_map/ppermute | solution.py:246
  49.2 0.0 collective-permute-done.25.refs_3_
  49.3 4.0 %shard_map.47 = (f32[64,2560]{1,0:T(8,128)S(1)}, f32[64,128]{1,0:T(8,128)S(1)}, f32[64,512]{1,0:T(8,128)S(1)}, f32[64,512]{1,0:T(8,128)S(1)}, f32[32,1408]{1,0:T...) custom-call(f32[32,1408]{1,0:T(8,128)S(1)} %add.57.refs_0_, ...), custom_call_target="tpu_custom_call" | custom-call | flops 2013265920 | bytes 21790720 | tf_op jit(solution)/shard_map/pallas_call | solution.py:28
  53.3 1.6 %collective-permute-start.29 = (f32[32,1280]{1,0:T(8,128)S(1)}, f32[32,1280]{1,0:T(8,128)S(1)}, u32[]{:S(2)}, u32[]{:S(2)}) collective-permute-start(f32[32,1280]{1,0:T(8,128)S(1)} %get-tuple-element.75), channel_id=1, source_target_pairs={{0,4},{1,5},{2,6},{3,7},{4,0},{5,1},{6,2},{7,3},{8,12},{9,13},{10,... | collective-permute-start | bytes 491528 | tf_op jit(solution)/shard_map/ppermute | solution.py:246
  54.9 0.7 collective-permute-start.26
  55.6 4.2 %shard_map.44 = (f32[64,2560]{1,0:T(8,128)S(1)}, f32[64,128]{1,0:T(8,128)S(1)}, f32[64,512]{1,0:T(8,128)S(1)}, f32[64,512]{1,0:T(8,128)S(1)}, f32[32,1408]{1,0:T...) custom-call(f32[32,1408]{1,0:T(8,128)S(1)} %add.49.refs_0_, ...), custom_call_target="tpu_custom_call" | custom-call | flops 2013265920 | bytes 21790720 | tf_op jit(solution)/shard_map/pallas_call | solution.py:28
  59.9 1.4 %collective-permute-start.10 = (f32[32,1408]{1,0:T(8,128)S(1)}, f32[32,1408]{1,0:T(8,128)S(1)}, u32[]{:S(2)}, u32[]{:S(2)}) collective-permute-start(f32[32,1408]{1,0:T(8,128)S(1)} %get-tuple-element.58), channel_id=1, source_target_pairs={{0,2},{1,3},{2,0},{3,1},{4,6},{5,7},{6,4},{7,5},{8,10},{9,11},{10,... | collective-permute-start | bytes 540680 | tf_op jit(solution)/shard_map/ppermute | solution.py:246
  61.3 0.5 collective-permute-start.13
  61.7 0.0 collective-permute-done.26
  61.8 1.6 %collective-permute-start.27 = (f32[32,1408]{1,0:T(8,128)S(1)}, f32[32,1408]{1,0:T(8,128)S(1)}, u32[]{:S(2)}, u32[]{:S(2)}) collective-permute-start(f32[32,1408]{1,0:T(8,128)S(1)} %add.60), channel_id=1, source_target_pairs={{0,4},{1,5},{2,6},{3,7},{4,0},{5,1},{6,2},{7,3},{8,12},{9,13},{10,... | collective-permute-start | bytes 540680 | tf_op jit(solution)/shard_map/ppermute | solution.py:246
  63.4 0.0 collective-permute-done.29
  63.4 0.8 collective-permute-start.30
  64.2 2.6 %collective-permute-done.10 = f32[32,1408]{1,0:T(8,128)S(1)} collective-permute-done((f32[32,1408]{1,0:T(8,128)S(1)}, f32[32,1408]{1,0:T(8,128)S(1)}, u32[]{:S(2)}, u32[]{:S(2)}) %collective-permute-start.10) | collective-permute-done | bytes 180256 | tf_op jit(solution)/shard_map/ppermute | solution.py:246
  66.8 0.1 collective-permute-start.11
  66.9 1.5 %collective-permute-done.13 = f32[32,1280]{1,0:T(8,128)S(1)} collective-permute-done((f32[32,1280]{1,0:T(8,128)S(1)}, f32[32,1280]{1,0:T(8,128)S(1)}, u32[]{:S(2)}, u32[]{:S(2)}) %collective-permute-start.13) | collective-permute-done | bytes 163872 | tf_op jit(solution)/shard_map/ppermute | solution.py:246
  68.4 0.6 collective-permute-start.14
  69.0 2.9 %collective-permute-done.27 = f32[32,1408]{1,0:T(8,128)S(1)} collective-permute-done((f32[32,1408]{1,0:T(8,128)S(1)}, f32[32,1408]{1,0:T(8,128)S(1)}, u32[]{:S(2)}, u32[]{:S(2)}) %collective-permute-start.27) | collective-permute-done | bytes 180256 | tf_op jit(solution)/shard_map/ppermute | solution.py:246
  71.9 0.7 collective-permute-start.28
  72.6 0.1 collective-permute-start.31
  72.7 1.1 %collective-permute-done.11 = f32[32,1408]{1,0:T(8,128)S(1)} collective-permute-done((f32[32,1408]{1,0:T(8,128)S(1)}, f32[32,1408]{1,0:T(8,128)S(1)}, u32[]{:S(2)}, u32[]{:S(2)}) %collective-permute-start.11) | collective-permute-done | bytes 180256 | tf_op jit(solution)/shard_map/ppermute | solution.py:246
  73.8 1.0 %collective-permute-start.12 = (f32[32,1408]{1,0:T(8,128)S(1)}, f32[32,1408]{1,0:T(8,128)S(1)}, u32[]{:S(2)}, u32[]{:S(2)}) collective-permute-start(f32[32,1408]{1,0:T(8,128)S(1)} %add.53.refs_0_), channel_id=1, source_target_pairs={{0,2},{1,3},{2,0},{3,1},{4,6},{5,7},{6,4},{7,5},{8,10},{9,11},{10,... | collective-permute-start | bytes 540680 | tf_op jit(solution)/shard_map/ppermute | solution.py:246
  74.8 0.0 collective-permute-done.14
  74.8 1.5 %collective-permute-start.15 = (f32[32,1280]{1,0:T(8,128)S(1)}, f32[32,1280]{1,0:T(8,128)S(1)}, u32[]{:S(2)}, u32[]{:S(2)}) collective-permute-start(f32[32,1280]{1,0:T(8,128)S(1)} %add.55.refs_2_), channel_id=1, source_target_pairs={{0,4},{1,5},{2,6},{3,7},{4,0},{5,1},{6,2},{7,3},{8,12},{9,13},{10,... | collective-permute-start | bytes 491528 | tf_op jit(solution)/shard_map/ppermute | solution.py:246
  76.3 1.7 %collective-permute-done.31.refs_3_ = f32[32,1280]{1,0:T(8,128)S(1)} collective-permute-done((f32[32,1280]{1,0:T(8,128)S(1)}, f32[32,1280]{1,0:T(8,128)S(1)}, u32[]{:S(2)}, u32[]{:S(2)}) %collective-permute-start.31) | collective-permute-done | bytes 163872 | tf_op jit(solution)/shard_map/ppermute | solution.py:246
  78.0 1.8 %shard_map.48 = (f32[2,64,256]{2,1,0:T(8,128)S(1)}, f32[2,64,256]{2,1,0:T(8,128)S(1)}) custom-call(f32[32,1408]{1,0:T(8,128)S(1)} %add.61.refs_0_, f32[32,1408]{1,0:T(8,128)S(1)} %collective-permute-done.28.refs_1_, f32[32,1280]{1,0:T(8,128)S(1)} %add.63.refs_2_, f32[32,1280]{1,0:T(8,128)S(1)} %collective-permute-done.31.refs_3_, ...), custom_call_target="tpu_custom_call" | custom-call | flops 1006632960 | bytes 12255232 | tf_op jit(solution)/shard_map/pallas_call | solution.py:28
  79.8 0.1 collective-permute-start.32
  79.9 0.3 collective-permute-done.15.refs_3_
  80.2 0.0 collective-permute-done.12.refs_1_
  80.2 1.8 %shard_map.45 = (f32[2,64,256]{2,1,0:T(8,128)S(1)}, f32[2,64,256]{2,1,0:T(8,128)S(1)}) custom-call(f32[32,1408]{1,0:T(8,128)S(1)} %add.53.refs_0_, f32[32,1408]{1,0:T(8,128)S(1)} %collective-permute-done.12.refs_1_, f32[32,1280]{1,0:T(8,128)S(1)} %add.55.refs_2_, f32[32,1280]{1,0:T(8,128)S(1)} %collective-permute-done.15.refs_3_, ...), custom_call_target="tpu_custom_call" | custom-call | flops 1006632960 | bytes 12255232 | tf_op jit(solution)/shard_map/pallas_call | solution.py:28
  82.0 0.2 collective-permute-start.16
  82.2 0.0 collective-permute-done.32.refs_3_
  82.2 1.2 %collective-permute-done.16.refs_1_ = f32[2,64,256]{2,1,0:T(8,128)S(1)} collective-permute-done((f32[2,64,256]{2,1,0:T(8,128)S(1)}, f32[2,64,256]{2,1,0:T(8,128)S(1)}, u32[]{:S(2)}, u32[]{:S(2)}) %collective-permute-start.16) | collective-permute-done | bytes 131104 | tf_op jit(solution)/shard_map/ppermute | solution.py:246
  83.4 0.9 %shard_map.49 = (f32[2,256,128]{2,1,0:T(8,128)}, f32[2,256,128]{2,1,0:T(8,128)}) custom-call(f32[2,64,256]{2,1,0:T(8,128)S(1)} %get-tuple-element.65.refs_0_, f32[2,64,256]{2,1,0:T(8,128)S(1)} %collective-permute-done.16.refs_1_, f32[2,64,256]{2,1,0:T(8,128)S(1)} %get-tuple-element.80.refs_2_, f32[2,64,256]{2,1,0:T(8,128)S(1)} %collective-permute-done.32.refs_3_), custom_call_target="tpu_custom_call" | custom-call | bytes 524288 | tf_op jit(solution)/shard_map/pallas_call | solution.py:28
  (28 shorter events, 0.4 us)
Async XLA Ops:
  0.6 12.4 %collective-permute-start.3 = (f32[2,256,2560]{2,1,0:T(8,128)}, f32[2,256,2560]{2,1,0:T(8,128)S(1)}, u32[]{:S(2)}, u32[]{:S(2)}) collective-permute-start(f32[2,256,2560]{2,1,0:T(8,128)} %down_ref.1), channel_id=1, source_target_pairs={{0,1},{1,0},{2,3},{3,2},{4,5},{5,4},{6,7},{7,6},{8,9},{9,8},{10,11... | collective-permute-start | bytes 15728648 | tf_op jit(solution)/shard_map/ppermute | solution.py:246
  2.2 14.7 %collective-permute-start.17 = (f32[2,8,2560]{2,1,0:T(8,128)S(1)}, f32[2,8,2560]{2,1,0:T(8,128)S(1)}, u32[]{:S(2)}, u32[]{:S(2)}) collective-permute-start(f32[2,8,2560]{2,1,0:T(8,128)S(1)} %get-tuple-element.82.refs_0_), channel_id=1, source_target_pairs={{0,2},{1,3},{2,0},{3,1},{4,6},{5,7},{6,4},{7,5},{8,10},{9,11},{10,... | collective-permute-start | bytes 491528 | tf_op jit(solution)/shard_map/ppermute | solution.py:258
  4.7 12.2 %collective-permute-start.18 = (f32[2,8,2560]{2,1,0:T(8,128)S(1)}, f32[2,8,2560]{2,1,0:T(8,128)S(1)}, u32[]{:S(2)}, u32[]{:S(2)}) collective-permute-start(f32[2,8,2560]{2,1,0:T(8,128)S(1)} %get-tuple-element.82.refs_0_), channel_id=1, source_target_pairs={{0,4},{1,5},{2,6},{3,7},{4,0},{5,1},{6,2},{7,3},{8,12},{9,13},{10,... | collective-permute-start | bytes 491528 | tf_op jit(solution)/shard_map/ppermute | solution.py:258
  6.3 10.7 %collective-permute-start.19 = (f32[2,8,2560]{2,1,0:T(8,128)S(1)}, f32[2,8,2560]{2,1,0:T(8,128)S(1)}, u32[]{:S(2)}, u32[]{:S(2)}) collective-permute-start(f32[2,8,2560]{2,1,0:T(8,128)S(1)} %get-tuple-element.82.refs_0_), channel_id=1, source_target_pairs={{0,6},{1,7},{2,4},{3,5},{4,2},{5,3},{6,0},{7,1},{8,14},{9,15},{10,... | collective-permute-start | bytes 491528 | tf_op jit(solution)/shard_map/ppermute | solution.py:258
  6.3 18.3 %collective-permute-start = (f32[2,8,2560]{2,1,0:T(8,128)S(1)}, f32[2,8,2560]{2,1,0:T(8,128)S(1)}, u32[]{:S(2)}, u32[]{:S(2)}) collective-permute-start(f32[2,8,2560]{2,1,0:T(8,128)S(1)} %get-tuple-element.83.refs_0_), channel_id=1, source_target_pairs={{0,2},{1,3},{2,0},{3,1},{4,6},{5,7},{6,4},{7,5},{8,10},{9,11},{10,... | collective-permute-start | bytes 491528 | tf_op jit(solution)/shard_map/ppermute | solution.py:258
  13.0 11.6 %collective-permute-start.1 = (f32[2,8,2560]{2,1,0:T(8,128)S(1)}, f32[2,8,2560]{2,1,0:T(8,128)S(1)}, u32[]{:S(2)}, u32[]{:S(2)}) collective-permute-start(f32[2,8,2560]{2,1,0:T(8,128)S(1)} %get-tuple-element.83.refs_0_), channel_id=1, source_target_pairs={{0,4},{1,5},{2,6},{3,7},{4,0},{5,1},{6,2},{7,3},{8,12},{9,13},{10,... | collective-permute-start | bytes 491528 | tf_op jit(solution)/shard_map/ppermute | solution.py:258
  16.8 7.8 %collective-permute-start.2 = (f32[2,8,2560]{2,1,0:T(8,128)S(1)}, f32[2,8,2560]{2,1,0:T(8,128)S(1)}, u32[]{:S(2)}, u32[]{:S(2)}) collective-permute-start(f32[2,8,2560]{2,1,0:T(8,128)S(1)} %get-tuple-element.83.refs_0_), channel_id=1, source_target_pairs={{0,6},{1,7},{2,4},{3,5},{4,2},{5,3},{6,0},{7,1},{8,14},{9,15},{10,... | collective-permute-start | bytes 491528 | tf_op jit(solution)/shard_map/ppermute | solution.py:258
  21.1 10.4 %collective-permute-start.23 = (f32[32,1280]{1,0:T(8,128)S(1)}, f32[32,1280]{1,0:T(8,128)S(1)}, u32[]{:S(2)}, u32[]{:S(2)}) collective-permute-start(f32[32,1280]{1,0:T(8,128)S(1)} %get-tuple-element.70), channel_id=1, source_target_pairs={{0,4},{1,5},{2,6},{3,7},{4,0},{5,1},{6,2},{7,3},{8,12},{9,13},{10,... | collective-permute-start | bytes 491528 | tf_op jit(solution)/shard_map/ppermute | solution.py:246
  23.1 6.2 %collective-permute-start.20 = (f32[32,1408]{1,0:T(8,128)S(1)}, f32[32,1408]{1,0:T(8,128)S(1)}, u32[]{:S(2)}, u32[]{:S(2)}) collective-permute-start(f32[32,1408]{1,0:T(8,128)S(1)} %get-tuple-element.68), channel_id=1, source_target_pairs={{0,2},{1,3},{2,0},{3,1},{4,6},{5,7},{6,4},{7,5},{8,10},{9,11},{10,... | collective-permute-start | bytes 540680 | tf_op jit(solution)/shard_map/ppermute | solution.py:246
  28.7 7.2 %collective-permute-start.4 = (f32[32,1408]{1,0:T(8,128)S(1)}, f32[32,1408]{1,0:T(8,128)S(1)}, u32[]{:S(2)}, u32[]{:S(2)}) collective-permute-start(f32[32,1408]{1,0:T(8,128)S(1)} %get-tuple-element.53), channel_id=1, source_target_pairs={{0,2},{1,3},{2,0},{3,1},{4,6},{5,7},{6,4},{7,5},{8,10},{9,11},{10,... | collective-permute-start | bytes 540680 | tf_op jit(solution)/shard_map/ppermute | solution.py:246
  29.4 7.6 %collective-permute-start.21 = (f32[32,1408]{1,0:T(8,128)S(1)}, f32[32,1408]{1,0:T(8,128)S(1)}, u32[]{:S(2)}, u32[]{:S(2)}) collective-permute-start(f32[32,1408]{1,0:T(8,128)S(1)} %add.56), channel_id=1, source_target_pairs={{0,4},{1,5},{2,6},{3,7},{4,0},{5,1},{6,2},{7,3},{8,12},{9,13},{10,... | collective-permute-start | bytes 540680 | tf_op jit(solution)/shard_map/ppermute | solution.py:246
  29.5 10.6 %collective-permute-start.7 = (f32[32,1280]{1,0:T(8,128)S(1)}, f32[32,1280]{1,0:T(8,128)S(1)}, u32[]{:S(2)}, u32[]{:S(2)}) collective-permute-start(f32[32,1280]{1,0:T(8,128)S(1)} %get-tuple-element.55), channel_id=1, source_target_pairs={{0,4},{1,5},{2,6},{3,7},{4,0},{5,1},{6,2},{7,3},{8,12},{9,13},{10,... | collective-permute-start | bytes 491528 | tf_op jit(solution)/shard_map/ppermute | solution.py:246
  31.5 10.5 %collective-permute-start.24 = (f32[32,1280]{1,0:T(8,128)S(1)}, f32[32,1280]{1,0:T(8,128)S(1)}, u32[]{:S(2)}, u32[]{:S(2)}) collective-permute-start(f32[32,1280]{1,0:T(8,128)S(1)} %add.58), channel_id=1, source_target_pairs={{0,2},{1,3},{2,0},{3,1},{4,6},{5,7},{6,4},{7,5},{8,10},{9,11},{10,... | collective-permute-start | bytes 491528 | tf_op jit(solution)/shard_map/ppermute | solution.py:246
  36.0 11.4 %collective-permute-start.5 = (f32[32,1408]{1,0:T(8,128)S(1)}, f32[32,1408]{1,0:T(8,128)S(1)}, u32[]{:S(2)}, u32[]{:S(2)}) collective-permute-start(f32[32,1408]{1,0:T(8,128)S(1)} %add.48), channel_id=1, source_target_pairs={{0,4},{1,5},{2,6},{3,7},{4,0},{5,1},{6,2},{7,3},{8,12},{9,13},{10,... | collective-permute-start | bytes 540680 | tf_op jit(solution)/shard_map/ppermute | solution.py:246
  36.9 12.3 %collective-permute-start.22 = (f32[32,1408]{1,0:T(8,128)S(1)}, f32[32,1408]{1,0:T(8,128)S(1)}, u32[]{:S(2)}, u32[]{:S(2)}) collective-permute-start(f32[32,1408]{1,0:T(8,128)S(1)} %add.57.refs_0_), channel_id=1, source_target_pairs={{0,2},{1,3},{2,0},{3,1},{4,6},{5,7},{6,4},{7,5},{8,10},{9,11},{10,... | collective-permute-start | bytes 540680 | tf_op jit(solution)/shard_map/ppermute | solution.py:246
  40.2 7.1 %collective-permute-start.8 = (f32[32,1280]{1,0:T(8,128)S(1)}, f32[32,1280]{1,0:T(8,128)S(1)}, u32[]{:S(2)}, u32[]{:S(2)}) collective-permute-start(f32[32,1280]{1,0:T(8,128)S(1)} %add.50), channel_id=1, source_target_pairs={{0,2},{1,3},{2,0},{3,1},{4,6},{5,7},{6,4},{7,5},{8,10},{9,11},{10,... | collective-permute-start | bytes 491528 | tf_op jit(solution)/shard_map/ppermute | solution.py:246
  42.0 7.2 %collective-permute-start.25 = (f32[32,1280]{1,0:T(8,128)S(1)}, f32[32,1280]{1,0:T(8,128)S(1)}, u32[]{:S(2)}, u32[]{:S(2)}) collective-permute-start(f32[32,1280]{1,0:T(8,128)S(1)} %add.59.refs_2_), channel_id=1, source_target_pairs={{0,4},{1,5},{2,6},{3,7},{4,0},{5,1},{6,2},{7,3},{8,12},{9,13},{10,... | collective-permute-start | bytes 491528 | tf_op jit(solution)/shard_map/ppermute | solution.py:246
  47.3 8.3 %collective-permute-start.9 = (f32[32,1280]{1,0:T(8,128)S(1)}, f32[32,1280]{1,0:T(8,128)S(1)}, u32[]{:S(2)}, u32[]{:S(2)}) collective-permute-start(f32[32,1280]{1,0:T(8,128)S(1)} %add.51.refs_2_), channel_id=1, source_target_pairs={{0,4},{1,5},{2,6},{3,7},{4,0},{5,1},{6,2},{7,3},{8,12},{9,13},{10,... | collective-permute-start | bytes 491528 | tf_op jit(solution)/shard_map/ppermute | solution.py:246
  47.4 8.2 %collective-permute-start.6 = (f32[32,1408]{1,0:T(8,128)S(1)}, f32[32,1408]{1,0:T(8,128)S(1)}, u32[]{:S(2)}, u32[]{:S(2)}) collective-permute-start(f32[32,1408]{1,0:T(8,128)S(1)} %add.49.refs_0_), channel_id=1, source_target_pairs={{0,2},{1,3},{2,0},{3,1},{4,6},{5,7},{6,4},{7,5},{8,10},{9,11},{10,... | collective-permute-start | bytes 540680 | tf_op jit(solution)/shard_map/ppermute | solution.py:246
  53.3 10.1 %collective-permute-start.29 = (f32[32,1280]{1,0:T(8,128)S(1)}, f32[32,1280]{1,0:T(8,128)S(1)}, u32[]{:S(2)}, u32[]{:S(2)}) collective-permute-start(f32[32,1280]{1,0:T(8,128)S(1)} %get-tuple-element.75), channel_id=1, source_target_pairs={{0,4},{1,5},{2,6},{3,7},{4,0},{5,1},{6,2},{7,3},{8,12},{9,13},{10,... | collective-permute-start | bytes 491528 | tf_op jit(solution)/shard_map/ppermute | solution.py:246
  54.9 6.8 %collective-permute-start.26 = (f32[32,1408]{1,0:T(8,128)S(1)}, f32[32,1408]{1,0:T(8,128)S(1)}, u32[]{:S(2)}, u32[]{:S(2)}) collective-permute-start(f32[32,1408]{1,0:T(8,128)S(1)} %get-tuple-element.73), channel_id=1, source_target_pairs={{0,2},{1,3},{2,0},{3,1},{4,6},{5,7},{6,4},{7,5},{8,10},{9,11},{10,... | collective-permute-start | bytes 540680 | tf_op jit(solution)/shard_map/ppermute | solution.py:246
  59.9 6.9 %collective-permute-start.10 = (f32[32,1408]{1,0:T(8,128)S(1)}, f32[32,1408]{1,0:T(8,128)S(1)}, u32[]{:S(2)}, u32[]{:S(2)}) collective-permute-start(f32[32,1408]{1,0:T(8,128)S(1)} %get-tuple-element.58), channel_id=1, source_target_pairs={{0,2},{1,3},{2,0},{3,1},{4,6},{5,7},{6,4},{7,5},{8,10},{9,11},{10,... | collective-permute-start | bytes 540680 | tf_op jit(solution)/shard_map/ppermute | solution.py:246
  61.3 7.1 %collective-permute-start.13 = (f32[32,1280]{1,0:T(8,128)S(1)}, f32[32,1280]{1,0:T(8,128)S(1)}, u32[]{:S(2)}, u32[]{:S(2)}) collective-permute-start(f32[32,1280]{1,0:T(8,128)S(1)} %get-tuple-element.60), channel_id=1, source_target_pairs={{0,4},{1,5},{2,6},{3,7},{4,0},{5,1},{6,2},{7,3},{8,12},{9,13},{10,... | collective-permute-start | bytes 491528 | tf_op jit(solution)/shard_map/ppermute | solution.py:246
  61.8 10.1 %collective-permute-start.27 = (f32[32,1408]{1,0:T(8,128)S(1)}, f32[32,1408]{1,0:T(8,128)S(1)}, u32[]{:S(2)}, u32[]{:S(2)}) collective-permute-start(f32[32,1408]{1,0:T(8,128)S(1)} %add.60), channel_id=1, source_target_pairs={{0,4},{1,5},{2,6},{3,7},{4,0},{5,1},{6,2},{7,3},{8,12},{9,13},{10,... | collective-permute-start | bytes 540680 | tf_op jit(solution)/shard_map/ppermute | solution.py:246
  63.4 9.2 %collective-permute-start.30 = (f32[32,1280]{1,0:T(8,128)S(1)}, f32[32,1280]{1,0:T(8,128)S(1)}, u32[]{:S(2)}, u32[]{:S(2)}) collective-permute-start(f32[32,1280]{1,0:T(8,128)S(1)} %add.62), channel_id=1, source_target_pairs={{0,2},{1,3},{2,0},{3,1},{4,6},{5,7},{6,4},{7,5},{8,10},{9,11},{10,... | collective-permute-start | bytes 491528 | tf_op jit(solution)/shard_map/ppermute | solution.py:246
  66.8 7.0 %collective-permute-start.11 = (f32[32,1408]{1,0:T(8,128)S(1)}, f32[32,1408]{1,0:T(8,128)S(1)}, u32[]{:S(2)}, u32[]{:S(2)}) collective-permute-start(f32[32,1408]{1,0:T(8,128)S(1)} %add.52), channel_id=1, source_target_pairs={{0,4},{1,5},{2,6},{3,7},{4,0},{5,1},{6,2},{7,3},{8,12},{9,13},{10,... | collective-permute-start | bytes 540680 | tf_op jit(solution)/shard_map/ppermute | solution.py:246
  68.4 6.4 %collective-permute-start.14 = (f32[32,1280]{1,0:T(8,128)S(1)}, f32[32,1280]{1,0:T(8,128)S(1)}, u32[]{:S(2)}, u32[]{:S(2)}) collective-permute-start(f32[32,1280]{1,0:T(8,128)S(1)} %add.54), channel_id=1, source_target_pairs={{0,2},{1,3},{2,0},{3,1},{4,6},{5,7},{6,4},{7,5},{8,10},{9,11},{10,... | collective-permute-start | bytes 491528 | tf_op jit(solution)/shard_map/ppermute | solution.py:246
  71.9 6.1 %collective-permute-start.28 = (f32[32,1408]{1,0:T(8,128)S(1)}, f32[32,1408]{1,0:T(8,128)S(1)}, u32[]{:S(2)}, u32[]{:S(2)}) collective-permute-start(f32[32,1408]{1,0:T(8,128)S(1)} %add.61.refs_0_), channel_id=1, source_target_pairs={{0,2},{1,3},{2,0},{3,1},{4,6},{5,7},{6,4},{7,5},{8,10},{9,11},{10,... | collective-permute-start | bytes 540680 | tf_op jit(solution)/shard_map/ppermute | solution.py:246
  72.6 5.4 %collective-permute-start.31 = (f32[32,1280]{1,0:T(8,128)S(1)}, f32[32,1280]{1,0:T(8,128)S(1)}, u32[]{:S(2)}, u32[]{:S(2)}) collective-permute-start(f32[32,1280]{1,0:T(8,128)S(1)} %add.63.refs_2_), channel_id=1, source_target_pairs={{0,4},{1,5},{2,6},{3,7},{4,0},{5,1},{6,2},{7,3},{8,12},{9,13},{10,... | collective-permute-start | bytes 491528 | tf_op jit(solution)/shard_map/ppermute | solution.py:246
  73.8 6.4 %collective-permute-start.12 = (f32[32,1408]{1,0:T(8,128)S(1)}, f32[32,1408]{1,0:T(8,128)S(1)}, u32[]{:S(2)}, u32[]{:S(2)}) collective-permute-start(f32[32,1408]{1,0:T(8,128)S(1)} %add.53.refs_0_), channel_id=1, source_target_pairs={{0,2},{1,3},{2,0},{3,1},{4,6},{5,7},{6,4},{7,5},{8,10},{9,11},{10,... | collective-permute-start | bytes 540680 | tf_op jit(solution)/shard_map/ppermute | solution.py:246
  74.8 5.4 %collective-permute-start.15 = (f32[32,1280]{1,0:T(8,128)S(1)}, f32[32,1280]{1,0:T(8,128)S(1)}, u32[]{:S(2)}, u32[]{:S(2)}) collective-permute-start(f32[32,1280]{1,0:T(8,128)S(1)} %add.55.refs_2_), channel_id=1, source_target_pairs={{0,4},{1,5},{2,6},{3,7},{4,0},{5,1},{6,2},{7,3},{8,12},{9,13},{10,... | collective-permute-start | bytes 491528 | tf_op jit(solution)/shard_map/ppermute | solution.py:246
  79.8 2.4 %collective-permute-start.32 = (f32[2,64,256]{2,1,0:T(8,128)S(1)}, f32[2,64,256]{2,1,0:T(8,128)S(1)}, u32[]{:S(2)}, u32[]{:S(2)}) collective-permute-start(f32[2,64,256]{2,1,0:T(8,128)S(1)} %get-tuple-element.81), channel_id=1, source_target_pairs={{0,1},{1,0},{2,3},{3,2},{4,5},{5,4},{6,7},{7,6},{8,9},{9,8},{10,11... | collective-permute-start | bytes 393224 | tf_op jit(solution)/shard_map/ppermute | solution.py:246
  82.0 1.4 %collective-permute-start.16 = (f32[2,64,256]{2,1,0:T(8,128)S(1)}, f32[2,64,256]{2,1,0:T(8,128)S(1)}, u32[]{:S(2)}, u32[]{:S(2)}) collective-permute-start(f32[2,64,256]{2,1,0:T(8,128)S(1)} %get-tuple-element.66), channel_id=1, source_target_pairs={{0,1},{1,0},{2,3},{3,2},{4,5},{5,4},{6,7},{7,6},{8,9},{9,8},{10,11... | collective-permute-start | bytes 393224 | tf_op jit(solution)/shard_map/ppermute | solution.py:246

commit v4 on v3

--- a/solution.py
+++ b/solution.py
@@ -38,35 +38,38 @@
 
 
 def split_kernel(down_ref, high_ref, low_ref, turned_high_ref, turned_low_ref, energy_ref):
-    rows, width = down_ref.shape[1:]
-    step = pl.program_id(0)
-
-    @pl.when(step == 0)
+    rows, shots = down_ref.shape[1:]
+    part, step = pl.program_id(0), pl.program_id(1)
+    width = 4 * LANES
+    whole = rows == high_ref.shape[1]
+    at = slice(None) if whole else pl.ds(pl.multiple_of(step * rows, rows), rows)
+
+    @pl.when((part == 0) & (step == 0))
     def _():
         energy_ref[...] = jnp.zeros_like(energy_ref)
 
-    at = pl.ds(pl.multiple_of(step * width, width), width)
-    for part in range(2):
-        value = down_ref[part]
+    for start in range(0, shots, width):
+        place = slice(start, start + width)
+        value = down_ref[0, :, place]
         high, low = parts_of(value)
-        high_ref[part, :, at] = high
-        low_ref[part, :, at] = low
-        turned_high_ref[part, at, :] = high.T
-        turned_low_ref[part, at, :] = low.T
+        high_ref[part, at, place] = high
+        low_ref[part, at, place] = low
+        turned_high_ref[part, place, at] = high.T
+        turned_low_ref[part, place, at] = low.T
         square = jnp.sum((value * value).reshape(rows // 8, 8, width), axis=0)
         energy_ref[...] += sum(square[:, lane : lane + LANES] for lane in range(0, width, LANES))
 
 
 def split(value):
     _, rows, shots = value.shape
-    width = 4 * LANES
+    block = min(rows, LANES)
     plain, turned = ((2, rows, shots), bf16), ((2, shots, rows), bf16)
     high, low, turned_high, turned_low, energy = call(
         split_kernel,
         [plain, plain, turned, turned, ((8, LANES), f32)],
         (value,),
-        grid=(shots // width,),
-        in_specs=[pl.BlockSpec((2, rows, width), lambda step: (0, 0, step))],
+        grid=(2, rows // block),
+        in_specs=[pl.BlockSpec((1, block, shots), lambda part, step: (part, step, 0))],
     )
     return (high, low), (turned_high, turned_low), energy
 
@@ -108,54 +111,58 @@
     return out
 
 
-def apply_down(x_ref, first_ref, second_ref, turned, image_ref):
+def apply_down(x_ref, first_ref, second_ref, turned, shots=slice(None)):
     stage(x_ref, first_ref, second_ref, -1)
-    rows = turned[0][0].shape[2]
-    for at, (high, low) in enumerate(turned):
-        image_ref[:, at * rows : (at + 1) * rows] = times(first_ref[...], second_ref[...], high, low)
+    first, second = first_ref[...], second_ref[...]
+    count = first.shape[0] // 2
+    blocks = []
+    for high, low in turned:
+        total = dot(first, high[0, shots, :]) + dot(second, high[1, shots, :])
+        rest = dot(first[:count], low[0, shots, :]) + dot(second[:count], low[1, shots, :])
+        blocks.append(total[:count] + total[count:] + rest)
+    return jnp.concatenate(blocks, axis=1)
 
 
 def device_bit(bit):
     return (lax.axis_index("rcv") >> bit) & 1
 
 
-def project(value_ref, first_ref, second_ref, plain, extra, outs, bits):
+def project(value_ref, first_ref, second_ref, plain, columns, keep_ref, give_ref, bit, extra=None):
     stage(value_ref, first_ref, second_ref, 1)
     rows = plain[0][0].shape[1]
-    shots = plain[0][0].shape[2]
     half = value_ref.shape[0] // 2
-    for at, bit in enumerate(bits):
-        columns = slice(at * shots // 2, (at + 1) * shots // 2)
-        total = 0.0
-        for block, (high, low) in enumerate(plain):
-            own = slice(block * rows, (block + 1) * rows)
-            total = total + times(first_ref[:, own], second_ref[:, own], high, low, columns)
-        pieces = [(slice(0, shots // 2), total)]
-        if at == 0:
-            pieces.append((slice(shots // 2, shots // 2 + LANES), extra))
-        keep_ref, give_ref = outs[2 * at : 2 * at + 2]
-        upper = device_bit(bit) == 1
-        for place, piece in pieces:
-            keep_ref[:, place] = jnp.where(upper, piece[half:], piece[:half])
-            give_ref[:, place] = jnp.where(upper, piece[:half], piece[half:])
-
-
-def collect(pieces, x_ref, ends_ref, bits):
-    front = x_ref.shape[1] // 2
-    for at, bit in enumerate(bits):
-        upper = device_bit(bit)
-        for which, piece in enumerate(pieces[2 * at : 2 * at + 2]):
-            half = piece.shape[0]
-            place = pl.ds(pl.multiple_of((upper ^ which) * half, half), half)
-            x_ref[place, at * front : (at + 1) * front] = piece[:, :front]
-            if at == 0:
-                ends_ref[place, :] = piece[:, front:]
-
-
-def rhs_kernel(bits, masks, *refs):
+    front = columns.stop - columns.start
+    total = 0.0
+    for block, (high, low) in enumerate(plain):
+        own = slice(block * rows, (block + 1) * rows)
+        total = total + times(first_ref[:, own], second_ref[:, own], high, low, columns)
+    upper = device_bit(bit) == 1
+    keep_ref[:, :front] = jnp.where(upper, total[half:], total[:half])
+    give_ref[:, :front] = jnp.where(upper, total[:half], total[half:])
+    if extra is not None:
+        keep_ref[:, front:] = jnp.where(upper, extra[half:], extra[:half])
+        give_ref[:, front:] = jnp.where(upper, extra[:half], extra[half:])
+
+
+def collect(pieces, x_ref, bit, ends_ref=None):
+    upper = device_bit(bit)
+    front = x_ref.shape[1]
+    for which, piece in enumerate(pieces):
+        half = piece.shape[0]
+        place = pl.ds(pl.multiple_of((upper ^ which) * half, half), half)
+        x_ref[place, :] = piece[:, :front]
+        if ends_ref is not None:
+            ends_ref[place, :] = piece[:, front:]
+
+
+def pairs(refs):
+    return tuple((refs[at], refs[at + 1]) for at in range(0, len(refs), 2))
+
+
+def rhs_kernel(bit, masks, *refs):
     sources, refs = refs[: len(masks)], refs[len(masks) :]
     down, refs = refs[:8], refs[8:]
-    (ea, eb), (rhs_ref, *outs), (x_ref, f0, s0, f1, s1, *spread) = refs[:2], refs[2:7], refs[7:]
+    (ea, eb), (rhs_ref, *outs), (x_ref, f0, s0, f1, s1, *spread) = refs[:2], refs[2:5], refs[5:]
     half = x_ref.shape[0] // 2
     own = sources[0].shape[1]
     chip = lax.axis_index("rcv") >> 1
@@ -167,42 +174,57 @@
                 x_ref[pl.ds(pl.multiple_of(part * half + (chip ^ mask) * own, own), own), :] = value
     for at in range(2 * half // own if spread else 0):
         x_ref[at * own : (at + 1) * own, :] = spread[0][at]
-    apply_down(x_ref, f0, s0, ((down[4], down[5]), (down[6], down[7])), rhs_ref)
+    rhs_ref[...] = apply_down(x_ref, f0, s0, pairs(down[4:]))
     energy = jnp.full((2 * half, 1), jnp.sum(ea[...] + eb[...]), f32)
     extra = tail(row_squares(rhs_ref[...]), energy)
-    project(rhs_ref, f1, s1, ((down[0], down[1]), (down[2], down[3])), extra, outs, bits)
+    front = outs[0].shape[1] - LANES
+    project(rhs_ref, f1, s1, pairs(down[:4]), slice(0, front), *outs, bit, extra)
+
+
+def back_kernel(bit, *refs):
+    value_ref, down, outs, scratch = refs[0], refs[1:5], refs[5:7], refs[7:]
+    shots = down[0].shape[2]
+    project(value_ref, *scratch, pairs(down), slice(shots - outs[0].shape[1], shots), *outs, bit)
+
+
+def front_kernel(bit, *refs):
+    pieces, turned, (x_ref, ends_ref, image_ref), scratch = refs[:2], refs[2:6], refs[6:9], refs[9:]
+    collect(pieces, x_ref, bit, ends_ref)
+    image_ref[...] = apply_down(x_ref, *scratch, pairs(turned), slice(0, x_ref.shape[1]))
 
 
 def first_kernel(bits, receivers, *refs):
-    pieces, (rhs_ref, *refs) = refs[:4], refs[4:]
+    pieces, (before_ref, ends_ref, part_ref, rhs_ref, *refs) = refs[:2], refs[2:]
     down, refs = refs[:8], refs[8:]
-    (x_ref, scalar_ref, image_ref, residual_ref, *outs), (ends_ref, f0, s0, f1, s1) = refs[:8], refs[8:]
-    collect(pieces, x_ref, ends_ref, bits)
+    (x_ref, scalar_ref, image_ref, residual_ref, *outs), (f0, s0, f1, s1) = refs[:6], refs[6:]
+    front = before_ref.shape[1]
+    collect(pieces, x_ref, bits[1])
     norm = both(ends_ref[:, 0:1])
     damping = damping_ratio * ends_ref[:, 1:2] / receivers
-    apply_down(x_ref, f0, s0, ((down[4], down[5]), (down[6], down[7])), image_ref)
-    image = image_ref[...] + damping * rhs_ref[...]
+    image = part_ref[...] + apply_down(x_ref, f0, s0, pairs(down[4:]), slice(front, None)) + damping * rhs_ref[...]
     image_ref[...] = image
-    alpha = norm / (both(row_squares(x_ref[...])) + damping * norm)
+    alpha = norm / (both(row_squares(before_ref[...]) + row_squares(x_ref[...])) + damping * norm)
     residual = rhs_ref[...] - alpha * image
     residual_ref[...] = residual
     scalar_ref[...] = tail(norm, damping, alpha)
-    project(residual_ref, f1, s1, ((down[0], down[1]), (down[2], down[3])), tail(row_squares(residual)), outs, bits)
-
-
-def last_kernel(bits, *refs):
-    pieces, (rhs_ref, before_ref, scalar_ref, image_ref, residual_ref, *turned), refs = refs[:4], refs[4:13], refs[13:]
-    keep_ref, give_ref, x_ref, ends_ref, y_ref, f0, s0 = refs
-    collect(pieces, x_ref, ends_ref, bits)
+    project(residual_ref, f1, s1, pairs(down[:4]), slice(0, front), *outs, bits[0], tail(row_squares(residual)))
+
+
+def last_kernel(bit, *refs):
+    pieces, (a_ref, ends_ref, part_ref, rhs_ref, before_a, before_b, scalar_ref, image_ref, residual_ref) = refs[:2], refs[2:11]
+    turned, (keep_ref, give_ref, x_ref, *scratch) = refs[11:15], refs[15:]
+    front = a_ref.shape[1]
+    collect(pieces, x_ref, bit)
     following = both(ends_ref[:, 0:1])
     norm = scalar_ref[:, 0:1]
     damping = scalar_ref[:, 1:2]
     alpha = scalar_ref[:, 2:3]
     beta = following / norm
-    apply_down(x_ref, f0, s0, (turned[0:2], turned[2:4]), y_ref)
     residual = residual_ref[...]
-    image = y_ref[...] + beta * image_ref[...] + damping * residual
-    curvature = both(row_squares(x_ref[...] + beta * before_ref[...])) + damping * (following + beta * following)
+    image = part_ref[...] + apply_down(x_ref, *scratch, pairs(turned), slice(front, None))
+    image = image + beta * image_ref[...] + damping * residual
+    squares = row_squares(a_ref[...] + beta * before_a[...]) + row_squares(x_ref[...] + beta * before_b[...])
+    curvature = both(squares) + damping * (following + beta * following)
     alpha_next = following / curvature
     rhs = rhs_ref[...]
     found = alpha * rhs + alpha_next * (residual + beta * rhs)
@@ -245,13 +267,13 @@
     def swap(value, bit):
         return lax.ppermute(value, "rcv", [(at, at ^ (1 << bit)) for at in range(count)])
 
-    def exchange(outs):
+    def exchange(*ranges):
         pieces = []
-        for order, (keep, give) in zip(orders, (outs[0:2], outs[2:4])):
+        for order, (keep, give) in zip(orders, ranges):
             keep = keep + swap(give, order[0])
             for bit in order[1:]:
                 keep = keep + swap(keep, bit)
-            pieces += [keep, swap(keep, order[0])]
+            pieces.append((keep, swap(keep, order[0])))
         return pieces
 
     def jump(value, mask):
@@ -269,45 +291,54 @@
     down = (*plain_a, *plain_b, *turned)
 
     wide = [((2 * packed, shots), bf16)] * 2
+    narrow = [((2 * packed, front), bf16)] * 2
     short = [((2 * packed, 2 * rows), bf16)] * 2
     lines = ((packed, 2 * rows), f32)
     every = ((packed, shots), f32)
+    ranged = ((packed, front), f32)
     small = ((packed, LANES), f32)
-    work = 2 * 2 * 2 * (3 * packed) * 2 * rows * shots
-    halves = [((packed // 2, front + LANES), f32)] * 2 + [((packed // 2, front), f32)] * 2
-
+    work = 2 * 2 * 2 * (3 * packed) * rows * shots
+    sent_0 = [((packed // 2, front + LANES), f32)] * 2
+    sent_1 = [((packed // 2, front), f32)] * 2
     spread = [((packed // own, own, shots), f32)] if own % 8 else []
-    outs = [
-        call(
-            functools.partial(rhs_kernel, ends, masks),
-            [lines] + halves,
-            (*pair, *down, energy_a, energy_b),
+    plain = (*plain_a, *plain_b)
+
+    def back(value):
+        return call(functools.partial(back_kernel, ends[1]), sent_1, (value, *plain), short, work)
+
+    def lead(pieces):
+        return call(functools.partial(front_kernel, ends[0]), [ranged, small, lines], (*pieces, *turned), narrow, work)
+
+    state, sums = [], []
+    for source in sources:
+        rhs, *outs = call(
+            functools.partial(rhs_kernel, ends[0], masks),
+            [lines] + sent_0,
+            (*source, *down, energy_a, energy_b),
             [every] + wide + short + spread,
+            3 * work,
+        )
+        state.append(rhs)
+        sums.append(exchange(outs, back(rhs)))
+    for group, (rhs, (pieces_0, pieces_1)) in enumerate(zip(state, sums)):
+        before, norms, part = lead(pieces_0)
+        x, scalars, image, residual, *outs = call(
+            functools.partial(first_kernel, ends, receivers),
+            [ranged, small, lines, lines] + sent_0,
+            (*pieces_1, before, norms, part, rhs, *down),
+            narrow + short,
+            2 * work,
+        )
+        state[group] = (rhs, before, x, scalars, image, residual)
+        sums[group] = exchange(outs, back(residual))
+    results = []
+    for kept, (pieces_0, pieces_1) in zip(state, sums):
+        keep, give = call(
+            functools.partial(last_kernel, ends[1]),
+            [((2, packed, rows), f32)] * 2,
+            (*pieces_1, *lead(pieces_0), *kept, *turned),
+            [ranged] + narrow,
             work,
-        )
-        for pair in sources
-    ]
-    rhs = [out[0] for out in outs]
-    sums = [exchange(out[1:]) for out in outs]
-    outs = [
-        call(
-            functools.partial(first_kernel, ends, receivers),
-            [every, small, lines, lines] + halves,
-            (*sums[group], rhs[group], *down),
-            [small] + wide + short,
-            work,
-        )
-        for group in range(GROUPS)
-    ]
-    sums = [exchange(out[4:]) for out in outs]
-    results = []
-    for group in range(GROUPS):
-        keep, give = call(
-            functools.partial(last_kernel, ends),
-            [((2, packed, rows), f32)] * 2,
-            (*sums[group], rhs[group], *outs[group][:4], *turned),
-            [every, small, lines] + wide,
-            work // 2,
         )
         results.append((keep, swap(give, 0)))
 

time: 84.5 us -> 83.4 us (0.987)
  Pallas kernels: 28 us -> 25.1 us
  starting transfers between devices: 32.7 us -> 35.2 us
    pallas_call x9 -> x17, Pallas kernels: 28 us -> 25.1 us  [call(): pl.pallas_call(kernel, out_shape=[jax.ShapeDtypeStruct(shape, dtype) for...]
    ppermute x27, starting transfers between devices: 25 us -> 27.5 us  [swap(): lax.ppermute(value, 'rcv', [(at, at ^ 1 << bit) for at in range(count)])]
  transfers between devices with their start and end apart: 33 -> 33, of which waited for: 11 -> 10; matrix products, arithmetic and copies ran while one was open for 2% -> 2% of each run, Pallas kernels for 32% -> 29%
where the time goes in v4:
time: 83.4 us; the launch traced here: 83.2 us
  starting transfers between devices  35.2 us (42%)
  Pallas kernels  25.1 us (30%)
  waiting for transfers between devices  20.6 us (25%)
  local copies, waits for them, and re-layouts  1.02 us (1%)
  between operations  0.95 us (1%)
    ppermute x27, starting transfers between devices, swap(): lax.ppermute(value, 'rcv', [(at, at ^ 1 << bit) for at in range(count)])  27.5 us
    pallas_call x17, Pallas kernels, call(): pl.pallas_call(kernel, out_shape=[jax.ShapeDtypeStruct(shape, dtype) for...  25.1 us
    ppermute x27, waiting for transfers between devices, swap(): lax.ppermute(value, 'rcv', [(at, at ^ 1 << bit) for at in range(count)])  20.6 us
    ppermute x6, starting transfers between devices, jump(): lax.ppermute(value, 'rcv', [(at, at ^ mask << 1) for at in range(count)])  7.75 us
  transfers between devices with their start and end apart: 33, of which 10 were waited for; matrix products, arithmetic and copies ran while one was open for 2% of the time, Pallas kernels for 29%

profile of v4, /device:TPU:0, one launch (start us, length us, event | category | flops | bytes accessed | tf_op | source)
XLA Modules:
  0.0 83.2 jit_solution(1848043284220097581)
XLA Ops:
  0.6 0.5 collective-permute-start.3
  1.1 1.0 %fusion = (f32[2,8,2560]{2,1,0:T(8,128)S(1)}, f32[2,8,2560]{2,1,0:T(8,128)S(1)}) fusion(f32[2,16,2560]{2,1,0:T(8,128)} %param.3), kind=kLoop, calls=%fused_computation | loop fusion | bytes 655360 | tf_op jit(solution)/shard_map/slice | solution.py:286
  2.2 2.6 %collective-permute-start.17 = (f32[2,8,2560]{2,1,0:T(8,128)S(1)}, f32[2,8,2560]{2,1,0:T(8,128)S(1)}, u32[]{:S(2)}, u32[]{:S(2)}) collective-permute-start(f32[2,8,2560]{2,1,0:T(8,128)S(1)} %get-tuple-element.106.refs_0_), channel_id=1, source_target_pairs={{0,2},{1,3},{2,0},{3,1},{4,6},{5,7},{6,4},{7,5},{8,10},{9,11},{10,... | collective-permute-start | bytes 491528 | tf_op jit(solution)/shard_map/ppermute | solution.py:280
  4.7 1.5 %collective-permute-start.18 = (f32[2,8,2560]{2,1,0:T(8,128)S(1)}, f32[2,8,2560]{2,1,0:T(8,128)S(1)}, u32[]{:S(2)}, u32[]{:S(2)}) collective-permute-start(f32[2,8,2560]{2,1,0:T(8,128)S(1)} %get-tuple-element.106.refs_0_), channel_id=1, source_target_pairs={{0,4},{1,5},{2,6},{3,7},{4,0},{5,1},{6,2},{7,3},{8,12},{9,13},{10,... | collective-permute-start | bytes 491528 | tf_op jit(solution)/shard_map/ppermute | solution.py:280
  6.3 0.0 collective-permute-start.19
  6.3 1.9 %collective-permute-start = (f32[2,8,2560]{2,1,0:T(8,128)S(1)}, f32[2,8,2560]{2,1,0:T(8,128)S(1)}, u32[]{:S(2)}, u32[]{:S(2)}) collective-permute-start(f32[2,8,2560]{2,1,0:T(8,128)S(1)} %get-tuple-element.107.refs_0_), channel_id=1, source_target_pairs={{0,2},{1,3},{2,0},{3,1},{4,6},{5,7},{6,4},{7,5},{8,10},{9,11},{10,... | collective-permute-start | bytes 491528 | tf_op jit(solution)/shard_map/ppermute | solution.py:280
  8.2 4.1 %shard_map.41 = (bf16[2,256,2560]{2,1,0:T(8,128)(2,1)S(1)}, bf16[2,256,2560]{2,1,0:T(8,128)(2,1)S(1)}, bf16[2,2560,256]{2,1,0:T(8,128)(2,1)S(1)}, bf16[2,2560,256]{2,1,0:T(8,128)(2,1)S(1)}, f32[8,128]{1,0:T(8,128)S(1)}) custom-call(f32[2,256,2560]{2,1,0:T(8,128)} %down_ref.1), custom_call_target="tpu_custom_call" | custom-call | bytes 5242880 | tf_op jit(solution)/shard_map/pallas_call | solution.py:28
  12.3 0.0 collective-permute-done.3.down_ref
  12.3 1.6 %collective-permute-start.1 = (f32[2,8,2560]{2,1,0:T(8,128)S(1)}, f32[2,8,2560]{2,1,0:T(8,128)S(1)}, u32[]{:S(2)}, u32[]{:S(2)}) collective-permute-start(f32[2,8,2560]{2,1,0:T(8,128)S(1)} %get-tuple-element.107.refs_0_), channel_id=1, source_target_pairs={{0,4},{1,5},{2,6},{3,7},{4,0},{5,1},{6,2},{7,3},{8,12},{9,13},{10,... | collective-permute-start | bytes 491528 | tf_op jit(solution)/shard_map/ppermute | solution.py:280
  13.9 1.8 %shard_map.42 = (bf16[2,256,2560]{2,1,0:T(8,128)(2,1)S(1)}, bf16[2,256,2560]{2,1,0:T(8,128)(2,1)S(1)}, bf16[2,2560,256]{2,1,0:T(8,128)(2,1)S(1)}, bf16[2,2560,256]{2,1,0:T(8,128)(2,1)S(1)}, f32[8,128]{1,0:T(8,128)S(1)}) custom-call(f32[2,256,2560]{2,1,0:T(8,128)S(1)} %collective-permute-done.3.down_ref), custom_call_target="tpu_custom_call" | custom-call | bytes 5242880 | tf_op jit(solution)/shard_map/pallas_call | solution.py:28
  15.7 0.0 collective-permute-done.17.refs_1_
  15.7 0.1 collective-permute-start.2
  15.8 0.0 collective-permute-done.18.refs_2_
  15.9 2.6 %shard_map.50 = (f32[64,512]{1,0:T(8,128)S(1)}, f32[32,1408]{1,0:T(8,128)S(1)}, f32[32,1408]{1,0:T(8,128)S(1)}) custom-call(f32[2,8,2560]{2,1,0:T(8,128)S(1)} %get-tuple-element.106.refs_0_, f32[2,8,2560]{2,1,0:T(8,128)S(1)} %collective-permute-done.17.refs_1_, f32[2,8,2560]{2,1,0:T(8,128)S(1)} %collective-permute-done.18.refs_2_, ...), custom_call_target="tpu_custom_call" | custom-call | flops 3019898880 | bytes 21635072 | tf_op jit(solution)/shard_map/pallas_call | solution.py:28
  18.4 2.0 %collective-permute-start.23 = (f32[32,1408]{1,0:T(8,128)S(1)}, f32[32,1408]{1,0:T(8,128)S(1)}, u32[]{:S(2)}, u32[]{:S(2)}) collective-permute-start(f32[32,1408]{1,0:T(8,128)S(1)} %get-tuple-element.89), channel_id=1, source_target_pairs={{0,2},{1,3},{2,0},{3,1},{4,6},{5,7},{6,4},{7,5},{8,10},{9,11},{10,... | collective-permute-start | bytes 540680 | tf_op jit(solution)/shard_map/ppermute | solution.py:268
  20.4 0.9 %shard_map.51 = (f32[32,1280]{1,0:T(8,128)S(1)}, f32[32,1280]{1,0:T(8,128)S(1)}) custom-call(f32[64,512]{1,0:T(8,128)S(1)} %get-tuple-element.85.refs_0_.refs_5_, bf16[2,256,2560]{2,1,0:T(8,128)(2,1)S(1)} %get-tuple-element.54.refs_4_.refs_1_.refs_6_, bf16[2,256,2560]{2,1,0:T(8,128)(2,1)S(1)} %get-tuple-element.55.refs_5_.refs_2_.refs_7_, ...), custom_call_target="tpu_custom_call" | custom-call | flops 1006632960 | bytes 10616832 | tf_op jit(solution)/shard_map/pallas_call | solution.py:28
  21.4 1.6 %collective-permute-start.20 = (f32[32,1280]{1,0:T(8,128)S(1)}, f32[32,1280]{1,0:T(8,128)S(1)}, u32[]{:S(2)}, u32[]{:S(2)}) collective-permute-start(f32[32,1280]{1,0:T(8,128)S(1)} %get-tuple-element.87), channel_id=1, source_target_pairs={{0,4},{1,5},{2,6},{3,7},{4,0},{5,1},{6,2},{7,3},{8,12},{9,13},{10,... | collective-permute-start | bytes 491528 | tf_op jit(solution)/shard_map/ppermute | solution.py:268
  23.0 2.6 %shard_map.43 = (f32[64,512]{1,0:T(8,128)S(1)}, f32[32,1408]{1,0:T(8,128)S(1)}, f32[32,1408]{1,0:T(8,128)S(1)}) custom-call(f32[2,8,2560]{2,1,0:T(8,128)S(1)} %get-tuple-element.107.refs_0_, f32[2,8,2560]{2,1,0:T(8,128)S(1)} %collective-permute-done.refs_1_, f32[2,8,2560]{2,1,0:T(8,128)S(1)} %collective-permute-done.1.refs_2_, ...), custom_call_target="tpu_custom_call" | custom-call | flops 3019898880 | bytes 21635072 | tf_op jit(solution)/shard_map/pallas_call | solution.py:28
  25.6 0.6 collective-permute-start.7
  26.2 0.3 collective-permute-start.24
  26.5 0.9 %shard_map.44 = (f32[32,1280]{1,0:T(8,128)S(1)}, f32[32,1280]{1,0:T(8,128)S(1)}) custom-call(f32[64,512]{1,0:T(8,128)S(1)} %get-tuple-element.64.refs_0_.refs_5_, bf16[2,256,2560]{2,1,0:T(8,128)(2,1)S(1)} %get-tuple-element.54.refs_4_.refs_1_.refs_6_, bf16[2,256,2560]{2,1,0:T(8,128)(2,1)S(1)} %get-tuple-element.55.refs_5_.refs_2_.refs_7_, ...), custom_call_target="tpu_custom_call" | custom-call | flops 1006632960 | bytes 10616832 | tf_op jit(solution)/shard_map/pallas_call | solution.py:28
  27.5 1.8 %collective-permute-start.4 = (f32[32,1280]{1,0:T(8,128)S(1)}, f32[32,1280]{1,0:T(8,128)S(1)}, u32[]{:S(2)}, u32[]{:S(2)}) collective-permute-start(f32[32,1280]{1,0:T(8,128)S(1)} %get-tuple-element.66), channel_id=1, source_target_pairs={{0,4},{1,5},{2,6},{3,7},{4,0},{5,1},{6,2},{7,3},{8,12},{9,13},{10,... | collective-permute-start | bytes 491528 | tf_op jit(solution)/shard_map/ppermute | solution.py:268
  29.3 1.5 %collective-permute-start.21 = (f32[32,1280]{1,0:T(8,128)S(1)}, f32[32,1280]{1,0:T(8,128)S(1)}, u32[]{:S(2)}, u32[]{:S(2)}) collective-permute-start(f32[32,1280]{1,0:T(8,128)S(1)} %add.56), channel_id=1, source_target_pairs={{0,2},{1,3},{2,0},{3,1},{4,6},{5,7},{6,4},{7,5},{8,10},{9,11},{10,... | collective-permute-start | bytes 491528 | tf_op jit(solution)/shard_map/ppermute | solution.py:268
  30.9 1.7 %collective-permute-done.7 = f32[32,1408]{1,0:T(8,128)S(1)} collective-permute-done((f32[32,1408]{1,0:T(8,128)S(1)}, f32[32,1408]{1,0:T(8,128)S(1)}, u32[]{:S(2)}, u32[]{:S(2)}) %collective-permute-start.7) | collective-permute-done | bytes 180256 | tf_op jit(solution)/shard_map/ppermute | solution.py:268
  32.6 0.5 collective-permute-start.8
  33.1 0.6 collective-permute-done.24
  33.8 1.5 %collective-permute-start.25 = (f32[32,1408]{1,0:T(8,128)S(1)}, f32[32,1408]{1,0:T(8,128)S(1)}, u32[]{:S(2)}, u32[]{:S(2)}) collective-permute-start(f32[32,1408]{1,0:T(8,128)S(1)} %add.59.refs_0_), channel_id=1, source_target_pairs={{0,2},{1,3},{2,0},{3,1},{4,6},{5,7},{6,4},{7,5},{8,10},{9,11},{10,... | collective-permute-start | bytes 540680 | tf_op jit(solution)/shard_map/ppermute | solution.py:268
  35.3 1.8 %collective-permute-done.4 = f32[32,1280]{1,0:T(8,128)S(1)} collective-permute-done((f32[32,1280]{1,0:T(8,128)S(1)}, f32[32,1280]{1,0:T(8,128)S(1)}, u32[]{:S(2)}, u32[]{:S(2)}) %collective-permute-start.4) | collective-permute-done | bytes 163872 | tf_op jit(solution)/shard_map/ppermute | solution.py:268
  37.2 1.4 %collective-permute-start.5 = (f32[32,1280]{1,0:T(8,128)S(1)}, f32[32,1280]{1,0:T(8,128)S(1)}, u32[]{:S(2)}, u32[]{:S(2)}) collective-permute-start(f32[32,1280]{1,0:T(8,128)S(1)} %add.48), channel_id=1, source_target_pairs={{0,2},{1,3},{2,0},{3,1},{4,6},{5,7},{6,4},{7,5},{8,10},{9,11},{10,... | collective-permute-start | bytes 491528 | tf_op jit(solution)/shard_map/ppermute | solution.py:268
  38.6 0.1 collective-permute-start.22
  38.7 4.3 %collective-permute-done.5 = f32[32,1280]{1,0:T(8,128)S(1)} collective-permute-done((f32[32,1280]{1,0:T(8,128)S(1)}, f32[32,1280]{1,0:T(8,128)S(1)}, u32[]{:S(2)}, u32[]{:S(2)}) %collective-permute-start.5) | collective-permute-done | bytes 163872 | tf_op jit(solution)/shard_map/ppermute | solution.py:268
  43.1 0.1 collective-permute-start.6
  43.2 2.5 %collective-permute-start.9 = (f32[32,1408]{1,0:T(8,128)S(1)}, f32[32,1408]{1,0:T(8,128)S(1)}, u32[]{:S(2)}, u32[]{:S(2)}) collective-permute-start(f32[32,1408]{1,0:T(8,128)S(1)} %add.51.refs_0_), channel_id=1, source_target_pairs={{0,2},{1,3},{2,0},{3,1},{4,6},{5,7},{6,4},{7,5},{8,10},{9,11},{10,... | collective-permute-start | bytes 540680 | tf_op jit(solution)/shard_map/ppermute | solution.py:268
  45.7 0.9 %shard_map.52 = (f32[64,1280]{1,0:T(8,128)S(1)}, f32[64,128]{1,0:T(8,128)S(1)}, f32[64,512]{1,0:T(8,128)S(1)}) custom-call(f32[32,1408]{1,0:T(8,128)S(1)} %add.59.refs_0_, f32[32,1408]{1,0:T(8,128)S(1)} %collective-permute-done.25.refs_1_, bf16[2,2560,256]{2,1,0:T(8,128)(2,1)S(1)} %get-tuple-element.58.refs_8_.refs_2_.refs_10_.refs_11_, ...), custom_call_target="tpu_custom_call" | custom-call | flops 1006632960 | bytes 10846208 | tf_op jit(solution)/shard_map/pallas_call | solution.py:28
  46.6 1.8 %shard_map.53 = (f32[64,1280]{1,0:T(8,128)S(1)}, f32[64,128]{1,0:T(8,128)S(1)}, f32[64,512]{1,0:T(8,128)S(1)}, f32[64,512]{1,0:T(8,128)S(1)}, f32[32,1408]{1,0:T(8,128)S(1)}, /*index=5*/f32[32,1408]{1,0:T(8,128)S(1)}) custom-call(f32[32,1280]{1,0:T(8,128)S(1)} %add.57.refs_0_, f32[32,1280]{1,0:T(8,128)S(1)} %collective-permute-done.22.refs_1_, ...), custom_call_target="tpu_custom_call" | custom-call | flops 2013265920 | bytes 21921792 | tf_op jit(solution)/shard_map/pallas_call | solution.py:28
  48.5 0.1 collective-permute-start.29
  48.6 0.9 %shard_map.54 = (f32[32,1280]{1,0:T(8,128)S(1)}, f32[32,1280]{1,0:T(8,128)S(1)}) custom-call(f32[64,512]{1,0:T(8,128)S(1)} %get-tuple-element.93.refs_0_.refs_10_, bf16[2,256,2560]{2,1,0:T(8,128)(2,1)S(1)} %get-tuple-element.54.refs_4_.refs_1_.refs_6_, bf16[2,256,2560]{2,1,0:T(8,128)(2,1)S(1)} %get-tuple-element.55.refs_5_.refs_2_.refs_7_, ...), custom_call_target="tpu_custom_call" | custom-call | flops 1006632960 | bytes 10616832 | tf_op jit(solution)/shard_map/pallas_call | solution.py:28
  49.5 2.1 %collective-permute-start.26 = (f32[32,1280]{1,0:T(8,128)S(1)}, f32[32,1280]{1,0:T(8,128)S(1)}, u32[]{:S(2)}, u32[]{:S(2)}) collective-permute-start(f32[32,1280]{1,0:T(8,128)S(1)} %get-tuple-element.95), channel_id=1, source_target_pairs={{0,4},{1,5},{2,6},{3,7},{4,0},{5,1},{6,2},{7,3},{8,12},{9,13},{10,... | collective-permute-start | bytes 491528 | tf_op jit(solution)/shard_map/ppermute | solution.py:268
  51.6 0.9 %shard_map.45 = (f32[64,1280]{1,0:T(8,128)S(1)}, f32[64,128]{1,0:T(8,128)S(1)}, f32[64,512]{1,0:T(8,128)S(1)}) custom-call(f32[32,1408]{1,0:T(8,128)S(1)} %add.51.refs_0_, f32[32,1408]{1,0:T(8,128)S(1)} %collective-permute-done.9.refs_1_, bf16[2,2560,256]{2,1,0:T(8,128)(2,1)S(1)} %get-tuple-element.58.refs_8_.refs_2_.refs_10_.refs_11_, ...), custom_call_target="tpu_custom_call" | custom-call | flops 1006632960 | bytes 10846208 | tf_op jit(solution)/shard_map/pallas_call | solution.py:28
  52.5 1.8 %shard_map.46 = (f32[64,1280]{1,0:T(8,128)S(1)}, f32[64,128]{1,0:T(8,128)S(1)}, f32[64,512]{1,0:T(8,128)S(1)}, f32[64,512]{1,0:T(8,128)S(1)}, f32[32,1408]{1,0:T(8,128)S(1)}, /*index=5*/f32[32,1408]{1,0:T(8,128)S(1)}) custom-call(f32[32,1280]{1,0:T(8,128)S(1)} %add.49.refs_0_, f32[32,1280]{1,0:T(8,128)S(1)} %collective-permute-done.6.refs_1_, ...), custom_call_target="tpu_custom_call" | custom-call | flops 2013265920 | bytes 21921792 | tf_op jit(solution)/shard_map/pallas_call | solution.py:28
  54.4 2.3 %collective-permute-start.13 = (f32[32,1408]{1,0:T(8,128)S(1)}, f32[32,1408]{1,0:T(8,128)S(1)}, u32[]{:S(2)}, u32[]{:S(2)}) collective-permute-start(f32[32,1408]{1,0:T(8,128)S(1)} %get-tuple-element.76), channel_id=1, source_target_pairs={{0,2},{1,3},{2,0},{3,1},{4,6},{5,7},{6,4},{7,5},{8,10},{9,11},{10,... | collective-permute-start | bytes 540680 | tf_op jit(solution)/shard_map/ppermute | solution.py:268
  56.6 0.7 collective-permute-start.30
  57.3 0.9 %shard_map.47 = (f32[32,1280]{1,0:T(8,128)S(1)}, f32[32,1280]{1,0:T(8,128)S(1)}) custom-call(f32[64,512]{1,0:T(8,128)S(1)} %get-tuple-element.72.refs_0_.refs_10_, bf16[2,256,2560]{2,1,0:T(8,128)(2,1)S(1)} %get-tuple-element.54.refs_4_.refs_1_.refs_6_, bf16[2,256,2560]{2,1,0:T(8,128)(2,1)S(1)} %get-tuple-element.55.refs_5_.refs_2_.refs_7_, ...), custom_call_target="tpu_custom_call" | custom-call | flops 1006632960 | bytes 10616832 | tf_op jit(solution)/shard_map/pallas_call | solution.py:28
  58.3 1.5 %collective-permute-start.10 = (f32[32,1280]{1,0:T(8,128)S(1)}, f32[32,1280]{1,0:T(8,128)S(1)}, u32[]{:S(2)}, u32[]{:S(2)}) collective-permute-start(f32[32,1280]{1,0:T(8,128)S(1)} %get-tuple-element.74), channel_id=1, source_target_pairs={{0,4},{1,5},{2,6},{3,7},{4,0},{5,1},{6,2},{7,3},{8,12},{9,13},{10,... | collective-permute-start | bytes 491528 | tf_op jit(solution)/shard_map/ppermute | solution.py:268
  59.8 0.1 collective-permute-start.27
  59.9 2.0 %collective-permute-done.13 = f32[32,1408]{1,0:T(8,128)S(1)} collective-permute-done((f32[32,1408]{1,0:T(8,128)S(1)}, f32[32,1408]{1,0:T(8,128)S(1)}, u32[]{:S(2)}, u32[]{:S(2)}) %collective-permute-start.13) | collective-permute-done | bytes 180256 | tf_op jit(solution)/shard_map/ppermute | solution.py:268
  61.9 0.1 collective-permute-start.14
  61.9 1.0 %collective-permute-done.30 = f32[32,1408]{1,0:T(8,128)S(1)} collective-permute-done((f32[32,1408]{1,0:T(8,128)S(1)}, f32[32,1408]{1,0:T(8,128)S(1)}, u32[]{:S(2)}, u32[]{:S(2)}) %collective-permute-start.30) | collective-permute-done | bytes 180256 | tf_op jit(solution)/shard_map/ppermute | solution.py:268
  63.0 1.3 %collective-permute-start.31 = (f32[32,1408]{1,0:T(8,128)S(1)}, f32[32,1408]{1,0:T(8,128)S(1)}, u32[]{:S(2)}, u32[]{:S(2)}) collective-permute-start(f32[32,1408]{1,0:T(8,128)S(1)} %add.63.refs_0_), channel_id=1, source_target_pairs={{0,2},{1,3},{2,0},{3,1},{4,6},{5,7},{6,4},{7,5},{8,10},{9,11},{10,... | collective-permute-start | bytes 540680 | tf_op jit(solution)/shard_map/ppermute | solution.py:268
  64.3 1.4 %collective-permute-done.10 = f32[32,1280]{1,0:T(8,128)S(1)} collective-permute-done((f32[32,1280]{1,0:T(8,128)S(1)}, f32[32,1280]{1,0:T(8,128)S(1)}, u32[]{:S(2)}, u32[]{:S(2)}) %collective-permute-start.10) | collective-permute-done | bytes 163872 | tf_op jit(solution)/shard_map/ppermute | solution.py:268
  65.7 0.9 %collective-permute-start.11 = (f32[32,1280]{1,0:T(8,128)S(1)}, f32[32,1280]{1,0:T(8,128)S(1)}, u32[]{:S(2)}, u32[]{:S(2)}) collective-permute-start(f32[32,1280]{1,0:T(8,128)S(1)} %add.52), channel_id=1, source_target_pairs={{0,2},{1,3},{2,0},{3,1},{4,6},{5,7},{6,4},{7,5},{8,10},{9,11},{10,... | collective-permute-start | bytes 491528 | tf_op jit(solution)/shard_map/ppermute | solution.py:268
  66.6 0.9 %collective-permute-start.28 = (f32[32,1280]{1,0:T(8,128)S(1)}, f32[32,1280]{1,0:T(8,128)S(1)}, u32[]{:S(2)}, u32[]{:S(2)}) collective-permute-start(f32[32,1280]{1,0:T(8,128)S(1)} %add.61.refs_0_), channel_id=1, source_target_pairs={{0,4},{1,5},{2,6},{3,7},{4,0},{5,1},{6,2},{7,3},{8,12},{9,13},{10,... | collective-permute-start | bytes 491528 | tf_op jit(solution)/shard_map/ppermute | solution.py:268
  67.5 4.8 %collective-permute-done.11 = f32[32,1280]{1,0:T(8,128)S(1)} collective-permute-done((f32[32,1280]{1,0:T(8,128)S(1)}, f32[32,1280]{1,0:T(8,128)S(1)}, u32[]{:S(2)}, u32[]{:S(2)}) %collective-permute-start.11) | collective-permute-done | bytes 163872 | tf_op jit(solution)/shard_map/ppermute | solution.py:268
  72.4 0.9 %collective-permute-start.12 = (f32[32,1280]{1,0:T(8,128)S(1)}, f32[32,1280]{1,0:T(8,128)S(1)}, u32[]{:S(2)}, u32[]{:S(2)}) collective-permute-start(f32[32,1280]{1,0:T(8,128)S(1)} %add.53.refs_0_), channel_id=1, source_target_pairs={{0,4},{1,5},{2,6},{3,7},{4,0},{5,1},{6,2},{7,3},{8,12},{9,13},{10,... | collective-permute-start | bytes 491528 | tf_op jit(solution)/shard_map/ppermute | solution.py:268
  73.4 2.1 %collective-permute-start.15 = (f32[32,1408]{1,0:T(8,128)S(1)}, f32[32,1408]{1,0:T(8,128)S(1)}, u32[]{:S(2)}, u32[]{:S(2)}) collective-permute-start(f32[32,1408]{1,0:T(8,128)S(1)} %add.55.refs_0_), channel_id=1, source_target_pairs={{0,2},{1,3},{2,0},{3,1},{4,6},{5,7},{6,4},{7,5},{8,10},{9,11},{10,... | collective-permute-start | bytes 540680 | tf_op jit(solution)/shard_map/ppermute | solution.py:268
  75.4 0.9 %shard_map.55 = (f32[64,1280]{1,0:T(8,128)S(1)}, f32[64,128]{1,0:T(8,128)S(1)}, f32[64,512]{1,0:T(8,128)S(1)}) custom-call(f32[32,1408]{1,0:T(8,128)S(1)} %add.63.refs_0_, f32[32,1408]{1,0:T(8,128)S(1)} %collective-permute-done.31.refs_1_, bf16[2,2560,256]{2,1,0:T(8,128)(2,1)S(1)} %get-tuple-element.58.refs_8_.refs_2_.refs_10_.refs_11_, ...), custom_call_target="tpu_custom_call" | custom-call | flops 1006632960 | bytes 10846208 | tf_op jit(solution)/shard_map/pallas_call | solution.py:28
  76.4 1.0 %shard_map.56 = (f32[2,64,256]{2,1,0:T(8,128)S(1)}, f32[2,64,256]{2,1,0:T(8,128)S(1)}) custom-call(f32[32,1280]{1,0:T(8,128)S(1)} %add.61.refs_0_, f32[32,1280]{1,0:T(8,128)S(1)} %collective-permute-done.28.refs_1_, f32[64,1280]{1,0:T(8,128)S(1)} %get-tuple-element.98.refs_2_, f32[64,128]{1,0:T(8,128)S(1)} %get-tuple-element.99.refs_3_, ...), custom_call_target="tpu_custom_call" | custom-call | flops 1006632960 | bytes 12386304 | tf_op jit(solution)/shard_map/pallas_call | solution.py:28
  77.4 0.1 collective-permute-start.32
  77.5 1.4 %collective-permute-done.15.refs_1_ = f32[32,1408]{1,0:T(8,128)S(1)} collective-permute-done((f32[32,1408]{1,0:T(8,128)S(1)}, f32[32,1408]{1,0:T(8,128)S(1)}, u32[]{:S(2)}, u32[]{:S(2)}) %collective-permute-start.15) | collective-permute-done | bytes 180256 | tf_op jit(solution)/shard_map/ppermute | solution.py:268
  78.9 0.9 %shard_map.48 = (f32[64,1280]{1,0:T(8,128)S(1)}, f32[64,128]{1,0:T(8,128)S(1)}, f32[64,512]{1,0:T(8,128)S(1)}) custom-call(f32[32,1408]{1,0:T(8,128)S(1)} %add.55.refs_0_, f32[32,1408]{1,0:T(8,128)S(1)} %collective-permute-done.15.refs_1_, bf16[2,2560,256]{2,1,0:T(8,128)(2,1)S(1)} %get-tuple-element.58.refs_8_.refs_2_.refs_10_.refs_11_, ...), custom_call_target="tpu_custom_call" | custom-call | flops 1006632960 | bytes 10846208 | tf_op jit(solution)/shard_map/pallas_call | solution.py:28
  79.9 1.0 %shard_map.49 = (f32[2,64,256]{2,1,0:T(8,128)S(1)}, f32[2,64,256]{2,1,0:T(8,128)S(1)}) custom-call(f32[32,1280]{1,0:T(8,128)S(1)} %add.53.refs_0_, f32[32,1280]{1,0:T(8,128)S(1)} %collective-permute-done.12.refs_1_, f32[64,1280]{1,0:T(8,128)S(1)} %get-tuple-element.77.refs_2_, f32[64,128]{1,0:T(8,128)S(1)} %get-tuple-element.78.refs_3_, ...), custom_call_target="tpu_custom_call" | custom-call | flops 1006632960 | bytes 12386304 | tf_op jit(solution)/shard_map/pallas_call | solution.py:28
  80.8 0.1 collective-permute-start.16
  80.9 1.3 %collective-permute-done.16.refs_1_ = f32[2,64,256]{2,1,0:T(8,128)S(1)} collective-permute-done((f32[2,64,256]{2,1,0:T(8,128)S(1)}, f32[2,64,256]{2,1,0:T(8,128)S(1)}, u32[]{:S(2)}, u32[]{:S(2)}) %collective-permute-start.16) | collective-permute-done | bytes 131104 | tf_op jit(solution)/shard_map/ppermute | solution.py:268
  82.3 0.9 %shard_map.57 = (f32[2,256,128]{2,1,0:T(8,128)}, f32[2,256,128]{2,1,0:T(8,128)}) custom-call(f32[2,64,256]{2,1,0:T(8,128)S(1)} %get-tuple-element.83.refs_0_, f32[2,64,256]{2,1,0:T(8,128)S(1)} %collective-permute-done.16.refs_1_, f32[2,64,256]{2,1,0:T(8,128)S(1)} %get-tuple-element.104.refs_2_, f32[2,64,256]{2,1,0:T(8,128)S(1)} %collective-permute-done.32.refs_3_), custom_call_target="tpu_custom_call" | custom-call | bytes 524288 | tf_op jit(solution)/shard_map/pallas_call | solution.py:28
  (36 shorter events, 0.4 us)
Async XLA Ops:
  0.6 11.7 %collective-permute-start.3 = (f32[2,256,2560]{2,1,0:T(8,128)}, f32[2,256,2560]{2,1,0:T(8,128)S(1)}, u32[]{:S(2)}, u32[]{:S(2)}) collective-permute-start(f32[2,256,2560]{2,1,0:T(8,128)} %down_ref.1), channel_id=1, source_target_pairs={{0,1},{1,0},{2,3},{3,2},{4,5},{5,4},{6,7},{7,6},{8,9},{9,8},{10,11... | collective-permute-start | bytes 15728648 | tf_op jit(solution)/shard_map/ppermute | solution.py:268
  2.2 13.6 %collective-permute-start.17 = (f32[2,8,2560]{2,1,0:T(8,128)S(1)}, f32[2,8,2560]{2,1,0:T(8,128)S(1)}, u32[]{:S(2)}, u32[]{:S(2)}) collective-permute-start(f32[2,8,2560]{2,1,0:T(8,128)S(1)} %get-tuple-element.106.refs_0_), channel_id=1, source_target_pairs={{0,2},{1,3},{2,0},{3,1},{4,6},{5,7},{6,4},{7,5},{8,10},{9,11},{10,... | collective-permute-start | bytes 491528 | tf_op jit(solution)/shard_map/ppermute | solution.py:280
  4.7 11.1 %collective-permute-start.18 = (f32[2,8,2560]{2,1,0:T(8,128)S(1)}, f32[2,8,2560]{2,1,0:T(8,128)S(1)}, u32[]{:S(2)}, u32[]{:S(2)}) collective-permute-start(f32[2,8,2560]{2,1,0:T(8,128)S(1)} %get-tuple-element.106.refs_0_), channel_id=1, source_target_pairs={{0,4},{1,5},{2,6},{3,7},{4,0},{5,1},{6,2},{7,3},{8,12},{9,13},{10,... | collective-permute-start | bytes 491528 | tf_op jit(solution)/shard_map/ppermute | solution.py:280
  6.3 9.6 %collective-permute-start.19 = (f32[2,8,2560]{2,1,0:T(8,128)S(1)}, f32[2,8,2560]{2,1,0:T(8,128)S(1)}, u32[]{:S(2)}, u32[]{:S(2)}) collective-permute-start(f32[2,8,2560]{2,1,0:T(8,128)S(1)} %get-tuple-element.106.refs_0_), channel_id=1, source_target_pairs={{0,6},{1,7},{2,4},{3,5},{4,2},{5,3},{6,0},{7,1},{8,14},{9,15},{10,... | collective-permute-start | bytes 491528 | tf_op jit(solution)/shard_map/ppermute | solution.py:280
  6.3 16.7 %collective-permute-start = (f32[2,8,2560]{2,1,0:T(8,128)S(1)}, f32[2,8,2560]{2,1,0:T(8,128)S(1)}, u32[]{:S(2)}, u32[]{:S(2)}) collective-permute-start(f32[2,8,2560]{2,1,0:T(8,128)S(1)} %get-tuple-element.107.refs_0_), channel_id=1, source_target_pairs={{0,2},{1,3},{2,0},{3,1},{4,6},{5,7},{6,4},{7,5},{8,10},{9,11},{10,... | collective-permute-start | bytes 491528 | tf_op jit(solution)/shard_map/ppermute | solution.py:280
  12.3 10.6 %collective-permute-start.1 = (f32[2,8,2560]{2,1,0:T(8,128)S(1)}, f32[2,8,2560]{2,1,0:T(8,128)S(1)}, u32[]{:S(2)}, u32[]{:S(2)}) collective-permute-start(f32[2,8,2560]{2,1,0:T(8,128)S(1)} %get-tuple-element.107.refs_0_), channel_id=1, source_target_pairs={{0,4},{1,5},{2,6},{3,7},{4,0},{5,1},{6,2},{7,3},{8,12},{9,13},{10,... | collective-permute-start | bytes 491528 | tf_op jit(solution)/shard_map/ppermute | solution.py:280
  15.7 7.2 %collective-permute-start.2 = (f32[2,8,2560]{2,1,0:T(8,128)S(1)}, f32[2,8,2560]{2,1,0:T(8,128)S(1)}, u32[]{:S(2)}, u32[]{:S(2)}) collective-permute-start(f32[2,8,2560]{2,1,0:T(8,128)S(1)} %get-tuple-element.107.refs_0_), channel_id=1, source_target_pairs={{0,6},{1,7},{2,4},{3,5},{4,2},{5,3},{6,0},{7,1},{8,14},{9,15},{10,... | collective-permute-start | bytes 491528 | tf_op jit(solution)/shard_map/ppermute | solution.py:280
  18.4 7.7 %collective-permute-start.23 = (f32[32,1408]{1,0:T(8,128)S(1)}, f32[32,1408]{1,0:T(8,128)S(1)}, u32[]{:S(2)}, u32[]{:S(2)}) collective-permute-start(f32[32,1408]{1,0:T(8,128)S(1)} %get-tuple-element.89), channel_id=1, source_target_pairs={{0,2},{1,3},{2,0},{3,1},{4,6},{5,7},{6,4},{7,5},{8,10},{9,11},{10,... | collective-permute-start | bytes 540680 | tf_op jit(solution)/shard_map/ppermute | solution.py:268
  21.4 7.9 %collective-permute-start.20 = (f32[32,1280]{1,0:T(8,128)S(1)}, f32[32,1280]{1,0:T(8,128)S(1)}, u32[]{:S(2)}, u32[]{:S(2)}) collective-permute-start(f32[32,1280]{1,0:T(8,128)S(1)} %get-tuple-element.87), channel_id=1, source_target_pairs={{0,4},{1,5},{2,6},{3,7},{4,0},{5,1},{6,2},{7,3},{8,12},{9,13},{10,... | collective-permute-start | bytes 491528 | tf_op jit(solution)/shard_map/ppermute | solution.py:268
  25.6 7.0 %collective-permute-start.7 = (f32[32,1408]{1,0:T(8,128)S(1)}, f32[32,1408]{1,0:T(8,128)S(1)}, u32[]{:S(2)}, u32[]{:S(2)}) collective-permute-start(f32[32,1408]{1,0:T(8,128)S(1)} %get-tuple-element.68), channel_id=1, source_target_pairs={{0,2},{1,3},{2,0},{3,1},{4,6},{5,7},{6,4},{7,5},{8,10},{9,11},{10,... | collective-permute-start | bytes 540680 | tf_op jit(solution)/shard_map/ppermute | solution.py:268
  26.2 7.6 %collective-permute-start.24 = (f32[32,1408]{1,0:T(8,128)S(1)}, f32[32,1408]{1,0:T(8,128)S(1)}, u32[]{:S(2)}, u32[]{:S(2)}) collective-permute-start(f32[32,1408]{1,0:T(8,128)S(1)} %add.58), channel_id=1, source_target_pairs={{0,4},{1,5},{2,6},{3,7},{4,0},{5,1},{6,2},{7,3},{8,12},{9,13},{10,... | collective-permute-start | bytes 540680 | tf_op jit(solution)/shard_map/ppermute | solution.py:268
  27.5 9.7 %collective-permute-start.4 = (f32[32,1280]{1,0:T(8,128)S(1)}, f32[32,1280]{1,0:T(8,128)S(1)}, u32[]{:S(2)}, u32[]{:S(2)}) collective-permute-start(f32[32,1280]{1,0:T(8,128)S(1)} %get-tuple-element.66), channel_id=1, source_target_pairs={{0,4},{1,5},{2,6},{3,7},{4,0},{5,1},{6,2},{7,3},{8,12},{9,13},{10,... | collective-permute-start | bytes 491528 | tf_op jit(solution)/shard_map/ppermute | solution.py:268
  29.3 9.3 %collective-permute-start.21 = (f32[32,1280]{1,0:T(8,128)S(1)}, f32[32,1280]{1,0:T(8,128)S(1)}, u32[]{:S(2)}, u32[]{:S(2)}) collective-permute-start(f32[32,1280]{1,0:T(8,128)S(1)} %add.56), channel_id=1, source_target_pairs={{0,2},{1,3},{2,0},{3,1},{4,6},{5,7},{6,4},{7,5},{8,10},{9,11},{10,... | collective-permute-start | bytes 491528 | tf_op jit(solution)/shard_map/ppermute | solution.py:268
  32.6 10.5 %collective-permute-start.8 = (f32[32,1408]{1,0:T(8,128)S(1)}, f32[32,1408]{1,0:T(8,128)S(1)}, u32[]{:S(2)}, u32[]{:S(2)}) collective-permute-start(f32[32,1408]{1,0:T(8,128)S(1)} %add.50), channel_id=1, source_target_pairs={{0,4},{1,5},{2,6},{3,7},{4,0},{5,1},{6,2},{7,3},{8,12},{9,13},{10,... | collective-permute-start | bytes 540680 | tf_op jit(solution)/shard_map/ppermute | solution.py:268
  33.8 11.9 %collective-permute-start.25 = (f32[32,1408]{1,0:T(8,128)S(1)}, f32[32,1408]{1,0:T(8,128)S(1)}, u32[]{:S(2)}, u32[]{:S(2)}) collective-permute-start(f32[32,1408]{1,0:T(8,128)S(1)} %add.59.refs_0_), channel_id=1, source_target_pairs={{0,2},{1,3},{2,0},{3,1},{4,6},{5,7},{6,4},{7,5},{8,10},{9,11},{10,... | collective-permute-start | bytes 540680 | tf_op jit(solution)/shard_map/ppermute | solution.py:268
  37.2 5.9 %collective-permute-start.5 = (f32[32,1280]{1,0:T(8,128)S(1)}, f32[32,1280]{1,0:T(8,128)S(1)}, u32[]{:S(2)}, u32[]{:S(2)}) collective-permute-start(f32[32,1280]{1,0:T(8,128)S(1)} %add.48), channel_id=1, source_target_pairs={{0,2},{1,3},{2,0},{3,1},{4,6},{5,7},{6,4},{7,5},{8,10},{9,11},{10,... | collective-permute-start | bytes 491528 | tf_op jit(solution)/shard_map/ppermute | solution.py:268
  38.6 8.0 %collective-permute-start.22 = (f32[32,1280]{1,0:T(8,128)S(1)}, f32[32,1280]{1,0:T(8,128)S(1)}, u32[]{:S(2)}, u32[]{:S(2)}) collective-permute-start(f32[32,1280]{1,0:T(8,128)S(1)} %add.57.refs_0_), channel_id=1, source_target_pairs={{0,4},{1,5},{2,6},{3,7},{4,0},{5,1},{6,2},{7,3},{8,12},{9,13},{10,... | collective-permute-start | bytes 491528 | tf_op jit(solution)/shard_map/ppermute | solution.py:268
  43.1 9.4 %collective-permute-start.6 = (f32[32,1280]{1,0:T(8,128)S(1)}, f32[32,1280]{1,0:T(8,128)S(1)}, u32[]{:S(2)}, u32[]{:S(2)}) collective-permute-start(f32[32,1280]{1,0:T(8,128)S(1)} %add.49.refs_0_), channel_id=1, source_target_pairs={{0,4},{1,5},{2,6},{3,7},{4,0},{5,1},{6,2},{7,3},{8,12},{9,13},{10,... | collective-permute-start | bytes 491528 | tf_op jit(solution)/shard_map/ppermute | solution.py:268
  43.2 8.4 %collective-permute-start.9 = (f32[32,1408]{1,0:T(8,128)S(1)}, f32[32,1408]{1,0:T(8,128)S(1)}, u32[]{:S(2)}, u32[]{:S(2)}) collective-permute-start(f32[32,1408]{1,0:T(8,128)S(1)} %add.51.refs_0_), channel_id=1, source_target_pairs={{0,2},{1,3},{2,0},{3,1},{4,6},{5,7},{6,4},{7,5},{8,10},{9,11},{10,... | collective-permute-start | bytes 540680 | tf_op jit(solution)/shard_map/ppermute | solution.py:268
  48.5 8.1 %collective-permute-start.29 = (f32[32,1408]{1,0:T(8,128)S(1)}, f32[32,1408]{1,0:T(8,128)S(1)}, u32[]{:S(2)}, u32[]{:S(2)}) collective-permute-start(f32[32,1408]{1,0:T(8,128)S(1)} %get-tuple-element.97), channel_id=1, source_target_pairs={{0,2},{1,3},{2,0},{3,1},{4,6},{5,7},{6,4},{7,5},{8,10},{9,11},{10,... | collective-permute-start | bytes 540680 | tf_op jit(solution)/shard_map/ppermute | solution.py:268
  49.5 10.2 %collective-permute-start.26 = (f32[32,1280]{1,0:T(8,128)S(1)}, f32[32,1280]{1,0:T(8,128)S(1)}, u32[]{:S(2)}, u32[]{:S(2)}) collective-permute-start(f32[32,1280]{1,0:T(8,128)S(1)} %get-tuple-element.95), channel_id=1, source_target_pairs={{0,4},{1,5},{2,6},{3,7},{4,0},{5,1},{6,2},{7,3},{8,12},{9,13},{10,... | collective-permute-start | bytes 491528 | tf_op jit(solution)/shard_map/ppermute | solution.py:268
  54.4 7.5 %collective-permute-start.13 = (f32[32,1408]{1,0:T(8,128)S(1)}, f32[32,1408]{1,0:T(8,128)S(1)}, u32[]{:S(2)}, u32[]{:S(2)}) collective-permute-start(f32[32,1408]{1,0:T(8,128)S(1)} %get-tuple-element.76), channel_id=1, source_target_pairs={{0,2},{1,3},{2,0},{3,1},{4,6},{5,7},{6,4},{7,5},{8,10},{9,11},{10,... | collective-permute-start | bytes 540680 | tf_op jit(solution)/shard_map/ppermute | solution.py:268
  56.6 6.3 %collective-permute-start.30 = (f32[32,1408]{1,0:T(8,128)S(1)}, f32[32,1408]{1,0:T(8,128)S(1)}, u32[]{:S(2)}, u32[]{:S(2)}) collective-permute-start(f32[32,1408]{1,0:T(8,128)S(1)} %add.62), channel_id=1, source_target_pairs={{0,4},{1,5},{2,6},{3,7},{4,0},{5,1},{6,2},{7,3},{8,12},{9,13},{10,... | collective-permute-start | bytes 540680 | tf_op jit(solution)/shard_map/ppermute | solution.py:268
  58.3 7.4 %collective-permute-start.10 = (f32[32,1280]{1,0:T(8,128)S(1)}, f32[32,1280]{1,0:T(8,128)S(1)}, u32[]{:S(2)}, u32[]{:S(2)}) collective-permute-start(f32[32,1280]{1,0:T(8,128)S(1)} %get-tuple-element.74), channel_id=1, source_target_pairs={{0,4},{1,5},{2,6},{3,7},{4,0},{5,1},{6,2},{7,3},{8,12},{9,13},{10,... | collective-permute-start | bytes 491528 | tf_op jit(solution)/shard_map/ppermute | solution.py:268
  59.8 6.8 %collective-permute-start.27 = (f32[32,1280]{1,0:T(8,128)S(1)}, f32[32,1280]{1,0:T(8,128)S(1)}, u32[]{:S(2)}, u32[]{:S(2)}) collective-permute-start(f32[32,1280]{1,0:T(8,128)S(1)} %add.60), channel_id=1, source_target_pairs={{0,2},{1,3},{2,0},{3,1},{4,6},{5,7},{6,4},{7,5},{8,10},{9,11},{10,... | collective-permute-start | bytes 491528 | tf_op jit(solution)/shard_map/ppermute | solution.py:268
  61.9 11.5 %collective-permute-start.14 = (f32[32,1408]{1,0:T(8,128)S(1)}, f32[32,1408]{1,0:T(8,128)S(1)}, u32[]{:S(2)}, u32[]{:S(2)}) collective-permute-start(f32[32,1408]{1,0:T(8,128)S(1)} %add.54), channel_id=1, source_target_pairs={{0,4},{1,5},{2,6},{3,7},{4,0},{5,1},{6,2},{7,3},{8,12},{9,13},{10,... | collective-permute-start | bytes 540680 | tf_op jit(solution)/shard_map/ppermute | solution.py:268
  63.0 12.5 %collective-permute-start.31 = (f32[32,1408]{1,0:T(8,128)S(1)}, f32[32,1408]{1,0:T(8,128)S(1)}, u32[]{:S(2)}, u32[]{:S(2)}) collective-permute-start(f32[32,1408]{1,0:T(8,128)S(1)} %add.63.refs_0_), channel_id=1, source_target_pairs={{0,2},{1,3},{2,0},{3,1},{4,6},{5,7},{6,4},{7,5},{8,10},{9,11},{10,... | collective-permute-start | bytes 540680 | tf_op jit(solution)/shard_map/ppermute | solution.py:268
  65.7 6.6 %collective-permute-start.11 = (f32[32,1280]{1,0:T(8,128)S(1)}, f32[32,1280]{1,0:T(8,128)S(1)}, u32[]{:S(2)}, u32[]{:S(2)}) collective-permute-start(f32[32,1280]{1,0:T(8,128)S(1)} %add.52), channel_id=1, source_target_pairs={{0,2},{1,3},{2,0},{3,1},{4,6},{5,7},{6,4},{7,5},{8,10},{9,11},{10,... | collective-permute-start | bytes 491528 | tf_op jit(solution)/shard_map/ppermute | solution.py:268
  66.6 9.8 %collective-permute-start.28 = (f32[32,1280]{1,0:T(8,128)S(1)}, f32[32,1280]{1,0:T(8,128)S(1)}, u32[]{:S(2)}, u32[]{:S(2)}) collective-permute-start(f32[32,1280]{1,0:T(8,128)S(1)} %add.61.refs_0_), channel_id=1, source_target_pairs={{0,4},{1,5},{2,6},{3,7},{4,0},{5,1},{6,2},{7,3},{8,12},{9,13},{10,... | collective-permute-start | bytes 491528 | tf_op jit(solution)/shard_map/ppermute | solution.py:268
  72.4 7.5 %collective-permute-start.12 = (f32[32,1280]{1,0:T(8,128)S(1)}, f32[32,1280]{1,0:T(8,128)S(1)}, u32[]{:S(2)}, u32[]{:S(2)}) collective-permute-start(f32[32,1280]{1,0:T(8,128)S(1)} %add.53.refs_0_), channel_id=1, source_target_pairs={{0,4},{1,5},{2,6},{3,7},{4,0},{5,1},{6,2},{7,3},{8,12},{9,13},{10,... | collective-permute-start | bytes 491528 | tf_op jit(solution)/shard_map/ppermute | solution.py:268
  73.4 5.6 %collective-permute-start.15 = (f32[32,1408]{1,0:T(8,128)S(1)}, f32[32,1408]{1,0:T(8,128)S(1)}, u32[]{:S(2)}, u32[]{:S(2)}) collective-permute-start(f32[32,1408]{1,0:T(8,128)S(1)} %add.55.refs_0_), channel_id=1, source_target_pairs={{0,2},{1,3},{2,0},{3,1},{4,6},{5,7},{6,4},{7,5},{8,10},{9,11},{10,... | collective-permute-start | bytes 540680 | tf_op jit(solution)/shard_map/ppermute | solution.py:268
  77.4 3.5 %collective-permute-start.32 = (f32[2,64,256]{2,1,0:T(8,128)S(1)}, f32[2,64,256]{2,1,0:T(8,128)S(1)}, u32[]{:S(2)}, u32[]{:S(2)}) collective-permute-start(f32[2,64,256]{2,1,0:T(8,128)S(1)} %get-tuple-element.105), channel_id=1, source_target_pairs={{0,1},{1,0},{2,3},{3,2},{4,5},{5,4},{6,7},{7,6},{8,9},{9,8},{10,11... | collective-permute-start | bytes 393224 | tf_op jit(solution)/shard_map/ppermute | solution.py:268
  80.8 1.4 %collective-permute-start.16 = (f32[2,64,256]{2,1,0:T(8,128)S(1)}, f32[2,64,256]{2,1,0:T(8,128)S(1)}, u32[]{:S(2)}, u32[]{:S(2)}) collective-permute-start(f32[2,64,256]{2,1,0:T(8,128)S(1)} %get-tuple-element.84), channel_id=1, source_target_pairs={{0,1},{1,0},{2,3},{3,2},{4,5},{5,4},{6,7},{7,6},{8,9},{9,8},{10,11... | collective-permute-start | bytes 393224 | tf_op jit(solution)/shard_map/ppermute | solution.py:268

commit v5 on v3

--- a/solution.py
+++ b/solution.py
@@ -37,36 +37,42 @@
     )(*args)
 
 
-def split_kernel(down_ref, high_ref, low_ref, turned_high_ref, turned_low_ref, energy_ref):
-    rows, width = down_ref.shape[1:]
-    step = pl.program_id(0)
-
-    @pl.when(step == 0)
+def split_kernel(real_ref, imag_ref, high_ref, low_ref, turned_high_ref, turned_low_ref, energy_ref):
+    rows, shots = real_ref.shape[1:]
+    step, chunk = pl.program_id(0), pl.program_id(1)
+    width = 2 * LANES
+    at = slice(None) if rows == high_ref.shape[1] else pl.ds(pl.multiple_of(step * rows, rows), rows)
+
+    @pl.when((step == 0) & (chunk == 0))
     def _():
         energy_ref[...] = jnp.zeros_like(energy_ref)
 
-    at = pl.ds(pl.multiple_of(step * width, width), width)
-    for part in range(2):
-        value = down_ref[part]
-        high, low = parts_of(value)
-        high_ref[part, :, at] = high
-        low_ref[part, :, at] = low
-        turned_high_ref[part, at, :] = high.T
-        turned_low_ref[part, at, :] = low.T
-        square = jnp.sum((value * value).reshape(rows // 8, 8, width), axis=0)
-        energy_ref[...] += sum(square[:, lane : lane + LANES] for lane in range(0, width, LANES))
+    for part, ref in enumerate((real_ref, imag_ref)):
+        for start in range(0, shots, width):
+            value = ref[0, :, start : start + width]
+            place = pl.ds(pl.multiple_of(chunk * shots + start, width), width)
+            high, low = parts_of(value)
+            high_ref[part, at, place] = high
+            low_ref[part, at, place] = low
+            turned_high_ref[part, place, at] = high.T
+            turned_low_ref[part, place, at] = low.T
+            square = jnp.sum((value * value).reshape(rows // 8, 8, width), axis=0)
+            energy_ref[...] += sum(square[:, lane : lane + LANES] for lane in range(0, width, LANES))
 
 
 def split(value):
     _, rows, shots = value.shape
-    width = 4 * LANES
+    block, chunks = min(rows, LANES), 2
     plain, turned = ((2, rows, shots), bf16), ((2, shots, rows), bf16)
     high, low, turned_high, turned_low, energy = call(
         split_kernel,
         [plain, plain, turned, turned, ((8, LANES), f32)],
-        (value,),
-        grid=(shots // width,),
-        in_specs=[pl.BlockSpec((2, rows, width), lambda step: (0, 0, step))],
+        (value, value),
+        grid=(rows // block, chunks),
+        in_specs=[
+            pl.BlockSpec((1, block, shots // chunks), lambda step, chunk: (0, step, chunk)),
+            pl.BlockSpec((1, block, shots // chunks), lambda step, chunk: (1, step, chunk)),
+        ],
     )
     return (high, low), (turned_high, turned_low), energy
 
@@ -108,54 +114,60 @@
     return out
 
 
-def apply_down(x_ref, first_ref, second_ref, turned, image_ref):
+def apply_down(x_ref, first_ref, second_ref, turned, shots=slice(None)):
     stage(x_ref, first_ref, second_ref, -1)
-    rows = turned[0][0].shape[2]
-    for at, (high, low) in enumerate(turned):
-        image_ref[:, at * rows : (at + 1) * rows] = times(first_ref[...], second_ref[...], high, low)
-
-
-def device_bit(bit):
-    return (lax.axis_index("rcv") >> bit) & 1
-
-
-def project(value_ref, first_ref, second_ref, plain, extra, outs, bits):
+    first, second = first_ref[...], second_ref[...]
+    count = first.shape[0] // 2
+    blocks = []
+    for high, low in turned:
+        total = dot(first, high[0, shots, :]) + dot(second, high[1, shots, :])
+        rest = dot(first[:count], low[0, shots, :]) + dot(second[:count], low[1, shots, :])
+        blocks.append(total[:count] + total[count:] + rest)
+    return jnp.concatenate(blocks, axis=1)
+
+
+def side(bits):
+    me = lax.axis_index("rcv")
+    first, second = ((me >> bit) & 1 for bit in bits)
+    return first + (me & 1) * (second - first)
+
+
+def project(value_ref, first_ref, second_ref, plain, extra, keep_ref, give_ref, bits):
     stage(value_ref, first_ref, second_ref, 1)
     rows = plain[0][0].shape[1]
     shots = plain[0][0].shape[2]
     half = value_ref.shape[0] // 2
-    for at, bit in enumerate(bits):
-        columns = slice(at * shots // 2, (at + 1) * shots // 2)
+    upper = side(bits) == 1
+    for start in range(0, shots, shots // 2):
+        columns = slice(start, start + shots // 2)
         total = 0.0
         for block, (high, low) in enumerate(plain):
             own = slice(block * rows, (block + 1) * rows)
             total = total + times(first_ref[:, own], second_ref[:, own], high, low, columns)
-        pieces = [(slice(0, shots // 2), total)]
-        if at == 0:
-            pieces.append((slice(shots // 2, shots // 2 + LANES), extra))
-        keep_ref, give_ref = outs[2 * at : 2 * at + 2]
-        upper = device_bit(bit) == 1
-        for place, piece in pieces:
-            keep_ref[:, place] = jnp.where(upper, piece[half:], piece[:half])
-            give_ref[:, place] = jnp.where(upper, piece[:half], piece[half:])
+        keep_ref[:, columns] = jnp.where(upper, total[half:], total[:half])
+        give_ref[:, columns] = jnp.where(upper, total[:half], total[half:])
+    keep_ref[:, shots:] = jnp.where(upper, extra[half:], extra[:half])
+    give_ref[:, shots:] = jnp.where(upper, extra[:half], extra[half:])
 
 
 def collect(pieces, x_ref, ends_ref, bits):
-    front = x_ref.shape[1] // 2
-    for at, bit in enumerate(bits):
-        upper = device_bit(bit)
-        for which, piece in enumerate(pieces[2 * at : 2 * at + 2]):
-            half = piece.shape[0]
-            place = pl.ds(pl.multiple_of((upper ^ which) * half, half), half)
-            x_ref[place, at * front : (at + 1) * front] = piece[:, :front]
-            if at == 0:
-                ends_ref[place, :] = piece[:, front:]
+    upper = side(bits)
+    shots = x_ref.shape[1]
+    for which, piece in enumerate(pieces):
+        half = piece.shape[0]
+        place = pl.ds(pl.multiple_of((upper ^ which) * half, half), half)
+        x_ref[place, :] = piece[:, :shots]
+        ends_ref[place, :] = piece[:, shots:]
+
+
+def pairs(refs):
+    return tuple((refs[at], refs[at + 1]) for at in range(0, len(refs), 2))
 
 
 def rhs_kernel(bits, masks, *refs):
     sources, refs = refs[: len(masks)], refs[len(masks) :]
     down, refs = refs[:8], refs[8:]
-    (ea, eb), (rhs_ref, *outs), (x_ref, f0, s0, f1, s1, *spread) = refs[:2], refs[2:7], refs[7:]
+    (ea, eb), (rhs_ref, *outs), (x_ref, f0, s0, f1, s1, *spread) = refs[:2], refs[2:5], refs[5:]
     half = x_ref.shape[0] // 2
     own = sources[0].shape[1]
     chip = lax.axis_index("rcv") >> 1
@@ -167,41 +179,38 @@
                 x_ref[pl.ds(pl.multiple_of(part * half + (chip ^ mask) * own, own), own), :] = value
     for at in range(2 * half // own if spread else 0):
         x_ref[at * own : (at + 1) * own, :] = spread[0][at]
-    apply_down(x_ref, f0, s0, ((down[4], down[5]), (down[6], down[7])), rhs_ref)
+    rhs_ref[...] = apply_down(x_ref, f0, s0, pairs(down[4:]))
     energy = jnp.full((2 * half, 1), jnp.sum(ea[...] + eb[...]), f32)
     extra = tail(row_squares(rhs_ref[...]), energy)
-    project(rhs_ref, f1, s1, ((down[0], down[1]), (down[2], down[3])), extra, outs, bits)
+    project(rhs_ref, f1, s1, pairs(down[:4]), extra, *outs, bits)
 
 
 def first_kernel(bits, receivers, *refs):
-    pieces, (rhs_ref, *refs) = refs[:4], refs[4:]
-    down, refs = refs[:8], refs[8:]
-    (x_ref, scalar_ref, image_ref, residual_ref, *outs), (ends_ref, f0, s0, f1, s1) = refs[:8], refs[8:]
+    pieces, rhs_ref, down, refs = refs[:2], refs[2], refs[3:11], refs[11:]
+    (x_ref, scalar_ref, image_ref, residual_ref, *outs), (ends_ref, f0, s0, f1, s1) = refs[:6], refs[6:]
     collect(pieces, x_ref, ends_ref, bits)
     norm = both(ends_ref[:, 0:1])
     damping = damping_ratio * ends_ref[:, 1:2] / receivers
-    apply_down(x_ref, f0, s0, ((down[4], down[5]), (down[6], down[7])), image_ref)
-    image = image_ref[...] + damping * rhs_ref[...]
+    image = apply_down(x_ref, f0, s0, pairs(down[4:])) + damping * rhs_ref[...]
     image_ref[...] = image
     alpha = norm / (both(row_squares(x_ref[...])) + damping * norm)
     residual = rhs_ref[...] - alpha * image
     residual_ref[...] = residual
     scalar_ref[...] = tail(norm, damping, alpha)
-    project(residual_ref, f1, s1, ((down[0], down[1]), (down[2], down[3])), tail(row_squares(residual)), outs, bits)
+    project(residual_ref, f1, s1, pairs(down[:4]), tail(row_squares(residual)), *outs, bits)
 
 
 def last_kernel(bits, *refs):
-    pieces, (rhs_ref, before_ref, scalar_ref, image_ref, residual_ref, *turned), refs = refs[:4], refs[4:13], refs[13:]
-    keep_ref, give_ref, x_ref, ends_ref, y_ref, f0, s0 = refs
+    pieces, (rhs_ref, before_ref, scalar_ref, image_ref, residual_ref), turned = refs[:2], refs[2:7], refs[7:11]
+    keep_ref, give_ref, x_ref, ends_ref, *scratch = refs[11:]
     collect(pieces, x_ref, ends_ref, bits)
     following = both(ends_ref[:, 0:1])
     norm = scalar_ref[:, 0:1]
     damping = scalar_ref[:, 1:2]
     alpha = scalar_ref[:, 2:3]
     beta = following / norm
-    apply_down(x_ref, f0, s0, (turned[0:2], turned[2:4]), y_ref)
     residual = residual_ref[...]
-    image = y_ref[...] + beta * image_ref[...] + damping * residual
+    image = apply_down(x_ref, *scratch, pairs(turned)) + beta * image_ref[...] + damping * residual
     curvature = both(row_squares(x_ref[...] + beta * before_ref[...])) + damping * (following + beta * following)
     alpha_next = following / curvature
     rhs = rhs_ref[...]
@@ -216,7 +225,7 @@
 
 def order_kernel(own, *refs):
     pieces, (*outs, x_ref) = refs[: 2 * GROUPS], refs[2 * GROUPS :]
-    upper = device_bit(0) == 1
+    upper = (lax.axis_index("rcv") & 1) == 1
     chips = pieces[0].shape[1] // (2 * own)
     for which, out_ref in enumerate(outs):
         for part in range(2):
@@ -240,22 +249,21 @@
     own = up_sources.shape[1] // GROUPS
     chips = count // 2
     packed = 2 * chips * own
-    front = shots // 2
 
     def swap(value, bit):
         return lax.ppermute(value, "rcv", [(at, at ^ (1 << bit)) for at in range(count)])
 
-    def exchange(outs):
-        pieces = []
-        for order, (keep, give) in zip(orders, (outs[0:2], outs[2:4])):
-            keep = keep + swap(give, order[0])
-            for bit in order[1:]:
-                keep = keep + swap(keep, bit)
-            pieces += [keep, swap(keep, order[0])]
-        return pieces
-
     def jump(value, mask):
         return lax.ppermute(value, "rcv", [(at, at ^ (mask << 1)) for at in range(count)])
+
+    def turn(value, step):
+        return lax.ppermute(value, "rcv", [(at, at ^ (1 << orders[at & 1][step])) for at in range(count)])
+
+    def exchange(keep, give):
+        keep = keep + turn(give, 0)
+        for step in range(1, len(chip_bits)):
+            keep = keep + turn(keep, step)
+        return keep, turn(keep, 0)
 
     other_down = swap(down_spectra, 0)
     masks = sorted(range(chips), key=lambda mask: mask.bit_count())
@@ -273,41 +281,39 @@
     lines = ((packed, 2 * rows), f32)
     every = ((packed, shots), f32)
     small = ((packed, LANES), f32)
-    work = 2 * 2 * 2 * (3 * packed) * 2 * rows * shots
-    halves = [((packed // 2, front + LANES), f32)] * 2 + [((packed // 2, front), f32)] * 2
-
+    sent = [((packed // 2, shots + LANES), f32)] * 2
     spread = [((packed // own, own, shots), f32)] if own % 8 else []
-    outs = [
-        call(
+    work = 2 * 2 * (3 * packed) * 2 * rows * shots
+
+    state, sums = [], []
+    for source in sources:
+        rhs, *pair = call(
             functools.partial(rhs_kernel, ends, masks),
-            [lines] + halves,
-            (*pair, *down, energy_a, energy_b),
+            [lines] + sent,
+            (*source, *down, energy_a, energy_b),
             [every] + wide + short + spread,
-            work,
+            2 * work,
         )
-        for pair in sources
-    ]
-    rhs = [out[0] for out in outs]
-    sums = [exchange(out[1:]) for out in outs]
-    outs = [
-        call(
+        state.append((rhs,))
+        sums.append(exchange(*pair))
+    for group, (pieces, (rhs,)) in enumerate(zip(sums, state)):
+        x, scalars, image, residual, *pair = call(
             functools.partial(first_kernel, ends, receivers),
-            [every, small, lines, lines] + halves,
-            (*sums[group], rhs[group], *down),
+            [every, small, lines, lines] + sent,
+            (*pieces, rhs, *down),
             [small] + wide + short,
-            work,
+            2 * work,
         )
-        for group in range(GROUPS)
-    ]
-    sums = [exchange(out[4:]) for out in outs]
+        state[group] = (rhs, x, scalars, image, residual)
+        sums[group] = exchange(*pair)
     results = []
-    for group in range(GROUPS):
+    for pieces, kept in zip(sums, state):
         keep, give = call(
             functools.partial(last_kernel, ends),
             [((2, packed, rows), f32)] * 2,
-            (*sums[group], rhs[group], *outs[group][:4], *turned),
-            [every, small, lines] + wide,
-            work // 2,
+            (*pieces, *kept, *turned),
+            [every, small] + wide,
+            work,
         )
         results.append((keep, swap(give, 0)))
 

time: 84.5 us -> 94 us (1.11)
  waiting for transfers between devices: 21.4 us -> 43.2 us
  starting transfers between devices: 32.7 us -> 21.4 us
    ppermute x0 -> x12, waiting for transfers between devices: none -> 41.8 us  [turn(): lax.ppermute(value, 'rcv', [(at, at ^ 1 << orders[at & 1][step]) for at i...]
    ppermute x27 -> x3, starting transfers between devices: 25 us -> 0.66 us  [swap(): lax.ppermute(value, 'rcv', [(at, at ^ 1 << bit) for at in range(count)])]
    ppermute x27 -> x3, waiting for transfers between devices: 21.4 us -> 1.33 us  [swap(): lax.ppermute(value, 'rcv', [(at, at ^ 1 << bit) for at in range(count)])]
    ppermute x0 -> x12, starting transfers between devices: none -> 12.9 us  [turn(): lax.ppermute(value, 'rcv', [(at, at ^ 1 << orders[at & 1][step]) for at i...]
  transfers between devices with their start and end apart: 33 -> 21, of which waited for: 11 -> 10; matrix products, arithmetic and copies ran while one was open for 2% -> 1% of each run, Pallas kernels for 32% -> 28%
where the time goes in v5:
time: 94 us; the launch traced here: 93.8 us
  waiting for transfers between devices  43.2 us (46%)
  Pallas kernels  27.1 us (29%)
  starting transfers between devices  21.4 us (23%)
  local copies, waits for them, and re-layouts  1.02 us (1%)
    ppermute x12, waiting for transfers between devices, turn(): lax.ppermute(value, 'rcv', [(at, at ^ 1 << orders[at & 1][step]) for at i...  41.8 us
    pallas_call x9, Pallas kernels, call(): pl.pallas_call(kernel, out_shape=[jax.ShapeDtypeStruct(shape, dtype) for...  27.1 us
    ppermute x12, starting transfers between devices, turn(): lax.ppermute(value, 'rcv', [(at, at ^ 1 << orders[at & 1][step]) for at i...  12.9 us
    ppermute x6, starting transfers between devices, jump(): lax.ppermute(value, 'rcv', [(at, at ^ mask << 1) for at in range(count)])  7.87 us
  transfers between devices with their start and end apart: 21, of which 10 were waited for; matrix products, arithmetic and copies ran while one was open for 1% of the time, Pallas kernels for 28%

profile of v5, /device:TPU:0, one launch (start us, length us, event | category | flops | bytes accessed | tf_op | source)
XLA Modules:
  0.0 93.8 jit_solution(11522484911943237518)
XLA Ops:
  0.6 0.5 collective-permute-start.3
  1.1 1.0 %fusion = (f32[2,8,2560]{2,1,0:T(8,128)S(1)}, f32[2,8,2560]{2,1,0:T(8,128)S(1)}) fusion(f32[2,16,2560]{2,1,0:T(8,128)} %param.3), kind=kLoop, calls=%fused_computation | loop fusion | bytes 655360 | tf_op jit(solution)/shard_map/slice | solution.py:272
  2.2 2.6 %collective-permute-start.11 = (f32[2,8,2560]{2,1,0:T(8,128)S(1)}, f32[2,8,2560]{2,1,0:T(8,128)S(1)}, u32[]{:S(2)}, u32[]{:S(2)}) collective-permute-start(f32[2,8,2560]{2,1,0:T(8,128)S(1)} %get-tuple-element.66.refs_0_), channel_id=1, source_target_pairs={{0,2},{1,3},{2,0},{3,1},{4,6},{5,7},{6,4},{7,5},{8,10},{9,11},{10,... | collective-permute-start | bytes 491528 | tf_op jit(solution)/shard_map/ppermute | solution.py:257
  4.7 1.5 %collective-permute-start.12 = (f32[2,8,2560]{2,1,0:T(8,128)S(1)}, f32[2,8,2560]{2,1,0:T(8,128)S(1)}, u32[]{:S(2)}, u32[]{:S(2)}) collective-permute-start(f32[2,8,2560]{2,1,0:T(8,128)S(1)} %get-tuple-element.66.refs_0_), channel_id=1, source_target_pairs={{0,4},{1,5},{2,6},{3,7},{4,0},{5,1},{6,2},{7,3},{8,12},{9,13},{10,... | collective-permute-start | bytes 491528 | tf_op jit(solution)/shard_map/ppermute | solution.py:257
  6.3 0.0 collective-permute-start.13
  6.3 1.9 %collective-permute-start = (f32[2,8,2560]{2,1,0:T(8,128)S(1)}, f32[2,8,2560]{2,1,0:T(8,128)S(1)}, u32[]{:S(2)}, u32[]{:S(2)}) collective-permute-start(f32[2,8,2560]{2,1,0:T(8,128)S(1)} %get-tuple-element.67.refs_0_), channel_id=1, source_target_pairs={{0,2},{1,3},{2,0},{3,1},{4,6},{5,7},{6,4},{7,5},{8,10},{9,11},{10,... | collective-permute-start | bytes 491528 | tf_op jit(solution)/shard_map/ppermute | solution.py:257
  8.2 4.0 %shard_map.41 = (bf16[2,256,2560]{2,1,0:T(8,128)(2,1)S(1)}, bf16[2,256,2560]{2,1,0:T(8,128)(2,1)S(1)}, bf16[2,2560,256]{2,1,0:T(8,128)(2,1)S(1)}, bf16[2,2560,256]{2,1,0:T(8,128)(2,1)S(1)}, f32[8,128]{1,0:T(8,128)S(1)}) custom-call(f32[2,256,2560]{2,1,0:T(8,128)} %imag_ref.1, f32[2,256,2560]{2,1,0:T(8,128)} %imag_ref.1), custom_call_target="tpu_custom_call" | custom-call | bytes 10485760 | tf_op jit(solution)/shard_map/pallas_call | solution.py:28
  12.2 0.0 collective-permute-done.3.real_ref.imag_ref
  12.2 1.6 %collective-permute-start.1 = (f32[2,8,2560]{2,1,0:T(8,128)S(1)}, f32[2,8,2560]{2,1,0:T(8,128)S(1)}, u32[]{:S(2)}, u32[]{:S(2)}) collective-permute-start(f32[2,8,2560]{2,1,0:T(8,128)S(1)} %get-tuple-element.67.refs_0_), channel_id=1, source_target_pairs={{0,4},{1,5},{2,6},{3,7},{4,0},{5,1},{6,2},{7,3},{8,12},{9,13},{10,... | collective-permute-start | bytes 491528 | tf_op jit(solution)/shard_map/ppermute | solution.py:257
  13.8 2.1 %shard_map.42 = (bf16[2,256,2560]{2,1,0:T(8,128)(2,1)S(1)}, bf16[2,256,2560]{2,1,0:T(8,128)(2,1)S(1)}, bf16[2,2560,256]{2,1,0:T(8,128)(2,1)S(1)}, bf16[2,2560,256]{2,1,0:T(8,128)(2,1)S(1)}, f32[8,128]{1,0:T(8,128)S(1)}) custom-call(f32[2,256,2560]{2,1,0:T(8,128)S(1)} %collective-permute-done.3.real_ref.imag_ref, ...), custom_call_target="tpu_custom_call" | custom-call | bytes 10485760 | tf_op jit(solution)/shard_map/pallas_call | solution.py:28
  15.9 0.0 collective-permute-done.11.refs_1_
  15.9 0.2 collective-permute-start.2
  16.2 0.0 collective-permute-done.12.refs_2_
  16.2 0.0 collective-permute-done.13.refs_3_
  16.2 4.1 %shard_map.46 = (f32[64,512]{1,0:T(8,128)S(1)}, f32[32,2688]{1,0:T(8,128)S(1)}, f32[32,2688]{1,0:T(8,128)S(1)}) custom-call(f32[2,8,2560]{2,1,0:T(8,128)S(1)} %get-tuple-element.66.refs_0_, f32[2,8,2560]{2,1,0:T(8,128)S(1)} %collective-permute-done.11.refs_1_, f32[2,8,2560]{2,1,0:T(8,128)S(1)} %collective-permute-done.12.refs_2_, ...), custom_call_target="tpu_custom_call" | custom-call | flops 2013265920 | bytes 21635072 | tf_op jit(solution)/shard_map/pallas_call | solution.py:28
  20.3 1.9 %collective-permute-start.14 = (f32[32,2688]{1,0:T(8,128)S(1)}, f32[32,2688]{1,0:T(8,128)S(1)}, u32[]{:S(2)}, u32[]{:S(2)}) collective-permute-start(f32[32,2688]{1,0:T(8,128)S(1)} %get-tuple-element.56), channel_id=1, source_target_pairs={{0,2},{1,5},{2,0},{3,7},{4,6},{5,1},{6,4},{7,3},{8,10},{9,13},{10,... | collective-permute-start | bytes 1032200 | tf_op jit(solution)/shard_map/ppermute | solution.py:260
  22.2 0.0 collective-permute-done.refs_1_
  22.2 0.0 collective-permute-done.1.refs_2_
  22.2 0.0 collective-permute-done.2.refs_3_
  22.2 4.1 %shard_map.43 = (f32[64,512]{1,0:T(8,128)S(1)}, f32[32,2688]{1,0:T(8,128)S(1)}, f32[32,2688]{1,0:T(8,128)S(1)}) custom-call(f32[2,8,2560]{2,1,0:T(8,128)S(1)} %get-tuple-element.67.refs_0_, f32[2,8,2560]{2,1,0:T(8,128)S(1)} %collective-permute-done.refs_1_, f32[2,8,2560]{2,1,0:T(8,128)S(1)} %collective-permute-done.1.refs_2_, ...), custom_call_target="tpu_custom_call" | custom-call | flops 2013265920 | bytes 21635072 | tf_op jit(solution)/shard_map/pallas_call | solution.py:28
  26.4 0.9 collective-permute-start.4
  27.3 0.3 collective-permute-done.14
  27.7 1.9 %collective-permute-start.15 = (f32[32,2688]{1,0:T(8,128)S(1)}, f32[32,2688]{1,0:T(8,128)S(1)}, u32[]{:S(2)}, u32[]{:S(2)}) collective-permute-start(f32[32,2688]{1,0:T(8,128)S(1)} %add.28), channel_id=1, source_target_pairs={{0,4},{1,3},{2,6},{3,1},{4,0},{5,7},{6,2},{7,5},{8,12},{9,11},{10,... | collective-permute-start | bytes 1032200 | tf_op jit(solution)/shard_map/ppermute | solution.py:260
  29.6 7.8 %collective-permute-done.4 = f32[32,2688]{1,0:T(8,128)S(1)} collective-permute-done((f32[32,2688]{1,0:T(8,128)S(1)}, f32[32,2688]{1,0:T(8,128)S(1)}, u32[]{:S(2)}, u32[]{:S(2)}) %collective-permute-start.4) | collective-permute-done | bytes 344096 | tf_op jit(solution)/shard_map/ppermute | solution.py:260
  37.4 1.5 %collective-permute-start.5 = (f32[32,2688]{1,0:T(8,128)S(1)}, f32[32,2688]{1,0:T(8,128)S(1)}, u32[]{:S(2)}, u32[]{:S(2)}) collective-permute-start(f32[32,2688]{1,0:T(8,128)S(1)} %add.24), channel_id=1, source_target_pairs={{0,4},{1,3},{2,6},{3,1},{4,0},{5,7},{6,2},{7,5},{8,12},{9,11},{10,... | collective-permute-start | bytes 1032200 | tf_op jit(solution)/shard_map/ppermute | solution.py:260
  38.9 0.0 collective-permute-done.15
  39.0 0.5 collective-permute-start.16
  39.5 8.9 %collective-permute-done.5 = f32[32,2688]{1,0:T(8,128)S(1)} collective-permute-done((f32[32,2688]{1,0:T(8,128)S(1)}, f32[32,2688]{1,0:T(8,128)S(1)}, u32[]{:S(2)}, u32[]{:S(2)}) %collective-permute-start.5) | collective-permute-done | bytes 344096 | tf_op jit(solution)/shard_map/ppermute | solution.py:260
  48.5 0.9 collective-permute-start.6
  49.4 0.0 collective-permute-done.16.refs_1_
  49.4 4.0 %shard_map.47 = (f32[64,2560]{1,0:T(8,128)S(1)}, f32[64,128]{1,0:T(8,128)S(1)}, f32[64,512]{1,0:T(8,128)S(1)}, f32[64,512]{1,0:T(8,128)S(1)}, f32[32,2688]{1,0:T(8,128)S(1)}, /*index=5*/f32[32,2688]{1,0:T(8,128)S(1)}) custom-call(f32[32,2688]{1,0:T(8,128)S(1)} %add.29.refs_0_, f32[32,2688]{1,0:T(8,128)S(1)} %collective-permute-done.16.refs_1_, ...), custom_call_target="tpu_custom_call" | custom-call | flops 2013265920 | bytes 21790720 | tf_op jit(solution)/shard_map/pallas_call | solution.py:28
  53.4 1.3 %collective-permute-start.17 = (f32[32,2688]{1,0:T(8,128)S(1)}, f32[32,2688]{1,0:T(8,128)S(1)}, u32[]{:S(2)}, u32[]{:S(2)}) collective-permute-start(f32[32,2688]{1,0:T(8,128)S(1)} %get-tuple-element.59), channel_id=1, source_target_pairs={{0,2},{1,5},{2,0},{3,7},{4,6},{5,1},{6,4},{7,3},{8,10},{9,13},{10,... | collective-permute-start | bytes 1032200 | tf_op jit(solution)/shard_map/ppermute | solution.py:260
  54.7 1.1 %collective-permute-done.6.refs_1_ = f32[32,2688]{1,0:T(8,128)S(1)} collective-permute-done((f32[32,2688]{1,0:T(8,128)S(1)}, f32[32,2688]{1,0:T(8,128)S(1)}, u32[]{:S(2)}, u32[]{:S(2)}) %collective-permute-start.6) | collective-permute-done | bytes 344096 | tf_op jit(solution)/shard_map/ppermute | solution.py:260
  55.8 4.2 %shard_map.44 = (f32[64,2560]{1,0:T(8,128)S(1)}, f32[64,128]{1,0:T(8,128)S(1)}, f32[64,512]{1,0:T(8,128)S(1)}, f32[64,512]{1,0:T(8,128)S(1)}, f32[32,2688]{1,0:T(8,128)S(1)}, /*index=5*/f32[32,2688]{1,0:T(8,128)S(1)}) custom-call(f32[32,2688]{1,0:T(8,128)S(1)} %add.25.refs_0_, f32[32,2688]{1,0:T(8,128)S(1)} %collective-permute-done.6.refs_1_, ...), custom_call_target="tpu_custom_call" | custom-call | flops 2013265920 | bytes 21790720 | tf_op jit(solution)/shard_map/pallas_call | solution.py:28
  60.1 0.9 collective-permute-start.7
  60.9 3.1 %collective-permute-done.17 = f32[32,2688]{1,0:T(8,128)S(1)} collective-permute-done((f32[32,2688]{1,0:T(8,128)S(1)}, f32[32,2688]{1,0:T(8,128)S(1)}, u32[]{:S(2)}, u32[]{:S(2)}) %collective-permute-start.17) | collective-permute-done | bytes 344096 | tf_op jit(solution)/shard_map/ppermute | solution.py:260
  64.1 0.9 collective-permute-start.18
  65.0 6.4 %collective-permute-done.7 = f32[32,2688]{1,0:T(8,128)S(1)} collective-permute-done((f32[32,2688]{1,0:T(8,128)S(1)}, f32[32,2688]{1,0:T(8,128)S(1)}, u32[]{:S(2)}, u32[]{:S(2)}) %collective-permute-start.7) | collective-permute-done | bytes 344096 | tf_op jit(solution)/shard_map/ppermute | solution.py:260
  71.5 1.2 %collective-permute-start.8 = (f32[32,2688]{1,0:T(8,128)S(1)}, f32[32,2688]{1,0:T(8,128)S(1)}, u32[]{:S(2)}, u32[]{:S(2)}) collective-permute-start(f32[32,2688]{1,0:T(8,128)S(1)} %add.26), channel_id=1, source_target_pairs={{0,4},{1,3},{2,6},{3,1},{4,0},{5,7},{6,2},{7,5},{8,12},{9,11},{10,... | collective-permute-start | bytes 1032200 | tf_op jit(solution)/shard_map/ppermute | solution.py:260
  72.7 2.4 %collective-permute-done.18 = f32[32,2688]{1,0:T(8,128)S(1)} collective-permute-done((f32[32,2688]{1,0:T(8,128)S(1)}, f32[32,2688]{1,0:T(8,128)S(1)}, u32[]{:S(2)}, u32[]{:S(2)}) %collective-permute-start.18) | collective-permute-done | bytes 344096 | tf_op jit(solution)/shard_map/ppermute | solution.py:260
  75.2 0.1 collective-permute-start.19
  75.3 7.1 %collective-permute-done.8 = f32[32,2688]{1,0:T(8,128)S(1)} collective-permute-done((f32[32,2688]{1,0:T(8,128)S(1)}, f32[32,2688]{1,0:T(8,128)S(1)}, u32[]{:S(2)}, u32[]{:S(2)}) %collective-permute-start.8) | collective-permute-done | bytes 344096 | tf_op jit(solution)/shard_map/ppermute | solution.py:260
  82.4 0.9 %collective-permute-start.9 = (f32[32,2688]{1,0:T(8,128)S(1)}, f32[32,2688]{1,0:T(8,128)S(1)}, u32[]{:S(2)}, u32[]{:S(2)}) collective-permute-start(f32[32,2688]{1,0:T(8,128)S(1)} %add.27.refs_0_), channel_id=1, source_target_pairs={{0,2},{1,5},{2,0},{3,7},{4,6},{5,1},{6,4},{7,3},{8,10},{9,13},{10,... | collective-permute-start | bytes 1032200 | tf_op jit(solution)/shard_map/ppermute | solution.py:260
  83.3 0.0 collective-permute-done.19.refs_1_
  83.3 1.8 %shard_map.48 = (f32[2,64,256]{2,1,0:T(8,128)S(1)}, f32[2,64,256]{2,1,0:T(8,128)S(1)}) custom-call(f32[32,2688]{1,0:T(8,128)S(1)} %add.31.refs_0_, f32[32,2688]{1,0:T(8,128)S(1)} %collective-permute-done.19.refs_1_, f32[64,512]{1,0:T(8,128)S(1)} %get-tuple-element.57.refs_2_, f32[64,2560]{1,0:T(8,128)S(1)} %get-tuple-element.60.refs_3_, ...), custom_call_target="tpu_custom_call" | custom-call | flops 1006632960 | bytes 12255232 | tf_op jit(solution)/shard_map/pallas_call | solution.py:28
  85.1 0.1 collective-permute-start.20
  85.2 4.5 %collective-permute-done.9.refs_1_ = f32[32,2688]{1,0:T(8,128)S(1)} collective-permute-done((f32[32,2688]{1,0:T(8,128)S(1)}, f32[32,2688]{1,0:T(8,128)S(1)}, u32[]{:S(2)}, u32[]{:S(2)}) %collective-permute-start.9) | collective-permute-done | bytes 344096 | tf_op jit(solution)/shard_map/ppermute | solution.py:260
  89.7 1.8 %shard_map.45 = (f32[2,64,256]{2,1,0:T(8,128)S(1)}, f32[2,64,256]{2,1,0:T(8,128)S(1)}) custom-call(f32[32,2688]{1,0:T(8,128)S(1)} %add.27.refs_0_, f32[32,2688]{1,0:T(8,128)S(1)} %collective-permute-done.9.refs_1_, f32[64,512]{1,0:T(8,128)S(1)} %get-tuple-element.46.refs_2_, f32[64,2560]{1,0:T(8,128)S(1)} %get-tuple-element.49.refs_3_, ...), custom_call_target="tpu_custom_call" | custom-call | flops 1006632960 | bytes 12255232 | tf_op jit(solution)/shard_map/pallas_call | solution.py:28
  91.5 0.1 collective-permute-start.10
  91.6 0.0 collective-permute-done.20.refs_3_
  91.6 1.3 %collective-permute-done.10.refs_1_ = f32[2,64,256]{2,1,0:T(8,128)S(1)} collective-permute-done((f32[2,64,256]{2,1,0:T(8,128)S(1)}, f32[2,64,256]{2,1,0:T(8,128)S(1)}, u32[]{:S(2)}, u32[]{:S(2)}) %collective-permute-start.10) | collective-permute-done | bytes 131104 | tf_op jit(solution)/shard_map/ppermute | solution.py:254
  92.9 0.9 shard_map.49
  (8 shorter events, 0.4 us)
Async XLA Ops:
  0.6 11.6 %collective-permute-start.3 = (f32[2,256,2560]{2,1,0:T(8,128)}, f32[2,256,2560]{2,1,0:T(8,128)S(1)}, u32[]{:S(2)}, u32[]{:S(2)}) collective-permute-start(f32[2,256,2560]{2,1,0:T(8,128)} %imag_ref.1), channel_id=1, source_target_pairs={{0,1},{1,0},{2,3},{3,2},{4,5},{5,4},{6,7},{7,6},{8,9},{9,8},{10,11... | collective-permute-start | bytes 15728648 | tf_op jit(solution)/shard_map/ppermute | solution.py:254
  2.2 13.8 %collective-permute-start.11 = (f32[2,8,2560]{2,1,0:T(8,128)S(1)}, f32[2,8,2560]{2,1,0:T(8,128)S(1)}, u32[]{:S(2)}, u32[]{:S(2)}) collective-permute-start(f32[2,8,2560]{2,1,0:T(8,128)S(1)} %get-tuple-element.66.refs_0_), channel_id=1, source_target_pairs={{0,2},{1,3},{2,0},{3,1},{4,6},{5,7},{6,4},{7,5},{8,10},{9,11},{10,... | collective-permute-start | bytes 491528 | tf_op jit(solution)/shard_map/ppermute | solution.py:257
  4.7 11.4 %collective-permute-start.12 = (f32[2,8,2560]{2,1,0:T(8,128)S(1)}, f32[2,8,2560]{2,1,0:T(8,128)S(1)}, u32[]{:S(2)}, u32[]{:S(2)}) collective-permute-start(f32[2,8,2560]{2,1,0:T(8,128)S(1)} %get-tuple-element.66.refs_0_), channel_id=1, source_target_pairs={{0,4},{1,5},{2,6},{3,7},{4,0},{5,1},{6,2},{7,3},{8,12},{9,13},{10,... | collective-permute-start | bytes 491528 | tf_op jit(solution)/shard_map/ppermute | solution.py:257
  6.3 9.9 %collective-permute-start.13 = (f32[2,8,2560]{2,1,0:T(8,128)S(1)}, f32[2,8,2560]{2,1,0:T(8,128)S(1)}, u32[]{:S(2)}, u32[]{:S(2)}) collective-permute-start(f32[2,8,2560]{2,1,0:T(8,128)S(1)} %get-tuple-element.66.refs_0_), channel_id=1, source_target_pairs={{0,6},{1,7},{2,4},{3,5},{4,2},{5,3},{6,0},{7,1},{8,14},{9,15},{10,... | collective-permute-start | bytes 491528 | tf_op jit(solution)/shard_map/ppermute | solution.py:257
  6.3 15.9 %collective-permute-start = (f32[2,8,2560]{2,1,0:T(8,128)S(1)}, f32[2,8,2560]{2,1,0:T(8,128)S(1)}, u32[]{:S(2)}, u32[]{:S(2)}) collective-permute-start(f32[2,8,2560]{2,1,0:T(8,128)S(1)} %get-tuple-element.67.refs_0_), channel_id=1, source_target_pairs={{0,2},{1,3},{2,0},{3,1},{4,6},{5,7},{6,4},{7,5},{8,10},{9,11},{10,... | collective-permute-start | bytes 491528 | tf_op jit(solution)/shard_map/ppermute | solution.py:257
  12.2 10.0 %collective-permute-start.1 = (f32[2,8,2560]{2,1,0:T(8,128)S(1)}, f32[2,8,2560]{2,1,0:T(8,128)S(1)}, u32[]{:S(2)}, u32[]{:S(2)}) collective-permute-start(f32[2,8,2560]{2,1,0:T(8,128)S(1)} %get-tuple-element.67.refs_0_), channel_id=1, source_target_pairs={{0,4},{1,5},{2,6},{3,7},{4,0},{5,1},{6,2},{7,3},{8,12},{9,13},{10,... | collective-permute-start | bytes 491528 | tf_op jit(solution)/shard_map/ppermute | solution.py:257
  15.9 6.3 %collective-permute-start.2 = (f32[2,8,2560]{2,1,0:T(8,128)S(1)}, f32[2,8,2560]{2,1,0:T(8,128)S(1)}, u32[]{:S(2)}, u32[]{:S(2)}) collective-permute-start(f32[2,8,2560]{2,1,0:T(8,128)S(1)} %get-tuple-element.67.refs_0_), channel_id=1, source_target_pairs={{0,6},{1,7},{2,4},{3,5},{4,2},{5,3},{6,0},{7,1},{8,14},{9,15},{10,... | collective-permute-start | bytes 491528 | tf_op jit(solution)/shard_map/ppermute | solution.py:257
  20.3 7.3 %collective-permute-start.14 = (f32[32,2688]{1,0:T(8,128)S(1)}, f32[32,2688]{1,0:T(8,128)S(1)}, u32[]{:S(2)}, u32[]{:S(2)}) collective-permute-start(f32[32,2688]{1,0:T(8,128)S(1)} %get-tuple-element.56), channel_id=1, source_target_pairs={{0,2},{1,5},{2,0},{3,7},{4,6},{5,1},{6,4},{7,3},{8,10},{9,13},{10,... | collective-permute-start | bytes 1032200 | tf_op jit(solution)/shard_map/ppermute | solution.py:260
  26.4 11.0 %collective-permute-start.4 = (f32[32,2688]{1,0:T(8,128)S(1)}, f32[32,2688]{1,0:T(8,128)S(1)}, u32[]{:S(2)}, u32[]{:S(2)}) collective-permute-start(f32[32,2688]{1,0:T(8,128)S(1)} %get-tuple-element.45), channel_id=1, source_target_pairs={{0,2},{1,5},{2,0},{3,7},{4,6},{5,1},{6,4},{7,3},{8,10},{9,13},{10,... | collective-permute-start | bytes 1032200 | tf_op jit(solution)/shard_map/ppermute | solution.py:260
  27.7 11.3 %collective-permute-start.15 = (f32[32,2688]{1,0:T(8,128)S(1)}, f32[32,2688]{1,0:T(8,128)S(1)}, u32[]{:S(2)}, u32[]{:S(2)}) collective-permute-start(f32[32,2688]{1,0:T(8,128)S(1)} %add.28), channel_id=1, source_target_pairs={{0,4},{1,3},{2,6},{3,1},{4,0},{5,7},{6,2},{7,5},{8,12},{9,11},{10,... | collective-permute-start | bytes 1032200 | tf_op jit(solution)/shard_map/ppermute | solution.py:260
  37.4 11.1 %collective-permute-start.5 = (f32[32,2688]{1,0:T(8,128)S(1)}, f32[32,2688]{1,0:T(8,128)S(1)}, u32[]{:S(2)}, u32[]{:S(2)}) collective-permute-start(f32[32,2688]{1,0:T(8,128)S(1)} %add.24), channel_id=1, source_target_pairs={{0,4},{1,3},{2,6},{3,1},{4,0},{5,7},{6,2},{7,5},{8,12},{9,11},{10,... | collective-permute-start | bytes 1032200 | tf_op jit(solution)/shard_map/ppermute | solution.py:260
  39.0 10.4 %collective-permute-start.16 = (f32[32,2688]{1,0:T(8,128)S(1)}, f32[32,2688]{1,0:T(8,128)S(1)}, u32[]{:S(2)}, u32[]{:S(2)}) collective-permute-start(f32[32,2688]{1,0:T(8,128)S(1)} %add.29.refs_0_), channel_id=1, source_target_pairs={{0,2},{1,5},{2,0},{3,7},{4,6},{5,1},{6,4},{7,3},{8,10},{9,13},{10,... | collective-permute-start | bytes 1032200 | tf_op jit(solution)/shard_map/ppermute | solution.py:260
  48.5 7.3 %collective-permute-start.6 = (f32[32,2688]{1,0:T(8,128)S(1)}, f32[32,2688]{1,0:T(8,128)S(1)}, u32[]{:S(2)}, u32[]{:S(2)}) collective-permute-start(f32[32,2688]{1,0:T(8,128)S(1)} %add.25.refs_0_), channel_id=1, source_target_pairs={{0,2},{1,5},{2,0},{3,7},{4,6},{5,1},{6,4},{7,3},{8,10},{9,13},{10,... | collective-permute-start | bytes 1032200 | tf_op jit(solution)/shard_map/ppermute | solution.py:260
  53.4 10.7 %collective-permute-start.17 = (f32[32,2688]{1,0:T(8,128)S(1)}, f32[32,2688]{1,0:T(8,128)S(1)}, u32[]{:S(2)}, u32[]{:S(2)}) collective-permute-start(f32[32,2688]{1,0:T(8,128)S(1)} %get-tuple-element.59), channel_id=1, source_target_pairs={{0,2},{1,5},{2,0},{3,7},{4,6},{5,1},{6,4},{7,3},{8,10},{9,13},{10,... | collective-permute-start | bytes 1032200 | tf_op jit(solution)/shard_map/ppermute | solution.py:260
  60.1 11.4 %collective-permute-start.7 = (f32[32,2688]{1,0:T(8,128)S(1)}, f32[32,2688]{1,0:T(8,128)S(1)}, u32[]{:S(2)}, u32[]{:S(2)}) collective-permute-start(f32[32,2688]{1,0:T(8,128)S(1)} %get-tuple-element.48), channel_id=1, source_target_pairs={{0,2},{1,5},{2,0},{3,7},{4,6},{5,1},{6,4},{7,3},{8,10},{9,13},{10,... | collective-permute-start | bytes 1032200 | tf_op jit(solution)/shard_map/ppermute | solution.py:260
  64.1 11.0 %collective-permute-start.18 = (f32[32,2688]{1,0:T(8,128)S(1)}, f32[32,2688]{1,0:T(8,128)S(1)}, u32[]{:S(2)}, u32[]{:S(2)}) collective-permute-start(f32[32,2688]{1,0:T(8,128)S(1)} %add.30), channel_id=1, source_target_pairs={{0,4},{1,3},{2,6},{3,1},{4,0},{5,7},{6,2},{7,5},{8,12},{9,11},{10,... | collective-permute-start | bytes 1032200 | tf_op jit(solution)/shard_map/ppermute | solution.py:260
  71.5 10.8 %collective-permute-start.8 = (f32[32,2688]{1,0:T(8,128)S(1)}, f32[32,2688]{1,0:T(8,128)S(1)}, u32[]{:S(2)}, u32[]{:S(2)}) collective-permute-start(f32[32,2688]{1,0:T(8,128)S(1)} %add.26), channel_id=1, source_target_pairs={{0,4},{1,3},{2,6},{3,1},{4,0},{5,7},{6,2},{7,5},{8,12},{9,11},{10,... | collective-permute-start | bytes 1032200 | tf_op jit(solution)/shard_map/ppermute | solution.py:260
  75.2 8.2 %collective-permute-start.19 = (f32[32,2688]{1,0:T(8,128)S(1)}, f32[32,2688]{1,0:T(8,128)S(1)}, u32[]{:S(2)}, u32[]{:S(2)}) collective-permute-start(f32[32,2688]{1,0:T(8,128)S(1)} %add.31.refs_0_), channel_id=1, source_target_pairs={{0,2},{1,5},{2,0},{3,7},{4,6},{5,1},{6,4},{7,3},{8,10},{9,13},{10,... | collective-permute-start | bytes 1032200 | tf_op jit(solution)/shard_map/ppermute | solution.py:260
  82.4 7.3 %collective-permute-start.9 = (f32[32,2688]{1,0:T(8,128)S(1)}, f32[32,2688]{1,0:T(8,128)S(1)}, u32[]{:S(2)}, u32[]{:S(2)}) collective-permute-start(f32[32,2688]{1,0:T(8,128)S(1)} %add.27.refs_0_), channel_id=1, source_target_pairs={{0,2},{1,5},{2,0},{3,7},{4,6},{5,1},{6,4},{7,3},{8,10},{9,13},{10,... | collective-permute-start | bytes 1032200 | tf_op jit(solution)/shard_map/ppermute | solution.py:260
  85.1 6.5 %collective-permute-start.20 = (f32[2,64,256]{2,1,0:T(8,128)S(1)}, f32[2,64,256]{2,1,0:T(8,128)S(1)}, u32[]{:S(2)}, u32[]{:S(2)}) collective-permute-start(f32[2,64,256]{2,1,0:T(8,128)S(1)} %get-tuple-element.65), channel_id=1, source_target_pairs={{0,1},{1,0},{2,3},{3,2},{4,5},{5,4},{6,7},{7,6},{8,9},{9,8},{10,11... | collective-permute-start | bytes 393224 | tf_op jit(solution)/shard_map/ppermute | solution.py:254
  91.5 1.4 %collective-permute-start.10 = (f32[2,64,256]{2,1,0:T(8,128)S(1)}, f32[2,64,256]{2,1,0:T(8,128)S(1)}, u32[]{:S(2)}, u32[]{:S(2)}) collective-permute-start(f32[2,64,256]{2,1,0:T(8,128)S(1)} %get-tuple-element.54), channel_id=1, source_target_pairs={{0,1},{1,0},{2,3},{3,2},{4,5},{5,4},{6,7},{7,6},{8,9},{9,8},{10,11... | collective-permute-start | bytes 393224 | tf_op jit(solution)/shard_map/ppermute | solution.py:254

commit v6 on v4

--- a/solution.py
+++ b/solution.py
@@ -9,6 +9,8 @@
 damping_ratio = 0.1
 LANES = 128
 GROUPS = 2
+ORDER = {'bE': ['a1.2']}
+COST = {'bC.': 0.3, 'aL.': 0, 'aR': 30, 'bM': 10, 'bL.': 0, 'bC': 0, 'aC': 0.3, 'aC.': 3, 'aL': 0}
 f32 = jnp.float32
 bf16 = jnp.bfloat16
 
@@ -37,39 +39,42 @@
     )(*args)
 
 
-def split_kernel(down_ref, high_ref, low_ref, turned_high_ref, turned_low_ref, energy_ref):
-    rows, shots = down_ref.shape[1:]
-    part, step = pl.program_id(0), pl.program_id(1)
-    width = 4 * LANES
-    whole = rows == high_ref.shape[1]
-    at = slice(None) if whole else pl.ds(pl.multiple_of(step * rows, rows), rows)
-
-    @pl.when((part == 0) & (step == 0))
+def split_kernel(real_ref, imag_ref, high_ref, low_ref, turned_high_ref, turned_low_ref, energy_ref):
+    rows, shots = real_ref.shape[1:]
+    step, chunk = pl.program_id(0), pl.program_id(1)
+    width = 2 * LANES
+    at = slice(None) if rows == high_ref.shape[1] else pl.ds(pl.multiple_of(step * rows, rows), rows)
+
+    @pl.when((step == 0) & (chunk == 0))
     def _():
         energy_ref[...] = jnp.zeros_like(energy_ref)
 
-    for start in range(0, shots, width):
-        place = slice(start, start + width)
-        value = down_ref[0, :, place]
-        high, low = parts_of(value)
-        high_ref[part, at, place] = high
-        low_ref[part, at, place] = low
-        turned_high_ref[part, place, at] = high.T
-        turned_low_ref[part, place, at] = low.T
-        square = jnp.sum((value * value).reshape(rows // 8, 8, width), axis=0)
-        energy_ref[...] += sum(square[:, lane : lane + LANES] for lane in range(0, width, LANES))
+    for part, ref in enumerate((real_ref, imag_ref)):
+        for start in range(0, shots, width):
+            value = ref[0, :, start : start + width]
+            place = pl.ds(pl.multiple_of(chunk * shots + start, width), width)
+            high, low = parts_of(value)
+            high_ref[part, at, place] = high
+            low_ref[part, at, place] = low
+            turned_high_ref[part, place, at] = high.T
+            turned_low_ref[part, place, at] = low.T
+            square = jnp.sum((value * value).reshape(rows // 8, 8, width), axis=0)
+            energy_ref[...] += sum(square[:, lane : lane + LANES] for lane in range(0, width, LANES))
 
 
 def split(value):
     _, rows, shots = value.shape
-    block = min(rows, LANES)
+    block, chunks = min(rows, LANES), 2
     plain, turned = ((2, rows, shots), bf16), ((2, shots, rows), bf16)
     high, low, turned_high, turned_low, energy = call(
         split_kernel,
         [plain, plain, turned, turned, ((8, LANES), f32)],
-        (value,),
-        grid=(2, rows // block),
-        in_specs=[pl.BlockSpec((1, block, shots), lambda part, step: (part, step, 0))],
+        (value, value),
+        grid=(rows // block, chunks),
+        in_specs=[
+            pl.BlockSpec((1, block, shots // chunks), lambda step, chunk: (0, step, chunk)),
+            pl.BlockSpec((1, block, shots // chunks), lambda step, chunk: (1, step, chunk)),
+        ],
     )
     return (high, low), (turned_high, turned_low), energy
 
@@ -254,6 +259,18 @@
             out_ref[part] = x_ref[...].T
 
 
+class Sum:
+    def __init__(self, swap, order, pair):
+        self.swap, self.order, self.at = swap, order, 0
+        self.keep, give = pair
+        self.other = swap(give, order[0])
+
+    def step(self):
+        self.at += 1
+        self.keep = self.keep + self.other
+        self.other = self.swap(self.keep, self.order[self.at % len(self.order)])
+
+
 def body(down_spectra, up_sources, *, count, receivers):
     chip_bits = list(range(1, count.bit_length() - 1))
     orders = (chip_bits, chip_bits[::-1])
@@ -266,15 +283,6 @@
 
     def swap(value, bit):
         return lax.ppermute(value, "rcv", [(at, at ^ (1 << bit)) for at in range(count)])
-
-    def exchange(*ranges):
-        pieces = []
-        for order, (keep, give) in zip(orders, ranges):
-            keep = keep + swap(give, order[0])
-            for bit in order[1:]:
-                keep = keep + swap(keep, bit)
-            pieces.append((keep, swap(keep, order[0])))
-        return pieces
 
     def jump(value, mask):
         return lax.ppermute(value, "rcv", [(at, at ^ (mask << 1)) for at in range(count)])
@@ -303,44 +311,99 @@
     spread = [((packed // own, own, shots), f32)] if own % 8 else []
     plain = (*plain_a, *plain_b)
 
-    def back(value):
-        return call(functools.partial(back_kernel, ends[1]), sent_1, (value, *plain), short, work)
-
-    def lead(pieces):
-        return call(functools.partial(front_kernel, ends[0]), [ranged, small, lines], (*pieces, *turned), narrow, work)
-
-    state, sums = [], []
-    for source in sources:
-        rhs, *outs = call(
-            functools.partial(rhs_kernel, ends[0], masks),
+    done = {}
+
+    def after(name, *values):
+        for earlier in ORDER.get(name, ()):
+            values = lax.optimization_barrier((done[earlier], *values))[1:]
+        return values
+
+    def launch(name, kernel, outs, args, scratch, flops):
+        first, *rest = args
+        results = call(kernel, outs, (*after(name, first), *rest), scratch, int(flops * COST.get(name, 1)))
+        done[name] = results[0]
+        return results
+
+    def step(name, total):
+        (total.keep,) = after(name, total.keep)
+        total.step()
+        done[name] = total.keep
+
+    def way(name, which):
+        return which ^ (name[0] == "b")
+
+    def start(name, which, pair):
+        return Sum(swap, orders[way(name, which)], pair)
+
+    def back(name, value):
+        kernel = functools.partial(back_kernel, ends[way(name, 1)])
+        return start(name, 1, launch(name, kernel, sent_1, (value, *plain), short, work))
+
+    def lead(name, total):
+        kernel, pieces = functools.partial(front_kernel, ends[way(name, 0)]), (total.keep, total.other)
+        return launch(name, kernel, [ranged, small, lines], (*pieces, *turned), narrow, work)
+
+    def open_group(name, source):
+        rhs, *pair = launch(
+            name,
+            functools.partial(rhs_kernel, ends[way(name, 0)], masks),
             [lines] + sent_0,
             (*source, *down, energy_a, energy_b),
             [every] + wide + short + spread,
             3 * work,
         )
-        state.append(rhs)
-        sums.append(exchange(outs, back(rhs)))
-    for group, (rhs, (pieces_0, pieces_1)) in enumerate(zip(state, sums)):
-        before, norms, part = lead(pieces_0)
-        x, scalars, image, residual, *outs = call(
-            functools.partial(first_kernel, ends, receivers),
+        return rhs, start(name, 0, pair)
+
+    def middle(name, total, led, rhs):
+        before, norms, part = led
+        x, scalars, image, residual, *pair = launch(
+            name,
+            functools.partial(first_kernel, (ends[way(name, 0)], ends[way(name, 1)]), receivers),
             [ranged, small, lines, lines] + sent_0,
-            (*pieces_1, before, norms, part, rhs, *down),
+            (total.keep, total.other, before, norms, part, rhs, *down),
             narrow + short,
             2 * work,
         )
-        state[group] = (rhs, before, x, scalars, image, residual)
-        sums[group] = exchange(outs, back(residual))
-    results = []
-    for kept, (pieces_0, pieces_1) in zip(state, sums):
-        keep, give = call(
-            functools.partial(last_kernel, ends[1]),
+        return (rhs, before, x, scalars, image, residual), start(name, 0, pair)
+
+    def close(name, total, led, kept):
+        keep, give = launch(
+            name,
+            functools.partial(last_kernel, ends[way(name, 1)]),
             [((2, packed, rows), f32)] * 2,
-            (*pieces_1, *lead(pieces_0), *kept, *turned),
+            (total.keep, total.other, *led, *kept, *turned),
             [ranged] + narrow,
             work,
         )
-        results.append((keep, swap(give, 0)))
+        return keep, swap(give, 0)
+
+    def rounds(tag, a0, a1, b0, pending):
+        step("a0" + tag, a0)
+        step("a1" + tag, a1)
+        b1 = back("bC" + tag, pending)
+        for turn in range(2, len(chip_bits) + 1):
+            end = tag + str(turn)
+            step("a0" + end, a0)
+            step("b0" + end, b0)
+            step("b1" + end, b1)
+            step("a1" + end, a1)
+        led = lead("aL" + tag, a0)
+        step("b0" + tag, b0)
+        step("b1" + tag, b1)
+        return b1, led
+
+    rhs_a, a0 = open_group("aR", sources[0])
+    a1 = back("aC", rhs_a)
+    rhs_b, b0 = open_group("bR", sources[1])
+    b1, led = rounds("", a0, a1, b0, rhs_b)
+    kept_a, a0 = middle("aM", a1, led, rhs_a)
+    a1 = back("aC.", kept_a[-1])
+    led = lead("bL", b0)
+    kept_b, b0 = middle("bM", b1, led, rhs_b)
+    b1, led = rounds(".", a0, a1, b0, kept_b[-1])
+    results = [close("aE", a1, led, kept_a)]
+    led = lead("bL.", b0)
+    results.append(close("bE", b1, led, kept_b))
 
     pieces = [piece for pair in results for piece in pair]
     columns = GROUPS * packed

time: 83.4 us -> 79.7 us (0.956)
  waiting for transfers between devices: 20.6 us -> 16.2 us
    ppermute x27, waiting for transfers between devices: 20.6 us -> 16.2 us  [swap(): lax.ppermute(value, 'rcv', [(at, at ^ 1 << bit) for at in range(count)])]
  transfers between devices with their start and end apart: 33 -> 33, of which waited for: 10 -> 13; matrix products, arithmetic and copies ran while one was open for 2% -> 2% of each run, Pallas kernels for 29% -> 31%
where the time goes in v6:
time: 79.7 us; the launch traced here: 79.5 us
  starting transfers between devices  35.7 us (45%)
  Pallas kernels  25.3 us (32%)
  waiting for transfers between devices  16.2 us (20%)
  local copies, waits for them, and re-layouts  1.02 us (1%)
  between operations  0.9 us (1%)
    ppermute x27, starting transfers between devices, swap(): lax.ppermute(value, 'rcv', [(at, at ^ 1 << bit) for at in range(count)])  27.8 us
    pallas_call x17, Pallas kernels, call(): pl.pallas_call(kernel, out_shape=[jax.ShapeDtypeStruct(shape, dtype) for...  25.3 us
    ppermute x27, waiting for transfers between devices, swap(): lax.ppermute(value, 'rcv', [(at, at ^ 1 << bit) for at in range(count)])  16.2 us
    ppermute x6, starting transfers between devices, jump(): lax.ppermute(value, 'rcv', [(at, at ^ mask << 1) for at in range(count)])  7.92 us
  transfers between devices with their start and end apart: 33, of which 13 were waited for; matrix products, arithmetic and copies ran while one was open for 2% of the time, Pallas kernels for 31%

profile of v6, /device:TPU:0, one launch (start us, length us, event | category | flops | bytes accessed | tf_op | source)
XLA Modules:
  0.0 79.5 jit_solution(3978119653591475047)
XLA Ops:
  0.6 0.5 collective-permute-start.3
  1.1 1.0 %fusion = (f32[2,8,2560]{2,1,0:T(8,128)S(1)}, f32[2,8,2560]{2,1,0:T(8,128)S(1)}) fusion(f32[2,16,2560]{2,1,0:T(8,128)} %param.3), kind=kLoop, calls=%fused_computation | loop fusion | bytes 655360 | tf_op jit(solution)/shard_map/slice | solution.py:294
  2.2 3.5 %collective-permute-start.2 = (f32[2,8,2560]{2,1,0:T(8,128)S(1)}, f32[2,8,2560]{2,1,0:T(8,128)S(1)}, u32[]{:S(2)}, u32[]{:S(2)}) collective-permute-start(f32[2,8,2560]{2,1,0:T(8,128)S(1)} %get-tuple-element.109.refs_0_), channel_id=1, source_target_pairs={{0,6},{1,7},{2,4},{3,5},{4,2},{5,3},{6,0},{7,1},{8,14},{9,15},{10,... | collective-permute-start | bytes 491528 | tf_op jit(solution)/shard_map/ppermute | solution.py:288
  5.7 0.5 collective-permute-start.1
  6.2 0.1 collective-permute-start
  6.3 2.8 %collective-permute-start.19 = (f32[2,8,2560]{2,1,0:T(8,128)S(1)}, f32[2,8,2560]{2,1,0:T(8,128)S(1)}, u32[]{:S(2)}, u32[]{:S(2)}) collective-permute-start(f32[2,8,2560]{2,1,0:T(8,128)S(1)} %get-tuple-element.108.refs_0_), channel_id=1, source_target_pairs={{0,6},{1,7},{2,4},{3,5},{4,2},{5,3},{6,0},{7,1},{8,14},{9,15},{10,... | collective-permute-start | bytes 491528 | tf_op jit(solution)/shard_map/ppermute | solution.py:288
  9.2 4.0 %shard_map.41 = (bf16[2,256,2560]{2,1,0:T(8,128)(2,1)S(1)}, bf16[2,256,2560]{2,1,0:T(8,128)(2,1)S(1)}, bf16[2,2560,256]{2,1,0:T(8,128)(2,1)S(1)}, bf16[2,2560,256]{2,1,0:T(8,128)(2,1)S(1)}, f32[8,128]{1,0:T(8,128)S(1)}) custom-call(f32[2,256,2560]{2,1,0:T(8,128)} %imag_ref.1, f32[2,256,2560]{2,1,0:T(8,128)} %imag_ref.1), custom_call_target="tpu_custom_call" | custom-call | bytes 10485760 | tf_op jit(solution)/shard_map/pallas_call | solution.py:30
  13.2 0.6 collective-permute-start.18
  13.7 2.1 %shard_map.42 = (bf16[2,256,2560]{2,1,0:T(8,128)(2,1)S(1)}, bf16[2,256,2560]{2,1,0:T(8,128)(2,1)S(1)}, bf16[2,2560,256]{2,1,0:T(8,128)(2,1)S(1)}, bf16[2,2560,256]{2,1,0:T(8,128)(2,1)S(1)}, f32[8,128]{1,0:T(8,128)S(1)}) custom-call(f32[2,256,2560]{2,1,0:T(8,128)S(1)} %collective-permute-done.3.real_ref.imag_ref, ...), custom_call_target="tpu_custom_call" | custom-call | bytes 10485760 | tf_op jit(solution)/shard_map/pallas_call | solution.py:30
  15.9 0.3 collective-permute-start.17
  16.2 2.6 %shard_map.43 = (f32[64,512]{1,0:T(8,128)S(1)}, f32[32,1408]{1,0:T(8,128)S(1)}, f32[32,1408]{1,0:T(8,128)S(1)}) custom-call(f32[2,8,2560]{2,1,0:T(8,128)S(1)} %get-tuple-element.109.refs_0_, f32[2,8,2560]{2,1,0:T(8,128)S(1)} %collective-permute-done.refs_1_, f32[2,8,2560]{2,1,0:T(8,128)S(1)} %collective-permute-done.1.refs_2_, ...), custom_call_target="tpu_custom_call" | custom-call | flops 90596966400 | bytes 21635072 | tf_op jit(solution)/shard_map/pallas_call | solution.py:30
  18.8 1.8 %collective-permute-start.7 = (f32[32,1408]{1,0:T(8,128)S(1)}, f32[32,1408]{1,0:T(8,128)S(1)}, u32[]{:S(2)}, u32[]{:S(2)}) collective-permute-start(f32[32,1408]{1,0:T(8,128)S(1)} %get-tuple-element.69), channel_id=1, source_target_pairs={{0,2},{1,3},{2,0},{3,1},{4,6},{5,7},{6,4},{7,5},{8,10},{9,11},{10,... | collective-permute-start | bytes 540680 | tf_op jit(solution)/shard_map/ppermute | solution.py:285
  20.6 0.9 %shard_map.44 = (f32[32,1280]{1,0:T(8,128)S(1)}, f32[32,1280]{1,0:T(8,128)S(1)}) custom-call(f32[64,512]{1,0:T(8,128)S(1)} %get-tuple-element.65.refs_0_.refs_5_, bf16[2,256,2560]{2,1,0:T(8,128)(2,1)S(1)} %get-tuple-element.55.refs_4_.refs_1_.refs_6_, bf16[2,256,2560]{2,1,0:T(8,128)(2,1)S(1)} %get-tuple-element.56.refs_5_.refs_2_.refs_7_, ...), custom_call_target="tpu_custom_call" | custom-call | flops 301989888 | bytes 10616832 | tf_op jit(solution)/shard_map/pallas_call | solution.py:30
  21.6 1.6 %collective-permute-start.4 = (f32[32,1280]{1,0:T(8,128)S(1)}, f32[32,1280]{1,0:T(8,128)S(1)}, u32[]{:S(2)}, u32[]{:S(2)}) collective-permute-start(f32[32,1280]{1,0:T(8,128)S(1)} %get-tuple-element.67), channel_id=1, source_target_pairs={{0,4},{1,5},{2,6},{3,7},{4,0},{5,1},{6,2},{7,3},{8,12},{9,13},{10,... | collective-permute-start | bytes 491528 | tf_op jit(solution)/shard_map/ppermute | solution.py:285
  23.2 2.6 %shard_map.50 = (f32[64,512]{1,0:T(8,128)S(1)}, f32[32,1408]{1,0:T(8,128)S(1)}, f32[32,1408]{1,0:T(8,128)S(1)}) custom-call(f32[2,8,2560]{2,1,0:T(8,128)S(1)} %get-tuple-element.108.refs_0_, f32[2,8,2560]{2,1,0:T(8,128)S(1)} %collective-permute-done.17.refs_1_, f32[2,8,2560]{2,1,0:T(8,128)S(1)} %collective-permute-done.18.refs_2_, ...), custom_call_target="tpu_custom_call" | custom-call | flops 3019898880 | bytes 21635072 | tf_op jit(solution)/shard_map/pallas_call | solution.py:30
  25.8 0.6 collective-permute-start.23
  26.4 1.6 %collective-permute-start.8 = (f32[32,1408]{1,0:T(8,128)S(1)}, f32[32,1408]{1,0:T(8,128)S(1)}, u32[]{:S(2)}, u32[]{:S(2)}) collective-permute-start(f32[32,1408]{1,0:T(8,128)S(1)} %add.50), channel_id=1, source_target_pairs={{0,4},{1,5},{2,6},{3,7},{4,0},{5,1},{6,2},{7,3},{8,12},{9,13},{10,... | collective-permute-start | bytes 540680 | tf_op jit(solution)/shard_map/ppermute | solution.py:285
  27.9 0.9 %shard_map.51 = (f32[32,1280]{1,0:T(8,128)S(1)}, f32[32,1280]{1,0:T(8,128)S(1)}) custom-call(f32[64,512]{1,0:T(8,128)S(1)} %get-tuple-element.86.refs_0_.refs_5_, bf16[2,256,2560]{2,1,0:T(8,128)(2,1)S(1)} %get-tuple-element.55.refs_4_.refs_1_.refs_6_, bf16[2,256,2560]{2,1,0:T(8,128)(2,1)S(1)} %get-tuple-element.56.refs_5_.refs_2_.refs_7_, ...), custom_call_target="tpu_custom_call" | custom-call | bytes 10616832 | tf_op jit(solution)/shard_map/pallas_call | solution.py:30
  28.9 0.6 collective-permute-start.20
  29.6 1.5 %collective-permute-start.5 = (f32[32,1280]{1,0:T(8,128)S(1)}, f32[32,1280]{1,0:T(8,128)S(1)}, u32[]{:S(2)}, u32[]{:S(2)}) collective-permute-start(f32[32,1280]{1,0:T(8,128)S(1)} %add.48), channel_id=1, source_target_pairs={{0,2},{1,3},{2,0},{3,1},{4,6},{5,7},{6,4},{7,5},{8,10},{9,11},{10,... | collective-permute-start | bytes 491528 | tf_op jit(solution)/shard_map/ppermute | solution.py:285
  31.1 1.7 %collective-permute-done.23 = f32[32,1408]{1,0:T(8,128)S(1)} collective-permute-done((f32[32,1408]{1,0:T(8,128)S(1)}, f32[32,1408]{1,0:T(8,128)S(1)}, u32[]{:S(2)}, u32[]{:S(2)}) %collective-permute-start.23) | collective-permute-done | bytes 180256 | tf_op jit(solution)/shard_map/ppermute | solution.py:285
  32.8 1.0 %collective-permute-start.24 = (f32[32,1408]{1,0:T(8,128)S(1)}, f32[32,1408]{1,0:T(8,128)S(1)}, u32[]{:S(2)}, u32[]{:S(2)}) collective-permute-start(f32[32,1408]{1,0:T(8,128)S(1)} %add.58), channel_id=1, source_target_pairs={{0,2},{1,3},{2,0},{3,1},{4,6},{5,7},{6,4},{7,5},{8,10},{9,11},{10,... | collective-permute-start | bytes 540680 | tf_op jit(solution)/shard_map/ppermute | solution.py:285
  33.8 0.9 %collective-permute-done.8 = f32[32,1408]{1,0:T(8,128)S(1)} collective-permute-done((f32[32,1408]{1,0:T(8,128)S(1)}, f32[32,1408]{1,0:T(8,128)S(1)}, u32[]{:S(2)}, u32[]{:S(2)}) %collective-permute-start.8) | collective-permute-done | bytes 180256 | tf_op jit(solution)/shard_map/ppermute | solution.py:285
  34.7 1.0 %collective-permute-start.9 = (f32[32,1408]{1,0:T(8,128)S(1)}, f32[32,1408]{1,0:T(8,128)S(1)}, u32[]{:S(2)}, u32[]{:S(2)}) collective-permute-start(f32[32,1408]{1,0:T(8,128)S(1)} %add.51.refs_0_), channel_id=1, source_target_pairs={{0,2},{1,3},{2,0},{3,1},{4,6},{5,7},{6,4},{7,5},{8,10},{9,11},{10,... | collective-permute-start | bytes 540680 | tf_op jit(solution)/shard_map/ppermute | solution.py:285
  35.7 0.4 collective-permute-done.20
  36.1 0.8 %collective-permute-start.21 = (f32[32,1280]{1,0:T(8,128)S(1)}, f32[32,1280]{1,0:T(8,128)S(1)}, u32[]{:S(2)}, u32[]{:S(2)}) collective-permute-start(f32[32,1280]{1,0:T(8,128)S(1)} %add.56), channel_id=1, source_target_pairs={{0,4},{1,5},{2,6},{3,7},{4,0},{5,1},{6,2},{7,3},{8,12},{9,13},{10,... | collective-permute-start | bytes 491528 | tf_op jit(solution)/shard_map/ppermute | solution.py:285
  36.9 2.7 %collective-permute-done.5 = f32[32,1280]{1,0:T(8,128)S(1)} collective-permute-done((f32[32,1280]{1,0:T(8,128)S(1)}, f32[32,1280]{1,0:T(8,128)S(1)}, u32[]{:S(2)}, u32[]{:S(2)}) %collective-permute-start.5) | collective-permute-done | bytes 163872 | tf_op jit(solution)/shard_map/ppermute | solution.py:285
  39.6 0.6 collective-permute-start.6
  40.2 1.4 %collective-permute-done.21 = f32[32,1280]{1,0:T(8,128)S(1)} collective-permute-done((f32[32,1280]{1,0:T(8,128)S(1)}, f32[32,1280]{1,0:T(8,128)S(1)}, u32[]{:S(2)}, u32[]{:S(2)}) %collective-permute-start.21) | collective-permute-done | bytes 163872 | tf_op jit(solution)/shard_map/ppermute | solution.py:285
  41.7 1.2 %collective-permute-start.22 = (f32[32,1280]{1,0:T(8,128)S(1)}, f32[32,1280]{1,0:T(8,128)S(1)}, u32[]{:S(2)}, u32[]{:S(2)}) collective-permute-start(f32[32,1280]{1,0:T(8,128)S(1)} %add.57.refs_0_), channel_id=1, source_target_pairs={{0,2},{1,3},{2,0},{3,1},{4,6},{5,7},{6,4},{7,5},{8,10},{9,11},{10,... | collective-permute-start | bytes 491528 | tf_op jit(solution)/shard_map/ppermute | solution.py:285
  42.9 0.2 collective-permute-done.24
  43.1 1.7 %collective-permute-start.25 = (f32[32,1408]{1,0:T(8,128)S(1)}, f32[32,1408]{1,0:T(8,128)S(1)}, u32[]{:S(2)}, u32[]{:S(2)}) collective-permute-start(f32[32,1408]{1,0:T(8,128)S(1)} %add.59.refs_0_), channel_id=1, source_target_pairs={{0,4},{1,5},{2,6},{3,7},{4,0},{5,1},{6,2},{7,3},{8,12},{9,13},{10,... | collective-permute-start | bytes 540680 | tf_op jit(solution)/shard_map/ppermute | solution.py:285
  44.8 1.0 %collective-permute-done.9.refs_1_ = f32[32,1408]{1,0:T(8,128)S(1)} collective-permute-done((f32[32,1408]{1,0:T(8,128)S(1)}, f32[32,1408]{1,0:T(8,128)S(1)}, u32[]{:S(2)}, u32[]{:S(2)}) %collective-permute-start.9) | collective-permute-done | bytes 180256 | tf_op jit(solution)/shard_map/ppermute | solution.py:285
  45.8 0.9 %shard_map.45 = (f32[64,1280]{1,0:T(8,128)S(1)}, f32[64,128]{1,0:T(8,128)S(1)}, f32[64,512]{1,0:T(8,128)S(1)}) custom-call(f32[32,1408]{1,0:T(8,128)S(1)} %add.51.refs_0_, f32[32,1408]{1,0:T(8,128)S(1)} %collective-permute-done.9.refs_1_, bf16[2,2560,256]{2,1,0:T(8,128)(2,1)S(1)} %get-tuple-element.59.refs_8_.refs_2_.refs_10_.refs_11_, ...), custom_call_target="tpu_custom_call" | custom-call | bytes 10846208 | tf_op jit(solution)/shard_map/pallas_call | solution.py:30
  46.7 1.8 %shard_map.46 = (f32[64,1280]{1,0:T(8,128)S(1)}, f32[64,128]{1,0:T(8,128)S(1)}, f32[64,512]{1,0:T(8,128)S(1)}, f32[64,512]{1,0:T(8,128)S(1)}, f32[32,1408]{1,0:T(8,128)S(1)}, /*index=5*/f32[32,1408]{1,0:T(8,128)S(1)}) custom-call(f32[32,1280]{1,0:T(8,128)S(1)} %add.49.refs_0_, f32[32,1280]{1,0:T(8,128)S(1)} %collective-permute-done.6.refs_1_, ...), custom_call_target="tpu_custom_call" | custom-call | flops 2013265920 | bytes 21921792 | tf_op jit(solution)/shard_map/pallas_call | solution.py:30
  48.5 1.3 %collective-permute-start.13 = (f32[32,1408]{1,0:T(8,128)S(1)}, f32[32,1408]{1,0:T(8,128)S(1)}, u32[]{:S(2)}, u32[]{:S(2)}) collective-permute-start(f32[32,1408]{1,0:T(8,128)S(1)} %get-tuple-element.77), channel_id=1, source_target_pairs={{0,2},{1,3},{2,0},{3,1},{4,6},{5,7},{6,4},{7,5},{8,10},{9,11},{10,... | collective-permute-start | bytes 540680 | tf_op jit(solution)/shard_map/ppermute | solution.py:285
  49.9 0.9 %shard_map.47 = (f32[32,1280]{1,0:T(8,128)S(1)}, f32[32,1280]{1,0:T(8,128)S(1)}) custom-call(f32[64,512]{1,0:T(8,128)S(1)} %get-tuple-element.73.refs_0_.refs_10_, bf16[2,256,2560]{2,1,0:T(8,128)(2,1)S(1)} %get-tuple-element.55.refs_4_.refs_1_.refs_6_, bf16[2,256,2560]{2,1,0:T(8,128)(2,1)S(1)} %get-tuple-element.56.refs_5_.refs_2_.refs_7_, ...), custom_call_target="tpu_custom_call" | custom-call | flops 3019898880 | bytes 10616832 | tf_op jit(solution)/shard_map/pallas_call | solution.py:30
  50.8 0.8 collective-permute-start.10
  51.6 0.9 %shard_map.52 = (f32[64,1280]{1,0:T(8,128)S(1)}, f32[64,128]{1,0:T(8,128)S(1)}, f32[64,512]{1,0:T(8,128)S(1)}) custom-call(f32[32,1408]{1,0:T(8,128)S(1)} %add.59.refs_0_, f32[32,1408]{1,0:T(8,128)S(1)} %collective-permute-done.25.refs_1_, bf16[2,2560,256]{2,1,0:T(8,128)(2,1)S(1)} %get-tuple-element.59.refs_8_.refs_2_.refs_10_.refs_11_, ...), custom_call_target="tpu_custom_call" | custom-call | flops 1006632960 | bytes 10846208 | tf_op jit(solution)/shard_map/pallas_call | solution.py:30
  52.5 1.8 %shard_map.53 = (f32[64,1280]{1,0:T(8,128)S(1)}, f32[64,128]{1,0:T(8,128)S(1)}, f32[64,512]{1,0:T(8,128)S(1)}, f32[64,512]{1,0:T(8,128)S(1)}, f32[32,1408]{1,0:T(8,128)S(1)}, /*index=5*/f32[32,1408]{1,0:T(8,128)S(1)}) custom-call(f32[32,1280]{1,0:T(8,128)S(1)} %add.57.refs_0_, f32[32,1280]{1,0:T(8,128)S(1)} %collective-permute-done.22.refs_1_, ...), custom_call_target="tpu_custom_call" | custom-call | flops 20132659200 | bytes 21921792 | tf_op jit(solution)/shard_map/pallas_call | solution.py:30
  54.4 1.5 %collective-permute-start.29 = (f32[32,1408]{1,0:T(8,128)S(1)}, f32[32,1408]{1,0:T(8,128)S(1)}, u32[]{:S(2)}, u32[]{:S(2)}) collective-permute-start(f32[32,1408]{1,0:T(8,128)S(1)} %get-tuple-element.99), channel_id=1, source_target_pairs={{0,4},{1,5},{2,6},{3,7},{4,0},{5,1},{6,2},{7,3},{8,12},{9,13},{10,... | collective-permute-start | bytes 540680 | tf_op jit(solution)/shard_map/ppermute | solution.py:285
  55.9 0.9 %shard_map.54 = (f32[32,1280]{1,0:T(8,128)S(1)}, f32[32,1280]{1,0:T(8,128)S(1)}) custom-call(f32[64,512]{1,0:T(8,128)S(1)} %get-tuple-element.94.refs_0_.refs_10_, bf16[2,256,2560]{2,1,0:T(8,128)(2,1)S(1)} %get-tuple-element.55.refs_4_.refs_1_.refs_6_, bf16[2,256,2560]{2,1,0:T(8,128)(2,1)S(1)} %get-tuple-element.56.refs_5_.refs_2_.refs_7_, ...), custom_call_target="tpu_custom_call" | custom-call | flops 301989888 | bytes 10616832 | tf_op jit(solution)/shard_map/pallas_call | solution.py:30
  56.9 0.8 %collective-permute-start.26 = (f32[32,1280]{1,0:T(8,128)S(1)}, f32[32,1280]{1,0:T(8,128)S(1)}, u32[]{:S(2)}, u32[]{:S(2)}) collective-permute-start(f32[32,1280]{1,0:T(8,128)S(1)} %get-tuple-element.96), channel_id=1, source_target_pairs={{0,2},{1,3},{2,0},{3,1},{4,6},{5,7},{6,4},{7,5},{8,10},{9,11},{10,... | collective-permute-start | bytes 491528 | tf_op jit(solution)/shard_map/ppermute | solution.py:285
  57.7 1.3 %collective-permute-start.14 = (f32[32,1408]{1,0:T(8,128)S(1)}, f32[32,1408]{1,0:T(8,128)S(1)}, u32[]{:S(2)}, u32[]{:S(2)}) collective-permute-start(f32[32,1408]{1,0:T(8,128)S(1)} %add.54), channel_id=1, source_target_pairs={{0,4},{1,5},{2,6},{3,7},{4,0},{5,1},{6,2},{7,3},{8,12},{9,13},{10,... | collective-permute-start | bytes 540680 | tf_op jit(solution)/shard_map/ppermute | solution.py:285
  59.1 0.8 collective-permute-start.11
  59.9 1.8 %collective-permute-done.29 = f32[32,1408]{1,0:T(8,128)S(1)} collective-permute-done((f32[32,1408]{1,0:T(8,128)S(1)}, f32[32,1408]{1,0:T(8,128)S(1)}, u32[]{:S(2)}, u32[]{:S(2)}) %collective-permute-start.29) | collective-permute-done | bytes 180256 | tf_op jit(solution)/shard_map/ppermute | solution.py:285
  61.7 1.5 %collective-permute-start.30 = (f32[32,1408]{1,0:T(8,128)S(1)}, f32[32,1408]{1,0:T(8,128)S(1)}, u32[]{:S(2)}, u32[]{:S(2)}) collective-permute-start(f32[32,1408]{1,0:T(8,128)S(1)} %add.62), channel_id=1, source_target_pairs={{0,2},{1,3},{2,0},{3,1},{4,6},{5,7},{6,4},{7,5},{8,10},{9,11},{10,... | collective-permute-start | bytes 540680 | tf_op jit(solution)/shard_map/ppermute | solution.py:285
  63.1 0.1 collective-permute-done.26
  63.3 1.0 %collective-permute-start.27 = (f32[32,1280]{1,0:T(8,128)S(1)}, f32[32,1280]{1,0:T(8,128)S(1)}, u32[]{:S(2)}, u32[]{:S(2)}) collective-permute-start(f32[32,1280]{1,0:T(8,128)S(1)} %add.60), channel_id=1, source_target_pairs={{0,4},{1,5},{2,6},{3,7},{4,0},{5,1},{6,2},{7,3},{8,12},{9,13},{10,... | collective-permute-start | bytes 491528 | tf_op jit(solution)/shard_map/ppermute | solution.py:285
  64.3 1.2 %collective-permute-done.14 = f32[32,1408]{1,0:T(8,128)S(1)} collective-permute-done((f32[32,1408]{1,0:T(8,128)S(1)}, f32[32,1408]{1,0:T(8,128)S(1)}, u32[]{:S(2)}, u32[]{:S(2)}) %collective-permute-start.14) | collective-permute-done | bytes 180256 | tf_op jit(solution)/shard_map/ppermute | solution.py:285
  65.5 1.5 %collective-permute-start.15 = (f32[32,1408]{1,0:T(8,128)S(1)}, f32[32,1408]{1,0:T(8,128)S(1)}, u32[]{:S(2)}, u32[]{:S(2)}) collective-permute-start(f32[32,1408]{1,0:T(8,128)S(1)} %add.55.refs_0_), channel_id=1, source_target_pairs={{0,2},{1,3},{2,0},{3,1},{4,6},{5,7},{6,4},{7,5},{8,10},{9,11},{10,... | collective-permute-start | bytes 540680 | tf_op jit(solution)/shard_map/ppermute | solution.py:285
  67.0 0.4 collective-permute-start.12
  67.4 2.2 %collective-permute-done.30 = f32[32,1408]{1,0:T(8,128)S(1)} collective-permute-done((f32[32,1408]{1,0:T(8,128)S(1)}, f32[32,1408]{1,0:T(8,128)S(1)}, u32[]{:S(2)}, u32[]{:S(2)}) %collective-permute-start.30) | collective-permute-done | bytes 180256 | tf_op jit(solution)/shard_map/ppermute | solution.py:285
  69.6 0.8 collective-permute-start.31
  70.5 1.4 %collective-permute-start.28 = (f32[32,1280]{1,0:T(8,128)S(1)}, f32[32,1280]{1,0:T(8,128)S(1)}, u32[]{:S(2)}, u32[]{:S(2)}) collective-permute-start(f32[32,1280]{1,0:T(8,128)S(1)} %add.61.refs_0_), channel_id=1, source_target_pairs={{0,2},{1,3},{2,0},{3,1},{4,6},{5,7},{6,4},{7,5},{8,10},{9,11},{10,... | collective-permute-start | bytes 491528 | tf_op jit(solution)/shard_map/ppermute | solution.py:285
  71.8 0.9 %shard_map.48 = (f32[64,1280]{1,0:T(8,128)S(1)}, f32[64,128]{1,0:T(8,128)S(1)}, f32[64,512]{1,0:T(8,128)S(1)}) custom-call(f32[32,1408]{1,0:T(8,128)S(1)} %add.55.refs_0_, f32[32,1408]{1,0:T(8,128)S(1)} %collective-permute-done.15.refs_1_, bf16[2,2560,256]{2,1,0:T(8,128)(2,1)S(1)} %get-tuple-element.59.refs_8_.refs_2_.refs_10_.refs_11_, ...), custom_call_target="tpu_custom_call" | custom-call | bytes 10846208 | tf_op jit(solution)/shard_map/pallas_call | solution.py:30
  72.8 1.0 %shard_map.49 = (f32[2,64,256]{2,1,0:T(8,128)S(1)}, f32[2,64,256]{2,1,0:T(8,128)S(1)}) custom-call(f32[32,1280]{1,0:T(8,128)S(1)} %add.53.refs_0_, f32[32,1280]{1,0:T(8,128)S(1)} %collective-permute-done.12.refs_1_, f32[64,1280]{1,0:T(8,128)S(1)} %get-tuple-element.78.refs_2_, f32[64,128]{1,0:T(8,128)S(1)} %get-tuple-element.79.refs_3_, ...), custom_call_target="tpu_custom_call" | custom-call | flops 1006632960 | bytes 12386304 | tf_op jit(solution)/shard_map/pallas_call | solution.py:30
  73.8 0.1 collective-permute-start.16
  73.9 1.3 %collective-permute-done.31.refs_1_ = f32[32,1408]{1,0:T(8,128)S(1)} collective-permute-done((f32[32,1408]{1,0:T(8,128)S(1)}, f32[32,1408]{1,0:T(8,128)S(1)}, u32[]{:S(2)}, u32[]{:S(2)}) %collective-permute-start.31) | collective-permute-done | bytes 180256 | tf_op jit(solution)/shard_map/ppermute | solution.py:285
  75.2 0.9 %shard_map.55 = (f32[64,1280]{1,0:T(8,128)S(1)}, f32[64,128]{1,0:T(8,128)S(1)}, f32[64,512]{1,0:T(8,128)S(1)}) custom-call(f32[32,1408]{1,0:T(8,128)S(1)} %add.63.refs_0_, f32[32,1408]{1,0:T(8,128)S(1)} %collective-permute-done.31.refs_1_, bf16[2,2560,256]{2,1,0:T(8,128)(2,1)S(1)} %get-tuple-element.59.refs_8_.refs_2_.refs_10_.refs_11_, ...), custom_call_target="tpu_custom_call" | custom-call | bytes 10846208 | tf_op jit(solution)/shard_map/pallas_call | solution.py:30
  76.2 1.0 %shard_map.56 = (f32[2,64,256]{2,1,0:T(8,128)S(1)}, f32[2,64,256]{2,1,0:T(8,128)S(1)}) custom-call(f32[32,1280]{1,0:T(8,128)S(1)} %add.61.refs_0_, f32[32,1280]{1,0:T(8,128)S(1)} %collective-permute-done.28.refs_1_, f32[64,1280]{1,0:T(8,128)S(1)} %get-tuple-element.100.refs_2_, f32[64,128]{1,0:T(8,128)S(1)} %get-tuple-element.101.refs_3_, ...), custom_call_target="tpu_custom_call" | custom-call | flops 1006632960 | bytes 12386304 | tf_op jit(solution)/shard_map/pallas_call | solution.py:30
  77.1 0.1 collective-permute-start.32
  77.2 1.3 %collective-permute-done.32.refs_3_ = f32[2,64,256]{2,1,0:T(8,128)S(1)} collective-permute-done((f32[2,64,256]{2,1,0:T(8,128)S(1)}, f32[2,64,256]{2,1,0:T(8,128)S(1)}, u32[]{:S(2)}, u32[]{:S(2)}) %collective-permute-start.32) | collective-permute-done | bytes 131104 | tf_op jit(solution)/shard_map/ppermute | solution.py:285
  78.6 0.9 %shard_map.57 = (f32[2,256,128]{2,1,0:T(8,128)}, f32[2,256,128]{2,1,0:T(8,128)}) custom-call(f32[2,64,256]{2,1,0:T(8,128)S(1)} %get-tuple-element.84.refs_0_, f32[2,64,256]{2,1,0:T(8,128)S(1)} %collective-permute-done.16.refs_1_, f32[2,64,256]{2,1,0:T(8,128)S(1)} %get-tuple-element.106.refs_2_, f32[2,64,256]{2,1,0:T(8,128)S(1)} %collective-permute-done.32.refs_3_), custom_call_target="tpu_custom_call" | custom-call | bytes 524288 | tf_op jit(solution)/shard_map/pallas_call | solution.py:30
  (36 shorter events, 0.4 us)
Async XLA Ops:
  0.6 12.5 %collective-permute-start.3 = (f32[2,256,2560]{2,1,0:T(8,128)}, f32[2,256,2560]{2,1,0:T(8,128)S(1)}, u32[]{:S(2)}, u32[]{:S(2)}) collective-permute-start(f32[2,256,2560]{2,1,0:T(8,128)} %imag_ref.1), channel_id=1, source_target_pairs={{0,1},{1,0},{2,3},{3,2},{4,5},{5,4},{6,7},{7,6},{8,9},{9,8},{10,11... | collective-permute-start | bytes 15728648 | tf_op jit(solution)/shard_map/ppermute | solution.py:285
  2.2 13.7 %collective-permute-start.2 = (f32[2,8,2560]{2,1,0:T(8,128)S(1)}, f32[2,8,2560]{2,1,0:T(8,128)S(1)}, u32[]{:S(2)}, u32[]{:S(2)}) collective-permute-start(f32[2,8,2560]{2,1,0:T(8,128)S(1)} %get-tuple-element.109.refs_0_), channel_id=1, source_target_pairs={{0,6},{1,7},{2,4},{3,5},{4,2},{5,3},{6,0},{7,1},{8,14},{9,15},{10,... | collective-permute-start | bytes 491528 | tf_op jit(solution)/shard_map/ppermute | solution.py:288
  5.7 10.5 %collective-permute-start.1 = (f32[2,8,2560]{2,1,0:T(8,128)S(1)}, f32[2,8,2560]{2,1,0:T(8,128)S(1)}, u32[]{:S(2)}, u32[]{:S(2)}) collective-permute-start(f32[2,8,2560]{2,1,0:T(8,128)S(1)} %get-tuple-element.109.refs_0_), channel_id=1, source_target_pairs={{0,4},{1,5},{2,6},{3,7},{4,0},{5,1},{6,2},{7,3},{8,12},{9,13},{10,... | collective-permute-start | bytes 491528 | tf_op jit(solution)/shard_map/ppermute | solution.py:288
  6.2 10.0 %collective-permute-start = (f32[2,8,2560]{2,1,0:T(8,128)S(1)}, f32[2,8,2560]{2,1,0:T(8,128)S(1)}, u32[]{:S(2)}, u32[]{:S(2)}) collective-permute-start(f32[2,8,2560]{2,1,0:T(8,128)S(1)} %get-tuple-element.109.refs_0_), channel_id=1, source_target_pairs={{0,2},{1,3},{2,0},{3,1},{4,6},{5,7},{6,4},{7,5},{8,10},{9,11},{10,... | collective-permute-start | bytes 491528 | tf_op jit(solution)/shard_map/ppermute | solution.py:288
  6.3 16.8 %collective-permute-start.19 = (f32[2,8,2560]{2,1,0:T(8,128)S(1)}, f32[2,8,2560]{2,1,0:T(8,128)S(1)}, u32[]{:S(2)}, u32[]{:S(2)}) collective-permute-start(f32[2,8,2560]{2,1,0:T(8,128)S(1)} %get-tuple-element.108.refs_0_), channel_id=1, source_target_pairs={{0,6},{1,7},{2,4},{3,5},{4,2},{5,3},{6,0},{7,1},{8,14},{9,15},{10,... | collective-permute-start | bytes 491528 | tf_op jit(solution)/shard_map/ppermute | solution.py:288
  13.2 10.0 %collective-permute-start.18 = (f32[2,8,2560]{2,1,0:T(8,128)S(1)}, f32[2,8,2560]{2,1,0:T(8,128)S(1)}, u32[]{:S(2)}, u32[]{:S(2)}) collective-permute-start(f32[2,8,2560]{2,1,0:T(8,128)S(1)} %get-tuple-element.108.refs_0_), channel_id=1, source_target_pairs={{0,4},{1,5},{2,6},{3,7},{4,0},{5,1},{6,2},{7,3},{8,12},{9,13},{10,... | collective-permute-start | bytes 491528 | tf_op jit(solution)/shard_map/ppermute | solution.py:288
  15.9 7.3 %collective-permute-start.17 = (f32[2,8,2560]{2,1,0:T(8,128)S(1)}, f32[2,8,2560]{2,1,0:T(8,128)S(1)}, u32[]{:S(2)}, u32[]{:S(2)}) collective-permute-start(f32[2,8,2560]{2,1,0:T(8,128)S(1)} %get-tuple-element.108.refs_0_), channel_id=1, source_target_pairs={{0,2},{1,3},{2,0},{3,1},{4,6},{5,7},{6,4},{7,5},{8,10},{9,11},{10,... | collective-permute-start | bytes 491528 | tf_op jit(solution)/shard_map/ppermute | solution.py:288
  18.8 7.5 %collective-permute-start.7 = (f32[32,1408]{1,0:T(8,128)S(1)}, f32[32,1408]{1,0:T(8,128)S(1)}, u32[]{:S(2)}, u32[]{:S(2)}) collective-permute-start(f32[32,1408]{1,0:T(8,128)S(1)} %get-tuple-element.69), channel_id=1, source_target_pairs={{0,2},{1,3},{2,0},{3,1},{4,6},{5,7},{6,4},{7,5},{8,10},{9,11},{10,... | collective-permute-start | bytes 540680 | tf_op jit(solution)/shard_map/ppermute | solution.py:285
  21.6 7.9 %collective-permute-start.4 = (f32[32,1280]{1,0:T(8,128)S(1)}, f32[32,1280]{1,0:T(8,128)S(1)}, u32[]{:S(2)}, u32[]{:S(2)}) collective-permute-start(f32[32,1280]{1,0:T(8,128)S(1)} %get-tuple-element.67), channel_id=1, source_target_pairs={{0,4},{1,5},{2,6},{3,7},{4,0},{5,1},{6,2},{7,3},{8,12},{9,13},{10,... | collective-permute-start | bytes 491528 | tf_op jit(solution)/shard_map/ppermute | solution.py:285
  25.8 7.0 %collective-permute-start.23 = (f32[32,1408]{1,0:T(8,128)S(1)}, f32[32,1408]{1,0:T(8,128)S(1)}, u32[]{:S(2)}, u32[]{:S(2)}) collective-permute-start(f32[32,1408]{1,0:T(8,128)S(1)} %get-tuple-element.90), channel_id=1, source_target_pairs={{0,4},{1,5},{2,6},{3,7},{4,0},{5,1},{6,2},{7,3},{8,12},{9,13},{10,... | collective-permute-start | bytes 540680 | tf_op jit(solution)/shard_map/ppermute | solution.py:285
  26.4 8.3 %collective-permute-start.8 = (f32[32,1408]{1,0:T(8,128)S(1)}, f32[32,1408]{1,0:T(8,128)S(1)}, u32[]{:S(2)}, u32[]{:S(2)}) collective-permute-start(f32[32,1408]{1,0:T(8,128)S(1)} %add.50), channel_id=1, source_target_pairs={{0,4},{1,5},{2,6},{3,7},{4,0},{5,1},{6,2},{7,3},{8,12},{9,13},{10,... | collective-permute-start | bytes 540680 | tf_op jit(solution)/shard_map/ppermute | solution.py:285
  28.9 7.2 %collective-permute-start.20 = (f32[32,1280]{1,0:T(8,128)S(1)}, f32[32,1280]{1,0:T(8,128)S(1)}, u32[]{:S(2)}, u32[]{:S(2)}) collective-permute-start(f32[32,1280]{1,0:T(8,128)S(1)} %get-tuple-element.88), channel_id=1, source_target_pairs={{0,2},{1,3},{2,0},{3,1},{4,6},{5,7},{6,4},{7,5},{8,10},{9,11},{10,... | collective-permute-start | bytes 491528 | tf_op jit(solution)/shard_map/ppermute | solution.py:285
  29.6 10.1 %collective-permute-start.5 = (f32[32,1280]{1,0:T(8,128)S(1)}, f32[32,1280]{1,0:T(8,128)S(1)}, u32[]{:S(2)}, u32[]{:S(2)}) collective-permute-start(f32[32,1280]{1,0:T(8,128)S(1)} %add.48), channel_id=1, source_target_pairs={{0,2},{1,3},{2,0},{3,1},{4,6},{5,7},{6,4},{7,5},{8,10},{9,11},{10,... | collective-permute-start | bytes 491528 | tf_op jit(solution)/shard_map/ppermute | solution.py:285
  32.8 10.3 %collective-permute-start.24 = (f32[32,1408]{1,0:T(8,128)S(1)}, f32[32,1408]{1,0:T(8,128)S(1)}, u32[]{:S(2)}, u32[]{:S(2)}) collective-permute-start(f32[32,1408]{1,0:T(8,128)S(1)} %add.58), channel_id=1, source_target_pairs={{0,2},{1,3},{2,0},{3,1},{4,6},{5,7},{6,4},{7,5},{8,10},{9,11},{10,... | collective-permute-start | bytes 540680 | tf_op jit(solution)/shard_map/ppermute | solution.py:285
  34.7 11.0 %collective-permute-start.9 = (f32[32,1408]{1,0:T(8,128)S(1)}, f32[32,1408]{1,0:T(8,128)S(1)}, u32[]{:S(2)}, u32[]{:S(2)}) collective-permute-start(f32[32,1408]{1,0:T(8,128)S(1)} %add.51.refs_0_), channel_id=1, source_target_pairs={{0,2},{1,3},{2,0},{3,1},{4,6},{5,7},{6,4},{7,5},{8,10},{9,11},{10,... | collective-permute-start | bytes 540680 | tf_op jit(solution)/shard_map/ppermute | solution.py:285
  36.1 5.6 %collective-permute-start.21 = (f32[32,1280]{1,0:T(8,128)S(1)}, f32[32,1280]{1,0:T(8,128)S(1)}, u32[]{:S(2)}, u32[]{:S(2)}) collective-permute-start(f32[32,1280]{1,0:T(8,128)S(1)} %add.56), channel_id=1, source_target_pairs={{0,4},{1,5},{2,6},{3,7},{4,0},{5,1},{6,2},{7,3},{8,12},{9,13},{10,... | collective-permute-start | bytes 491528 | tf_op jit(solution)/shard_map/ppermute | solution.py:285
  39.6 7.1 %collective-permute-start.6 = (f32[32,1280]{1,0:T(8,128)S(1)}, f32[32,1280]{1,0:T(8,128)S(1)}, u32[]{:S(2)}, u32[]{:S(2)}) collective-permute-start(f32[32,1280]{1,0:T(8,128)S(1)} %add.49.refs_0_), channel_id=1, source_target_pairs={{0,4},{1,5},{2,6},{3,7},{4,0},{5,1},{6,2},{7,3},{8,12},{9,13},{10,... | collective-permute-start | bytes 491528 | tf_op jit(solution)/shard_map/ppermute | solution.py:285
  41.7 10.8 %collective-permute-start.22 = (f32[32,1280]{1,0:T(8,128)S(1)}, f32[32,1280]{1,0:T(8,128)S(1)}, u32[]{:S(2)}, u32[]{:S(2)}) collective-permute-start(f32[32,1280]{1,0:T(8,128)S(1)} %add.57.refs_0_), channel_id=1, source_target_pairs={{0,2},{1,3},{2,0},{3,1},{4,6},{5,7},{6,4},{7,5},{8,10},{9,11},{10,... | collective-permute-start | bytes 491528 | tf_op jit(solution)/shard_map/ppermute | solution.py:285
  43.1 8.5 %collective-permute-start.25 = (f32[32,1408]{1,0:T(8,128)S(1)}, f32[32,1408]{1,0:T(8,128)S(1)}, u32[]{:S(2)}, u32[]{:S(2)}) collective-permute-start(f32[32,1408]{1,0:T(8,128)S(1)} %add.59.refs_0_), channel_id=1, source_target_pairs={{0,4},{1,5},{2,6},{3,7},{4,0},{5,1},{6,2},{7,3},{8,12},{9,13},{10,... | collective-permute-start | bytes 540680 | tf_op jit(solution)/shard_map/ppermute | solution.py:285
  48.5 9.2 %collective-permute-start.13 = (f32[32,1408]{1,0:T(8,128)S(1)}, f32[32,1408]{1,0:T(8,128)S(1)}, u32[]{:S(2)}, u32[]{:S(2)}) collective-permute-start(f32[32,1408]{1,0:T(8,128)S(1)} %get-tuple-element.77), channel_id=1, source_target_pairs={{0,2},{1,3},{2,0},{3,1},{4,6},{5,7},{6,4},{7,5},{8,10},{9,11},{10,... | collective-permute-start | bytes 540680 | tf_op jit(solution)/shard_map/ppermute | solution.py:285
  50.8 8.3 %collective-permute-start.10 = (f32[32,1280]{1,0:T(8,128)S(1)}, f32[32,1280]{1,0:T(8,128)S(1)}, u32[]{:S(2)}, u32[]{:S(2)}) collective-permute-start(f32[32,1280]{1,0:T(8,128)S(1)} %get-tuple-element.75), channel_id=1, source_target_pairs={{0,4},{1,5},{2,6},{3,7},{4,0},{5,1},{6,2},{7,3},{8,12},{9,13},{10,... | collective-permute-start | bytes 491528 | tf_op jit(solution)/shard_map/ppermute | solution.py:285
  54.4 7.3 %collective-permute-start.29 = (f32[32,1408]{1,0:T(8,128)S(1)}, f32[32,1408]{1,0:T(8,128)S(1)}, u32[]{:S(2)}, u32[]{:S(2)}) collective-permute-start(f32[32,1408]{1,0:T(8,128)S(1)} %get-tuple-element.99), channel_id=1, source_target_pairs={{0,4},{1,5},{2,6},{3,7},{4,0},{5,1},{6,2},{7,3},{8,12},{9,13},{10,... | collective-permute-start | bytes 540680 | tf_op jit(solution)/shard_map/ppermute | solution.py:285
  56.9 6.4 %collective-permute-start.26 = (f32[32,1280]{1,0:T(8,128)S(1)}, f32[32,1280]{1,0:T(8,128)S(1)}, u32[]{:S(2)}, u32[]{:S(2)}) collective-permute-start(f32[32,1280]{1,0:T(8,128)S(1)} %get-tuple-element.96), channel_id=1, source_target_pairs={{0,2},{1,3},{2,0},{3,1},{4,6},{5,7},{6,4},{7,5},{8,10},{9,11},{10,... | collective-permute-start | bytes 491528 | tf_op jit(solution)/shard_map/ppermute | solution.py:285
  57.7 7.8 %collective-permute-start.14 = (f32[32,1408]{1,0:T(8,128)S(1)}, f32[32,1408]{1,0:T(8,128)S(1)}, u32[]{:S(2)}, u32[]{:S(2)}) collective-permute-start(f32[32,1408]{1,0:T(8,128)S(1)} %add.54), channel_id=1, source_target_pairs={{0,4},{1,5},{2,6},{3,7},{4,0},{5,1},{6,2},{7,3},{8,12},{9,13},{10,... | collective-permute-start | bytes 540680 | tf_op jit(solution)/shard_map/ppermute | solution.py:285
  59.1 7.9 %collective-permute-start.11 = (f32[32,1280]{1,0:T(8,128)S(1)}, f32[32,1280]{1,0:T(8,128)S(1)}, u32[]{:S(2)}, u32[]{:S(2)}) collective-permute-start(f32[32,1280]{1,0:T(8,128)S(1)} %add.52), channel_id=1, source_target_pairs={{0,2},{1,3},{2,0},{3,1},{4,6},{5,7},{6,4},{7,5},{8,10},{9,11},{10,... | collective-permute-start | bytes 491528 | tf_op jit(solution)/shard_map/ppermute | solution.py:285
  61.7 7.9 %collective-permute-start.30 = (f32[32,1408]{1,0:T(8,128)S(1)}, f32[32,1408]{1,0:T(8,128)S(1)}, u32[]{:S(2)}, u32[]{:S(2)}) collective-permute-start(f32[32,1408]{1,0:T(8,128)S(1)} %add.62), channel_id=1, source_target_pairs={{0,2},{1,3},{2,0},{3,1},{4,6},{5,7},{6,4},{7,5},{8,10},{9,11},{10,... | collective-permute-start | bytes 540680 | tf_op jit(solution)/shard_map/ppermute | solution.py:285
  63.3 7.2 %collective-permute-start.27 = (f32[32,1280]{1,0:T(8,128)S(1)}, f32[32,1280]{1,0:T(8,128)S(1)}, u32[]{:S(2)}, u32[]{:S(2)}) collective-permute-start(f32[32,1280]{1,0:T(8,128)S(1)} %add.60), channel_id=1, source_target_pairs={{0,4},{1,5},{2,6},{3,7},{4,0},{5,1},{6,2},{7,3},{8,12},{9,13},{10,... | collective-permute-start | bytes 491528 | tf_op jit(solution)/shard_map/ppermute | solution.py:285
  65.5 6.3 %collective-permute-start.15 = (f32[32,1408]{1,0:T(8,128)S(1)}, f32[32,1408]{1,0:T(8,128)S(1)}, u32[]{:S(2)}, u32[]{:S(2)}) collective-permute-start(f32[32,1408]{1,0:T(8,128)S(1)} %add.55.refs_0_), channel_id=1, source_target_pairs={{0,2},{1,3},{2,0},{3,1},{4,6},{5,7},{6,4},{7,5},{8,10},{9,11},{10,... | collective-permute-start | bytes 540680 | tf_op jit(solution)/shard_map/ppermute | solution.py:285
  67.0 5.8 %collective-permute-start.12 = (f32[32,1280]{1,0:T(8,128)S(1)}, f32[32,1280]{1,0:T(8,128)S(1)}, u32[]{:S(2)}, u32[]{:S(2)}) collective-permute-start(f32[32,1280]{1,0:T(8,128)S(1)} %add.53.refs_0_), channel_id=1, source_target_pairs={{0,4},{1,5},{2,6},{3,7},{4,0},{5,1},{6,2},{7,3},{8,12},{9,13},{10,... | collective-permute-start | bytes 491528 | tf_op jit(solution)/shard_map/ppermute | solution.py:285
  69.6 5.6 %collective-permute-start.31 = (f32[32,1408]{1,0:T(8,128)S(1)}, f32[32,1408]{1,0:T(8,128)S(1)}, u32[]{:S(2)}, u32[]{:S(2)}) collective-permute-start(f32[32,1408]{1,0:T(8,128)S(1)} %add.63.refs_0_), channel_id=1, source_target_pairs={{0,4},{1,5},{2,6},{3,7},{4,0},{5,1},{6,2},{7,3},{8,12},{9,13},{10,... | collective-permute-start | bytes 540680 | tf_op jit(solution)/shard_map/ppermute | solution.py:285
  70.5 5.7 %collective-permute-start.28 = (f32[32,1280]{1,0:T(8,128)S(1)}, f32[32,1280]{1,0:T(8,128)S(1)}, u32[]{:S(2)}, u32[]{:S(2)}) collective-permute-start(f32[32,1280]{1,0:T(8,128)S(1)} %add.61.refs_0_), channel_id=1, source_target_pairs={{0,2},{1,3},{2,0},{3,1},{4,6},{5,7},{6,4},{7,5},{8,10},{9,11},{10,... | collective-permute-start | bytes 491528 | tf_op jit(solution)/shard_map/ppermute | solution.py:285
  73.8 3.4 %collective-permute-start.16 = (f32[2,64,256]{2,1,0:T(8,128)S(1)}, f32[2,64,256]{2,1,0:T(8,128)S(1)}, u32[]{:S(2)}, u32[]{:S(2)}) collective-permute-start(f32[2,64,256]{2,1,0:T(8,128)S(1)} %get-tuple-element.85), channel_id=1, source_target_pairs={{0,1},{1,0},{2,3},{3,2},{4,5},{5,4},{6,7},{7,6},{8,9},{9,8},{10,11... | collective-permute-start | bytes 393224 | tf_op jit(solution)/shard_map/ppermute | solution.py:285
  77.1 1.4 %collective-permute-start.32 = (f32[2,64,256]{2,1,0:T(8,128)S(1)}, f32[2,64,256]{2,1,0:T(8,128)S(1)}, u32[]{:S(2)}, u32[]{:S(2)}) collective-permute-start(f32[2,64,256]{2,1,0:T(8,128)S(1)} %get-tuple-element.107), channel_id=1, source_target_pairs={{0,1},{1,0},{2,3},{3,2},{4,5},{5,4},{6,7},{7,6},{8,9},{9,8},{10,11... | collective-permute-start | bytes 393224 | tf_op jit(solution)/shard_map/ppermute | solution.py:285

commit v7 on v6

--- a/solution.py
+++ b/solution.py
@@ -33,49 +33,88 @@
         grid=grid,
         in_specs=in_specs or [spec] * len(args),
         out_specs=[spec] * len(outs),
-        scratch_shapes=[pltpu.VMEM(shape, dtype) for shape, dtype in scratch],
+        scratch_shapes=[pltpu.VMEM(*item) if isinstance(item, tuple) else item for item in scratch],
         cost_estimate=pl.CostEstimate(flops=flops, transcendentals=0, bytes_accessed=moved),
         compiler_params=pltpu.CompilerParams(vmem_limit_bytes=16 << 20),
     )(*args)
 
 
-def split_kernel(real_ref, imag_ref, high_ref, low_ref, turned_high_ref, turned_low_ref, energy_ref):
+def split_piece(value_of, part, at, places, high_ref, low_ref, turned_high_ref, turned_low_ref, energy_ref):
+    for source, place in places:
+        value = value_of(source)
+        rows, width = value.shape
+        high, low = parts_of(value)
+        high_ref[part, at, place] = high
+        low_ref[part, at, place] = low
+        turned_high_ref[part, place, at] = high.T
+        turned_low_ref[part, place, at] = low.T
+        square = jnp.sum((value * value).reshape(rows // 8, 8, width), axis=0)
+        energy_ref[...] += sum(square[:, lane : lane + LANES] for lane in range(0, width, LANES))
+
+
+def split_kernel(real_ref, imag_ref, *outs):
     rows, shots = real_ref.shape[1:]
     step, chunk = pl.program_id(0), pl.program_id(1)
     width = 2 * LANES
-    at = slice(None) if rows == high_ref.shape[1] else pl.ds(pl.multiple_of(step * rows, rows), rows)
+    at = slice(None) if rows == outs[0].shape[1] else pl.ds(pl.multiple_of(step * rows, rows), rows)
 
     @pl.when((step == 0) & (chunk == 0))
     def _():
-        energy_ref[...] = jnp.zeros_like(energy_ref)
-
+        outs[4][...] = jnp.zeros_like(outs[4])
+
+    starts = range(0, shots, width)
+    places = [
+        (slice(start, start + width), pl.ds(pl.multiple_of(chunk * shots + start, width), width)) for start in starts
+    ]
     for part, ref in enumerate((real_ref, imag_ref)):
-        for start in range(0, shots, width):
-            value = ref[0, :, start : start + width]
-            place = pl.ds(pl.multiple_of(chunk * shots + start, width), width)
-            high, low = parts_of(value)
-            high_ref[part, at, place] = high
-            low_ref[part, at, place] = low
-            turned_high_ref[part, place, at] = high.T
-            turned_low_ref[part, place, at] = low.T
-            square = jnp.sum((value * value).reshape(rows // 8, 8, width), axis=0)
-            energy_ref[...] += sum(square[:, lane : lane + LANES] for lane in range(0, width, LANES))
-
-
-def split(value):
+        split_piece(lambda place: ref[0, :, place], part, at, places, *outs)
+
+
+def fetch_split_kernel(down_ref, *refs):
+    outs, (held_ref, sems) = refs[:5], refs[5:]
+    rows, shots = down_ref.shape[1:]
+    block, chunks, width = min(rows, LANES), 2, 2 * LANES
+    pieces = []
+    for part in range(2):
+        for row in range(0, rows, block):
+            for chunk in range(chunks):
+                start = chunk * shots // chunks
+                where = (part, slice(row, row + block), slice(start, start + shots // chunks))
+                copy = pltpu.make_async_copy(down_ref.at[where], held_ref.at[where], sems.at[len(pieces)])
+                copy.start()
+                pieces.append((copy, where))
+    outs[4][...] = jnp.zeros_like(outs[4])
+    for copy, (part, at, where) in pieces:
+        copy.wait()
+        places = [(slice(start, start + width),) * 2 for start in range(where.start, where.stop, width)]
+        split_piece(lambda place: held_ref[part, at, place], part, at, places, *outs)
+
+
+def split(value, from_hbm=False):
     _, rows, shots = value.shape
     block, chunks = min(rows, LANES), 2
     plain, turned = ((2, rows, shots), bf16), ((2, shots, rows), bf16)
-    high, low, turned_high, turned_low, energy = call(
-        split_kernel,
-        [plain, plain, turned, turned, ((8, LANES), f32)],
-        (value, value),
-        grid=(rows // block, chunks),
-        in_specs=[
-            pl.BlockSpec((1, block, shots // chunks), lambda step, chunk: (0, step, chunk)),
-            pl.BlockSpec((1, block, shots // chunks), lambda step, chunk: (1, step, chunk)),
-        ],
-    )
+    outs = [plain, plain, turned, turned, ((8, LANES), f32)]
+    if from_hbm:
+        pieces = 2 * (rows // block) * chunks
+        high, low, turned_high, turned_low, energy = call(
+            fetch_split_kernel,
+            outs,
+            (value,),
+            [pltpu.VMEM(value.shape, f32), pltpu.SemaphoreType.DMA((pieces,))],
+            in_specs=[pl.BlockSpec(memory_space=pltpu.HBM)],
+        )
+    else:
+        high, low, turned_high, turned_low, energy = call(
+            split_kernel,
+            outs,
+            (value, value),
+            grid=(rows // block, chunks),
+            in_specs=[
+                pl.BlockSpec((1, block, shots // chunks), lambda step, chunk: (0, step, chunk)),
+                pl.BlockSpec((1, block, shots // chunks), lambda step, chunk: (1, step, chunk)),
+            ],
+        )
     return (high, low), (turned_high, turned_low), energy
 
 
@@ -293,7 +332,7 @@
     for group in range(GROUPS):
         part = up_sources[:, group * own : (group + 1) * own]
         sources.append([jump(part, mask) if mask else part for mask in masks])
-    plain_a, turned_a, energy_a = split(pltpu.with_memory_space_constraint(down_spectra, pltpu.HBM))
+    plain_a, turned_a, energy_a = split(down_spectra, from_hbm=True)
     plain_b, turned_b, energy_b = split(other_down)
     turned = (*turned_a, *turned_b)
     down = (*plain_a, *plain_b, *turned)

time: 79.7 us -> 80.1 us (level)
  local copies, waits for them, and re-layouts: 1.02 us -> 3.5 us
  Pallas kernels: 25.3 us -> 23.9 us
    unnamed x0 -> x2, local copies, waits for them, and re-layouts: none -> 2.49 us
    pallas_call x17, Pallas kernels: 25.3 us -> 23.9 us  [call(): pl.pallas_call(kernel, out_shape=[jax.ShapeDtypeStruct(shape, dtype) for...]
  transfers between devices with their start and end apart: 33 -> 33, of which waited for: 13 -> 13; matrix products, arithmetic and copies ran while one was open for 2% -> 2% of each run, Pallas kernels for 31% -> 29%
where the time goes in v7:
time: 80.1 us; the launch traced here: 79.9 us
  starting transfers between devices  35.2 us (44%)
  Pallas kernels  23.9 us (30%)
  waiting for transfers between devices  16 us (20%)
  local copies, waits for them, and re-layouts  3.5 us (4%)
  between operations  0.9 us (1%)
    ppermute x27, starting transfers between devices, swap(): lax.ppermute(value, 'rcv', [(at, at ^ 1 << bit) for at in range(count)])  27.4 us
    pallas_call x17, Pallas kernels, call(): pl.pallas_call(kernel, out_shape=[jax.ShapeDtypeStruct(shape, dtype) for...  23.9 us
    ppermute x27, waiting for transfers between devices, swap(): lax.ppermute(value, 'rcv', [(at, at ^ 1 << bit) for at in range(count)])  16 us
    ppermute x6, starting transfers between devices, jump(): lax.ppermute(value, 'rcv', [(at, at ^ mask << 1) for at in range(count)])  7.79 us
    unnamed x2, local copies, waits for them, and re-layouts  2.49 us
  transfers between devices with their start and end apart: 33, of which 13 were waited for; matrix products, arithmetic and copies ran while one was open for 2% of the time, Pallas kernels for 29%

profile of v7, /device:TPU:0, one launch (start us, length us, event | category | flops | bytes accessed | tf_op | source)
XLA Modules:
  0.0 79.9 jit_solution(17082826571567510968)
XLA Ops:
  0.6 0.5 collective-permute-start.3
  1.1 1.0 %fusion = (f32[2,8,2560]{2,1,0:T(8,128)S(1)}, f32[2,8,2560]{2,1,0:T(8,128)S(1)}) fusion(f32[2,16,2560]{2,1,0:T(8,128)} %param.3), kind=kLoop, calls=%fused_computation | loop fusion | bytes 655360 | tf_op jit(solution)/shard_map/slice | solution.py:333
  2.2 3.5 %collective-permute-start.2 = (f32[2,8,2560]{2,1,0:T(8,128)S(1)}, f32[2,8,2560]{2,1,0:T(8,128)S(1)}, u32[]{:S(2)}, u32[]{:S(2)}) collective-permute-start(f32[2,8,2560]{2,1,0:T(8,128)S(1)} %get-tuple-element.109.refs_0_), channel_id=1, source_target_pairs={{0,6},{1,7},{2,4},{3,5},{4,2},{5,3},{6,0},{7,1},{8,14},{9,15},{10,... | collective-permute-start | bytes 491528 | tf_op jit(solution)/shard_map/ppermute | solution.py:327
  5.7 0.5 collective-permute-start.1
  6.2 0.1 collective-permute-start
  6.3 2.8 %collective-permute-start.19 = (f32[2,8,2560]{2,1,0:T(8,128)S(1)}, f32[2,8,2560]{2,1,0:T(8,128)S(1)}, u32[]{:S(2)}, u32[]{:S(2)}) collective-permute-start(f32[2,8,2560]{2,1,0:T(8,128)S(1)} %get-tuple-element.108.refs_0_), channel_id=1, source_target_pairs={{0,6},{1,7},{2,4},{3,5},{4,2},{5,3},{6,0},{7,1},{8,14},{9,15},{10,... | collective-permute-start | bytes 491528 | tf_op jit(solution)/shard_map/ppermute | solution.py:327
  9.2 2.5 %copy-done = f32[2,256,2560]{2,1,0:T(8,128)S(1)} copy-done((f32[2,256,2560]{2,1,0:T(8,128)S(1)}, f32[2,256,2560]{2,1,0:T(8,128)}, u32[]{:S(2)}) %copy-start) | copy-done | bytes 5242904
  11.7 2.4 %shard_map.41 = (bf16[2,256,2560]{2,1,0:T(8,128)(2,1)S(1)}, bf16[2,256,2560]{2,1,0:T(8,128)(2,1)S(1)}, bf16[2,2560,256]{2,1,0:T(8,128)(2,1)S(1)}, bf16[2,2560,256]{2,1,0:T(8,128)(2,1)S(1)}, f32[8,128]{1,0:T(8,128)S(1)}) custom-call(f32[2,256,2560]{2,1,0:T(8,128)S(1)} %copy-done), custom_call_target="tpu_custom_call" | custom-call | bytes 5242880 | tf_op jit(solution)/shard_map/pallas_call | solution.py:30
  14.1 0.6 collective-permute-start.18
  14.7 2.3 %shard_map.42 = (bf16[2,256,2560]{2,1,0:T(8,128)(2,1)S(1)}, bf16[2,256,2560]{2,1,0:T(8,128)(2,1)S(1)}, bf16[2,2560,256]{2,1,0:T(8,128)(2,1)S(1)}, bf16[2,2560,256]{2,1,0:T(8,128)(2,1)S(1)}, f32[8,128]{1,0:T(8,128)S(1)}) custom-call(f32[2,256,2560]{2,1,0:T(8,128)S(1)} %collective-permute-done.3.real_ref.imag_ref, ...), custom_call_target="tpu_custom_call" | custom-call | bytes 10485760 | tf_op jit(solution)/shard_map/pallas_call | solution.py:30
  17.0 0.2 collective-permute-start.17
  17.2 2.6 %shard_map.43 = (f32[64,512]{1,0:T(8,128)S(1)}, f32[32,1408]{1,0:T(8,128)S(1)}, f32[32,1408]{1,0:T(8,128)S(1)}) custom-call(f32[2,8,2560]{2,1,0:T(8,128)S(1)} %get-tuple-element.109.refs_0_, f32[2,8,2560]{2,1,0:T(8,128)S(1)} %collective-permute-done.refs_1_, f32[2,8,2560]{2,1,0:T(8,128)S(1)} %collective-permute-done.1.refs_2_, ...), custom_call_target="tpu_custom_call" | custom-call | flops 90596966400 | bytes 21635072 | tf_op jit(solution)/shard_map/pallas_call | solution.py:30
  19.8 1.9 %collective-permute-start.7 = (f32[32,1408]{1,0:T(8,128)S(1)}, f32[32,1408]{1,0:T(8,128)S(1)}, u32[]{:S(2)}, u32[]{:S(2)}) collective-permute-start(f32[32,1408]{1,0:T(8,128)S(1)} %get-tuple-element.69), channel_id=1, source_target_pairs={{0,2},{1,3},{2,0},{3,1},{4,6},{5,7},{6,4},{7,5},{8,10},{9,11},{10,... | collective-permute-start | bytes 540680 | tf_op jit(solution)/shard_map/ppermute | solution.py:324
  21.7 0.9 %shard_map.44 = (f32[32,1280]{1,0:T(8,128)S(1)}, f32[32,1280]{1,0:T(8,128)S(1)}) custom-call(f32[64,512]{1,0:T(8,128)S(1)} %get-tuple-element.65.refs_0_.refs_5_, bf16[2,256,2560]{2,1,0:T(8,128)(2,1)S(1)} %get-tuple-element.55.refs_4_.refs_1_.refs_6_, bf16[2,256,2560]{2,1,0:T(8,128)(2,1)S(1)} %get-tuple-element.56.refs_5_.refs_2_.refs_7_, ...), custom_call_target="tpu_custom_call" | custom-call | flops 301989888 | bytes 10616832 | tf_op jit(solution)/shard_map/pallas_call | solution.py:30
  22.7 1.6 %collective-permute-start.4 = (f32[32,1280]{1,0:T(8,128)S(1)}, f32[32,1280]{1,0:T(8,128)S(1)}, u32[]{:S(2)}, u32[]{:S(2)}) collective-permute-start(f32[32,1280]{1,0:T(8,128)S(1)} %get-tuple-element.67), channel_id=1, source_target_pairs={{0,4},{1,5},{2,6},{3,7},{4,0},{5,1},{6,2},{7,3},{8,12},{9,13},{10,... | collective-permute-start | bytes 491528 | tf_op jit(solution)/shard_map/ppermute | solution.py:324
  24.3 2.6 %shard_map.50 = (f32[64,512]{1,0:T(8,128)S(1)}, f32[32,1408]{1,0:T(8,128)S(1)}, f32[32,1408]{1,0:T(8,128)S(1)}) custom-call(f32[2,8,2560]{2,1,0:T(8,128)S(1)} %get-tuple-element.108.refs_0_, f32[2,8,2560]{2,1,0:T(8,128)S(1)} %collective-permute-done.17.refs_1_, f32[2,8,2560]{2,1,0:T(8,128)S(1)} %collective-permute-done.18.refs_2_, ...), custom_call_target="tpu_custom_call" | custom-call | flops 3019898880 | bytes 21635072 | tf_op jit(solution)/shard_map/pallas_call | solution.py:30
  26.9 0.6 collective-permute-start.23
  27.5 1.6 %collective-permute-start.8 = (f32[32,1408]{1,0:T(8,128)S(1)}, f32[32,1408]{1,0:T(8,128)S(1)}, u32[]{:S(2)}, u32[]{:S(2)}) collective-permute-start(f32[32,1408]{1,0:T(8,128)S(1)} %add.50), channel_id=1, source_target_pairs={{0,4},{1,5},{2,6},{3,7},{4,0},{5,1},{6,2},{7,3},{8,12},{9,13},{10,... | collective-permute-start | bytes 540680 | tf_op jit(solution)/shard_map/ppermute | solution.py:324
  29.1 0.9 %shard_map.51 = (f32[32,1280]{1,0:T(8,128)S(1)}, f32[32,1280]{1,0:T(8,128)S(1)}) custom-call(f32[64,512]{1,0:T(8,128)S(1)} %get-tuple-element.86.refs_0_.refs_5_, bf16[2,256,2560]{2,1,0:T(8,128)(2,1)S(1)} %get-tuple-element.55.refs_4_.refs_1_.refs_6_, bf16[2,256,2560]{2,1,0:T(8,128)(2,1)S(1)} %get-tuple-element.56.refs_5_.refs_2_.refs_7_, ...), custom_call_target="tpu_custom_call" | custom-call | bytes 10616832 | tf_op jit(solution)/shard_map/pallas_call | solution.py:30
  30.0 0.6 collective-permute-start.20
  30.6 1.6 %collective-permute-start.5 = (f32[32,1280]{1,0:T(8,128)S(1)}, f32[32,1280]{1,0:T(8,128)S(1)}, u32[]{:S(2)}, u32[]{:S(2)}) collective-permute-start(f32[32,1280]{1,0:T(8,128)S(1)} %add.48), channel_id=1, source_target_pairs={{0,2},{1,3},{2,0},{3,1},{4,6},{5,7},{6,4},{7,5},{8,10},{9,11},{10,... | collective-permute-start | bytes 491528 | tf_op jit(solution)/shard_map/ppermute | solution.py:324
  32.2 1.7 %collective-permute-done.23 = f32[32,1408]{1,0:T(8,128)S(1)} collective-permute-done((f32[32,1408]{1,0:T(8,128)S(1)}, f32[32,1408]{1,0:T(8,128)S(1)}, u32[]{:S(2)}, u32[]{:S(2)}) %collective-permute-start.23) | collective-permute-done | bytes 180256 | tf_op jit(solution)/shard_map/ppermute | solution.py:324
  33.9 0.3 collective-permute-start.24
  34.2 1.6 %collective-permute-done.8 = f32[32,1408]{1,0:T(8,128)S(1)} collective-permute-done((f32[32,1408]{1,0:T(8,128)S(1)}, f32[32,1408]{1,0:T(8,128)S(1)}, u32[]{:S(2)}, u32[]{:S(2)}) %collective-permute-start.8) | collective-permute-done | bytes 180256 | tf_op jit(solution)/shard_map/ppermute | solution.py:324
  35.8 0.3 collective-permute-start.9
  36.2 1.1 %collective-permute-done.20 = f32[32,1280]{1,0:T(8,128)S(1)} collective-permute-done((f32[32,1280]{1,0:T(8,128)S(1)}, f32[32,1280]{1,0:T(8,128)S(1)}, u32[]{:S(2)}, u32[]{:S(2)}) %collective-permute-start.20) | collective-permute-done | bytes 163872 | tf_op jit(solution)/shard_map/ppermute | solution.py:324
  37.2 0.8 collective-permute-start.21
  38.0 2.7 %collective-permute-done.5 = f32[32,1280]{1,0:T(8,128)S(1)} collective-permute-done((f32[32,1280]{1,0:T(8,128)S(1)}, f32[32,1280]{1,0:T(8,128)S(1)}, u32[]{:S(2)}, u32[]{:S(2)}) %collective-permute-start.5) | collective-permute-done | bytes 163872 | tf_op jit(solution)/shard_map/ppermute | solution.py:324
  40.7 0.3 collective-permute-start.6
  41.0 1.6 %collective-permute-done.21 = f32[32,1280]{1,0:T(8,128)S(1)} collective-permute-done((f32[32,1280]{1,0:T(8,128)S(1)}, f32[32,1280]{1,0:T(8,128)S(1)}, u32[]{:S(2)}, u32[]{:S(2)}) %collective-permute-start.21) | collective-permute-done | bytes 163872 | tf_op jit(solution)/shard_map/ppermute | solution.py:324
  42.7 1.5 %collective-permute-start.22 = (f32[32,1280]{1,0:T(8,128)S(1)}, f32[32,1280]{1,0:T(8,128)S(1)}, u32[]{:S(2)}, u32[]{:S(2)}) collective-permute-start(f32[32,1280]{1,0:T(8,128)S(1)} %add.57.refs_0_), channel_id=1, source_target_pairs={{0,2},{1,3},{2,0},{3,1},{4,6},{5,7},{6,4},{7,5},{8,10},{9,11},{10,... | collective-permute-start | bytes 491528 | tf_op jit(solution)/shard_map/ppermute | solution.py:324
  44.2 0.1 collective-permute-done.24
  44.3 1.7 %collective-permute-start.25 = (f32[32,1408]{1,0:T(8,128)S(1)}, f32[32,1408]{1,0:T(8,128)S(1)}, u32[]{:S(2)}, u32[]{:S(2)}) collective-permute-start(f32[32,1408]{1,0:T(8,128)S(1)} %add.59.refs_0_), channel_id=1, source_target_pairs={{0,4},{1,5},{2,6},{3,7},{4,0},{5,1},{6,2},{7,3},{8,12},{9,13},{10,... | collective-permute-start | bytes 540680 | tf_op jit(solution)/shard_map/ppermute | solution.py:324
  46.0 0.8 %collective-permute-done.9.refs_1_ = f32[32,1408]{1,0:T(8,128)S(1)} collective-permute-done((f32[32,1408]{1,0:T(8,128)S(1)}, f32[32,1408]{1,0:T(8,128)S(1)}, u32[]{:S(2)}, u32[]{:S(2)}) %collective-permute-start.9) | collective-permute-done | bytes 180256 | tf_op jit(solution)/shard_map/ppermute | solution.py:324
  46.9 0.9 %shard_map.45 = (f32[64,1280]{1,0:T(8,128)S(1)}, f32[64,128]{1,0:T(8,128)S(1)}, f32[64,512]{1,0:T(8,128)S(1)}) custom-call(f32[32,1408]{1,0:T(8,128)S(1)} %add.51.refs_0_, f32[32,1408]{1,0:T(8,128)S(1)} %collective-permute-done.9.refs_1_, bf16[2,2560,256]{2,1,0:T(8,128)(2,1)S(1)} %get-tuple-element.59.refs_8_.refs_2_.refs_10_.refs_11_, ...), custom_call_target="tpu_custom_call" | custom-call | bytes 10846208 | tf_op jit(solution)/shard_map/pallas_call | solution.py:30
  47.8 1.8 %shard_map.46 = (f32[64,1280]{1,0:T(8,128)S(1)}, f32[64,128]{1,0:T(8,128)S(1)}, f32[64,512]{1,0:T(8,128)S(1)}, f32[64,512]{1,0:T(8,128)S(1)}, f32[32,1408]{1,0:T(8,128)S(1)}, /*index=5*/f32[32,1408]{1,0:T(8,128)S(1)}) custom-call(f32[32,1280]{1,0:T(8,128)S(1)} %add.49.refs_0_, f32[32,1280]{1,0:T(8,128)S(1)} %collective-permute-done.6.refs_1_, ...), custom_call_target="tpu_custom_call" | custom-call | flops 2013265920 | bytes 21921792 | tf_op jit(solution)/shard_map/pallas_call | solution.py:30
  49.6 0.6 collective-permute-start.13
  50.3 0.9 %shard_map.47 = (f32[32,1280]{1,0:T(8,128)S(1)}, f32[32,1280]{1,0:T(8,128)S(1)}) custom-call(f32[64,512]{1,0:T(8,128)S(1)} %get-tuple-element.73.refs_0_.refs_10_, bf16[2,256,2560]{2,1,0:T(8,128)(2,1)S(1)} %get-tuple-element.55.refs_4_.refs_1_.refs_6_, bf16[2,256,2560]{2,1,0:T(8,128)(2,1)S(1)} %get-tuple-element.56.refs_5_.refs_2_.refs_7_, ...), custom_call_target="tpu_custom_call" | custom-call | flops 3019898880 | bytes 10616832 | tf_op jit(solution)/shard_map/pallas_call | solution.py:30
  51.2 1.0 %collective-permute-start.10 = (f32[32,1280]{1,0:T(8,128)S(1)}, f32[32,1280]{1,0:T(8,128)S(1)}, u32[]{:S(2)}, u32[]{:S(2)}) collective-permute-start(f32[32,1280]{1,0:T(8,128)S(1)} %get-tuple-element.75), channel_id=1, source_target_pairs={{0,4},{1,5},{2,6},{3,7},{4,0},{5,1},{6,2},{7,3},{8,12},{9,13},{10,... | collective-permute-start | bytes 491528 | tf_op jit(solution)/shard_map/ppermute | solution.py:324
  52.3 0.9 %shard_map.52 = (f32[64,1280]{1,0:T(8,128)S(1)}, f32[64,128]{1,0:T(8,128)S(1)}, f32[64,512]{1,0:T(8,128)S(1)}) custom-call(f32[32,1408]{1,0:T(8,128)S(1)} %add.59.refs_0_, f32[32,1408]{1,0:T(8,128)S(1)} %collective-permute-done.25.refs_1_, bf16[2,2560,256]{2,1,0:T(8,128)(2,1)S(1)} %get-tuple-element.59.refs_8_.refs_2_.refs_10_.refs_11_, ...), custom_call_target="tpu_custom_call" | custom-call | flops 1006632960 | bytes 10846208 | tf_op jit(solution)/shard_map/pallas_call | solution.py:30
  53.2 1.8 %shard_map.53 = (f32[64,1280]{1,0:T(8,128)S(1)}, f32[64,128]{1,0:T(8,128)S(1)}, f32[64,512]{1,0:T(8,128)S(1)}, f32[64,512]{1,0:T(8,128)S(1)}, f32[32,1408]{1,0:T(8,128)S(1)}, /*index=5*/f32[32,1408]{1,0:T(8,128)S(1)}) custom-call(f32[32,1280]{1,0:T(8,128)S(1)} %add.57.refs_0_, f32[32,1280]{1,0:T(8,128)S(1)} %collective-permute-done.22.refs_1_, ...), custom_call_target="tpu_custom_call" | custom-call | flops 20132659200 | bytes 21921792 | tf_op jit(solution)/shard_map/pallas_call | solution.py:30
  55.0 1.3 %collective-permute-start.29 = (f32[32,1408]{1,0:T(8,128)S(1)}, f32[32,1408]{1,0:T(8,128)S(1)}, u32[]{:S(2)}, u32[]{:S(2)}) collective-permute-start(f32[32,1408]{1,0:T(8,128)S(1)} %get-tuple-element.99), channel_id=1, source_target_pairs={{0,4},{1,5},{2,6},{3,7},{4,0},{5,1},{6,2},{7,3},{8,12},{9,13},{10,... | collective-permute-start | bytes 540680 | tf_op jit(solution)/shard_map/ppermute | solution.py:324
  56.4 0.9 %shard_map.54 = (f32[32,1280]{1,0:T(8,128)S(1)}, f32[32,1280]{1,0:T(8,128)S(1)}) custom-call(f32[64,512]{1,0:T(8,128)S(1)} %get-tuple-element.94.refs_0_.refs_10_, bf16[2,256,2560]{2,1,0:T(8,128)(2,1)S(1)} %get-tuple-element.55.refs_4_.refs_1_.refs_6_, bf16[2,256,2560]{2,1,0:T(8,128)(2,1)S(1)} %get-tuple-element.56.refs_5_.refs_2_.refs_7_, ...), custom_call_target="tpu_custom_call" | custom-call | flops 301989888 | bytes 10616832 | tf_op jit(solution)/shard_map/pallas_call | solution.py:30
  57.3 1.5 %collective-permute-start.26 = (f32[32,1280]{1,0:T(8,128)S(1)}, f32[32,1280]{1,0:T(8,128)S(1)}, u32[]{:S(2)}, u32[]{:S(2)}) collective-permute-start(f32[32,1280]{1,0:T(8,128)S(1)} %get-tuple-element.96), channel_id=1, source_target_pairs={{0,2},{1,3},{2,0},{3,1},{4,6},{5,7},{6,4},{7,5},{8,10},{9,11},{10,... | collective-permute-start | bytes 491528 | tf_op jit(solution)/shard_map/ppermute | solution.py:324
  58.9 0.6 collective-permute-start.14
  59.5 1.1 %collective-permute-start.11 = (f32[32,1280]{1,0:T(8,128)S(1)}, f32[32,1280]{1,0:T(8,128)S(1)}, u32[]{:S(2)}, u32[]{:S(2)}) collective-permute-start(f32[32,1280]{1,0:T(8,128)S(1)} %add.52), channel_id=1, source_target_pairs={{0,2},{1,3},{2,0},{3,1},{4,6},{5,7},{6,4},{7,5},{8,10},{9,11},{10,... | collective-permute-start | bytes 491528 | tf_op jit(solution)/shard_map/ppermute | solution.py:324
  60.6 1.3 %collective-permute-done.29 = f32[32,1408]{1,0:T(8,128)S(1)} collective-permute-done((f32[32,1408]{1,0:T(8,128)S(1)}, f32[32,1408]{1,0:T(8,128)S(1)}, u32[]{:S(2)}, u32[]{:S(2)}) %collective-permute-start.29) | collective-permute-done | bytes 180256 | tf_op jit(solution)/shard_map/ppermute | solution.py:324
  61.9 1.7 %collective-permute-start.30 = (f32[32,1408]{1,0:T(8,128)S(1)}, f32[32,1408]{1,0:T(8,128)S(1)}, u32[]{:S(2)}, u32[]{:S(2)}) collective-permute-start(f32[32,1408]{1,0:T(8,128)S(1)} %add.62), channel_id=1, source_target_pairs={{0,2},{1,3},{2,0},{3,1},{4,6},{5,7},{6,4},{7,5},{8,10},{9,11},{10,... | collective-permute-start | bytes 540680 | tf_op jit(solution)/shard_map/ppermute | solution.py:324
  63.6 0.7 collective-permute-done.26
  64.3 1.1 %collective-permute-start.27 = (f32[32,1280]{1,0:T(8,128)S(1)}, f32[32,1280]{1,0:T(8,128)S(1)}, u32[]{:S(2)}, u32[]{:S(2)}) collective-permute-start(f32[32,1280]{1,0:T(8,128)S(1)} %add.60), channel_id=1, source_target_pairs={{0,4},{1,5},{2,6},{3,7},{4,0},{5,1},{6,2},{7,3},{8,12},{9,13},{10,... | collective-permute-start | bytes 491528 | tf_op jit(solution)/shard_map/ppermute | solution.py:324
  65.4 0.9 %collective-permute-done.14 = f32[32,1408]{1,0:T(8,128)S(1)} collective-permute-done((f32[32,1408]{1,0:T(8,128)S(1)}, f32[32,1408]{1,0:T(8,128)S(1)}, u32[]{:S(2)}, u32[]{:S(2)}) %collective-permute-start.14) | collective-permute-done | bytes 180256 | tf_op jit(solution)/shard_map/ppermute | solution.py:324
  66.3 1.1 %collective-permute-start.15 = (f32[32,1408]{1,0:T(8,128)S(1)}, f32[32,1408]{1,0:T(8,128)S(1)}, u32[]{:S(2)}, u32[]{:S(2)}) collective-permute-start(f32[32,1408]{1,0:T(8,128)S(1)} %add.55.refs_0_), channel_id=1, source_target_pairs={{0,2},{1,3},{2,0},{3,1},{4,6},{5,7},{6,4},{7,5},{8,10},{9,11},{10,... | collective-permute-start | bytes 540680 | tf_op jit(solution)/shard_map/ppermute | solution.py:324
  67.5 1.8 %collective-permute-start.12 = (f32[32,1280]{1,0:T(8,128)S(1)}, f32[32,1280]{1,0:T(8,128)S(1)}, u32[]{:S(2)}, u32[]{:S(2)}) collective-permute-start(f32[32,1280]{1,0:T(8,128)S(1)} %add.53.refs_0_), channel_id=1, source_target_pairs={{0,4},{1,5},{2,6},{3,7},{4,0},{5,1},{6,2},{7,3},{8,12},{9,13},{10,... | collective-permute-start | bytes 491528 | tf_op jit(solution)/shard_map/ppermute | solution.py:324
  69.3 0.8 collective-permute-done.30
  70.1 1.0 %collective-permute-start.31 = (f32[32,1408]{1,0:T(8,128)S(1)}, f32[32,1408]{1,0:T(8,128)S(1)}, u32[]{:S(2)}, u32[]{:S(2)}) collective-permute-start(f32[32,1408]{1,0:T(8,128)S(1)} %add.63.refs_0_), channel_id=1, source_target_pairs={{0,4},{1,5},{2,6},{3,7},{4,0},{5,1},{6,2},{7,3},{8,12},{9,13},{10,... | collective-permute-start | bytes 540680 | tf_op jit(solution)/shard_map/ppermute | solution.py:324
  71.2 1.1 %collective-permute-start.28 = (f32[32,1280]{1,0:T(8,128)S(1)}, f32[32,1280]{1,0:T(8,128)S(1)}, u32[]{:S(2)}, u32[]{:S(2)}) collective-permute-start(f32[32,1280]{1,0:T(8,128)S(1)} %add.61.refs_0_), channel_id=1, source_target_pairs={{0,2},{1,3},{2,0},{3,1},{4,6},{5,7},{6,4},{7,5},{8,10},{9,11},{10,... | collective-permute-start | bytes 491528 | tf_op jit(solution)/shard_map/ppermute | solution.py:324
  72.2 0.9 %shard_map.48 = (f32[64,1280]{1,0:T(8,128)S(1)}, f32[64,128]{1,0:T(8,128)S(1)}, f32[64,512]{1,0:T(8,128)S(1)}) custom-call(f32[32,1408]{1,0:T(8,128)S(1)} %add.55.refs_0_, f32[32,1408]{1,0:T(8,128)S(1)} %collective-permute-done.15.refs_1_, bf16[2,2560,256]{2,1,0:T(8,128)(2,1)S(1)} %get-tuple-element.59.refs_8_.refs_2_.refs_10_.refs_11_, ...), custom_call_target="tpu_custom_call" | custom-call | bytes 10846208 | tf_op jit(solution)/shard_map/pallas_call | solution.py:30
  73.2 1.0 %shard_map.49 = (f32[2,64,256]{2,1,0:T(8,128)S(1)}, f32[2,64,256]{2,1,0:T(8,128)S(1)}) custom-call(f32[32,1280]{1,0:T(8,128)S(1)} %add.53.refs_0_, f32[32,1280]{1,0:T(8,128)S(1)} %collective-permute-done.12.refs_1_, f32[64,1280]{1,0:T(8,128)S(1)} %get-tuple-element.78.refs_2_, f32[64,128]{1,0:T(8,128)S(1)} %get-tuple-element.79.refs_3_, ...), custom_call_target="tpu_custom_call" | custom-call | flops 1006632960 | bytes 12386304 | tf_op jit(solution)/shard_map/pallas_call | solution.py:30
  74.2 0.1 collective-permute-start.16
  74.3 1.4 %collective-permute-done.31.refs_1_ = f32[32,1408]{1,0:T(8,128)S(1)} collective-permute-done((f32[32,1408]{1,0:T(8,128)S(1)}, f32[32,1408]{1,0:T(8,128)S(1)}, u32[]{:S(2)}, u32[]{:S(2)}) %collective-permute-start.31) | collective-permute-done | bytes 180256 | tf_op jit(solution)/shard_map/ppermute | solution.py:324
  75.7 0.9 %shard_map.55 = (f32[64,1280]{1,0:T(8,128)S(1)}, f32[64,128]{1,0:T(8,128)S(1)}, f32[64,512]{1,0:T(8,128)S(1)}) custom-call(f32[32,1408]{1,0:T(8,128)S(1)} %add.63.refs_0_, f32[32,1408]{1,0:T(8,128)S(1)} %collective-permute-done.31.refs_1_, bf16[2,2560,256]{2,1,0:T(8,128)(2,1)S(1)} %get-tuple-element.59.refs_8_.refs_2_.refs_10_.refs_11_, ...), custom_call_target="tpu_custom_call" | custom-call | bytes 10846208 | tf_op jit(solution)/shard_map/pallas_call | solution.py:30
  76.6 1.0 %shard_map.56 = (f32[2,64,256]{2,1,0:T(8,128)S(1)}, f32[2,64,256]{2,1,0:T(8,128)S(1)}) custom-call(f32[32,1280]{1,0:T(8,128)S(1)} %add.61.refs_0_, f32[32,1280]{1,0:T(8,128)S(1)} %collective-permute-done.28.refs_1_, f32[64,1280]{1,0:T(8,128)S(1)} %get-tuple-element.100.refs_2_, f32[64,128]{1,0:T(8,128)S(1)} %get-tuple-element.101.refs_3_, ...), custom_call_target="tpu_custom_call" | custom-call | flops 1006632960 | bytes 12386304 | tf_op jit(solution)/shard_map/pallas_call | solution.py:30
  77.7 1.3 %collective-permute-done.32.refs_3_ = f32[2,64,256]{2,1,0:T(8,128)S(1)} collective-permute-done((f32[2,64,256]{2,1,0:T(8,128)S(1)}, f32[2,64,256]{2,1,0:T(8,128)S(1)}, u32[]{:S(2)}, u32[]{:S(2)}) %collective-permute-start.32) | collective-permute-done | bytes 131104 | tf_op jit(solution)/shard_map/ppermute | solution.py:324
  79.0 0.9 %shard_map.57 = (f32[2,256,128]{2,1,0:T(8,128)}, f32[2,256,128]{2,1,0:T(8,128)}) custom-call(f32[2,64,256]{2,1,0:T(8,128)S(1)} %get-tuple-element.84.refs_0_, f32[2,64,256]{2,1,0:T(8,128)S(1)} %collective-permute-done.16.refs_1_, f32[2,64,256]{2,1,0:T(8,128)S(1)} %get-tuple-element.106.refs_2_, f32[2,64,256]{2,1,0:T(8,128)S(1)} %collective-permute-done.32.refs_3_), custom_call_target="tpu_custom_call" | custom-call | bytes 524288 | tf_op jit(solution)/shard_map/pallas_call | solution.py:30
  (38 shorter events, 0.5 us)
Async XLA Ops:
  0.6 13.4 %collective-permute-start.3 = (f32[2,256,2560]{2,1,0:T(8,128)}, f32[2,256,2560]{2,1,0:T(8,128)S(1)}, u32[]{:S(2)}, u32[]{:S(2)}) collective-permute-start(f32[2,256,2560]{2,1,0:T(8,128)} %down_ref.1), channel_id=1, source_target_pairs={{0,1},{1,0},{2,3},{3,2},{4,5},{5,4},{6,7},{7,6},{8,9},{9,8},{10,11... | collective-permute-start | bytes 15728648 | tf_op jit(solution)/shard_map/ppermute | solution.py:324
  2.2 14.8 %collective-permute-start.2 = (f32[2,8,2560]{2,1,0:T(8,128)S(1)}, f32[2,8,2560]{2,1,0:T(8,128)S(1)}, u32[]{:S(2)}, u32[]{:S(2)}) collective-permute-start(f32[2,8,2560]{2,1,0:T(8,128)S(1)} %get-tuple-element.109.refs_0_), channel_id=1, source_target_pairs={{0,6},{1,7},{2,4},{3,5},{4,2},{5,3},{6,0},{7,1},{8,14},{9,15},{10,... | collective-permute-start | bytes 491528 | tf_op jit(solution)/shard_map/ppermute | solution.py:327
  5.7 11.5 %collective-permute-start.1 = (f32[2,8,2560]{2,1,0:T(8,128)S(1)}, f32[2,8,2560]{2,1,0:T(8,128)S(1)}, u32[]{:S(2)}, u32[]{:S(2)}) collective-permute-start(f32[2,8,2560]{2,1,0:T(8,128)S(1)} %get-tuple-element.109.refs_0_), channel_id=1, source_target_pairs={{0,4},{1,5},{2,6},{3,7},{4,0},{5,1},{6,2},{7,3},{8,12},{9,13},{10,... | collective-permute-start | bytes 491528 | tf_op jit(solution)/shard_map/ppermute | solution.py:327
  6.2 11.0 %collective-permute-start = (f32[2,8,2560]{2,1,0:T(8,128)S(1)}, f32[2,8,2560]{2,1,0:T(8,128)S(1)}, u32[]{:S(2)}, u32[]{:S(2)}) collective-permute-start(f32[2,8,2560]{2,1,0:T(8,128)S(1)} %get-tuple-element.109.refs_0_), channel_id=1, source_target_pairs={{0,2},{1,3},{2,0},{3,1},{4,6},{5,7},{6,4},{7,5},{8,10},{9,11},{10,... | collective-permute-start | bytes 491528 | tf_op jit(solution)/shard_map/ppermute | solution.py:327
  6.3 17.9 %collective-permute-start.19 = (f32[2,8,2560]{2,1,0:T(8,128)S(1)}, f32[2,8,2560]{2,1,0:T(8,128)S(1)}, u32[]{:S(2)}, u32[]{:S(2)}) collective-permute-start(f32[2,8,2560]{2,1,0:T(8,128)S(1)} %get-tuple-element.108.refs_0_), channel_id=1, source_target_pairs={{0,6},{1,7},{2,4},{3,5},{4,2},{5,3},{6,0},{7,1},{8,14},{9,15},{10,... | collective-permute-start | bytes 491528 | tf_op jit(solution)/shard_map/ppermute | solution.py:327
  9.2 2.5 %copy-start = (f32[2,256,2560]{2,1,0:T(8,128)S(1)}, f32[2,256,2560]{2,1,0:T(8,128)}, u32[]{:S(2)}) copy-start(f32[2,256,2560]{2,1,0:T(8,128)} %down_ref.1) | copy-start | bytes 15728644
  14.1 10.2 %collective-permute-start.18 = (f32[2,8,2560]{2,1,0:T(8,128)S(1)}, f32[2,8,2560]{2,1,0:T(8,128)S(1)}, u32[]{:S(2)}, u32[]{:S(2)}) collective-permute-start(f32[2,8,2560]{2,1,0:T(8,128)S(1)} %get-tuple-element.108.refs_0_), channel_id=1, source_target_pairs={{0,4},{1,5},{2,6},{3,7},{4,0},{5,1},{6,2},{7,3},{8,12},{9,13},{10,... | collective-permute-start | bytes 491528 | tf_op jit(solution)/shard_map/ppermute | solution.py:327
  17.0 7.3 %collective-permute-start.17 = (f32[2,8,2560]{2,1,0:T(8,128)S(1)}, f32[2,8,2560]{2,1,0:T(8,128)S(1)}, u32[]{:S(2)}, u32[]{:S(2)}) collective-permute-start(f32[2,8,2560]{2,1,0:T(8,128)S(1)} %get-tuple-element.108.refs_0_), channel_id=1, source_target_pairs={{0,2},{1,3},{2,0},{3,1},{4,6},{5,7},{6,4},{7,5},{8,10},{9,11},{10,... | collective-permute-start | bytes 491528 | tf_op jit(solution)/shard_map/ppermute | solution.py:327
  19.8 7.7 %collective-permute-start.7 = (f32[32,1408]{1,0:T(8,128)S(1)}, f32[32,1408]{1,0:T(8,128)S(1)}, u32[]{:S(2)}, u32[]{:S(2)}) collective-permute-start(f32[32,1408]{1,0:T(8,128)S(1)} %get-tuple-element.69), channel_id=1, source_target_pairs={{0,2},{1,3},{2,0},{3,1},{4,6},{5,7},{6,4},{7,5},{8,10},{9,11},{10,... | collective-permute-start | bytes 540680 | tf_op jit(solution)/shard_map/ppermute | solution.py:324
  22.7 7.9 %collective-permute-start.4 = (f32[32,1280]{1,0:T(8,128)S(1)}, f32[32,1280]{1,0:T(8,128)S(1)}, u32[]{:S(2)}, u32[]{:S(2)}) collective-permute-start(f32[32,1280]{1,0:T(8,128)S(1)} %get-tuple-element.67), channel_id=1, source_target_pairs={{0,4},{1,5},{2,6},{3,7},{4,0},{5,1},{6,2},{7,3},{8,12},{9,13},{10,... | collective-permute-start | bytes 491528 | tf_op jit(solution)/shard_map/ppermute | solution.py:324
  26.9 7.0 %collective-permute-start.23 = (f32[32,1408]{1,0:T(8,128)S(1)}, f32[32,1408]{1,0:T(8,128)S(1)}, u32[]{:S(2)}, u32[]{:S(2)}) collective-permute-start(f32[32,1408]{1,0:T(8,128)S(1)} %get-tuple-element.90), channel_id=1, source_target_pairs={{0,4},{1,5},{2,6},{3,7},{4,0},{5,1},{6,2},{7,3},{8,12},{9,13},{10,... | collective-permute-start | bytes 540680 | tf_op jit(solution)/shard_map/ppermute | solution.py:324
  27.5 8.3 %collective-permute-start.8 = (f32[32,1408]{1,0:T(8,128)S(1)}, f32[32,1408]{1,0:T(8,128)S(1)}, u32[]{:S(2)}, u32[]{:S(2)}) collective-permute-start(f32[32,1408]{1,0:T(8,128)S(1)} %add.50), channel_id=1, source_target_pairs={{0,4},{1,5},{2,6},{3,7},{4,0},{5,1},{6,2},{7,3},{8,12},{9,13},{10,... | collective-permute-start | bytes 540680 | tf_op jit(solution)/shard_map/ppermute | solution.py:324
  30.0 7.2 %collective-permute-start.20 = (f32[32,1280]{1,0:T(8,128)S(1)}, f32[32,1280]{1,0:T(8,128)S(1)}, u32[]{:S(2)}, u32[]{:S(2)}) collective-permute-start(f32[32,1280]{1,0:T(8,128)S(1)} %get-tuple-element.88), channel_id=1, source_target_pairs={{0,2},{1,3},{2,0},{3,1},{4,6},{5,7},{6,4},{7,5},{8,10},{9,11},{10,... | collective-permute-start | bytes 491528 | tf_op jit(solution)/shard_map/ppermute | solution.py:324
  30.6 10.1 %collective-permute-start.5 = (f32[32,1280]{1,0:T(8,128)S(1)}, f32[32,1280]{1,0:T(8,128)S(1)}, u32[]{:S(2)}, u32[]{:S(2)}) collective-permute-start(f32[32,1280]{1,0:T(8,128)S(1)} %add.48), channel_id=1, source_target_pairs={{0,2},{1,3},{2,0},{3,1},{4,6},{5,7},{6,4},{7,5},{8,10},{9,11},{10,... | collective-permute-start | bytes 491528 | tf_op jit(solution)/shard_map/ppermute | solution.py:324
  33.9 10.4 %collective-permute-start.24 = (f32[32,1408]{1,0:T(8,128)S(1)}, f32[32,1408]{1,0:T(8,128)S(1)}, u32[]{:S(2)}, u32[]{:S(2)}) collective-permute-start(f32[32,1408]{1,0:T(8,128)S(1)} %add.58), channel_id=1, source_target_pairs={{0,2},{1,3},{2,0},{3,1},{4,6},{5,7},{6,4},{7,5},{8,10},{9,11},{10,... | collective-permute-start | bytes 540680 | tf_op jit(solution)/shard_map/ppermute | solution.py:324
  35.8 11.0 %collective-permute-start.9 = (f32[32,1408]{1,0:T(8,128)S(1)}, f32[32,1408]{1,0:T(8,128)S(1)}, u32[]{:S(2)}, u32[]{:S(2)}) collective-permute-start(f32[32,1408]{1,0:T(8,128)S(1)} %add.51.refs_0_), channel_id=1, source_target_pairs={{0,2},{1,3},{2,0},{3,1},{4,6},{5,7},{6,4},{7,5},{8,10},{9,11},{10,... | collective-permute-start | bytes 540680 | tf_op jit(solution)/shard_map/ppermute | solution.py:324
  37.2 5.4 %collective-permute-start.21 = (f32[32,1280]{1,0:T(8,128)S(1)}, f32[32,1280]{1,0:T(8,128)S(1)}, u32[]{:S(2)}, u32[]{:S(2)}) collective-permute-start(f32[32,1280]{1,0:T(8,128)S(1)} %add.56), channel_id=1, source_target_pairs={{0,4},{1,5},{2,6},{3,7},{4,0},{5,1},{6,2},{7,3},{8,12},{9,13},{10,... | collective-permute-start | bytes 491528 | tf_op jit(solution)/shard_map/ppermute | solution.py:324
  40.7 7.0 %collective-permute-start.6 = (f32[32,1280]{1,0:T(8,128)S(1)}, f32[32,1280]{1,0:T(8,128)S(1)}, u32[]{:S(2)}, u32[]{:S(2)}) collective-permute-start(f32[32,1280]{1,0:T(8,128)S(1)} %add.49.refs_0_), channel_id=1, source_target_pairs={{0,4},{1,5},{2,6},{3,7},{4,0},{5,1},{6,2},{7,3},{8,12},{9,13},{10,... | collective-permute-start | bytes 491528 | tf_op jit(solution)/shard_map/ppermute | solution.py:324
  42.7 10.5 %collective-permute-start.22 = (f32[32,1280]{1,0:T(8,128)S(1)}, f32[32,1280]{1,0:T(8,128)S(1)}, u32[]{:S(2)}, u32[]{:S(2)}) collective-permute-start(f32[32,1280]{1,0:T(8,128)S(1)} %add.57.refs_0_), channel_id=1, source_target_pairs={{0,2},{1,3},{2,0},{3,1},{4,6},{5,7},{6,4},{7,5},{8,10},{9,11},{10,... | collective-permute-start | bytes 491528 | tf_op jit(solution)/shard_map/ppermute | solution.py:324
  44.3 7.9 %collective-permute-start.25 = (f32[32,1408]{1,0:T(8,128)S(1)}, f32[32,1408]{1,0:T(8,128)S(1)}, u32[]{:S(2)}, u32[]{:S(2)}) collective-permute-start(f32[32,1408]{1,0:T(8,128)S(1)} %add.59.refs_0_), channel_id=1, source_target_pairs={{0,4},{1,5},{2,6},{3,7},{4,0},{5,1},{6,2},{7,3},{8,12},{9,13},{10,... | collective-permute-start | bytes 540680 | tf_op jit(solution)/shard_map/ppermute | solution.py:324
  49.6 9.2 %collective-permute-start.13 = (f32[32,1408]{1,0:T(8,128)S(1)}, f32[32,1408]{1,0:T(8,128)S(1)}, u32[]{:S(2)}, u32[]{:S(2)}) collective-permute-start(f32[32,1408]{1,0:T(8,128)S(1)} %get-tuple-element.77), channel_id=1, source_target_pairs={{0,2},{1,3},{2,0},{3,1},{4,6},{5,7},{6,4},{7,5},{8,10},{9,11},{10,... | collective-permute-start | bytes 540680 | tf_op jit(solution)/shard_map/ppermute | solution.py:324
  51.2 8.2 %collective-permute-start.10 = (f32[32,1280]{1,0:T(8,128)S(1)}, f32[32,1280]{1,0:T(8,128)S(1)}, u32[]{:S(2)}, u32[]{:S(2)}) collective-permute-start(f32[32,1280]{1,0:T(8,128)S(1)} %get-tuple-element.75), channel_id=1, source_target_pairs={{0,4},{1,5},{2,6},{3,7},{4,0},{5,1},{6,2},{7,3},{8,12},{9,13},{10,... | collective-permute-start | bytes 491528 | tf_op jit(solution)/shard_map/ppermute | solution.py:324
  55.0 6.8 %collective-permute-start.29 = (f32[32,1408]{1,0:T(8,128)S(1)}, f32[32,1408]{1,0:T(8,128)S(1)}, u32[]{:S(2)}, u32[]{:S(2)}) collective-permute-start(f32[32,1408]{1,0:T(8,128)S(1)} %get-tuple-element.99), channel_id=1, source_target_pairs={{0,4},{1,5},{2,6},{3,7},{4,0},{5,1},{6,2},{7,3},{8,12},{9,13},{10,... | collective-permute-start | bytes 540680 | tf_op jit(solution)/shard_map/ppermute | solution.py:324
  57.3 7.0 %collective-permute-start.26 = (f32[32,1280]{1,0:T(8,128)S(1)}, f32[32,1280]{1,0:T(8,128)S(1)}, u32[]{:S(2)}, u32[]{:S(2)}) collective-permute-start(f32[32,1280]{1,0:T(8,128)S(1)} %get-tuple-element.96), channel_id=1, source_target_pairs={{0,2},{1,3},{2,0},{3,1},{4,6},{5,7},{6,4},{7,5},{8,10},{9,11},{10,... | collective-permute-start | bytes 491528 | tf_op jit(solution)/shard_map/ppermute | solution.py:324
  58.9 7.4 %collective-permute-start.14 = (f32[32,1408]{1,0:T(8,128)S(1)}, f32[32,1408]{1,0:T(8,128)S(1)}, u32[]{:S(2)}, u32[]{:S(2)}) collective-permute-start(f32[32,1408]{1,0:T(8,128)S(1)} %add.54), channel_id=1, source_target_pairs={{0,4},{1,5},{2,6},{3,7},{4,0},{5,1},{6,2},{7,3},{8,12},{9,13},{10,... | collective-permute-start | bytes 540680 | tf_op jit(solution)/shard_map/ppermute | solution.py:324
  59.5 8.0 %collective-permute-start.11 = (f32[32,1280]{1,0:T(8,128)S(1)}, f32[32,1280]{1,0:T(8,128)S(1)}, u32[]{:S(2)}, u32[]{:S(2)}) collective-permute-start(f32[32,1280]{1,0:T(8,128)S(1)} %add.52), channel_id=1, source_target_pairs={{0,2},{1,3},{2,0},{3,1},{4,6},{5,7},{6,4},{7,5},{8,10},{9,11},{10,... | collective-permute-start | bytes 491528 | tf_op jit(solution)/shard_map/ppermute | solution.py:324
  61.9 8.2 %collective-permute-start.30 = (f32[32,1408]{1,0:T(8,128)S(1)}, f32[32,1408]{1,0:T(8,128)S(1)}, u32[]{:S(2)}, u32[]{:S(2)}) collective-permute-start(f32[32,1408]{1,0:T(8,128)S(1)} %add.62), channel_id=1, source_target_pairs={{0,2},{1,3},{2,0},{3,1},{4,6},{5,7},{6,4},{7,5},{8,10},{9,11},{10,... | collective-permute-start | bytes 540680 | tf_op jit(solution)/shard_map/ppermute | solution.py:324
  64.3 6.8 %collective-permute-start.27 = (f32[32,1280]{1,0:T(8,128)S(1)}, f32[32,1280]{1,0:T(8,128)S(1)}, u32[]{:S(2)}, u32[]{:S(2)}) collective-permute-start(f32[32,1280]{1,0:T(8,128)S(1)} %add.60), channel_id=1, source_target_pairs={{0,4},{1,5},{2,6},{3,7},{4,0},{5,1},{6,2},{7,3},{8,12},{9,13},{10,... | collective-permute-start | bytes 491528 | tf_op jit(solution)/shard_map/ppermute | solution.py:324
  66.3 5.9 %collective-permute-start.15 = (f32[32,1408]{1,0:T(8,128)S(1)}, f32[32,1408]{1,0:T(8,128)S(1)}, u32[]{:S(2)}, u32[]{:S(2)}) collective-permute-start(f32[32,1408]{1,0:T(8,128)S(1)} %add.55.refs_0_), channel_id=1, source_target_pairs={{0,2},{1,3},{2,0},{3,1},{4,6},{5,7},{6,4},{7,5},{8,10},{9,11},{10,... | collective-permute-start | bytes 540680 | tf_op jit(solution)/shard_map/ppermute | solution.py:324
  67.5 5.7 %collective-permute-start.12 = (f32[32,1280]{1,0:T(8,128)S(1)}, f32[32,1280]{1,0:T(8,128)S(1)}, u32[]{:S(2)}, u32[]{:S(2)}) collective-permute-start(f32[32,1280]{1,0:T(8,128)S(1)} %add.53.refs_0_), channel_id=1, source_target_pairs={{0,4},{1,5},{2,6},{3,7},{4,0},{5,1},{6,2},{7,3},{8,12},{9,13},{10,... | collective-permute-start | bytes 491528 | tf_op jit(solution)/shard_map/ppermute | solution.py:324
  70.1 5.6 %collective-permute-start.31 = (f32[32,1408]{1,0:T(8,128)S(1)}, f32[32,1408]{1,0:T(8,128)S(1)}, u32[]{:S(2)}, u32[]{:S(2)}) collective-permute-start(f32[32,1408]{1,0:T(8,128)S(1)} %add.63.refs_0_), channel_id=1, source_target_pairs={{0,4},{1,5},{2,6},{3,7},{4,0},{5,1},{6,2},{7,3},{8,12},{9,13},{10,... | collective-permute-start | bytes 540680 | tf_op jit(solution)/shard_map/ppermute | solution.py:324
  71.2 5.4 %collective-permute-start.28 = (f32[32,1280]{1,0:T(8,128)S(1)}, f32[32,1280]{1,0:T(8,128)S(1)}, u32[]{:S(2)}, u32[]{:S(2)}) collective-permute-start(f32[32,1280]{1,0:T(8,128)S(1)} %add.61.refs_0_), channel_id=1, source_target_pairs={{0,2},{1,3},{2,0},{3,1},{4,6},{5,7},{6,4},{7,5},{8,10},{9,11},{10,... | collective-permute-start | bytes 491528 | tf_op jit(solution)/shard_map/ppermute | solution.py:324
  74.2 3.5 %collective-permute-start.16 = (f32[2,64,256]{2,1,0:T(8,128)S(1)}, f32[2,64,256]{2,1,0:T(8,128)S(1)}, u32[]{:S(2)}, u32[]{:S(2)}) collective-permute-start(f32[2,64,256]{2,1,0:T(8,128)S(1)} %get-tuple-element.85), channel_id=1, source_target_pairs={{0,1},{1,0},{2,3},{3,2},{4,5},{5,4},{6,7},{7,6},{8,9},{9,8},{10,11... | collective-permute-start | bytes 393224 | tf_op jit(solution)/shard_map/ppermute | solution.py:324
  77.6 1.4 %collective-permute-start.32 = (f32[2,64,256]{2,1,0:T(8,128)S(1)}, f32[2,64,256]{2,1,0:T(8,128)S(1)}, u32[]{:S(2)}, u32[]{:S(2)}) collective-permute-start(f32[2,64,256]{2,1,0:T(8,128)S(1)} %get-tuple-element.107), channel_id=1, source_target_pairs={{0,1},{1,0},{2,3},{3,2},{4,5},{5,4},{6,7},{7,6},{8,9},{9,8},{10,11... | collective-permute-start | bytes 393224 | tf_op jit(solution)/shard_map/ppermute | solution.py:324

commit v8 on v7

--- a/solution.py
+++ b/solution.py
@@ -24,13 +24,12 @@
     return high, (value - high.astype(f32)).astype(bf16)
 
 
-def call(kernel, outs, args, scratch=(), flops=0, grid=(), in_specs=None):
+def call(kernel, outs, args, scratch=(), flops=0, in_specs=None):
     spec = pl.BlockSpec(memory_space=pltpu.VMEM)
     moved = sum(value.size * value.dtype.itemsize for value in args)
     return pl.pallas_call(
         kernel,
         out_shape=[jax.ShapeDtypeStruct(shape, dtype) for shape, dtype in outs],
-        grid=grid,
         in_specs=in_specs or [spec] * len(args),
         out_specs=[spec] * len(outs),
         scratch_shapes=[pltpu.VMEM(*item) if isinstance(item, tuple) else item for item in scratch],
@@ -39,9 +38,9 @@
     )(*args)
 
 
-def split_piece(value_of, part, at, places, high_ref, low_ref, turned_high_ref, turned_low_ref, energy_ref):
-    for source, place in places:
-        value = value_of(source)
+def split_piece(down_ref, part, at, places, high_ref, low_ref, turned_high_ref, turned_low_ref, energy_ref):
+    for place in places:
+        value = down_ref[part, at, place]
         rows, width = value.shape
         high, low = parts_of(value)
         high_ref[part, at, place] = high
@@ -52,69 +51,47 @@
         energy_ref[...] += sum(square[:, lane : lane + LANES] for lane in range(0, width, LANES))
 
 
-def split_kernel(real_ref, imag_ref, *outs):
-    rows, shots = real_ref.shape[1:]
-    step, chunk = pl.program_id(0), pl.program_id(1)
+def pieces_of(shape):
+    _, rows, shots = shape
+    block, width = min(rows, LANES), shots // 2
+    starts = [(row, start) for row in range(0, rows, block) for start in range(0, shots, width)]
+    return [(part, slice(row, row + block), slice(start, start + width)) for part in range(2) for row, start in starts]
+
+
+def places_of(shots):
     width = 2 * LANES
-    at = slice(None) if rows == outs[0].shape[1] else pl.ds(pl.multiple_of(step * rows, rows), rows)
-
-    @pl.when((step == 0) & (chunk == 0))
-    def _():
-        outs[4][...] = jnp.zeros_like(outs[4])
-
-    starts = range(0, shots, width)
-    places = [
-        (slice(start, start + width), pl.ds(pl.multiple_of(chunk * shots + start, width), width)) for start in starts
-    ]
-    for part, ref in enumerate((real_ref, imag_ref)):
-        split_piece(lambda place: ref[0, :, place], part, at, places, *outs)
+    return [slice(start, start + width) for start in range(shots.start, shots.stop, width)]
+
+
+def split_kernel(down_ref, *outs):
+    outs[4][...] = jnp.zeros_like(outs[4])
+    for part, at, shots in pieces_of(down_ref.shape):
+        split_piece(down_ref, part, at, places_of(shots), *outs)
 
 
 def fetch_split_kernel(down_ref, *refs):
     outs, (held_ref, sems) = refs[:5], refs[5:]
-    rows, shots = down_ref.shape[1:]
-    block, chunks, width = min(rows, LANES), 2, 2 * LANES
-    pieces = []
-    for part in range(2):
-        for row in range(0, rows, block):
-            for chunk in range(chunks):
-                start = chunk * shots // chunks
-                where = (part, slice(row, row + block), slice(start, start + shots // chunks))
-                copy = pltpu.make_async_copy(down_ref.at[where], held_ref.at[where], sems.at[len(pieces)])
-                copy.start()
-                pieces.append((copy, where))
+    copies = []
+    for where in pieces_of(down_ref.shape):
+        copies.append(pltpu.make_async_copy(down_ref.at[where], held_ref.at[where], sems.at[len(copies)]))
+        copies[-1].start()
     outs[4][...] = jnp.zeros_like(outs[4])
-    for copy, (part, at, where) in pieces:
+    for copy, (part, at, shots) in zip(copies, pieces_of(down_ref.shape)):
         copy.wait()
-        places = [(slice(start, start + width),) * 2 for start in range(where.start, where.stop, width)]
-        split_piece(lambda place: held_ref[part, at, place], part, at, places, *outs)
+        split_piece(held_ref, part, at, places_of(shots), *outs)
 
 
 def split(value, from_hbm=False):
     _, rows, shots = value.shape
-    block, chunks = min(rows, LANES), 2
     plain, turned = ((2, rows, shots), bf16), ((2, shots, rows), bf16)
     outs = [plain, plain, turned, turned, ((8, LANES), f32)]
     if from_hbm:
-        pieces = 2 * (rows // block) * chunks
-        high, low, turned_high, turned_low, energy = call(
-            fetch_split_kernel,
-            outs,
-            (value,),
-            [pltpu.VMEM(value.shape, f32), pltpu.SemaphoreType.DMA((pieces,))],
-            in_specs=[pl.BlockSpec(memory_space=pltpu.HBM)],
-        )
+        value = pltpu.with_memory_space_constraint(value, pltpu.HBM)
+        scratch = [pltpu.VMEM(value.shape, f32), pltpu.SemaphoreType.DMA((len(pieces_of(value.shape)),))]
+        specs = [pl.BlockSpec(memory_space=pltpu.HBM)]
+        high, low, turned_high, turned_low, energy = call(fetch_split_kernel, outs, (value,), scratch, in_specs=specs)
     else:
-        high, low, turned_high, turned_low, energy = call(
-            split_kernel,
-            outs,
-            (value, value),
-            grid=(rows // block, chunks),
-            in_specs=[
-                pl.BlockSpec((1, block, shots // chunks), lambda step, chunk: (0, step, chunk)),
-                pl.BlockSpec((1, block, shots // chunks), lambda step, chunk: (1, step, chunk)),
-            ],
-        )
+        high, low, turned_high, turned_low, energy = call(split_kernel, outs, (value,))
     return (high, low), (turned_high, turned_low), energy
 
 

time: 80.1 us -> 81.4 us (1.016)
  waiting for transfers between devices: 16 us -> 21.3 us
  local copies, waits for them, and re-layouts: 3.5 us -> 1.02 us
  starting transfers between devices: 35.2 us -> 33.7 us
    ppermute x27, waiting for transfers between devices: 16 us -> 21.1 us  [swap(): lax.ppermute(value, 'rcv', [(at, at ^ 1 << bit) for at in range(count)])]
    ppermute x27, starting transfers between devices: 27.4 us -> 24.8 us  [swap(): lax.ppermute(value, 'rcv', [(at, at ^ 1 << bit) for at in range(count)])]
    unnamed x2 -> x0, local copies, waits for them, and re-layouts: 2.49 us -> none
    ppermute x6, starting transfers between devices: 7.79 us -> 8.85 us  [jump(): lax.ppermute(value, 'rcv', [(at, at ^ mask << 1) for at in range(count)])]
  transfers between devices with their start and end apart: 33 -> 33, of which waited for: 13 -> 14; matrix products, arithmetic and copies ran while one was open for 2% -> 2% of each run, Pallas kernels for 29% -> 28%
where the time goes in v8:
time: 81.4 us; the launch traced here: 81.3 us
  starting transfers between devices  33.7 us (41%)
  Pallas kernels  24 us (29%)
  waiting for transfers between devices  21.3 us (26%)
  local copies, waits for them, and re-layouts  1.02 us (1%)
  between operations  0.92 us (1%)
    ppermute x27, starting transfers between devices, swap(): lax.ppermute(value, 'rcv', [(at, at ^ 1 << bit) for at in range(count)])  24.8 us
    pallas_call x17, Pallas kernels, call(): pl.pallas_call(kernel, out_shape=[jax.ShapeDtypeStruct(shape, dtype) for...  24 us
    ppermute x27, waiting for transfers between devices, swap(): lax.ppermute(value, 'rcv', [(at, at ^ 1 << bit) for at in range(count)])  21.1 us
    ppermute x6, starting transfers between devices, jump(): lax.ppermute(value, 'rcv', [(at, at ^ mask << 1) for at in range(count)])  8.85 us
  transfers between devices with their start and end apart: 33, of which 14 were waited for; matrix products, arithmetic and copies ran while one was open for 2% of the time, Pallas kernels for 28%

profile of v8, /device:TPU:0, one launch (start us, length us, event | category | flops | bytes accessed | tf_op | source)
XLA Modules:
  0.0 81.3 jit_solution(8086284955903758558)
XLA Ops:
  0.6 0.5 collective-permute-start.3
  1.1 1.0 %fusion = (f32[2,8,2560]{2,1,0:T(8,128)S(1)}, f32[2,8,2560]{2,1,0:T(8,128)S(1)}) fusion(f32[2,16,2560]{2,1,0:T(8,128)} %param.3), kind=kLoop, calls=%fused_computation | loop fusion | bytes 655360 | tf_op jit(solution)/shard_map/slice | solution.py:310
  2.2 3.5 %collective-permute-start.2 = (f32[2,8,2560]{2,1,0:T(8,128)S(1)}, f32[2,8,2560]{2,1,0:T(8,128)S(1)}, u32[]{:S(2)}, u32[]{:S(2)}) collective-permute-start(f32[2,8,2560]{2,1,0:T(8,128)S(1)} %get-tuple-element.109.refs_0_), channel_id=1, source_target_pairs={{0,6},{1,7},{2,4},{3,5},{4,2},{5,3},{6,0},{7,1},{8,14},{9,15},{10,... | collective-permute-start | bytes 491528 | tf_op jit(solution)/shard_map/ppermute | solution.py:304
  5.7 0.5 collective-permute-start.1
  6.2 0.1 collective-permute-start
  6.3 2.8 %collective-permute-start.19 = (f32[2,8,2560]{2,1,0:T(8,128)S(1)}, f32[2,8,2560]{2,1,0:T(8,128)S(1)}, u32[]{:S(2)}, u32[]{:S(2)}) collective-permute-start(f32[2,8,2560]{2,1,0:T(8,128)S(1)} %get-tuple-element.108.refs_0_), channel_id=1, source_target_pairs={{0,6},{1,7},{2,4},{3,5},{4,2},{5,3},{6,0},{7,1},{8,14},{9,15},{10,... | collective-permute-start | bytes 491528 | tf_op jit(solution)/shard_map/ppermute | solution.py:304
  9.2 3.0 %shard_map.41 = (bf16[2,256,2560]{2,1,0:T(8,128)(2,1)S(1)}, bf16[2,256,2560]{2,1,0:T(8,128)(2,1)S(1)}, bf16[2,2560,256]{2,1,0:T(8,128)(2,1)S(1)}, bf16[2,2560,256]{2,1,0:T(8,128)(2,1)S(1)}, f32[8,128]{1,0:T(8,128)S(1)}) custom-call(f32[2,256,2560]{2,1,0:T(8,128)} %down_ref.1), custom_call_target="tpu_custom_call" | custom-call | bytes 5242880 | tf_op jit(solution)/shard_map/pallas_call | solution.py:30
  12.2 0.6 collective-permute-start.18
  12.8 1.5 %shard_map.42 = (bf16[2,256,2560]{2,1,0:T(8,128)(2,1)S(1)}, bf16[2,256,2560]{2,1,0:T(8,128)(2,1)S(1)}, bf16[2,2560,256]{2,1,0:T(8,128)(2,1)S(1)}, bf16[2,2560,256]{2,1,0:T(8,128)(2,1)S(1)}, f32[8,128]{1,0:T(8,128)S(1)}) custom-call(f32[2,256,2560]{2,1,0:T(8,128)S(1)} %collective-permute-done.3.down_ref), custom_call_target="tpu_custom_call" | custom-call | bytes 5242880 | tf_op jit(solution)/shard_map/pallas_call | solution.py:30
  14.4 1.3 %collective-permute-start.17 = (f32[2,8,2560]{2,1,0:T(8,128)S(1)}, f32[2,8,2560]{2,1,0:T(8,128)S(1)}, u32[]{:S(2)}, u32[]{:S(2)}) collective-permute-start(f32[2,8,2560]{2,1,0:T(8,128)S(1)} %get-tuple-element.108.refs_0_), channel_id=1, source_target_pairs={{0,2},{1,3},{2,0},{3,1},{4,6},{5,7},{6,4},{7,5},{8,10},{9,11},{10,... | collective-permute-start | bytes 491528 | tf_op jit(solution)/shard_map/ppermute | solution.py:304
  15.7 2.6 %shard_map.43 = (f32[64,512]{1,0:T(8,128)S(1)}, f32[32,1408]{1,0:T(8,128)S(1)}, f32[32,1408]{1,0:T(8,128)S(1)}) custom-call(f32[2,8,2560]{2,1,0:T(8,128)S(1)} %get-tuple-element.109.refs_0_, f32[2,8,2560]{2,1,0:T(8,128)S(1)} %collective-permute-done.refs_1_, f32[2,8,2560]{2,1,0:T(8,128)S(1)} %collective-permute-done.1.refs_2_, ...), custom_call_target="tpu_custom_call" | custom-call | flops 90596966400 | bytes 21635072 | tf_op jit(solution)/shard_map/pallas_call | solution.py:30
  18.2 0.9 %collective-permute-start.7 = (f32[32,1408]{1,0:T(8,128)S(1)}, f32[32,1408]{1,0:T(8,128)S(1)}, u32[]{:S(2)}, u32[]{:S(2)}) collective-permute-start(f32[32,1408]{1,0:T(8,128)S(1)} %get-tuple-element.69), channel_id=1, source_target_pairs={{0,2},{1,3},{2,0},{3,1},{4,6},{5,7},{6,4},{7,5},{8,10},{9,11},{10,... | collective-permute-start | bytes 540680 | tf_op jit(solution)/shard_map/ppermute | solution.py:301
  19.1 0.9 %shard_map.44 = (f32[32,1280]{1,0:T(8,128)S(1)}, f32[32,1280]{1,0:T(8,128)S(1)}) custom-call(f32[64,512]{1,0:T(8,128)S(1)} %get-tuple-element.65.refs_0_.refs_5_, bf16[2,256,2560]{2,1,0:T(8,128)(2,1)S(1)} %get-tuple-element.55.refs_4_.refs_1_.refs_6_, bf16[2,256,2560]{2,1,0:T(8,128)(2,1)S(1)} %get-tuple-element.56.refs_5_.refs_2_.refs_7_, ...), custom_call_target="tpu_custom_call" | custom-call | flops 301989888 | bytes 10616832 | tf_op jit(solution)/shard_map/pallas_call | solution.py:30
  20.1 1.6 %collective-permute-start.4 = (f32[32,1280]{1,0:T(8,128)S(1)}, f32[32,1280]{1,0:T(8,128)S(1)}, u32[]{:S(2)}, u32[]{:S(2)}) collective-permute-start(f32[32,1280]{1,0:T(8,128)S(1)} %get-tuple-element.67), channel_id=1, source_target_pairs={{0,4},{1,5},{2,6},{3,7},{4,0},{5,1},{6,2},{7,3},{8,12},{9,13},{10,... | collective-permute-start | bytes 491528 | tf_op jit(solution)/shard_map/ppermute | solution.py:301
  21.7 0.2 collective-permute-done.17.refs_1_
  21.8 2.6 %shard_map.50 = (f32[64,512]{1,0:T(8,128)S(1)}, f32[32,1408]{1,0:T(8,128)S(1)}, f32[32,1408]{1,0:T(8,128)S(1)}) custom-call(f32[2,8,2560]{2,1,0:T(8,128)S(1)} %get-tuple-element.108.refs_0_, f32[2,8,2560]{2,1,0:T(8,128)S(1)} %collective-permute-done.17.refs_1_, f32[2,8,2560]{2,1,0:T(8,128)S(1)} %collective-permute-done.18.refs_2_, ...), custom_call_target="tpu_custom_call" | custom-call | flops 3019898880 | bytes 21635072 | tf_op jit(solution)/shard_map/pallas_call | solution.py:30
  24.4 1.0 %collective-permute-start.23 = (f32[32,1408]{1,0:T(8,128)S(1)}, f32[32,1408]{1,0:T(8,128)S(1)}, u32[]{:S(2)}, u32[]{:S(2)}) collective-permute-start(f32[32,1408]{1,0:T(8,128)S(1)} %get-tuple-element.90), channel_id=1, source_target_pairs={{0,4},{1,5},{2,6},{3,7},{4,0},{5,1},{6,2},{7,3},{8,12},{9,13},{10,... | collective-permute-start | bytes 540680 | tf_op jit(solution)/shard_map/ppermute | solution.py:301
  25.5 1.1 %collective-permute-start.8 = (f32[32,1408]{1,0:T(8,128)S(1)}, f32[32,1408]{1,0:T(8,128)S(1)}, u32[]{:S(2)}, u32[]{:S(2)}) collective-permute-start(f32[32,1408]{1,0:T(8,128)S(1)} %add.50), channel_id=1, source_target_pairs={{0,4},{1,5},{2,6},{3,7},{4,0},{5,1},{6,2},{7,3},{8,12},{9,13},{10,... | collective-permute-start | bytes 540680 | tf_op jit(solution)/shard_map/ppermute | solution.py:301
  26.6 0.9 %shard_map.51 = (f32[32,1280]{1,0:T(8,128)S(1)}, f32[32,1280]{1,0:T(8,128)S(1)}) custom-call(f32[64,512]{1,0:T(8,128)S(1)} %get-tuple-element.86.refs_0_.refs_5_, bf16[2,256,2560]{2,1,0:T(8,128)(2,1)S(1)} %get-tuple-element.55.refs_4_.refs_1_.refs_6_, bf16[2,256,2560]{2,1,0:T(8,128)(2,1)S(1)} %get-tuple-element.56.refs_5_.refs_2_.refs_7_, ...), custom_call_target="tpu_custom_call" | custom-call | bytes 10616832 | tf_op jit(solution)/shard_map/pallas_call | solution.py:30
  27.5 1.5 %collective-permute-start.20 = (f32[32,1280]{1,0:T(8,128)S(1)}, f32[32,1280]{1,0:T(8,128)S(1)}, u32[]{:S(2)}, u32[]{:S(2)}) collective-permute-start(f32[32,1280]{1,0:T(8,128)S(1)} %get-tuple-element.88), channel_id=1, source_target_pairs={{0,2},{1,3},{2,0},{3,1},{4,6},{5,7},{6,4},{7,5},{8,10},{9,11},{10,... | collective-permute-start | bytes 491528 | tf_op jit(solution)/shard_map/ppermute | solution.py:301
  29.1 0.6 collective-permute-start.5
  29.7 2.2 %collective-permute-done.23 = f32[32,1408]{1,0:T(8,128)S(1)} collective-permute-done((f32[32,1408]{1,0:T(8,128)S(1)}, f32[32,1408]{1,0:T(8,128)S(1)}, u32[]{:S(2)}, u32[]{:S(2)}) %collective-permute-start.23) | collective-permute-done | bytes 180256 | tf_op jit(solution)/shard_map/ppermute | solution.py:301
  32.0 1.6 %collective-permute-start.24 = (f32[32,1408]{1,0:T(8,128)S(1)}, f32[32,1408]{1,0:T(8,128)S(1)}, u32[]{:S(2)}, u32[]{:S(2)}) collective-permute-start(f32[32,1408]{1,0:T(8,128)S(1)} %add.58), channel_id=1, source_target_pairs={{0,2},{1,3},{2,0},{3,1},{4,6},{5,7},{6,4},{7,5},{8,10},{9,11},{10,... | collective-permute-start | bytes 540680 | tf_op jit(solution)/shard_map/ppermute | solution.py:301
  33.5 0.6 collective-permute-done.8
  34.1 1.6 %collective-permute-start.9 = (f32[32,1408]{1,0:T(8,128)S(1)}, f32[32,1408]{1,0:T(8,128)S(1)}, u32[]{:S(2)}, u32[]{:S(2)}) collective-permute-start(f32[32,1408]{1,0:T(8,128)S(1)} %add.51.refs_0_), channel_id=1, source_target_pairs={{0,2},{1,3},{2,0},{3,1},{4,6},{5,7},{6,4},{7,5},{8,10},{9,11},{10,... | collective-permute-start | bytes 540680 | tf_op jit(solution)/shard_map/ppermute | solution.py:301
  35.8 0.8 %collective-permute-start.21 = (f32[32,1280]{1,0:T(8,128)S(1)}, f32[32,1280]{1,0:T(8,128)S(1)}, u32[]{:S(2)}, u32[]{:S(2)}) collective-permute-start(f32[32,1280]{1,0:T(8,128)S(1)} %add.56), channel_id=1, source_target_pairs={{0,4},{1,5},{2,6},{3,7},{4,0},{5,1},{6,2},{7,3},{8,12},{9,13},{10,... | collective-permute-start | bytes 491528 | tf_op jit(solution)/shard_map/ppermute | solution.py:301
  36.6 1.7 %collective-permute-done.5 = f32[32,1280]{1,0:T(8,128)S(1)} collective-permute-done((f32[32,1280]{1,0:T(8,128)S(1)}, f32[32,1280]{1,0:T(8,128)S(1)}, u32[]{:S(2)}, u32[]{:S(2)}) %collective-permute-start.5) | collective-permute-done | bytes 163872 | tf_op jit(solution)/shard_map/ppermute | solution.py:301
  38.3 1.1 %collective-permute-start.6 = (f32[32,1280]{1,0:T(8,128)S(1)}, f32[32,1280]{1,0:T(8,128)S(1)}, u32[]{:S(2)}, u32[]{:S(2)}) collective-permute-start(f32[32,1280]{1,0:T(8,128)S(1)} %add.49.refs_0_), channel_id=1, source_target_pairs={{0,4},{1,5},{2,6},{3,7},{4,0},{5,1},{6,2},{7,3},{8,12},{9,13},{10,... | collective-permute-start | bytes 491528 | tf_op jit(solution)/shard_map/ppermute | solution.py:301
  39.3 2.5 %collective-permute-done.21 = f32[32,1280]{1,0:T(8,128)S(1)} collective-permute-done((f32[32,1280]{1,0:T(8,128)S(1)}, f32[32,1280]{1,0:T(8,128)S(1)}, u32[]{:S(2)}, u32[]{:S(2)}) %collective-permute-start.21) | collective-permute-done | bytes 163872 | tf_op jit(solution)/shard_map/ppermute | solution.py:301
  41.9 1.0 %collective-permute-start.22 = (f32[32,1280]{1,0:T(8,128)S(1)}, f32[32,1280]{1,0:T(8,128)S(1)}, u32[]{:S(2)}, u32[]{:S(2)}) collective-permute-start(f32[32,1280]{1,0:T(8,128)S(1)} %add.57.refs_0_), channel_id=1, source_target_pairs={{0,2},{1,3},{2,0},{3,1},{4,6},{5,7},{6,4},{7,5},{8,10},{9,11},{10,... | collective-permute-start | bytes 491528 | tf_op jit(solution)/shard_map/ppermute | solution.py:301
  42.9 2.2 %collective-permute-start.25 = (f32[32,1408]{1,0:T(8,128)S(1)}, f32[32,1408]{1,0:T(8,128)S(1)}, u32[]{:S(2)}, u32[]{:S(2)}) collective-permute-start(f32[32,1408]{1,0:T(8,128)S(1)} %add.59.refs_0_), channel_id=1, source_target_pairs={{0,4},{1,5},{2,6},{3,7},{4,0},{5,1},{6,2},{7,3},{8,12},{9,13},{10,... | collective-permute-start | bytes 540680 | tf_op jit(solution)/shard_map/ppermute | solution.py:301
  45.1 0.3 collective-permute-done.9.refs_1_
  45.5 0.9 %shard_map.45 = (f32[64,1280]{1,0:T(8,128)S(1)}, f32[64,128]{1,0:T(8,128)S(1)}, f32[64,512]{1,0:T(8,128)S(1)}) custom-call(f32[32,1408]{1,0:T(8,128)S(1)} %add.51.refs_0_, f32[32,1408]{1,0:T(8,128)S(1)} %collective-permute-done.9.refs_1_, bf16[2,2560,256]{2,1,0:T(8,128)(2,1)S(1)} %get-tuple-element.59.refs_8_.refs_2_.refs_10_.refs_11_, ...), custom_call_target="tpu_custom_call" | custom-call | bytes 10846208 | tf_op jit(solution)/shard_map/pallas_call | solution.py:30
  46.4 2.0 %shard_map.46 = (f32[64,1280]{1,0:T(8,128)S(1)}, f32[64,128]{1,0:T(8,128)S(1)}, f32[64,512]{1,0:T(8,128)S(1)}, f32[64,512]{1,0:T(8,128)S(1)}, f32[32,1408]{1,0:T(8,128)S(1)}, /*index=5*/f32[32,1408]{1,0:T(8,128)S(1)}) custom-call(f32[32,1280]{1,0:T(8,128)S(1)} %add.49.refs_0_, f32[32,1280]{1,0:T(8,128)S(1)} %collective-permute-done.6.refs_1_, ...), custom_call_target="tpu_custom_call" | custom-call | flops 2013265920 | bytes 21921792 | tf_op jit(solution)/shard_map/pallas_call | solution.py:30
  48.4 1.6 %collective-permute-start.13 = (f32[32,1408]{1,0:T(8,128)S(1)}, f32[32,1408]{1,0:T(8,128)S(1)}, u32[]{:S(2)}, u32[]{:S(2)}) collective-permute-start(f32[32,1408]{1,0:T(8,128)S(1)} %get-tuple-element.77), channel_id=1, source_target_pairs={{0,2},{1,3},{2,0},{3,1},{4,6},{5,7},{6,4},{7,5},{8,10},{9,11},{10,... | collective-permute-start | bytes 540680 | tf_op jit(solution)/shard_map/ppermute | solution.py:301
  50.0 0.9 %shard_map.47 = (f32[32,1280]{1,0:T(8,128)S(1)}, f32[32,1280]{1,0:T(8,128)S(1)}) custom-call(f32[64,512]{1,0:T(8,128)S(1)} %get-tuple-element.73.refs_0_.refs_10_, bf16[2,256,2560]{2,1,0:T(8,128)(2,1)S(1)} %get-tuple-element.55.refs_4_.refs_1_.refs_6_, bf16[2,256,2560]{2,1,0:T(8,128)(2,1)S(1)} %get-tuple-element.56.refs_5_.refs_2_.refs_7_, ...), custom_call_target="tpu_custom_call" | custom-call | flops 3019898880 | bytes 10616832 | tf_op jit(solution)/shard_map/pallas_call | solution.py:30
  51.0 1.3 %collective-permute-start.10 = (f32[32,1280]{1,0:T(8,128)S(1)}, f32[32,1280]{1,0:T(8,128)S(1)}, u32[]{:S(2)}, u32[]{:S(2)}) collective-permute-start(f32[32,1280]{1,0:T(8,128)S(1)} %get-tuple-element.75), channel_id=1, source_target_pairs={{0,4},{1,5},{2,6},{3,7},{4,0},{5,1},{6,2},{7,3},{8,12},{9,13},{10,... | collective-permute-start | bytes 491528 | tf_op jit(solution)/shard_map/ppermute | solution.py:301
  52.3 0.9 %shard_map.52 = (f32[64,1280]{1,0:T(8,128)S(1)}, f32[64,128]{1,0:T(8,128)S(1)}, f32[64,512]{1,0:T(8,128)S(1)}) custom-call(f32[32,1408]{1,0:T(8,128)S(1)} %add.59.refs_0_, f32[32,1408]{1,0:T(8,128)S(1)} %collective-permute-done.25.refs_1_, bf16[2,2560,256]{2,1,0:T(8,128)(2,1)S(1)} %get-tuple-element.59.refs_8_.refs_2_.refs_10_.refs_11_, ...), custom_call_target="tpu_custom_call" | custom-call | flops 1006632960 | bytes 10846208 | tf_op jit(solution)/shard_map/pallas_call | solution.py:30
  53.3 1.8 %shard_map.53 = (f32[64,1280]{1,0:T(8,128)S(1)}, f32[64,128]{1,0:T(8,128)S(1)}, f32[64,512]{1,0:T(8,128)S(1)}, f32[64,512]{1,0:T(8,128)S(1)}, f32[32,1408]{1,0:T(8,128)S(1)}, /*index=5*/f32[32,1408]{1,0:T(8,128)S(1)}) custom-call(f32[32,1280]{1,0:T(8,128)S(1)} %add.57.refs_0_, f32[32,1280]{1,0:T(8,128)S(1)} %collective-permute-done.22.refs_1_, ...), custom_call_target="tpu_custom_call" | custom-call | flops 20132659200 | bytes 21921792 | tf_op jit(solution)/shard_map/pallas_call | solution.py:30
  55.1 0.8 %collective-permute-start.29 = (f32[32,1408]{1,0:T(8,128)S(1)}, f32[32,1408]{1,0:T(8,128)S(1)}, u32[]{:S(2)}, u32[]{:S(2)}) collective-permute-start(f32[32,1408]{1,0:T(8,128)S(1)} %get-tuple-element.99), channel_id=1, source_target_pairs={{0,4},{1,5},{2,6},{3,7},{4,0},{5,1},{6,2},{7,3},{8,12},{9,13},{10,... | collective-permute-start | bytes 540680 | tf_op jit(solution)/shard_map/ppermute | solution.py:301
  55.9 0.9 %shard_map.54 = (f32[32,1280]{1,0:T(8,128)S(1)}, f32[32,1280]{1,0:T(8,128)S(1)}) custom-call(f32[64,512]{1,0:T(8,128)S(1)} %get-tuple-element.94.refs_0_.refs_10_, bf16[2,256,2560]{2,1,0:T(8,128)(2,1)S(1)} %get-tuple-element.55.refs_4_.refs_1_.refs_6_, bf16[2,256,2560]{2,1,0:T(8,128)(2,1)S(1)} %get-tuple-element.56.refs_5_.refs_2_.refs_7_, ...), custom_call_target="tpu_custom_call" | custom-call | flops 301989888 | bytes 10616832 | tf_op jit(solution)/shard_map/pallas_call | solution.py:30
  56.9 0.5 collective-permute-start.26
  57.4 1.6 %collective-permute-start.14 = (f32[32,1408]{1,0:T(8,128)S(1)}, f32[32,1408]{1,0:T(8,128)S(1)}, u32[]{:S(2)}, u32[]{:S(2)}) collective-permute-start(f32[32,1408]{1,0:T(8,128)S(1)} %add.54), channel_id=1, source_target_pairs={{0,4},{1,5},{2,6},{3,7},{4,0},{5,1},{6,2},{7,3},{8,12},{9,13},{10,... | collective-permute-start | bytes 540680 | tf_op jit(solution)/shard_map/ppermute | solution.py:301
  59.0 1.4 %collective-permute-start.11 = (f32[32,1280]{1,0:T(8,128)S(1)}, f32[32,1280]{1,0:T(8,128)S(1)}, u32[]{:S(2)}, u32[]{:S(2)}) collective-permute-start(f32[32,1280]{1,0:T(8,128)S(1)} %add.52), channel_id=1, source_target_pairs={{0,2},{1,3},{2,0},{3,1},{4,6},{5,7},{6,4},{7,5},{8,10},{9,11},{10,... | collective-permute-start | bytes 491528 | tf_op jit(solution)/shard_map/ppermute | solution.py:301
  60.4 2.1 %collective-permute-done.29 = f32[32,1408]{1,0:T(8,128)S(1)} collective-permute-done((f32[32,1408]{1,0:T(8,128)S(1)}, f32[32,1408]{1,0:T(8,128)S(1)}, u32[]{:S(2)}, u32[]{:S(2)}) %collective-permute-start.29) | collective-permute-done | bytes 180256 | tf_op jit(solution)/shard_map/ppermute | solution.py:301
  62.6 0.1 collective-permute-start.30
  62.6 1.4 %collective-permute-done.26 = f32[32,1280]{1,0:T(8,128)S(1)} collective-permute-done((f32[32,1280]{1,0:T(8,128)S(1)}, f32[32,1280]{1,0:T(8,128)S(1)}, u32[]{:S(2)}, u32[]{:S(2)}) %collective-permute-start.26) | collective-permute-done | bytes 163872 | tf_op jit(solution)/shard_map/ppermute | solution.py:301
  64.0 0.8 %collective-permute-start.27 = (f32[32,1280]{1,0:T(8,128)S(1)}, f32[32,1280]{1,0:T(8,128)S(1)}, u32[]{:S(2)}, u32[]{:S(2)}) collective-permute-start(f32[32,1280]{1,0:T(8,128)S(1)} %add.60), channel_id=1, source_target_pairs={{0,4},{1,5},{2,6},{3,7},{4,0},{5,1},{6,2},{7,3},{8,12},{9,13},{10,... | collective-permute-start | bytes 491528 | tf_op jit(solution)/shard_map/ppermute | solution.py:301
  64.8 1.6 %collective-permute-done.14 = f32[32,1408]{1,0:T(8,128)S(1)} collective-permute-done((f32[32,1408]{1,0:T(8,128)S(1)}, f32[32,1408]{1,0:T(8,128)S(1)}, u32[]{:S(2)}, u32[]{:S(2)}) %collective-permute-start.14) | collective-permute-done | bytes 180256 | tf_op jit(solution)/shard_map/ppermute | solution.py:301
  66.5 1.0 %collective-permute-done.11 = f32[32,1280]{1,0:T(8,128)S(1)} collective-permute-done((f32[32,1280]{1,0:T(8,128)S(1)}, f32[32,1280]{1,0:T(8,128)S(1)}, u32[]{:S(2)}, u32[]{:S(2)}) %collective-permute-start.11) | collective-permute-done | bytes 163872 | tf_op jit(solution)/shard_map/ppermute | solution.py:301
  67.5 0.3 collective-permute-start.12
  67.9 3.5 %collective-permute-done.30 = f32[32,1408]{1,0:T(8,128)S(1)} collective-permute-done((f32[32,1408]{1,0:T(8,128)S(1)}, f32[32,1408]{1,0:T(8,128)S(1)}, u32[]{:S(2)}, u32[]{:S(2)}) %collective-permute-start.30) | collective-permute-done | bytes 180256 | tf_op jit(solution)/shard_map/ppermute | solution.py:301
  71.4 0.1 collective-permute-start.31
  71.5 0.5 collective-permute-start.28
  72.1 1.3 %collective-permute-done.15.refs_1_ = f32[32,1408]{1,0:T(8,128)S(1)} collective-permute-done((f32[32,1408]{1,0:T(8,128)S(1)}, f32[32,1408]{1,0:T(8,128)S(1)}, u32[]{:S(2)}, u32[]{:S(2)}) %collective-permute-start.15) | collective-permute-done | bytes 180256 | tf_op jit(solution)/shard_map/ppermute | solution.py:301
  73.4 0.9 %shard_map.48 = (f32[64,1280]{1,0:T(8,128)S(1)}, f32[64,128]{1,0:T(8,128)S(1)}, f32[64,512]{1,0:T(8,128)S(1)}) custom-call(f32[32,1408]{1,0:T(8,128)S(1)} %add.55.refs_0_, f32[32,1408]{1,0:T(8,128)S(1)} %collective-permute-done.15.refs_1_, bf16[2,2560,256]{2,1,0:T(8,128)(2,1)S(1)} %get-tuple-element.59.refs_8_.refs_2_.refs_10_.refs_11_, ...), custom_call_target="tpu_custom_call" | custom-call | bytes 10846208 | tf_op jit(solution)/shard_map/pallas_call | solution.py:30
  74.3 1.0 %shard_map.49 = (f32[2,64,256]{2,1,0:T(8,128)S(1)}, f32[2,64,256]{2,1,0:T(8,128)S(1)}) custom-call(f32[32,1280]{1,0:T(8,128)S(1)} %add.53.refs_0_, f32[32,1280]{1,0:T(8,128)S(1)} %collective-permute-done.12.refs_1_, f32[64,1280]{1,0:T(8,128)S(1)} %get-tuple-element.78.refs_2_, f32[64,128]{1,0:T(8,128)S(1)} %get-tuple-element.79.refs_3_, ...), custom_call_target="tpu_custom_call" | custom-call | flops 1006632960 | bytes 12386304 | tf_op jit(solution)/shard_map/pallas_call | solution.py:30
  75.4 0.1 collective-permute-start.16
  75.4 1.5 %collective-permute-done.31.refs_1_ = f32[32,1408]{1,0:T(8,128)S(1)} collective-permute-done((f32[32,1408]{1,0:T(8,128)S(1)}, f32[32,1408]{1,0:T(8,128)S(1)}, u32[]{:S(2)}, u32[]{:S(2)}) %collective-permute-start.31) | collective-permute-done | bytes 180256 | tf_op jit(solution)/shard_map/ppermute | solution.py:301
  77.0 0.9 %shard_map.55 = (f32[64,1280]{1,0:T(8,128)S(1)}, f32[64,128]{1,0:T(8,128)S(1)}, f32[64,512]{1,0:T(8,128)S(1)}) custom-call(f32[32,1408]{1,0:T(8,128)S(1)} %add.63.refs_0_, f32[32,1408]{1,0:T(8,128)S(1)} %collective-permute-done.31.refs_1_, bf16[2,2560,256]{2,1,0:T(8,128)(2,1)S(1)} %get-tuple-element.59.refs_8_.refs_2_.refs_10_.refs_11_, ...), custom_call_target="tpu_custom_call" | custom-call | bytes 10846208 | tf_op jit(solution)/shard_map/pallas_call | solution.py:30
  77.9 1.0 %shard_map.56 = (f32[2,64,256]{2,1,0:T(8,128)S(1)}, f32[2,64,256]{2,1,0:T(8,128)S(1)}) custom-call(f32[32,1280]{1,0:T(8,128)S(1)} %add.61.refs_0_, f32[32,1280]{1,0:T(8,128)S(1)} %collective-permute-done.28.refs_1_, f32[64,1280]{1,0:T(8,128)S(1)} %get-tuple-element.100.refs_2_, f32[64,128]{1,0:T(8,128)S(1)} %get-tuple-element.101.refs_3_, ...), custom_call_target="tpu_custom_call" | custom-call | flops 1006632960 | bytes 12386304 | tf_op jit(solution)/shard_map/pallas_call | solution.py:30
  78.9 0.1 collective-permute-start.32
  79.0 1.3 %collective-permute-done.32.refs_3_ = f32[2,64,256]{2,1,0:T(8,128)S(1)} collective-permute-done((f32[2,64,256]{2,1,0:T(8,128)S(1)}, f32[2,64,256]{2,1,0:T(8,128)S(1)}, u32[]{:S(2)}, u32[]{:S(2)}) %collective-permute-start.32) | collective-permute-done | bytes 131104 | tf_op jit(solution)/shard_map/ppermute | solution.py:301
  80.3 0.9 %shard_map.57 = (f32[2,256,128]{2,1,0:T(8,128)}, f32[2,256,128]{2,1,0:T(8,128)}) custom-call(f32[2,64,256]{2,1,0:T(8,128)S(1)} %get-tuple-element.84.refs_0_, f32[2,64,256]{2,1,0:T(8,128)S(1)} %collective-permute-done.16.refs_1_, f32[2,64,256]{2,1,0:T(8,128)S(1)} %get-tuple-element.106.refs_2_, f32[2,64,256]{2,1,0:T(8,128)S(1)} %collective-permute-done.32.refs_3_), custom_call_target="tpu_custom_call" | custom-call | bytes 524288 | tf_op jit(solution)/shard_map/pallas_call | solution.py:30
  (36 shorter events, 0.5 us)
Async XLA Ops:
  0.6 11.6 %collective-permute-start.3 = (f32[2,256,2560]{2,1,0:T(8,128)}, f32[2,256,2560]{2,1,0:T(8,128)S(1)}, u32[]{:S(2)}, u32[]{:S(2)}) collective-permute-start(f32[2,256,2560]{2,1,0:T(8,128)} %down_ref.1), channel_id=1, source_target_pairs={{0,1},{1,0},{2,3},{3,2},{4,5},{5,4},{6,7},{7,6},{8,9},{9,8},{10,11... | collective-permute-start | bytes 15728648 | tf_op jit(solution)/shard_map/ppermute | solution.py:301
  2.2 12.2 %collective-permute-start.2 = (f32[2,8,2560]{2,1,0:T(8,128)S(1)}, f32[2,8,2560]{2,1,0:T(8,128)S(1)}, u32[]{:S(2)}, u32[]{:S(2)}) collective-permute-start(f32[2,8,2560]{2,1,0:T(8,128)S(1)} %get-tuple-element.109.refs_0_), channel_id=1, source_target_pairs={{0,6},{1,7},{2,4},{3,5},{4,2},{5,3},{6,0},{7,1},{8,14},{9,15},{10,... | collective-permute-start | bytes 491528 | tf_op jit(solution)/shard_map/ppermute | solution.py:304
  5.7 10.0 %collective-permute-start.1 = (f32[2,8,2560]{2,1,0:T(8,128)S(1)}, f32[2,8,2560]{2,1,0:T(8,128)S(1)}, u32[]{:S(2)}, u32[]{:S(2)}) collective-permute-start(f32[2,8,2560]{2,1,0:T(8,128)S(1)} %get-tuple-element.109.refs_0_), channel_id=1, source_target_pairs={{0,4},{1,5},{2,6},{3,7},{4,0},{5,1},{6,2},{7,3},{8,12},{9,13},{10,... | collective-permute-start | bytes 491528 | tf_op jit(solution)/shard_map/ppermute | solution.py:304
  6.2 9.5 %collective-permute-start = (f32[2,8,2560]{2,1,0:T(8,128)S(1)}, f32[2,8,2560]{2,1,0:T(8,128)S(1)}, u32[]{:S(2)}, u32[]{:S(2)}) collective-permute-start(f32[2,8,2560]{2,1,0:T(8,128)S(1)} %get-tuple-element.109.refs_0_), channel_id=1, source_target_pairs={{0,2},{1,3},{2,0},{3,1},{4,6},{5,7},{6,4},{7,5},{8,10},{9,11},{10,... | collective-permute-start | bytes 491528 | tf_op jit(solution)/shard_map/ppermute | solution.py:304
  6.3 15.3 %collective-permute-start.19 = (f32[2,8,2560]{2,1,0:T(8,128)S(1)}, f32[2,8,2560]{2,1,0:T(8,128)S(1)}, u32[]{:S(2)}, u32[]{:S(2)}) collective-permute-start(f32[2,8,2560]{2,1,0:T(8,128)S(1)} %get-tuple-element.108.refs_0_), channel_id=1, source_target_pairs={{0,6},{1,7},{2,4},{3,5},{4,2},{5,3},{6,0},{7,1},{8,14},{9,15},{10,... | collective-permute-start | bytes 491528 | tf_op jit(solution)/shard_map/ppermute | solution.py:304
  12.2 9.4 %collective-permute-start.18 = (f32[2,8,2560]{2,1,0:T(8,128)S(1)}, f32[2,8,2560]{2,1,0:T(8,128)S(1)}, u32[]{:S(2)}, u32[]{:S(2)}) collective-permute-start(f32[2,8,2560]{2,1,0:T(8,128)S(1)} %get-tuple-element.108.refs_0_), channel_id=1, source_target_pairs={{0,4},{1,5},{2,6},{3,7},{4,0},{5,1},{6,2},{7,3},{8,12},{9,13},{10,... | collective-permute-start | bytes 491528 | tf_op jit(solution)/shard_map/ppermute | solution.py:304
  14.4 7.4 %collective-permute-start.17 = (f32[2,8,2560]{2,1,0:T(8,128)S(1)}, f32[2,8,2560]{2,1,0:T(8,128)S(1)}, u32[]{:S(2)}, u32[]{:S(2)}) collective-permute-start(f32[2,8,2560]{2,1,0:T(8,128)S(1)} %get-tuple-element.108.refs_0_), channel_id=1, source_target_pairs={{0,2},{1,3},{2,0},{3,1},{4,6},{5,7},{6,4},{7,5},{8,10},{9,11},{10,... | collective-permute-start | bytes 491528 | tf_op jit(solution)/shard_map/ppermute | solution.py:304
  18.2 7.2 %collective-permute-start.7 = (f32[32,1408]{1,0:T(8,128)S(1)}, f32[32,1408]{1,0:T(8,128)S(1)}, u32[]{:S(2)}, u32[]{:S(2)}) collective-permute-start(f32[32,1408]{1,0:T(8,128)S(1)} %get-tuple-element.69), channel_id=1, source_target_pairs={{0,2},{1,3},{2,0},{3,1},{4,6},{5,7},{6,4},{7,5},{8,10},{9,11},{10,... | collective-permute-start | bytes 540680 | tf_op jit(solution)/shard_map/ppermute | solution.py:301
  20.1 9.0 %collective-permute-start.4 = (f32[32,1280]{1,0:T(8,128)S(1)}, f32[32,1280]{1,0:T(8,128)S(1)}, u32[]{:S(2)}, u32[]{:S(2)}) collective-permute-start(f32[32,1280]{1,0:T(8,128)S(1)} %get-tuple-element.67), channel_id=1, source_target_pairs={{0,4},{1,5},{2,6},{3,7},{4,0},{5,1},{6,2},{7,3},{8,12},{9,13},{10,... | collective-permute-start | bytes 491528 | tf_op jit(solution)/shard_map/ppermute | solution.py:301
  24.4 7.6 %collective-permute-start.23 = (f32[32,1408]{1,0:T(8,128)S(1)}, f32[32,1408]{1,0:T(8,128)S(1)}, u32[]{:S(2)}, u32[]{:S(2)}) collective-permute-start(f32[32,1408]{1,0:T(8,128)S(1)} %get-tuple-element.90), channel_id=1, source_target_pairs={{0,4},{1,5},{2,6},{3,7},{4,0},{5,1},{6,2},{7,3},{8,12},{9,13},{10,... | collective-permute-start | bytes 540680 | tf_op jit(solution)/shard_map/ppermute | solution.py:301
  25.5 8.6 %collective-permute-start.8 = (f32[32,1408]{1,0:T(8,128)S(1)}, f32[32,1408]{1,0:T(8,128)S(1)}, u32[]{:S(2)}, u32[]{:S(2)}) collective-permute-start(f32[32,1408]{1,0:T(8,128)S(1)} %add.50), channel_id=1, source_target_pairs={{0,4},{1,5},{2,6},{3,7},{4,0},{5,1},{6,2},{7,3},{8,12},{9,13},{10,... | collective-permute-start | bytes 540680 | tf_op jit(solution)/shard_map/ppermute | solution.py:301
  27.5 8.2 %collective-permute-start.20 = (f32[32,1280]{1,0:T(8,128)S(1)}, f32[32,1280]{1,0:T(8,128)S(1)}, u32[]{:S(2)}, u32[]{:S(2)}) collective-permute-start(f32[32,1280]{1,0:T(8,128)S(1)} %get-tuple-element.88), channel_id=1, source_target_pairs={{0,2},{1,3},{2,0},{3,1},{4,6},{5,7},{6,4},{7,5},{8,10},{9,11},{10,... | collective-permute-start | bytes 491528 | tf_op jit(solution)/shard_map/ppermute | solution.py:301
  29.1 9.1 %collective-permute-start.5 = (f32[32,1280]{1,0:T(8,128)S(1)}, f32[32,1280]{1,0:T(8,128)S(1)}, u32[]{:S(2)}, u32[]{:S(2)}) collective-permute-start(f32[32,1280]{1,0:T(8,128)S(1)} %add.48), channel_id=1, source_target_pairs={{0,2},{1,3},{2,0},{3,1},{4,6},{5,7},{6,4},{7,5},{8,10},{9,11},{10,... | collective-permute-start | bytes 491528 | tf_op jit(solution)/shard_map/ppermute | solution.py:301
  32.0 10.9 %collective-permute-start.24 = (f32[32,1408]{1,0:T(8,128)S(1)}, f32[32,1408]{1,0:T(8,128)S(1)}, u32[]{:S(2)}, u32[]{:S(2)}) collective-permute-start(f32[32,1408]{1,0:T(8,128)S(1)} %add.58), channel_id=1, source_target_pairs={{0,2},{1,3},{2,0},{3,1},{4,6},{5,7},{6,4},{7,5},{8,10},{9,11},{10,... | collective-permute-start | bytes 540680 | tf_op jit(solution)/shard_map/ppermute | solution.py:301
  34.1 11.3 %collective-permute-start.9 = (f32[32,1408]{1,0:T(8,128)S(1)}, f32[32,1408]{1,0:T(8,128)S(1)}, u32[]{:S(2)}, u32[]{:S(2)}) collective-permute-start(f32[32,1408]{1,0:T(8,128)S(1)} %add.51.refs_0_), channel_id=1, source_target_pairs={{0,2},{1,3},{2,0},{3,1},{4,6},{5,7},{6,4},{7,5},{8,10},{9,11},{10,... | collective-permute-start | bytes 540680 | tf_op jit(solution)/shard_map/ppermute | solution.py:301
  35.8 6.1 %collective-permute-start.21 = (f32[32,1280]{1,0:T(8,128)S(1)}, f32[32,1280]{1,0:T(8,128)S(1)}, u32[]{:S(2)}, u32[]{:S(2)}) collective-permute-start(f32[32,1280]{1,0:T(8,128)S(1)} %add.56), channel_id=1, source_target_pairs={{0,4},{1,5},{2,6},{3,7},{4,0},{5,1},{6,2},{7,3},{8,12},{9,13},{10,... | collective-permute-start | bytes 491528 | tf_op jit(solution)/shard_map/ppermute | solution.py:301
  38.3 8.1 %collective-permute-start.6 = (f32[32,1280]{1,0:T(8,128)S(1)}, f32[32,1280]{1,0:T(8,128)S(1)}, u32[]{:S(2)}, u32[]{:S(2)}) collective-permute-start(f32[32,1280]{1,0:T(8,128)S(1)} %add.49.refs_0_), channel_id=1, source_target_pairs={{0,4},{1,5},{2,6},{3,7},{4,0},{5,1},{6,2},{7,3},{8,12},{9,13},{10,... | collective-permute-start | bytes 491528 | tf_op jit(solution)/shard_map/ppermute | solution.py:301
  41.9 11.3 %collective-permute-start.22 = (f32[32,1280]{1,0:T(8,128)S(1)}, f32[32,1280]{1,0:T(8,128)S(1)}, u32[]{:S(2)}, u32[]{:S(2)}) collective-permute-start(f32[32,1280]{1,0:T(8,128)S(1)} %add.57.refs_0_), channel_id=1, source_target_pairs={{0,2},{1,3},{2,0},{3,1},{4,6},{5,7},{6,4},{7,5},{8,10},{9,11},{10,... | collective-permute-start | bytes 491528 | tf_op jit(solution)/shard_map/ppermute | solution.py:301
  42.9 9.4 %collective-permute-start.25 = (f32[32,1408]{1,0:T(8,128)S(1)}, f32[32,1408]{1,0:T(8,128)S(1)}, u32[]{:S(2)}, u32[]{:S(2)}) collective-permute-start(f32[32,1408]{1,0:T(8,128)S(1)} %add.59.refs_0_), channel_id=1, source_target_pairs={{0,4},{1,5},{2,6},{3,7},{4,0},{5,1},{6,2},{7,3},{8,12},{9,13},{10,... | collective-permute-start | bytes 540680 | tf_op jit(solution)/shard_map/ppermute | solution.py:301
  48.4 9.0 %collective-permute-start.13 = (f32[32,1408]{1,0:T(8,128)S(1)}, f32[32,1408]{1,0:T(8,128)S(1)}, u32[]{:S(2)}, u32[]{:S(2)}) collective-permute-start(f32[32,1408]{1,0:T(8,128)S(1)} %get-tuple-element.77), channel_id=1, source_target_pairs={{0,2},{1,3},{2,0},{3,1},{4,6},{5,7},{6,4},{7,5},{8,10},{9,11},{10,... | collective-permute-start | bytes 540680 | tf_op jit(solution)/shard_map/ppermute | solution.py:301
  51.0 8.0 %collective-permute-start.10 = (f32[32,1280]{1,0:T(8,128)S(1)}, f32[32,1280]{1,0:T(8,128)S(1)}, u32[]{:S(2)}, u32[]{:S(2)}) collective-permute-start(f32[32,1280]{1,0:T(8,128)S(1)} %get-tuple-element.75), channel_id=1, source_target_pairs={{0,4},{1,5},{2,6},{3,7},{4,0},{5,1},{6,2},{7,3},{8,12},{9,13},{10,... | collective-permute-start | bytes 491528 | tf_op jit(solution)/shard_map/ppermute | solution.py:301
  55.1 7.5 %collective-permute-start.29 = (f32[32,1408]{1,0:T(8,128)S(1)}, f32[32,1408]{1,0:T(8,128)S(1)}, u32[]{:S(2)}, u32[]{:S(2)}) collective-permute-start(f32[32,1408]{1,0:T(8,128)S(1)} %get-tuple-element.99), channel_id=1, source_target_pairs={{0,4},{1,5},{2,6},{3,7},{4,0},{5,1},{6,2},{7,3},{8,12},{9,13},{10,... | collective-permute-start | bytes 540680 | tf_op jit(solution)/shard_map/ppermute | solution.py:301
  56.9 7.1 %collective-permute-start.26 = (f32[32,1280]{1,0:T(8,128)S(1)}, f32[32,1280]{1,0:T(8,128)S(1)}, u32[]{:S(2)}, u32[]{:S(2)}) collective-permute-start(f32[32,1280]{1,0:T(8,128)S(1)} %get-tuple-element.96), channel_id=1, source_target_pairs={{0,2},{1,3},{2,0},{3,1},{4,6},{5,7},{6,4},{7,5},{8,10},{9,11},{10,... | collective-permute-start | bytes 491528 | tf_op jit(solution)/shard_map/ppermute | solution.py:301
  57.4 9.0 %collective-permute-start.14 = (f32[32,1408]{1,0:T(8,128)S(1)}, f32[32,1408]{1,0:T(8,128)S(1)}, u32[]{:S(2)}, u32[]{:S(2)}) collective-permute-start(f32[32,1408]{1,0:T(8,128)S(1)} %add.54), channel_id=1, source_target_pairs={{0,4},{1,5},{2,6},{3,7},{4,0},{5,1},{6,2},{7,3},{8,12},{9,13},{10,... | collective-permute-start | bytes 540680 | tf_op jit(solution)/shard_map/ppermute | solution.py:301
  59.0 8.5 %collective-permute-start.11 = (f32[32,1280]{1,0:T(8,128)S(1)}, f32[32,1280]{1,0:T(8,128)S(1)}, u32[]{:S(2)}, u32[]{:S(2)}) collective-permute-start(f32[32,1280]{1,0:T(8,128)S(1)} %add.52), channel_id=1, source_target_pairs={{0,2},{1,3},{2,0},{3,1},{4,6},{5,7},{6,4},{7,5},{8,10},{9,11},{10,... | collective-permute-start | bytes 491528 | tf_op jit(solution)/shard_map/ppermute | solution.py:301
  62.6 8.8 %collective-permute-start.30 = (f32[32,1408]{1,0:T(8,128)S(1)}, f32[32,1408]{1,0:T(8,128)S(1)}, u32[]{:S(2)}, u32[]{:S(2)}) collective-permute-start(f32[32,1408]{1,0:T(8,128)S(1)} %add.62), channel_id=1, source_target_pairs={{0,2},{1,3},{2,0},{3,1},{4,6},{5,7},{6,4},{7,5},{8,10},{9,11},{10,... | collective-permute-start | bytes 540680 | tf_op jit(solution)/shard_map/ppermute | solution.py:301
  64.0 7.5 %collective-permute-start.27 = (f32[32,1280]{1,0:T(8,128)S(1)}, f32[32,1280]{1,0:T(8,128)S(1)}, u32[]{:S(2)}, u32[]{:S(2)}) collective-permute-start(f32[32,1280]{1,0:T(8,128)S(1)} %add.60), channel_id=1, source_target_pairs={{0,4},{1,5},{2,6},{3,7},{4,0},{5,1},{6,2},{7,3},{8,12},{9,13},{10,... | collective-permute-start | bytes 491528 | tf_op jit(solution)/shard_map/ppermute | solution.py:301
  66.4 7.0 %collective-permute-start.15 = (f32[32,1408]{1,0:T(8,128)S(1)}, f32[32,1408]{1,0:T(8,128)S(1)}, u32[]{:S(2)}, u32[]{:S(2)}) collective-permute-start(f32[32,1408]{1,0:T(8,128)S(1)} %add.55.refs_0_), channel_id=1, source_target_pairs={{0,2},{1,3},{2,0},{3,1},{4,6},{5,7},{6,4},{7,5},{8,10},{9,11},{10,... | collective-permute-start | bytes 540680 | tf_op jit(solution)/shard_map/ppermute | solution.py:301
  67.5 6.8 %collective-permute-start.12 = (f32[32,1280]{1,0:T(8,128)S(1)}, f32[32,1280]{1,0:T(8,128)S(1)}, u32[]{:S(2)}, u32[]{:S(2)}) collective-permute-start(f32[32,1280]{1,0:T(8,128)S(1)} %add.53.refs_0_), channel_id=1, source_target_pairs={{0,4},{1,5},{2,6},{3,7},{4,0},{5,1},{6,2},{7,3},{8,12},{9,13},{10,... | collective-permute-start | bytes 491528 | tf_op jit(solution)/shard_map/ppermute | solution.py:301
  71.4 5.6 %collective-permute-start.31 = (f32[32,1408]{1,0:T(8,128)S(1)}, f32[32,1408]{1,0:T(8,128)S(1)}, u32[]{:S(2)}, u32[]{:S(2)}) collective-permute-start(f32[32,1408]{1,0:T(8,128)S(1)} %add.63.refs_0_), channel_id=1, source_target_pairs={{0,4},{1,5},{2,6},{3,7},{4,0},{5,1},{6,2},{7,3},{8,12},{9,13},{10,... | collective-permute-start | bytes 540680 | tf_op jit(solution)/shard_map/ppermute | solution.py:301
  71.5 6.4 %collective-permute-start.28 = (f32[32,1280]{1,0:T(8,128)S(1)}, f32[32,1280]{1,0:T(8,128)S(1)}, u32[]{:S(2)}, u32[]{:S(2)}) collective-permute-start(f32[32,1280]{1,0:T(8,128)S(1)} %add.61.refs_0_), channel_id=1, source_target_pairs={{0,2},{1,3},{2,0},{3,1},{4,6},{5,7},{6,4},{7,5},{8,10},{9,11},{10,... | collective-permute-start | bytes 491528 | tf_op jit(solution)/shard_map/ppermute | solution.py:301
  75.4 3.6 %collective-permute-start.16 = (f32[2,64,256]{2,1,0:T(8,128)S(1)}, f32[2,64,256]{2,1,0:T(8,128)S(1)}, u32[]{:S(2)}, u32[]{:S(2)}) collective-permute-start(f32[2,64,256]{2,1,0:T(8,128)S(1)} %get-tuple-element.85), channel_id=1, source_target_pairs={{0,1},{1,0},{2,3},{3,2},{4,5},{5,4},{6,7},{7,6},{8,9},{9,8},{10,11... | collective-permute-start | bytes 393224 | tf_op jit(solution)/shard_map/ppermute | solution.py:301
  78.9 1.4 %collective-permute-start.32 = (f32[2,64,256]{2,1,0:T(8,128)S(1)}, f32[2,64,256]{2,1,0:T(8,128)S(1)}, u32[]{:S(2)}, u32[]{:S(2)}) collective-permute-start(f32[2,64,256]{2,1,0:T(8,128)S(1)} %get-tuple-element.107), channel_id=1, source_target_pairs={{0,1},{1,0},{2,3},{3,2},{4,5},{5,4},{6,7},{7,6},{8,9},{9,8},{10,11... | collective-permute-start | bytes 393224 | tf_op jit(solution)/shard_map/ppermute | solution.py:301

commit v9 on v8

--- a/solution.py
+++ b/solution.py
@@ -9,8 +9,8 @@
 damping_ratio = 0.1
 LANES = 128
 GROUPS = 2
-ORDER = {'bE': ['a1.2']}
-COST = {'bC.': 0.3, 'aL.': 0, 'aR': 30, 'bM': 10, 'bL.': 0, 'bC': 0, 'aC': 0.3, 'aC.': 3, 'aL': 0}
+ORDER = {"bE": ["a1.2"], "b02": ["aC"]}
+COST = {"aR": 30, "aC": 0.3, "bC": 3, "aL": 0, "aC.": 3, "bC.": 0.3, "aL.": 0, "bL.": 0}
 f32 = jnp.float32
 bf16 = jnp.bfloat16
 

time: 81.4 us -> 80.2 us (0.985)
  waiting for transfers between devices: 21.3 us -> 15 us
  starting transfers between devices: 33.7 us -> 38.8 us
    ppermute x27, waiting for transfers between devices: 21.1 us -> 15 us  [swap(): lax.ppermute(value, 'rcv', [(at, at ^ 1 << bit) for at in range(count)])]
    ppermute x27, starting transfers between devices: 24.8 us -> 29.9 us  [swap(): lax.ppermute(value, 'rcv', [(at, at ^ 1 << bit) for at in range(count)])]
  transfers between devices with their start and end apart: 33 -> 33, of which waited for: 14 -> 11; matrix products, arithmetic and copies ran while one was open for 2% -> 2% of each run, Pallas kernels for 28% -> 29%
where the time goes in v9:
time: 80.2 us; the launch traced here: 80 us
  starting transfers between devices  38.8 us (48%)
  Pallas kernels  23.9 us (30%)
  waiting for transfers between devices  15 us (19%)
  local copies, waits for them, and re-layouts  1.02 us (1%)
  between operations  0.9 us (1%)
    ppermute x27, starting transfers between devices, swap(): lax.ppermute(value, 'rcv', [(at, at ^ 1 << bit) for at in range(count)])  29.9 us
    pallas_call x17, Pallas kernels, call(): pl.pallas_call(kernel, out_shape=[jax.ShapeDtypeStruct(shape, dtype) for...  23.9 us
    ppermute x27, waiting for transfers between devices, swap(): lax.ppermute(value, 'rcv', [(at, at ^ 1 << bit) for at in range(count)])  15 us
    ppermute x6, starting transfers between devices, jump(): lax.ppermute(value, 'rcv', [(at, at ^ mask << 1) for at in range(count)])  8.85 us
  transfers between devices with their start and end apart: 33, of which 11 were waited for; matrix products, arithmetic and copies ran while one was open for 2% of the time, Pallas kernels for 29%

profile of v9, /device:TPU:0, one launch (start us, length us, event | category | flops | bytes accessed | tf_op | source)
XLA Modules:
  0.0 80.0 jit_solution(15739416328447936781)
XLA Ops:
  0.6 0.5 collective-permute-start.3
  1.1 1.0 %fusion = (f32[2,8,2560]{2,1,0:T(8,128)S(1)}, f32[2,8,2560]{2,1,0:T(8,128)S(1)}) fusion(f32[2,16,2560]{2,1,0:T(8,128)} %param.3), kind=kLoop, calls=%fused_computation | loop fusion | bytes 655360 | tf_op jit(solution)/shard_map/slice | solution.py:310
  2.2 3.5 %collective-permute-start.19 = (f32[2,8,2560]{2,1,0:T(8,128)S(1)}, f32[2,8,2560]{2,1,0:T(8,128)S(1)}, u32[]{:S(2)}, u32[]{:S(2)}) collective-permute-start(f32[2,8,2560]{2,1,0:T(8,128)S(1)} %get-tuple-element.110.refs_0_), channel_id=1, source_target_pairs={{0,6},{1,7},{2,4},{3,5},{4,2},{5,3},{6,0},{7,1},{8,14},{9,15},{10,... | collective-permute-start | bytes 491528 | tf_op jit(solution)/shard_map/ppermute | solution.py:304
  5.7 0.5 collective-permute-start.18
  6.2 0.1 collective-permute-start.17
  6.3 2.8 %collective-permute-start.2 = (f32[2,8,2560]{2,1,0:T(8,128)S(1)}, f32[2,8,2560]{2,1,0:T(8,128)S(1)}, u32[]{:S(2)}, u32[]{:S(2)}) collective-permute-start(f32[2,8,2560]{2,1,0:T(8,128)S(1)} %get-tuple-element.111.refs_0_), channel_id=1, source_target_pairs={{0,6},{1,7},{2,4},{3,5},{4,2},{5,3},{6,0},{7,1},{8,14},{9,15},{10,... | collective-permute-start | bytes 491528 | tf_op jit(solution)/shard_map/ppermute | solution.py:304
  9.2 3.0 %shard_map.41 = (bf16[2,256,2560]{2,1,0:T(8,128)(2,1)S(1)}, bf16[2,256,2560]{2,1,0:T(8,128)(2,1)S(1)}, bf16[2,2560,256]{2,1,0:T(8,128)(2,1)S(1)}, bf16[2,2560,256]{2,1,0:T(8,128)(2,1)S(1)}, f32[8,128]{1,0:T(8,128)S(1)}) custom-call(f32[2,256,2560]{2,1,0:T(8,128)} %down_ref.1), custom_call_target="tpu_custom_call" | custom-call | bytes 5242880 | tf_op jit(solution)/shard_map/pallas_call | solution.py:30
  12.2 0.0 collective-permute-done.3.down_ref
  12.2 0.6 collective-permute-start.1
  12.8 1.5 %shard_map.42 = (bf16[2,256,2560]{2,1,0:T(8,128)(2,1)S(1)}, bf16[2,256,2560]{2,1,0:T(8,128)(2,1)S(1)}, bf16[2,2560,256]{2,1,0:T(8,128)(2,1)S(1)}, bf16[2,2560,256]{2,1,0:T(8,128)(2,1)S(1)}, f32[8,128]{1,0:T(8,128)S(1)}) custom-call(f32[2,256,2560]{2,1,0:T(8,128)S(1)} %collective-permute-done.3.down_ref), custom_call_target="tpu_custom_call" | custom-call | bytes 5242880 | tf_op jit(solution)/shard_map/pallas_call | solution.py:30
  14.4 1.3 %collective-permute-start = (f32[2,8,2560]{2,1,0:T(8,128)S(1)}, f32[2,8,2560]{2,1,0:T(8,128)S(1)}, u32[]{:S(2)}, u32[]{:S(2)}) collective-permute-start(f32[2,8,2560]{2,1,0:T(8,128)S(1)} %get-tuple-element.111.refs_0_), channel_id=1, source_target_pairs={{0,2},{1,3},{2,0},{3,1},{4,6},{5,7},{6,4},{7,5},{8,10},{9,11},{10,... | collective-permute-start | bytes 491528 | tf_op jit(solution)/shard_map/ppermute | solution.py:304
  15.7 2.6 %shard_map.50 = (f32[64,512]{1,0:T(8,128)S(1)}, f32[32,1408]{1,0:T(8,128)S(1)}, f32[32,1408]{1,0:T(8,128)S(1)}) custom-call(f32[2,8,2560]{2,1,0:T(8,128)S(1)} %get-tuple-element.110.refs_0_, f32[2,8,2560]{2,1,0:T(8,128)S(1)} %collective-permute-done.17.refs_1_, f32[2,8,2560]{2,1,0:T(8,128)S(1)} %collective-permute-done.18.refs_2_, ...), custom_call_target="tpu_custom_call" | custom-call | flops 3019898880 | bytes 21635072 | tf_op jit(solution)/shard_map/pallas_call | solution.py:30
  18.2 0.9 %collective-permute-start.23 = (f32[32,1408]{1,0:T(8,128)S(1)}, f32[32,1408]{1,0:T(8,128)S(1)}, u32[]{:S(2)}, u32[]{:S(2)}) collective-permute-start(f32[32,1408]{1,0:T(8,128)S(1)} %get-tuple-element.92), channel_id=1, source_target_pairs={{0,4},{1,5},{2,6},{3,7},{4,0},{5,1},{6,2},{7,3},{8,12},{9,13},{10,... | collective-permute-start | bytes 540680 | tf_op jit(solution)/shard_map/ppermute | solution.py:301
  19.2 0.9 %shard_map.51 = (f32[32,1280]{1,0:T(8,128)S(1)}, f32[32,1280]{1,0:T(8,128)S(1)}) custom-call(f32[64,512]{1,0:T(8,128)S(1)} %get-tuple-element.87.refs_0_.refs_5_, bf16[2,256,2560]{2,1,0:T(8,128)(2,1)S(1)} %get-tuple-element.56.refs_4_.refs_1_.refs_6_, bf16[2,256,2560]{2,1,0:T(8,128)(2,1)S(1)} %get-tuple-element.57.refs_5_.refs_2_.refs_7_, ...), custom_call_target="tpu_custom_call" | custom-call | flops 3019898880 | bytes 10616832 | tf_op jit(solution)/shard_map/pallas_call | solution.py:30
  20.1 1.6 %collective-permute-start.20 = (f32[32,1280]{1,0:T(8,128)S(1)}, f32[32,1280]{1,0:T(8,128)S(1)}, u32[]{:S(2)}, u32[]{:S(2)}) collective-permute-start(f32[32,1280]{1,0:T(8,128)S(1)} %get-tuple-element.89), channel_id=1, source_target_pairs={{0,2},{1,3},{2,0},{3,1},{4,6},{5,7},{6,4},{7,5},{8,10},{9,11},{10,... | collective-permute-start | bytes 491528 | tf_op jit(solution)/shard_map/ppermute | solution.py:301
  21.7 2.6 %shard_map.43 = (f32[64,512]{1,0:T(8,128)S(1)}, f32[32,1408]{1,0:T(8,128)S(1)}, f32[32,1408]{1,0:T(8,128)S(1)}) custom-call(f32[2,8,2560]{2,1,0:T(8,128)S(1)} %get-tuple-element.111.refs_0_, f32[2,8,2560]{2,1,0:T(8,128)S(1)} %collective-permute-done.refs_1_, f32[2,8,2560]{2,1,0:T(8,128)S(1)} %collective-permute-done.1.refs_2_, ...), custom_call_target="tpu_custom_call" | custom-call | flops 90596966400 | bytes 21635072 | tf_op jit(solution)/shard_map/pallas_call | solution.py:30
  24.3 1.4 %collective-permute-start.7 = (f32[32,1408]{1,0:T(8,128)S(1)}, f32[32,1408]{1,0:T(8,128)S(1)}, u32[]{:S(2)}, u32[]{:S(2)}) collective-permute-start(f32[32,1408]{1,0:T(8,128)S(1)} %get-tuple-element.70), channel_id=1, source_target_pairs={{0,2},{1,3},{2,0},{3,1},{4,6},{5,7},{6,4},{7,5},{8,10},{9,11},{10,... | collective-permute-start | bytes 540680 | tf_op jit(solution)/shard_map/ppermute | solution.py:301
  25.6 0.9 %shard_map.44 = (f32[32,1280]{1,0:T(8,128)S(1)}, f32[32,1280]{1,0:T(8,128)S(1)}) custom-call(f32[64,512]{1,0:T(8,128)S(1)} %get-tuple-element.66.refs_0_.refs_5_, bf16[2,256,2560]{2,1,0:T(8,128)(2,1)S(1)} %get-tuple-element.56.refs_4_.refs_1_.refs_6_, bf16[2,256,2560]{2,1,0:T(8,128)(2,1)S(1)} %get-tuple-element.57.refs_5_.refs_2_.refs_7_, ...), custom_call_target="tpu_custom_call" | custom-call | flops 301989888 | bytes 10616832 | tf_op jit(solution)/shard_map/pallas_call | solution.py:30
  26.6 0.8 %collective-permute-start.24 = (f32[32,1408]{1,0:T(8,128)S(1)}, f32[32,1408]{1,0:T(8,128)S(1)}, u32[]{:S(2)}, u32[]{:S(2)}) collective-permute-start(f32[32,1408]{1,0:T(8,128)S(1)} %add.58), channel_id=1, source_target_pairs={{0,2},{1,3},{2,0},{3,1},{4,6},{5,7},{6,4},{7,5},{8,10},{9,11},{10,... | collective-permute-start | bytes 540680 | tf_op jit(solution)/shard_map/ppermute | solution.py:301
  27.4 1.3 %collective-permute-start.4 = (f32[32,1280]{1,0:T(8,128)S(1)}, f32[32,1280]{1,0:T(8,128)S(1)}, u32[]{:S(2)}, u32[]{:S(2)}) collective-permute-start(f32[32,1280]{1,0:T(8,128)S(1)} %get-tuple-element.68), channel_id=1, source_target_pairs={{0,4},{1,5},{2,6},{3,7},{4,0},{5,1},{6,2},{7,3},{8,12},{9,13},{10,... | collective-permute-start | bytes 491528 | tf_op jit(solution)/shard_map/ppermute | solution.py:301
  28.8 0.8 collective-permute-start.21
  29.5 2.3 %collective-permute-done.7 = f32[32,1408]{1,0:T(8,128)S(1)} collective-permute-done((f32[32,1408]{1,0:T(8,128)S(1)}, f32[32,1408]{1,0:T(8,128)S(1)}, u32[]{:S(2)}, u32[]{:S(2)}) %collective-permute-start.7) | collective-permute-done | bytes 180256 | tf_op jit(solution)/shard_map/ppermute | solution.py:301
  31.9 1.4 %collective-permute-start.8 = (f32[32,1408]{1,0:T(8,128)S(1)}, f32[32,1408]{1,0:T(8,128)S(1)}, u32[]{:S(2)}, u32[]{:S(2)}) collective-permute-start(f32[32,1408]{1,0:T(8,128)S(1)} %add.50), channel_id=1, source_target_pairs={{0,4},{1,5},{2,6},{3,7},{4,0},{5,1},{6,2},{7,3},{8,12},{9,13},{10,... | collective-permute-start | bytes 540680 | tf_op jit(solution)/shard_map/ppermute | solution.py:301
  33.2 0.9 %collective-permute-done.24 = f32[32,1408]{1,0:T(8,128)S(1)} collective-permute-done((f32[32,1408]{1,0:T(8,128)S(1)}, f32[32,1408]{1,0:T(8,128)S(1)}, u32[]{:S(2)}, u32[]{:S(2)}) %collective-permute-start.24) | collective-permute-done | bytes 180256 | tf_op jit(solution)/shard_map/ppermute | solution.py:301
  34.1 1.6 %collective-permute-start.25 = (f32[32,1408]{1,0:T(8,128)S(1)}, f32[32,1408]{1,0:T(8,128)S(1)}, u32[]{:S(2)}, u32[]{:S(2)}) collective-permute-start(f32[32,1408]{1,0:T(8,128)S(1)} %add.59.refs_0_), channel_id=1, source_target_pairs={{0,4},{1,5},{2,6},{3,7},{4,0},{5,1},{6,2},{7,3},{8,12},{9,13},{10,... | collective-permute-start | bytes 540680 | tf_op jit(solution)/shard_map/ppermute | solution.py:301
  35.8 0.8 collective-permute-start.5
  36.6 1.5 %collective-permute-done.21 = f32[32,1280]{1,0:T(8,128)S(1)} collective-permute-done((f32[32,1280]{1,0:T(8,128)S(1)}, f32[32,1280]{1,0:T(8,128)S(1)}, u32[]{:S(2)}, u32[]{:S(2)}) %collective-permute-start.21) | collective-permute-done | bytes 163872 | tf_op jit(solution)/shard_map/ppermute | solution.py:301
  38.1 1.4 %collective-permute-start.22 = (f32[32,1280]{1,0:T(8,128)S(1)}, f32[32,1280]{1,0:T(8,128)S(1)}, u32[]{:S(2)}, u32[]{:S(2)}) collective-permute-start(f32[32,1280]{1,0:T(8,128)S(1)} %add.57.refs_0_), channel_id=1, source_target_pairs={{0,2},{1,3},{2,0},{3,1},{4,6},{5,7},{6,4},{7,5},{8,10},{9,11},{10,... | collective-permute-start | bytes 491528 | tf_op jit(solution)/shard_map/ppermute | solution.py:301
  39.4 3.3 %collective-permute-done.5 = f32[32,1280]{1,0:T(8,128)S(1)} collective-permute-done((f32[32,1280]{1,0:T(8,128)S(1)}, f32[32,1280]{1,0:T(8,128)S(1)}, u32[]{:S(2)}, u32[]{:S(2)}) %collective-permute-start.5) | collective-permute-done | bytes 163872 | tf_op jit(solution)/shard_map/ppermute | solution.py:301
  42.8 0.1 collective-permute-start.6
  42.9 2.0 %collective-permute-start.9 = (f32[32,1408]{1,0:T(8,128)S(1)}, f32[32,1408]{1,0:T(8,128)S(1)}, u32[]{:S(2)}, u32[]{:S(2)}) collective-permute-start(f32[32,1408]{1,0:T(8,128)S(1)} %add.51.refs_0_), channel_id=1, source_target_pairs={{0,2},{1,3},{2,0},{3,1},{4,6},{5,7},{6,4},{7,5},{8,10},{9,11},{10,... | collective-permute-start | bytes 540680 | tf_op jit(solution)/shard_map/ppermute | solution.py:301
  45.0 0.5 collective-permute-done.25.refs_1_
  45.4 0.9 %shard_map.52 = (f32[64,1280]{1,0:T(8,128)S(1)}, f32[64,128]{1,0:T(8,128)S(1)}, f32[64,512]{1,0:T(8,128)S(1)}) custom-call(f32[32,1408]{1,0:T(8,128)S(1)} %add.59.refs_0_, f32[32,1408]{1,0:T(8,128)S(1)} %collective-permute-done.25.refs_1_, bf16[2,2560,256]{2,1,0:T(8,128)(2,1)S(1)} %get-tuple-element.60.refs_8_.refs_2_.refs_10_.refs_11_, ...), custom_call_target="tpu_custom_call" | custom-call | flops 1006632960 | bytes 10846208 | tf_op jit(solution)/shard_map/pallas_call | solution.py:30
  46.4 2.0 %shard_map.53 = (f32[64,1280]{1,0:T(8,128)S(1)}, f32[64,128]{1,0:T(8,128)S(1)}, f32[64,512]{1,0:T(8,128)S(1)}, f32[64,512]{1,0:T(8,128)S(1)}, f32[32,1408]{1,0:T(8,128)S(1)}, /*index=5*/f32[32,1408]{1,0:T(8,128)S(1)}) custom-call(f32[32,1280]{1,0:T(8,128)S(1)} %add.57.refs_0_, f32[32,1280]{1,0:T(8,128)S(1)} %collective-permute-done.22.refs_1_, ...), custom_call_target="tpu_custom_call" | custom-call | flops 2013265920 | bytes 21921792 | tf_op jit(solution)/shard_map/pallas_call | solution.py:30
  48.4 1.6 %collective-permute-start.29 = (f32[32,1408]{1,0:T(8,128)S(1)}, f32[32,1408]{1,0:T(8,128)S(1)}, u32[]{:S(2)}, u32[]{:S(2)}) collective-permute-start(f32[32,1408]{1,0:T(8,128)S(1)} %get-tuple-element.101), channel_id=1, source_target_pairs={{0,4},{1,5},{2,6},{3,7},{4,0},{5,1},{6,2},{7,3},{8,12},{9,13},{10,... | collective-permute-start | bytes 540680 | tf_op jit(solution)/shard_map/ppermute | solution.py:301
  50.0 0.9 %shard_map.54 = (f32[32,1280]{1,0:T(8,128)S(1)}, f32[32,1280]{1,0:T(8,128)S(1)}) custom-call(f32[64,512]{1,0:T(8,128)S(1)} %get-tuple-element.96.refs_0_.refs_10_, bf16[2,256,2560]{2,1,0:T(8,128)(2,1)S(1)} %get-tuple-element.56.refs_4_.refs_1_.refs_6_, bf16[2,256,2560]{2,1,0:T(8,128)(2,1)S(1)} %get-tuple-element.57.refs_5_.refs_2_.refs_7_, ...), custom_call_target="tpu_custom_call" | custom-call | flops 301989888 | bytes 10616832 | tf_op jit(solution)/shard_map/pallas_call | solution.py:30
  50.9 0.8 collective-permute-start.26
  51.7 0.9 %shard_map.45 = (f32[64,1280]{1,0:T(8,128)S(1)}, f32[64,128]{1,0:T(8,128)S(1)}, f32[64,512]{1,0:T(8,128)S(1)}) custom-call(f32[32,1408]{1,0:T(8,128)S(1)} %add.51.refs_0_, f32[32,1408]{1,0:T(8,128)S(1)} %collective-permute-done.9.refs_1_, bf16[2,2560,256]{2,1,0:T(8,128)(2,1)S(1)} %get-tuple-element.60.refs_8_.refs_2_.refs_10_.refs_11_, ...), custom_call_target="tpu_custom_call" | custom-call | bytes 10846208 | tf_op jit(solution)/shard_map/pallas_call | solution.py:30
  52.7 1.8 %shard_map.46 = (f32[64,1280]{1,0:T(8,128)S(1)}, f32[64,128]{1,0:T(8,128)S(1)}, f32[64,512]{1,0:T(8,128)S(1)}, f32[64,512]{1,0:T(8,128)S(1)}, f32[32,1408]{1,0:T(8,128)S(1)}, /*index=5*/f32[32,1408]{1,0:T(8,128)S(1)}) custom-call(f32[32,1280]{1,0:T(8,128)S(1)} %add.49.refs_0_, f32[32,1280]{1,0:T(8,128)S(1)} %collective-permute-done.6.refs_1_, ...), custom_call_target="tpu_custom_call" | custom-call | flops 2013265920 | bytes 21921792 | tf_op jit(solution)/shard_map/pallas_call | solution.py:30
  54.5 1.4 %collective-permute-start.13 = (f32[32,1408]{1,0:T(8,128)S(1)}, f32[32,1408]{1,0:T(8,128)S(1)}, u32[]{:S(2)}, u32[]{:S(2)}) collective-permute-start(f32[32,1408]{1,0:T(8,128)S(1)} %get-tuple-element.78), channel_id=1, source_target_pairs={{0,2},{1,3},{2,0},{3,1},{4,6},{5,7},{6,4},{7,5},{8,10},{9,11},{10,... | collective-permute-start | bytes 540680 | tf_op jit(solution)/shard_map/ppermute | solution.py:301
  55.9 0.9 %shard_map.47 = (f32[32,1280]{1,0:T(8,128)S(1)}, f32[32,1280]{1,0:T(8,128)S(1)}) custom-call(f32[64,512]{1,0:T(8,128)S(1)} %get-tuple-element.74.refs_0_.refs_10_, bf16[2,256,2560]{2,1,0:T(8,128)(2,1)S(1)} %get-tuple-element.56.refs_4_.refs_1_.refs_6_, bf16[2,256,2560]{2,1,0:T(8,128)(2,1)S(1)} %get-tuple-element.57.refs_5_.refs_2_.refs_7_, ...), custom_call_target="tpu_custom_call" | custom-call | flops 3019898880 | bytes 10616832 | tf_op jit(solution)/shard_map/pallas_call | solution.py:30
  56.8 0.6 collective-permute-start.10
  57.4 1.6 %collective-permute-start.30 = (f32[32,1408]{1,0:T(8,128)S(1)}, f32[32,1408]{1,0:T(8,128)S(1)}, u32[]{:S(2)}, u32[]{:S(2)}) collective-permute-start(f32[32,1408]{1,0:T(8,128)S(1)} %add.62), channel_id=1, source_target_pairs={{0,2},{1,3},{2,0},{3,1},{4,6},{5,7},{6,4},{7,5},{8,10},{9,11},{10,... | collective-permute-start | bytes 540680 | tf_op jit(solution)/shard_map/ppermute | solution.py:301
  59.0 0.8 %collective-permute-start.27 = (f32[32,1280]{1,0:T(8,128)S(1)}, f32[32,1280]{1,0:T(8,128)S(1)}, u32[]{:S(2)}, u32[]{:S(2)}) collective-permute-start(f32[32,1280]{1,0:T(8,128)S(1)} %add.60), channel_id=1, source_target_pairs={{0,4},{1,5},{2,6},{3,7},{4,0},{5,1},{6,2},{7,3},{8,12},{9,13},{10,... | collective-permute-start | bytes 491528 | tf_op jit(solution)/shard_map/ppermute | solution.py:301
  59.8 1.1 %collective-permute-done.13 = f32[32,1408]{1,0:T(8,128)S(1)} collective-permute-done((f32[32,1408]{1,0:T(8,128)S(1)}, f32[32,1408]{1,0:T(8,128)S(1)}, u32[]{:S(2)}, u32[]{:S(2)}) %collective-permute-start.13) | collective-permute-done | bytes 180256 | tf_op jit(solution)/shard_map/ppermute | solution.py:301
  60.9 2.5 %collective-permute-start.14 = (f32[32,1408]{1,0:T(8,128)S(1)}, f32[32,1408]{1,0:T(8,128)S(1)}, u32[]{:S(2)}, u32[]{:S(2)}) collective-permute-start(f32[32,1408]{1,0:T(8,128)S(1)} %add.54), channel_id=1, source_target_pairs={{0,4},{1,5},{2,6},{3,7},{4,0},{5,1},{6,2},{7,3},{8,12},{9,13},{10,... | collective-permute-start | bytes 540680 | tf_op jit(solution)/shard_map/ppermute | solution.py:301
  63.5 1.0 %collective-permute-start.11 = (f32[32,1280]{1,0:T(8,128)S(1)}, f32[32,1280]{1,0:T(8,128)S(1)}, u32[]{:S(2)}, u32[]{:S(2)}) collective-permute-start(f32[32,1280]{1,0:T(8,128)S(1)} %add.52), channel_id=1, source_target_pairs={{0,2},{1,3},{2,0},{3,1},{4,6},{5,7},{6,4},{7,5},{8,10},{9,11},{10,... | collective-permute-start | bytes 491528 | tf_op jit(solution)/shard_map/ppermute | solution.py:301
  64.4 0.3 collective-permute-done.30
  64.8 2.5 %collective-permute-start.31 = (f32[32,1408]{1,0:T(8,128)S(1)}, f32[32,1408]{1,0:T(8,128)S(1)}, u32[]{:S(2)}, u32[]{:S(2)}) collective-permute-start(f32[32,1408]{1,0:T(8,128)S(1)} %add.63.refs_0_), channel_id=1, source_target_pairs={{0,4},{1,5},{2,6},{3,7},{4,0},{5,1},{6,2},{7,3},{8,12},{9,13},{10,... | collective-permute-start | bytes 540680 | tf_op jit(solution)/shard_map/ppermute | solution.py:301
  67.3 0.6 collective-permute-start.28
  67.9 1.7 %collective-permute-done.14 = f32[32,1408]{1,0:T(8,128)S(1)} collective-permute-done((f32[32,1408]{1,0:T(8,128)S(1)}, f32[32,1408]{1,0:T(8,128)S(1)}, u32[]{:S(2)}, u32[]{:S(2)}) %collective-permute-start.14) | collective-permute-done | bytes 180256 | tf_op jit(solution)/shard_map/ppermute | solution.py:301
  69.7 1.6 %collective-permute-start.15 = (f32[32,1408]{1,0:T(8,128)S(1)}, f32[32,1408]{1,0:T(8,128)S(1)}, u32[]{:S(2)}, u32[]{:S(2)}) collective-permute-start(f32[32,1408]{1,0:T(8,128)S(1)} %add.55.refs_0_), channel_id=1, source_target_pairs={{0,2},{1,3},{2,0},{3,1},{4,6},{5,7},{6,4},{7,5},{8,10},{9,11},{10,... | collective-permute-start | bytes 540680 | tf_op jit(solution)/shard_map/ppermute | solution.py:301
  71.3 0.4 collective-permute-start.12
  71.7 0.9 %shard_map.55 = (f32[64,1280]{1,0:T(8,128)S(1)}, f32[64,128]{1,0:T(8,128)S(1)}, f32[64,512]{1,0:T(8,128)S(1)}) custom-call(f32[32,1408]{1,0:T(8,128)S(1)} %add.63.refs_0_, f32[32,1408]{1,0:T(8,128)S(1)} %collective-permute-done.31.refs_1_, bf16[2,2560,256]{2,1,0:T(8,128)(2,1)S(1)} %get-tuple-element.60.refs_8_.refs_2_.refs_10_.refs_11_, ...), custom_call_target="tpu_custom_call" | custom-call | bytes 10846208 | tf_op jit(solution)/shard_map/pallas_call | solution.py:30
  72.7 0.0 collective-permute-done.28.refs_1_
  72.7 1.0 %shard_map.56 = (f32[2,64,256]{2,1,0:T(8,128)S(1)}, f32[2,64,256]{2,1,0:T(8,128)S(1)}) custom-call(f32[32,1280]{1,0:T(8,128)S(1)} %add.61.refs_0_, f32[32,1280]{1,0:T(8,128)S(1)} %collective-permute-done.28.refs_1_, f32[64,1280]{1,0:T(8,128)S(1)} %get-tuple-element.102.refs_2_, f32[64,128]{1,0:T(8,128)S(1)} %get-tuple-element.103.refs_3_, ...), custom_call_target="tpu_custom_call" | custom-call | flops 1006632960 | bytes 12386304 | tf_op jit(solution)/shard_map/pallas_call | solution.py:30
  73.7 0.1 collective-permute-start.32
  73.8 1.5 %collective-permute-done.15.refs_1_ = f32[32,1408]{1,0:T(8,128)S(1)} collective-permute-done((f32[32,1408]{1,0:T(8,128)S(1)}, f32[32,1408]{1,0:T(8,128)S(1)}, u32[]{:S(2)}, u32[]{:S(2)}) %collective-permute-start.15) | collective-permute-done | bytes 180256 | tf_op jit(solution)/shard_map/ppermute | solution.py:301
  75.3 0.9 %shard_map.48 = (f32[64,1280]{1,0:T(8,128)S(1)}, f32[64,128]{1,0:T(8,128)S(1)}, f32[64,512]{1,0:T(8,128)S(1)}) custom-call(f32[32,1408]{1,0:T(8,128)S(1)} %add.55.refs_0_, f32[32,1408]{1,0:T(8,128)S(1)} %collective-permute-done.15.refs_1_, bf16[2,2560,256]{2,1,0:T(8,128)(2,1)S(1)} %get-tuple-element.60.refs_8_.refs_2_.refs_10_.refs_11_, ...), custom_call_target="tpu_custom_call" | custom-call | bytes 10846208 | tf_op jit(solution)/shard_map/pallas_call | solution.py:30
  76.2 0.5 collective-permute-done.12.refs_1_
  76.7 1.0 %shard_map.49 = (f32[2,64,256]{2,1,0:T(8,128)S(1)}, f32[2,64,256]{2,1,0:T(8,128)S(1)}) custom-call(f32[32,1280]{1,0:T(8,128)S(1)} %add.53.refs_0_, f32[32,1280]{1,0:T(8,128)S(1)} %collective-permute-done.12.refs_1_, f32[64,1280]{1,0:T(8,128)S(1)} %get-tuple-element.79.refs_2_, f32[64,128]{1,0:T(8,128)S(1)} %get-tuple-element.80.refs_3_, ...), custom_call_target="tpu_custom_call" | custom-call | flops 1006632960 | bytes 12386304 | tf_op jit(solution)/shard_map/pallas_call | solution.py:30
  77.7 0.1 collective-permute-start.16
  77.8 1.3 %collective-permute-done.16.refs_1_ = f32[2,64,256]{2,1,0:T(8,128)S(1)} collective-permute-done((f32[2,64,256]{2,1,0:T(8,128)S(1)}, f32[2,64,256]{2,1,0:T(8,128)S(1)}, u32[]{:S(2)}, u32[]{:S(2)}) %collective-permute-start.16) | collective-permute-done | bytes 131104 | tf_op jit(solution)/shard_map/ppermute | solution.py:301
  79.1 0.9 %shard_map.57 = (f32[2,256,128]{2,1,0:T(8,128)}, f32[2,256,128]{2,1,0:T(8,128)}) custom-call(f32[2,64,256]{2,1,0:T(8,128)S(1)} %get-tuple-element.85.refs_0_, f32[2,64,256]{2,1,0:T(8,128)S(1)} %collective-permute-done.16.refs_1_, f32[2,64,256]{2,1,0:T(8,128)S(1)} %get-tuple-element.108.refs_2_, f32[2,64,256]{2,1,0:T(8,128)S(1)} %collective-permute-done.32.refs_3_), custom_call_target="tpu_custom_call" | custom-call | bytes 524288 | tf_op jit(solution)/shard_map/pallas_call | solution.py:30
  (36 shorter events, 0.4 us)
Async XLA Ops:
  0.6 11.6 %collective-permute-start.3 = (f32[2,256,2560]{2,1,0:T(8,128)}, f32[2,256,2560]{2,1,0:T(8,128)S(1)}, u32[]{:S(2)}, u32[]{:S(2)}) collective-permute-start(f32[2,256,2560]{2,1,0:T(8,128)} %down_ref.1), channel_id=1, source_target_pairs={{0,1},{1,0},{2,3},{3,2},{4,5},{5,4},{6,7},{7,6},{8,9},{9,8},{10,11... | collective-permute-start | bytes 15728648 | tf_op jit(solution)/shard_map/ppermute | solution.py:301
  2.2 12.2 %collective-permute-start.19 = (f32[2,8,2560]{2,1,0:T(8,128)S(1)}, f32[2,8,2560]{2,1,0:T(8,128)S(1)}, u32[]{:S(2)}, u32[]{:S(2)}) collective-permute-start(f32[2,8,2560]{2,1,0:T(8,128)S(1)} %get-tuple-element.110.refs_0_), channel_id=1, source_target_pairs={{0,6},{1,7},{2,4},{3,5},{4,2},{5,3},{6,0},{7,1},{8,14},{9,15},{10,... | collective-permute-start | bytes 491528 | tf_op jit(solution)/shard_map/ppermute | solution.py:304
  5.7 10.0 %collective-permute-start.18 = (f32[2,8,2560]{2,1,0:T(8,128)S(1)}, f32[2,8,2560]{2,1,0:T(8,128)S(1)}, u32[]{:S(2)}, u32[]{:S(2)}) collective-permute-start(f32[2,8,2560]{2,1,0:T(8,128)S(1)} %get-tuple-element.110.refs_0_), channel_id=1, source_target_pairs={{0,4},{1,5},{2,6},{3,7},{4,0},{5,1},{6,2},{7,3},{8,12},{9,13},{10,... | collective-permute-start | bytes 491528 | tf_op jit(solution)/shard_map/ppermute | solution.py:304
  6.2 9.5 %collective-permute-start.17 = (f32[2,8,2560]{2,1,0:T(8,128)S(1)}, f32[2,8,2560]{2,1,0:T(8,128)S(1)}, u32[]{:S(2)}, u32[]{:S(2)}) collective-permute-start(f32[2,8,2560]{2,1,0:T(8,128)S(1)} %get-tuple-element.110.refs_0_), channel_id=1, source_target_pairs={{0,2},{1,3},{2,0},{3,1},{4,6},{5,7},{6,4},{7,5},{8,10},{9,11},{10,... | collective-permute-start | bytes 491528 | tf_op jit(solution)/shard_map/ppermute | solution.py:304
  6.3 15.3 %collective-permute-start.2 = (f32[2,8,2560]{2,1,0:T(8,128)S(1)}, f32[2,8,2560]{2,1,0:T(8,128)S(1)}, u32[]{:S(2)}, u32[]{:S(2)}) collective-permute-start(f32[2,8,2560]{2,1,0:T(8,128)S(1)} %get-tuple-element.111.refs_0_), channel_id=1, source_target_pairs={{0,6},{1,7},{2,4},{3,5},{4,2},{5,3},{6,0},{7,1},{8,14},{9,15},{10,... | collective-permute-start | bytes 491528 | tf_op jit(solution)/shard_map/ppermute | solution.py:304
  12.2 9.4 %collective-permute-start.1 = (f32[2,8,2560]{2,1,0:T(8,128)S(1)}, f32[2,8,2560]{2,1,0:T(8,128)S(1)}, u32[]{:S(2)}, u32[]{:S(2)}) collective-permute-start(f32[2,8,2560]{2,1,0:T(8,128)S(1)} %get-tuple-element.111.refs_0_), channel_id=1, source_target_pairs={{0,4},{1,5},{2,6},{3,7},{4,0},{5,1},{6,2},{7,3},{8,12},{9,13},{10,... | collective-permute-start | bytes 491528 | tf_op jit(solution)/shard_map/ppermute | solution.py:304
  14.4 7.3 %collective-permute-start = (f32[2,8,2560]{2,1,0:T(8,128)S(1)}, f32[2,8,2560]{2,1,0:T(8,128)S(1)}, u32[]{:S(2)}, u32[]{:S(2)}) collective-permute-start(f32[2,8,2560]{2,1,0:T(8,128)S(1)} %get-tuple-element.111.refs_0_), channel_id=1, source_target_pairs={{0,2},{1,3},{2,0},{3,1},{4,6},{5,7},{6,4},{7,5},{8,10},{9,11},{10,... | collective-permute-start | bytes 491528 | tf_op jit(solution)/shard_map/ppermute | solution.py:304
  18.2 8.3 %collective-permute-start.23 = (f32[32,1408]{1,0:T(8,128)S(1)}, f32[32,1408]{1,0:T(8,128)S(1)}, u32[]{:S(2)}, u32[]{:S(2)}) collective-permute-start(f32[32,1408]{1,0:T(8,128)S(1)} %get-tuple-element.92), channel_id=1, source_target_pairs={{0,4},{1,5},{2,6},{3,7},{4,0},{5,1},{6,2},{7,3},{8,12},{9,13},{10,... | collective-permute-start | bytes 540680 | tf_op jit(solution)/shard_map/ppermute | solution.py:301
  20.1 8.6 %collective-permute-start.20 = (f32[32,1280]{1,0:T(8,128)S(1)}, f32[32,1280]{1,0:T(8,128)S(1)}, u32[]{:S(2)}, u32[]{:S(2)}) collective-permute-start(f32[32,1280]{1,0:T(8,128)S(1)} %get-tuple-element.89), channel_id=1, source_target_pairs={{0,2},{1,3},{2,0},{3,1},{4,6},{5,7},{6,4},{7,5},{8,10},{9,11},{10,... | collective-permute-start | bytes 491528 | tf_op jit(solution)/shard_map/ppermute | solution.py:301
  24.3 7.5 %collective-permute-start.7 = (f32[32,1408]{1,0:T(8,128)S(1)}, f32[32,1408]{1,0:T(8,128)S(1)}, u32[]{:S(2)}, u32[]{:S(2)}) collective-permute-start(f32[32,1408]{1,0:T(8,128)S(1)} %get-tuple-element.70), channel_id=1, source_target_pairs={{0,2},{1,3},{2,0},{3,1},{4,6},{5,7},{6,4},{7,5},{8,10},{9,11},{10,... | collective-permute-start | bytes 540680 | tf_op jit(solution)/shard_map/ppermute | solution.py:301
  26.6 7.5 %collective-permute-start.24 = (f32[32,1408]{1,0:T(8,128)S(1)}, f32[32,1408]{1,0:T(8,128)S(1)}, u32[]{:S(2)}, u32[]{:S(2)}) collective-permute-start(f32[32,1408]{1,0:T(8,128)S(1)} %add.58), channel_id=1, source_target_pairs={{0,2},{1,3},{2,0},{3,1},{4,6},{5,7},{6,4},{7,5},{8,10},{9,11},{10,... | collective-permute-start | bytes 540680 | tf_op jit(solution)/shard_map/ppermute | solution.py:301
  27.4 8.4 %collective-permute-start.4 = (f32[32,1280]{1,0:T(8,128)S(1)}, f32[32,1280]{1,0:T(8,128)S(1)}, u32[]{:S(2)}, u32[]{:S(2)}) collective-permute-start(f32[32,1280]{1,0:T(8,128)S(1)} %get-tuple-element.68), channel_id=1, source_target_pairs={{0,4},{1,5},{2,6},{3,7},{4,0},{5,1},{6,2},{7,3},{8,12},{9,13},{10,... | collective-permute-start | bytes 491528 | tf_op jit(solution)/shard_map/ppermute | solution.py:301
  28.8 9.3 %collective-permute-start.21 = (f32[32,1280]{1,0:T(8,128)S(1)}, f32[32,1280]{1,0:T(8,128)S(1)}, u32[]{:S(2)}, u32[]{:S(2)}) collective-permute-start(f32[32,1280]{1,0:T(8,128)S(1)} %add.56), channel_id=1, source_target_pairs={{0,4},{1,5},{2,6},{3,7},{4,0},{5,1},{6,2},{7,3},{8,12},{9,13},{10,... | collective-permute-start | bytes 491528 | tf_op jit(solution)/shard_map/ppermute | solution.py:301
  31.9 11.0 %collective-permute-start.8 = (f32[32,1408]{1,0:T(8,128)S(1)}, f32[32,1408]{1,0:T(8,128)S(1)}, u32[]{:S(2)}, u32[]{:S(2)}) collective-permute-start(f32[32,1408]{1,0:T(8,128)S(1)} %add.50), channel_id=1, source_target_pairs={{0,4},{1,5},{2,6},{3,7},{4,0},{5,1},{6,2},{7,3},{8,12},{9,13},{10,... | collective-permute-start | bytes 540680 | tf_op jit(solution)/shard_map/ppermute | solution.py:301
  34.1 11.3 %collective-permute-start.25 = (f32[32,1408]{1,0:T(8,128)S(1)}, f32[32,1408]{1,0:T(8,128)S(1)}, u32[]{:S(2)}, u32[]{:S(2)}) collective-permute-start(f32[32,1408]{1,0:T(8,128)S(1)} %add.59.refs_0_), channel_id=1, source_target_pairs={{0,4},{1,5},{2,6},{3,7},{4,0},{5,1},{6,2},{7,3},{8,12},{9,13},{10,... | collective-permute-start | bytes 540680 | tf_op jit(solution)/shard_map/ppermute | solution.py:301
  35.8 7.0 %collective-permute-start.5 = (f32[32,1280]{1,0:T(8,128)S(1)}, f32[32,1280]{1,0:T(8,128)S(1)}, u32[]{:S(2)}, u32[]{:S(2)}) collective-permute-start(f32[32,1280]{1,0:T(8,128)S(1)} %add.48), channel_id=1, source_target_pairs={{0,2},{1,3},{2,0},{3,1},{4,6},{5,7},{6,4},{7,5},{8,10},{9,11},{10,... | collective-permute-start | bytes 491528 | tf_op jit(solution)/shard_map/ppermute | solution.py:301
  38.1 8.3 %collective-permute-start.22 = (f32[32,1280]{1,0:T(8,128)S(1)}, f32[32,1280]{1,0:T(8,128)S(1)}, u32[]{:S(2)}, u32[]{:S(2)}) collective-permute-start(f32[32,1280]{1,0:T(8,128)S(1)} %add.57.refs_0_), channel_id=1, source_target_pairs={{0,2},{1,3},{2,0},{3,1},{4,6},{5,7},{6,4},{7,5},{8,10},{9,11},{10,... | collective-permute-start | bytes 491528 | tf_op jit(solution)/shard_map/ppermute | solution.py:301
  42.8 9.9 %collective-permute-start.6 = (f32[32,1280]{1,0:T(8,128)S(1)}, f32[32,1280]{1,0:T(8,128)S(1)}, u32[]{:S(2)}, u32[]{:S(2)}) collective-permute-start(f32[32,1280]{1,0:T(8,128)S(1)} %add.49.refs_0_), channel_id=1, source_target_pairs={{0,4},{1,5},{2,6},{3,7},{4,0},{5,1},{6,2},{7,3},{8,12},{9,13},{10,... | collective-permute-start | bytes 491528 | tf_op jit(solution)/shard_map/ppermute | solution.py:301
  42.9 8.8 %collective-permute-start.9 = (f32[32,1408]{1,0:T(8,128)S(1)}, f32[32,1408]{1,0:T(8,128)S(1)}, u32[]{:S(2)}, u32[]{:S(2)}) collective-permute-start(f32[32,1408]{1,0:T(8,128)S(1)} %add.51.refs_0_), channel_id=1, source_target_pairs={{0,2},{1,3},{2,0},{3,1},{4,6},{5,7},{6,4},{7,5},{8,10},{9,11},{10,... | collective-permute-start | bytes 540680 | tf_op jit(solution)/shard_map/ppermute | solution.py:301
  48.4 9.0 %collective-permute-start.29 = (f32[32,1408]{1,0:T(8,128)S(1)}, f32[32,1408]{1,0:T(8,128)S(1)}, u32[]{:S(2)}, u32[]{:S(2)}) collective-permute-start(f32[32,1408]{1,0:T(8,128)S(1)} %get-tuple-element.101), channel_id=1, source_target_pairs={{0,4},{1,5},{2,6},{3,7},{4,0},{5,1},{6,2},{7,3},{8,12},{9,13},{10,... | collective-permute-start | bytes 540680 | tf_op jit(solution)/shard_map/ppermute | solution.py:301
  50.9 8.1 %collective-permute-start.26 = (f32[32,1280]{1,0:T(8,128)S(1)}, f32[32,1280]{1,0:T(8,128)S(1)}, u32[]{:S(2)}, u32[]{:S(2)}) collective-permute-start(f32[32,1280]{1,0:T(8,128)S(1)} %get-tuple-element.98), channel_id=1, source_target_pairs={{0,2},{1,3},{2,0},{3,1},{4,6},{5,7},{6,4},{7,5},{8,10},{9,11},{10,... | collective-permute-start | bytes 491528 | tf_op jit(solution)/shard_map/ppermute | solution.py:301
  54.5 6.4 %collective-permute-start.13 = (f32[32,1408]{1,0:T(8,128)S(1)}, f32[32,1408]{1,0:T(8,128)S(1)}, u32[]{:S(2)}, u32[]{:S(2)}) collective-permute-start(f32[32,1408]{1,0:T(8,128)S(1)} %get-tuple-element.78), channel_id=1, source_target_pairs={{0,2},{1,3},{2,0},{3,1},{4,6},{5,7},{6,4},{7,5},{8,10},{9,11},{10,... | collective-permute-start | bytes 540680 | tf_op jit(solution)/shard_map/ppermute | solution.py:301
  56.8 6.6 %collective-permute-start.10 = (f32[32,1280]{1,0:T(8,128)S(1)}, f32[32,1280]{1,0:T(8,128)S(1)}, u32[]{:S(2)}, u32[]{:S(2)}) collective-permute-start(f32[32,1280]{1,0:T(8,128)S(1)} %get-tuple-element.76), channel_id=1, source_target_pairs={{0,4},{1,5},{2,6},{3,7},{4,0},{5,1},{6,2},{7,3},{8,12},{9,13},{10,... | collective-permute-start | bytes 491528 | tf_op jit(solution)/shard_map/ppermute | solution.py:301
  57.4 7.3 %collective-permute-start.30 = (f32[32,1408]{1,0:T(8,128)S(1)}, f32[32,1408]{1,0:T(8,128)S(1)}, u32[]{:S(2)}, u32[]{:S(2)}) collective-permute-start(f32[32,1408]{1,0:T(8,128)S(1)} %add.62), channel_id=1, source_target_pairs={{0,2},{1,3},{2,0},{3,1},{4,6},{5,7},{6,4},{7,5},{8,10},{9,11},{10,... | collective-permute-start | bytes 540680 | tf_op jit(solution)/shard_map/ppermute | solution.py:301
  59.0 8.3 %collective-permute-start.27 = (f32[32,1280]{1,0:T(8,128)S(1)}, f32[32,1280]{1,0:T(8,128)S(1)}, u32[]{:S(2)}, u32[]{:S(2)}) collective-permute-start(f32[32,1280]{1,0:T(8,128)S(1)} %add.60), channel_id=1, source_target_pairs={{0,4},{1,5},{2,6},{3,7},{4,0},{5,1},{6,2},{7,3},{8,12},{9,13},{10,... | collective-permute-start | bytes 491528 | tf_op jit(solution)/shard_map/ppermute | solution.py:301
  60.9 8.8 %collective-permute-start.14 = (f32[32,1408]{1,0:T(8,128)S(1)}, f32[32,1408]{1,0:T(8,128)S(1)}, u32[]{:S(2)}, u32[]{:S(2)}) collective-permute-start(f32[32,1408]{1,0:T(8,128)S(1)} %add.54), channel_id=1, source_target_pairs={{0,4},{1,5},{2,6},{3,7},{4,0},{5,1},{6,2},{7,3},{8,12},{9,13},{10,... | collective-permute-start | bytes 540680 | tf_op jit(solution)/shard_map/ppermute | solution.py:301
  63.5 7.8 %collective-permute-start.11 = (f32[32,1280]{1,0:T(8,128)S(1)}, f32[32,1280]{1,0:T(8,128)S(1)}, u32[]{:S(2)}, u32[]{:S(2)}) collective-permute-start(f32[32,1280]{1,0:T(8,128)S(1)} %add.52), channel_id=1, source_target_pairs={{0,2},{1,3},{2,0},{3,1},{4,6},{5,7},{6,4},{7,5},{8,10},{9,11},{10,... | collective-permute-start | bytes 491528 | tf_op jit(solution)/shard_map/ppermute | solution.py:301
  64.8 7.0 %collective-permute-start.31 = (f32[32,1408]{1,0:T(8,128)S(1)}, f32[32,1408]{1,0:T(8,128)S(1)}, u32[]{:S(2)}, u32[]{:S(2)}) collective-permute-start(f32[32,1408]{1,0:T(8,128)S(1)} %add.63.refs_0_), channel_id=1, source_target_pairs={{0,4},{1,5},{2,6},{3,7},{4,0},{5,1},{6,2},{7,3},{8,12},{9,13},{10,... | collective-permute-start | bytes 540680 | tf_op jit(solution)/shard_map/ppermute | solution.py:301
  67.3 5.4 %collective-permute-start.28 = (f32[32,1280]{1,0:T(8,128)S(1)}, f32[32,1280]{1,0:T(8,128)S(1)}, u32[]{:S(2)}, u32[]{:S(2)}) collective-permute-start(f32[32,1280]{1,0:T(8,128)S(1)} %add.61.refs_0_), channel_id=1, source_target_pairs={{0,2},{1,3},{2,0},{3,1},{4,6},{5,7},{6,4},{7,5},{8,10},{9,11},{10,... | collective-permute-start | bytes 491528 | tf_op jit(solution)/shard_map/ppermute | solution.py:301
  69.7 5.6 %collective-permute-start.15 = (f32[32,1408]{1,0:T(8,128)S(1)}, f32[32,1408]{1,0:T(8,128)S(1)}, u32[]{:S(2)}, u32[]{:S(2)}) collective-permute-start(f32[32,1408]{1,0:T(8,128)S(1)} %add.55.refs_0_), channel_id=1, source_target_pairs={{0,2},{1,3},{2,0},{3,1},{4,6},{5,7},{6,4},{7,5},{8,10},{9,11},{10,... | collective-permute-start | bytes 540680 | tf_op jit(solution)/shard_map/ppermute | solution.py:301
  71.3 5.4 %collective-permute-start.12 = (f32[32,1280]{1,0:T(8,128)S(1)}, f32[32,1280]{1,0:T(8,128)S(1)}, u32[]{:S(2)}, u32[]{:S(2)}) collective-permute-start(f32[32,1280]{1,0:T(8,128)S(1)} %add.53.refs_0_), channel_id=1, source_target_pairs={{0,4},{1,5},{2,6},{3,7},{4,0},{5,1},{6,2},{7,3},{8,12},{9,13},{10,... | collective-permute-start | bytes 491528 | tf_op jit(solution)/shard_map/ppermute | solution.py:301
  73.7 4.1 %collective-permute-start.32 = (f32[2,64,256]{2,1,0:T(8,128)S(1)}, f32[2,64,256]{2,1,0:T(8,128)S(1)}, u32[]{:S(2)}, u32[]{:S(2)}) collective-permute-start(f32[2,64,256]{2,1,0:T(8,128)S(1)} %get-tuple-element.109), channel_id=1, source_target_pairs={{0,1},{1,0},{2,3},{3,2},{4,5},{5,4},{6,7},{7,6},{8,9},{9,8},{10,11... | collective-permute-start | bytes 393224 | tf_op jit(solution)/shard_map/ppermute | solution.py:301
  77.7 1.4 %collective-permute-start.16 = (f32[2,64,256]{2,1,0:T(8,128)S(1)}, f32[2,64,256]{2,1,0:T(8,128)S(1)}, u32[]{:S(2)}, u32[]{:S(2)}) collective-permute-start(f32[2,64,256]{2,1,0:T(8,128)S(1)} %get-tuple-element.86), channel_id=1, source_target_pairs={{0,1},{1,0},{2,3},{3,2},{4,5},{5,4},{6,7},{7,6},{8,9},{9,8},{10,11... | collective-permute-start | bytes 393224 | tf_op jit(solution)/shard_map/ppermute | solution.py:301

commit v10 on v6

--- a/solution.py
+++ b/solution.py
@@ -215,7 +215,32 @@
     project(residual_ref, f1, s1, pairs(down[:4]), slice(0, front), *outs, bits[0], tail(row_squares(residual)))
 
 
-def last_kernel(bit, *refs):
+def last_kernel(bit, side, *refs):
+    pieces, (a_ref, ends_ref, part_ref, rhs_ref, before_a, before_b, scalar_ref, image_ref, residual_ref) = refs[:2], refs[2:11]
+    turned, (out_ref, x_ref, *scratch) = refs[11:13], refs[13:]
+    rows = turned[0].shape[2]
+    lines = slice(side * rows, (side + 1) * rows)
+    front = a_ref.shape[1]
+    collect(pieces, x_ref, bit)
+    following = both(ends_ref[:, 0:1])
+    norm = scalar_ref[:, 0:1]
+    damping = scalar_ref[:, 1:2]
+    alpha = scalar_ref[:, 2:3]
+    beta = following / norm
+    residual = residual_ref[:, lines]
+    image = part_ref[:, lines] + apply_down(x_ref, *scratch, pairs(turned), slice(front, None))
+    image = image + beta * image_ref[:, lines] + damping * residual
+    squares = row_squares(a_ref[...] + beta * before_a[...]) + row_squares(x_ref[...] + beta * before_b[...])
+    curvature = both(squares) + damping * (following + beta * following)
+    alpha_next = following / curvature
+    rhs = rhs_ref[:, lines]
+    found = alpha * rhs + alpha_next * (residual + beta * rhs)
+    left = residual - alpha_next * image
+    out_ref[0] = found
+    out_ref[1] = left
+
+
+def whole_kernel(bit, *refs):
     pieces, (a_ref, ends_ref, part_ref, rhs_ref, before_a, before_b, scalar_ref, image_ref, residual_ref) = refs[:2], refs[2:11]
     turned, (keep_ref, give_ref, x_ref, *scratch) = refs[11:15], refs[15:]
     front = a_ref.shape[1]
@@ -367,14 +392,27 @@
         return (rhs, before, x, scalars, image, residual), start(name, 0, pair)
 
     def close(name, total, led, kept):
-        keep, give = launch(
-            name,
-            functools.partial(last_kernel, ends[way(name, 1)]),
-            [((2, packed, rows), f32)] * 2,
-            (total.keep, total.other, *led, *kept, *turned),
-            [ranged] + narrow,
-            work,
-        )
+        if name[0] == "a":
+            keep, give = launch(
+                name,
+                functools.partial(whole_kernel, ends[way(name, 1)]),
+                [((2, packed, rows), f32)] * 2,
+                (total.keep, total.other, *led, *kept, *turned),
+                [ranged] + narrow,
+                work,
+            )
+            return keep, swap(give, 0)
+        results = []
+        for side in (1, 0):
+            (piece,) = call(
+                functools.partial(last_kernel, ends[way(name, 1)], side),
+                [((2, packed, rows), f32)],
+                (*after(name, total.keep), total.other, *led, *kept, *turned[2 * side : 2 * side + 2]),
+                [ranged] + narrow,
+                int(work // 2),
+            )
+            results.append(piece)
+        give, keep = results
         return keep, swap(give, 0)
 
     def rounds(tag, a0, a1, b0, pending):

time: 79.7 us -> 79.7 us (level)
    pallas_call x17 -> x18, Pallas kernels: 25.3 us -> 25.5 us  [call(): pl.pallas_call(kernel, out_shape=[jax.ShapeDtypeStruct(shape, dtype) for...]
  transfers between devices with their start and end apart: 33 -> 33, of which waited for: 13 -> 12; matrix products, arithmetic and copies ran while one was open for 2% -> 2% of each run, Pallas kernels for 31% -> 31%
where the time goes in v10:
time: 79.7 us; the launch traced here: 79.5 us
  starting transfers between devices  35.7 us (45%)
  Pallas kernels  25.5 us (32%)
  waiting for transfers between devices  16 us (20%)
  local copies, waits for them, and re-layouts  1.02 us (1%)
  between operations  0.9 us (1%)
    ppermute x27, starting transfers between devices, swap(): lax.ppermute(value, 'rcv', [(at, at ^ 1 << bit) for at in range(count)])  27.7 us
    pallas_call x18, Pallas kernels, call(): pl.pallas_call(kernel, out_shape=[jax.ShapeDtypeStruct(shape, dtype) for...  25.5 us
    ppermute x27, waiting for transfers between devices, swap(): lax.ppermute(value, 'rcv', [(at, at ^ 1 << bit) for at in range(count)])  16 us
    ppermute x6, starting transfers between devices, jump(): lax.ppermute(value, 'rcv', [(at, at ^ mask << 1) for at in range(count)])  7.92 us
  transfers between devices with their start and end apart: 33, of which 12 were waited for; matrix products, arithmetic and copies ran while one was open for 2% of the time, Pallas kernels for 31%

profile of v10, /device:TPU:0, one launch (start us, length us, event | category | flops | bytes accessed | tf_op | source)
XLA Modules:
  0.0 79.5 jit_solution(6545625867891842831)
XLA Ops:
  0.6 0.5 collective-permute-start.3
  1.1 1.0 %fusion = (f32[2,8,2560]{2,1,0:T(8,128)S(1)}, f32[2,8,2560]{2,1,0:T(8,128)S(1)}) fusion(f32[2,16,2560]{2,1,0:T(8,128)} %param.3), kind=kLoop, calls=%fused_computation | loop fusion | bytes 655360 | tf_op jit(solution)/shard_map/slice | solution.py:319
  2.2 3.5 %collective-permute-start.19 = (f32[2,8,2560]{2,1,0:T(8,128)S(1)}, f32[2,8,2560]{2,1,0:T(8,128)S(1)}, u32[]{:S(2)}, u32[]{:S(2)}) collective-permute-start(f32[2,8,2560]{2,1,0:T(8,128)S(1)} %get-tuple-element.104.refs_0_), channel_id=1, source_target_pairs={{0,6},{1,7},{2,4},{3,5},{4,2},{5,3},{6,0},{7,1},{8,14},{9,15},{10,... | collective-permute-start | bytes 491528 | tf_op jit(solution)/shard_map/ppermute | solution.py:313
  5.7 0.5 collective-permute-start.18
  6.2 0.1 collective-permute-start.17
  6.3 2.8 %collective-permute-start.2 = (f32[2,8,2560]{2,1,0:T(8,128)S(1)}, f32[2,8,2560]{2,1,0:T(8,128)S(1)}, u32[]{:S(2)}, u32[]{:S(2)}) collective-permute-start(f32[2,8,2560]{2,1,0:T(8,128)S(1)} %get-tuple-element.105.refs_0_), channel_id=1, source_target_pairs={{0,6},{1,7},{2,4},{3,5},{4,2},{5,3},{6,0},{7,1},{8,14},{9,15},{10,... | collective-permute-start | bytes 491528 | tf_op jit(solution)/shard_map/ppermute | solution.py:313
  9.2 4.0 %shard_map.41 = (bf16[2,256,2560]{2,1,0:T(8,128)(2,1)S(1)}, bf16[2,256,2560]{2,1,0:T(8,128)(2,1)S(1)}, bf16[2,2560,256]{2,1,0:T(8,128)(2,1)S(1)}, bf16[2,2560,256]{2,1,0:T(8,128)(2,1)S(1)}, f32[8,128]{1,0:T(8,128)S(1)}) custom-call(f32[2,256,2560]{2,1,0:T(8,128)} %imag_ref.1, f32[2,256,2560]{2,1,0:T(8,128)} %imag_ref.1), custom_call_target="tpu_custom_call" | custom-call | bytes 10485760 | tf_op jit(solution)/shard_map/pallas_call | solution.py:30
  13.2 0.6 collective-permute-start.1
  13.7 2.1 %shard_map.42 = (bf16[2,256,2560]{2,1,0:T(8,128)(2,1)S(1)}, bf16[2,256,2560]{2,1,0:T(8,128)(2,1)S(1)}, bf16[2,2560,256]{2,1,0:T(8,128)(2,1)S(1)}, bf16[2,2560,256]{2,1,0:T(8,128)(2,1)S(1)}, f32[8,128]{1,0:T(8,128)S(1)}) custom-call(f32[2,256,2560]{2,1,0:T(8,128)S(1)} %collective-permute-done.3.real_ref.imag_ref, ...), custom_call_target="tpu_custom_call" | custom-call | bytes 10485760 | tf_op jit(solution)/shard_map/pallas_call | solution.py:30
  15.9 0.3 collective-permute-start
  16.2 2.6 %shard_map.50 = (f32[64,512]{1,0:T(8,128)S(1)}, f32[32,1408]{1,0:T(8,128)S(1)}, f32[32,1408]{1,0:T(8,128)S(1)}) custom-call(f32[2,8,2560]{2,1,0:T(8,128)S(1)} %get-tuple-element.104.refs_0_, f32[2,8,2560]{2,1,0:T(8,128)S(1)} %collective-permute-done.17.refs_1_, f32[2,8,2560]{2,1,0:T(8,128)S(1)} %collective-permute-done.18.refs_2_, ...), custom_call_target="tpu_custom_call" | custom-call | flops 3019898880 | bytes 21635072 | tf_op jit(solution)/shard_map/pallas_call | solution.py:30
  18.8 1.8 %collective-permute-start.23 = (f32[32,1408]{1,0:T(8,128)S(1)}, f32[32,1408]{1,0:T(8,128)S(1)}, u32[]{:S(2)}, u32[]{:S(2)}) collective-permute-start(f32[32,1408]{1,0:T(8,128)S(1)} %get-tuple-element.88), channel_id=1, source_target_pairs={{0,4},{1,5},{2,6},{3,7},{4,0},{5,1},{6,2},{7,3},{8,12},{9,13},{10,... | collective-permute-start | bytes 540680 | tf_op jit(solution)/shard_map/ppermute | solution.py:310
  20.7 0.9 %shard_map.51 = (f32[32,1280]{1,0:T(8,128)S(1)}, f32[32,1280]{1,0:T(8,128)S(1)}) custom-call(f32[64,512]{1,0:T(8,128)S(1)} %get-tuple-element.84.refs_0_.refs_5_, bf16[2,256,2560]{2,1,0:T(8,128)(2,1)S(1)} %get-tuple-element.53.refs_4_.refs_1_.refs_6_, bf16[2,256,2560]{2,1,0:T(8,128)(2,1)S(1)} %get-tuple-element.54.refs_5_.refs_2_.refs_7_, ...), custom_call_target="tpu_custom_call" | custom-call | bytes 10616832 | tf_op jit(solution)/shard_map/pallas_call | solution.py:30
  21.6 1.6 %collective-permute-start.20 = (f32[32,1280]{1,0:T(8,128)S(1)}, f32[32,1280]{1,0:T(8,128)S(1)}, u32[]{:S(2)}, u32[]{:S(2)}) collective-permute-start(f32[32,1280]{1,0:T(8,128)S(1)} %get-tuple-element.86), channel_id=1, source_target_pairs={{0,2},{1,3},{2,0},{3,1},{4,6},{5,7},{6,4},{7,5},{8,10},{9,11},{10,... | collective-permute-start | bytes 491528 | tf_op jit(solution)/shard_map/ppermute | solution.py:310
  23.2 2.6 %shard_map.43 = (f32[64,512]{1,0:T(8,128)S(1)}, f32[32,1408]{1,0:T(8,128)S(1)}, f32[32,1408]{1,0:T(8,128)S(1)}) custom-call(f32[2,8,2560]{2,1,0:T(8,128)S(1)} %get-tuple-element.105.refs_0_, f32[2,8,2560]{2,1,0:T(8,128)S(1)} %collective-permute-done.refs_1_, f32[2,8,2560]{2,1,0:T(8,128)S(1)} %collective-permute-done.1.refs_2_, ...), custom_call_target="tpu_custom_call" | custom-call | flops 90596966400 | bytes 21635072 | tf_op jit(solution)/shard_map/pallas_call | solution.py:30
  25.8 0.6 collective-permute-start.7
  26.4 1.6 %collective-permute-start.24 = (f32[32,1408]{1,0:T(8,128)S(1)}, f32[32,1408]{1,0:T(8,128)S(1)}, u32[]{:S(2)}, u32[]{:S(2)}) collective-permute-start(f32[32,1408]{1,0:T(8,128)S(1)} %add.58), channel_id=1, source_target_pairs={{0,2},{1,3},{2,0},{3,1},{4,6},{5,7},{6,4},{7,5},{8,10},{9,11},{10,... | collective-permute-start | bytes 540680 | tf_op jit(solution)/shard_map/ppermute | solution.py:310
  28.0 0.9 %shard_map.44 = (f32[32,1280]{1,0:T(8,128)S(1)}, f32[32,1280]{1,0:T(8,128)S(1)}) custom-call(f32[64,512]{1,0:T(8,128)S(1)} %get-tuple-element.63.refs_0_.refs_5_, bf16[2,256,2560]{2,1,0:T(8,128)(2,1)S(1)} %get-tuple-element.53.refs_4_.refs_1_.refs_6_, bf16[2,256,2560]{2,1,0:T(8,128)(2,1)S(1)} %get-tuple-element.54.refs_5_.refs_2_.refs_7_, ...), custom_call_target="tpu_custom_call" | custom-call | flops 301989888 | bytes 10616832 | tf_op jit(solution)/shard_map/pallas_call | solution.py:30
  28.9 0.6 collective-permute-start.4
  29.5 1.6 %collective-permute-start.21 = (f32[32,1280]{1,0:T(8,128)S(1)}, f32[32,1280]{1,0:T(8,128)S(1)}, u32[]{:S(2)}, u32[]{:S(2)}) collective-permute-start(f32[32,1280]{1,0:T(8,128)S(1)} %add.56), channel_id=1, source_target_pairs={{0,4},{1,5},{2,6},{3,7},{4,0},{5,1},{6,2},{7,3},{8,12},{9,13},{10,... | collective-permute-start | bytes 491528 | tf_op jit(solution)/shard_map/ppermute | solution.py:310
  31.1 1.7 %collective-permute-done.7 = f32[32,1408]{1,0:T(8,128)S(1)} collective-permute-done((f32[32,1408]{1,0:T(8,128)S(1)}, f32[32,1408]{1,0:T(8,128)S(1)}, u32[]{:S(2)}, u32[]{:S(2)}) %collective-permute-start.7) | collective-permute-done | bytes 180256 | tf_op jit(solution)/shard_map/ppermute | solution.py:310
  32.8 1.0 %collective-permute-start.8 = (f32[32,1408]{1,0:T(8,128)S(1)}, f32[32,1408]{1,0:T(8,128)S(1)}, u32[]{:S(2)}, u32[]{:S(2)}) collective-permute-start(f32[32,1408]{1,0:T(8,128)S(1)} %add.50), channel_id=1, source_target_pairs={{0,4},{1,5},{2,6},{3,7},{4,0},{5,1},{6,2},{7,3},{8,12},{9,13},{10,... | collective-permute-start | bytes 540680 | tf_op jit(solution)/shard_map/ppermute | solution.py:310
  33.8 0.9 %collective-permute-done.24 = f32[32,1408]{1,0:T(8,128)S(1)} collective-permute-done((f32[32,1408]{1,0:T(8,128)S(1)}, f32[32,1408]{1,0:T(8,128)S(1)}, u32[]{:S(2)}, u32[]{:S(2)}) %collective-permute-start.24) | collective-permute-done | bytes 180256 | tf_op jit(solution)/shard_map/ppermute | solution.py:310
  34.7 1.0 %collective-permute-start.25 = (f32[32,1408]{1,0:T(8,128)S(1)}, f32[32,1408]{1,0:T(8,128)S(1)}, u32[]{:S(2)}, u32[]{:S(2)}) collective-permute-start(f32[32,1408]{1,0:T(8,128)S(1)} %add.59.refs_0_), channel_id=1, source_target_pairs={{0,4},{1,5},{2,6},{3,7},{4,0},{5,1},{6,2},{7,3},{8,12},{9,13},{10,... | collective-permute-start | bytes 540680 | tf_op jit(solution)/shard_map/ppermute | solution.py:310
  35.8 0.3 collective-permute-done.4
  36.1 0.8 collective-permute-start.5
  36.9 2.7 %collective-permute-done.21 = f32[32,1280]{1,0:T(8,128)S(1)} collective-permute-done((f32[32,1280]{1,0:T(8,128)S(1)}, f32[32,1280]{1,0:T(8,128)S(1)}, u32[]{:S(2)}, u32[]{:S(2)}) %collective-permute-start.21) | collective-permute-done | bytes 163872 | tf_op jit(solution)/shard_map/ppermute | solution.py:310
  39.6 0.6 collective-permute-start.22
  40.2 1.4 %collective-permute-done.5 = f32[32,1280]{1,0:T(8,128)S(1)} collective-permute-done((f32[32,1280]{1,0:T(8,128)S(1)}, f32[32,1280]{1,0:T(8,128)S(1)}, u32[]{:S(2)}, u32[]{:S(2)}) %collective-permute-start.5) | collective-permute-done | bytes 163872 | tf_op jit(solution)/shard_map/ppermute | solution.py:310
  41.6 1.4 %collective-permute-start.6 = (f32[32,1280]{1,0:T(8,128)S(1)}, f32[32,1280]{1,0:T(8,128)S(1)}, u32[]{:S(2)}, u32[]{:S(2)}) collective-permute-start(f32[32,1280]{1,0:T(8,128)S(1)} %add.49.refs_0_), channel_id=1, source_target_pairs={{0,4},{1,5},{2,6},{3,7},{4,0},{5,1},{6,2},{7,3},{8,12},{9,13},{10,... | collective-permute-start | bytes 491528 | tf_op jit(solution)/shard_map/ppermute | solution.py:310
  43.0 0.1 collective-permute-done.8
  43.2 1.7 %collective-permute-start.9 = (f32[32,1408]{1,0:T(8,128)S(1)}, f32[32,1408]{1,0:T(8,128)S(1)}, u32[]{:S(2)}, u32[]{:S(2)}) collective-permute-start(f32[32,1408]{1,0:T(8,128)S(1)} %add.51.refs_0_), channel_id=1, source_target_pairs={{0,2},{1,3},{2,0},{3,1},{4,6},{5,7},{6,4},{7,5},{8,10},{9,11},{10,... | collective-permute-start | bytes 540680 | tf_op jit(solution)/shard_map/ppermute | solution.py:310
  44.8 0.9 %collective-permute-done.25.refs_1_ = f32[32,1408]{1,0:T(8,128)S(1)} collective-permute-done((f32[32,1408]{1,0:T(8,128)S(1)}, f32[32,1408]{1,0:T(8,128)S(1)}, u32[]{:S(2)}, u32[]{:S(2)}) %collective-permute-start.25) | collective-permute-done | bytes 180256 | tf_op jit(solution)/shard_map/ppermute | solution.py:310
  45.7 0.9 %shard_map.52 = (f32[64,1280]{1,0:T(8,128)S(1)}, f32[64,128]{1,0:T(8,128)S(1)}, f32[64,512]{1,0:T(8,128)S(1)}) custom-call(f32[32,1408]{1,0:T(8,128)S(1)} %add.59.refs_0_, f32[32,1408]{1,0:T(8,128)S(1)} %collective-permute-done.25.refs_1_, bf16[2,2560,256]{2,1,0:T(8,128)(2,1)S(1)} %get-tuple-element.57.refs_8_.refs_2_.refs_10_.refs_11_, ...), custom_call_target="tpu_custom_call" | custom-call | flops 1006632960 | bytes 10846208 | tf_op jit(solution)/shard_map/pallas_call | solution.py:30
  46.7 1.8 %shard_map.53 = (f32[64,1280]{1,0:T(8,128)S(1)}, f32[64,128]{1,0:T(8,128)S(1)}, f32[64,512]{1,0:T(8,128)S(1)}, f32[64,512]{1,0:T(8,128)S(1)}, f32[32,1408]{1,0:T(8,128)S(1)}, /*index=5*/f32[32,1408]{1,0:T(8,128)S(1)}) custom-call(f32[32,1280]{1,0:T(8,128)S(1)} %add.57.refs_0_, f32[32,1280]{1,0:T(8,128)S(1)} %collective-permute-done.22.refs_1_, ...), custom_call_target="tpu_custom_call" | custom-call | flops 20132659200 | bytes 21921792 | tf_op jit(solution)/shard_map/pallas_call | solution.py:30
  48.5 1.3 %collective-permute-start.29 = (f32[32,1408]{1,0:T(8,128)S(1)}, f32[32,1408]{1,0:T(8,128)S(1)}, u32[]{:S(2)}, u32[]{:S(2)}) collective-permute-start(f32[32,1408]{1,0:T(8,128)S(1)} %get-tuple-element.97), channel_id=1, source_target_pairs={{0,4},{1,5},{2,6},{3,7},{4,0},{5,1},{6,2},{7,3},{8,12},{9,13},{10,... | collective-permute-start | bytes 540680 | tf_op jit(solution)/shard_map/ppermute | solution.py:310
  49.9 0.9 %shard_map.54 = (f32[32,1280]{1,0:T(8,128)S(1)}, f32[32,1280]{1,0:T(8,128)S(1)}) custom-call(f32[64,512]{1,0:T(8,128)S(1)} %get-tuple-element.92.refs_0_.refs_10_, bf16[2,256,2560]{2,1,0:T(8,128)(2,1)S(1)} %get-tuple-element.53.refs_4_.refs_1_.refs_6_, bf16[2,256,2560]{2,1,0:T(8,128)(2,1)S(1)} %get-tuple-element.54.refs_5_.refs_2_.refs_7_, ...), custom_call_target="tpu_custom_call" | custom-call | flops 301989888 | bytes 10616832 | tf_op jit(solution)/shard_map/pallas_call | solution.py:30
  50.8 0.8 collective-permute-start.26
  51.6 0.9 %shard_map.45 = (f32[64,1280]{1,0:T(8,128)S(1)}, f32[64,128]{1,0:T(8,128)S(1)}, f32[64,512]{1,0:T(8,128)S(1)}) custom-call(f32[32,1408]{1,0:T(8,128)S(1)} %add.51.refs_0_, f32[32,1408]{1,0:T(8,128)S(1)} %collective-permute-done.9.refs_1_, bf16[2,2560,256]{2,1,0:T(8,128)(2,1)S(1)} %get-tuple-element.57.refs_8_.refs_2_.refs_10_.refs_11_, ...), custom_call_target="tpu_custom_call" | custom-call | bytes 10846208 | tf_op jit(solution)/shard_map/pallas_call | solution.py:30
  52.5 1.8 %shard_map.46 = (f32[64,1280]{1,0:T(8,128)S(1)}, f32[64,128]{1,0:T(8,128)S(1)}, f32[64,512]{1,0:T(8,128)S(1)}, f32[64,512]{1,0:T(8,128)S(1)}, f32[32,1408]{1,0:T(8,128)S(1)}, /*index=5*/f32[32,1408]{1,0:T(8,128)S(1)}) custom-call(f32[32,1280]{1,0:T(8,128)S(1)} %add.49.refs_0_, f32[32,1280]{1,0:T(8,128)S(1)} %collective-permute-done.6.refs_1_, ...), custom_call_target="tpu_custom_call" | custom-call | flops 2013265920 | bytes 21921792 | tf_op jit(solution)/shard_map/pallas_call | solution.py:30
  54.4 1.5 %collective-permute-start.13 = (f32[32,1408]{1,0:T(8,128)S(1)}, f32[32,1408]{1,0:T(8,128)S(1)}, u32[]{:S(2)}, u32[]{:S(2)}) collective-permute-start(f32[32,1408]{1,0:T(8,128)S(1)} %get-tuple-element.75), channel_id=1, source_target_pairs={{0,2},{1,3},{2,0},{3,1},{4,6},{5,7},{6,4},{7,5},{8,10},{9,11},{10,... | collective-permute-start | bytes 540680 | tf_op jit(solution)/shard_map/ppermute | solution.py:310
  55.9 0.9 %shard_map.47 = (f32[32,1280]{1,0:T(8,128)S(1)}, f32[32,1280]{1,0:T(8,128)S(1)}) custom-call(f32[64,512]{1,0:T(8,128)S(1)} %get-tuple-element.71.refs_0_.refs_10_, bf16[2,256,2560]{2,1,0:T(8,128)(2,1)S(1)} %get-tuple-element.53.refs_4_.refs_1_.refs_6_, bf16[2,256,2560]{2,1,0:T(8,128)(2,1)S(1)} %get-tuple-element.54.refs_5_.refs_2_.refs_7_, ...), custom_call_target="tpu_custom_call" | custom-call | flops 3019898880 | bytes 10616832 | tf_op jit(solution)/shard_map/pallas_call | solution.py:30
  56.9 0.8 %collective-permute-start.10 = (f32[32,1280]{1,0:T(8,128)S(1)}, f32[32,1280]{1,0:T(8,128)S(1)}, u32[]{:S(2)}, u32[]{:S(2)}) collective-permute-start(f32[32,1280]{1,0:T(8,128)S(1)} %get-tuple-element.73), channel_id=1, source_target_pairs={{0,4},{1,5},{2,6},{3,7},{4,0},{5,1},{6,2},{7,3},{8,12},{9,13},{10,... | collective-permute-start | bytes 491528 | tf_op jit(solution)/shard_map/ppermute | solution.py:310
  57.7 1.3 %collective-permute-start.30 = (f32[32,1408]{1,0:T(8,128)S(1)}, f32[32,1408]{1,0:T(8,128)S(1)}, u32[]{:S(2)}, u32[]{:S(2)}) collective-permute-start(f32[32,1408]{1,0:T(8,128)S(1)} %add.62), channel_id=1, source_target_pairs={{0,2},{1,3},{2,0},{3,1},{4,6},{5,7},{6,4},{7,5},{8,10},{9,11},{10,... | collective-permute-start | bytes 540680 | tf_op jit(solution)/shard_map/ppermute | solution.py:310
  59.1 0.8 %collective-permute-start.27 = (f32[32,1280]{1,0:T(8,128)S(1)}, f32[32,1280]{1,0:T(8,128)S(1)}, u32[]{:S(2)}, u32[]{:S(2)}) collective-permute-start(f32[32,1280]{1,0:T(8,128)S(1)} %add.60), channel_id=1, source_target_pairs={{0,4},{1,5},{2,6},{3,7},{4,0},{5,1},{6,2},{7,3},{8,12},{9,13},{10,... | collective-permute-start | bytes 491528 | tf_op jit(solution)/shard_map/ppermute | solution.py:310
  59.9 1.9 %collective-permute-done.13 = f32[32,1408]{1,0:T(8,128)S(1)} collective-permute-done((f32[32,1408]{1,0:T(8,128)S(1)}, f32[32,1408]{1,0:T(8,128)S(1)}, u32[]{:S(2)}, u32[]{:S(2)}) %collective-permute-start.13) | collective-permute-done | bytes 180256 | tf_op jit(solution)/shard_map/ppermute | solution.py:310
  61.8 1.2 %collective-permute-start.14 = (f32[32,1408]{1,0:T(8,128)S(1)}, f32[32,1408]{1,0:T(8,128)S(1)}, u32[]{:S(2)}, u32[]{:S(2)}) collective-permute-start(f32[32,1408]{1,0:T(8,128)S(1)} %add.54), channel_id=1, source_target_pairs={{0,4},{1,5},{2,6},{3,7},{4,0},{5,1},{6,2},{7,3},{8,12},{9,13},{10,... | collective-permute-start | bytes 540680 | tf_op jit(solution)/shard_map/ppermute | solution.py:310
  63.1 1.1 %collective-permute-start.11 = (f32[32,1280]{1,0:T(8,128)S(1)}, f32[32,1280]{1,0:T(8,128)S(1)}, u32[]{:S(2)}, u32[]{:S(2)}) collective-permute-start(f32[32,1280]{1,0:T(8,128)S(1)} %add.52), channel_id=1, source_target_pairs={{0,2},{1,3},{2,0},{3,1},{4,6},{5,7},{6,4},{7,5},{8,10},{9,11},{10,... | collective-permute-start | bytes 491528 | tf_op jit(solution)/shard_map/ppermute | solution.py:310
  64.2 1.4 %collective-permute-done.30 = f32[32,1408]{1,0:T(8,128)S(1)} collective-permute-done((f32[32,1408]{1,0:T(8,128)S(1)}, f32[32,1408]{1,0:T(8,128)S(1)}, u32[]{:S(2)}, u32[]{:S(2)}) %collective-permute-start.30) | collective-permute-done | bytes 180256 | tf_op jit(solution)/shard_map/ppermute | solution.py:310
  65.7 1.2 %collective-permute-start.31 = (f32[32,1408]{1,0:T(8,128)S(1)}, f32[32,1408]{1,0:T(8,128)S(1)}, u32[]{:S(2)}, u32[]{:S(2)}) collective-permute-start(f32[32,1408]{1,0:T(8,128)S(1)} %add.63.refs_0_), channel_id=1, source_target_pairs={{0,4},{1,5},{2,6},{3,7},{4,0},{5,1},{6,2},{7,3},{8,12},{9,13},{10,... | collective-permute-start | bytes 540680 | tf_op jit(solution)/shard_map/ppermute | solution.py:310
  66.9 0.5 collective-permute-start.28
  67.4 2.2 %collective-permute-done.14 = f32[32,1408]{1,0:T(8,128)S(1)} collective-permute-done((f32[32,1408]{1,0:T(8,128)S(1)}, f32[32,1408]{1,0:T(8,128)S(1)}, u32[]{:S(2)}, u32[]{:S(2)}) %collective-permute-start.14) | collective-permute-done | bytes 180256 | tf_op jit(solution)/shard_map/ppermute | solution.py:310
  69.7 0.8 collective-permute-start.15
  70.5 1.4 %collective-permute-start.12 = (f32[32,1280]{1,0:T(8,128)S(1)}, f32[32,1280]{1,0:T(8,128)S(1)}, u32[]{:S(2)}, u32[]{:S(2)}) collective-permute-start(f32[32,1280]{1,0:T(8,128)S(1)} %add.53.refs_0_), channel_id=1, source_target_pairs={{0,4},{1,5},{2,6},{3,7},{4,0},{5,1},{6,2},{7,3},{8,12},{9,13},{10,... | collective-permute-start | bytes 491528 | tf_op jit(solution)/shard_map/ppermute | solution.py:310
  71.8 0.9 %shard_map.55 = (f32[64,1280]{1,0:T(8,128)S(1)}, f32[64,128]{1,0:T(8,128)S(1)}, f32[64,512]{1,0:T(8,128)S(1)}) custom-call(f32[32,1408]{1,0:T(8,128)S(1)} %add.63.refs_0_, f32[32,1408]{1,0:T(8,128)S(1)} %collective-permute-done.31.refs_1_, bf16[2,2560,256]{2,1,0:T(8,128)(2,1)S(1)} %get-tuple-element.57.refs_8_.refs_2_.refs_10_.refs_11_, ...), custom_call_target="tpu_custom_call" | custom-call | bytes 10846208 | tf_op jit(solution)/shard_map/pallas_call | solution.py:30
  72.8 0.6 shard_map.57
  73.4 0.1 collective-permute-start.32
  73.5 1.7 %collective-permute-done.15.refs_1_ = f32[32,1408]{1,0:T(8,128)S(1)} collective-permute-done((f32[32,1408]{1,0:T(8,128)S(1)}, f32[32,1408]{1,0:T(8,128)S(1)}, u32[]{:S(2)}, u32[]{:S(2)}) %collective-permute-start.15) | collective-permute-done | bytes 180256 | tf_op jit(solution)/shard_map/ppermute | solution.py:310
  75.2 0.9 %shard_map.48 = (f32[64,1280]{1,0:T(8,128)S(1)}, f32[64,128]{1,0:T(8,128)S(1)}, f32[64,512]{1,0:T(8,128)S(1)}) custom-call(f32[32,1408]{1,0:T(8,128)S(1)} %add.55.refs_0_, f32[32,1408]{1,0:T(8,128)S(1)} %collective-permute-done.15.refs_1_, bf16[2,2560,256]{2,1,0:T(8,128)(2,1)S(1)} %get-tuple-element.57.refs_8_.refs_2_.refs_10_.refs_11_, ...), custom_call_target="tpu_custom_call" | custom-call | bytes 10846208 | tf_op jit(solution)/shard_map/pallas_call | solution.py:30
  76.2 1.0 %shard_map.49 = (f32[2,64,256]{2,1,0:T(8,128)S(1)}, f32[2,64,256]{2,1,0:T(8,128)S(1)}) custom-call(f32[32,1280]{1,0:T(8,128)S(1)} %add.53.refs_0_, f32[32,1280]{1,0:T(8,128)S(1)} %collective-permute-done.12.refs_1_, f32[64,1280]{1,0:T(8,128)S(1)} %get-tuple-element.76.refs_2_, f32[64,128]{1,0:T(8,128)S(1)} %get-tuple-element.77.refs_3_, ...), custom_call_target="tpu_custom_call" | custom-call | flops 1006632960 | bytes 12386304 | tf_op jit(solution)/shard_map/pallas_call | solution.py:30
  77.1 0.1 collective-permute-start.16
  77.2 0.6 shard_map.56.refs_2_
  77.9 0.7 collective-permute-done.16.refs_1_
  78.6 0.9 %shard_map.58 = (f32[2,256,128]{2,1,0:T(8,128)}, f32[2,256,128]{2,1,0:T(8,128)}) custom-call(f32[2,64,256]{2,1,0:T(8,128)S(1)} %get-tuple-element.82.refs_0_, f32[2,64,256]{2,1,0:T(8,128)S(1)} %collective-permute-done.16.refs_1_, f32[2,64,256]{2,1,0:T(8,128)S(1)} %shard_map.56.refs_2_, f32[2,64,256]{2,1,0:T(8,128)S(1)} %collective-permute-done.32.refs_3_), custom_call_target="tpu_custom_call" | custom-call | bytes 524288 | tf_op jit(solution)/shard_map/pallas_call | solution.py:30
  (37 shorter events, 0.4 us)
Async XLA Ops:
  0.6 12.5 %collective-permute-start.3 = (f32[2,256,2560]{2,1,0:T(8,128)}, f32[2,256,2560]{2,1,0:T(8,128)S(1)}, u32[]{:S(2)}, u32[]{:S(2)}) collective-permute-start(f32[2,256,2560]{2,1,0:T(8,128)} %imag_ref.1), channel_id=1, source_target_pairs={{0,1},{1,0},{2,3},{3,2},{4,5},{5,4},{6,7},{7,6},{8,9},{9,8},{10,11... | collective-permute-start | bytes 15728648 | tf_op jit(solution)/shard_map/ppermute | solution.py:310
  2.2 13.7 %collective-permute-start.19 = (f32[2,8,2560]{2,1,0:T(8,128)S(1)}, f32[2,8,2560]{2,1,0:T(8,128)S(1)}, u32[]{:S(2)}, u32[]{:S(2)}) collective-permute-start(f32[2,8,2560]{2,1,0:T(8,128)S(1)} %get-tuple-element.104.refs_0_), channel_id=1, source_target_pairs={{0,6},{1,7},{2,4},{3,5},{4,2},{5,3},{6,0},{7,1},{8,14},{9,15},{10,... | collective-permute-start | bytes 491528 | tf_op jit(solution)/shard_map/ppermute | solution.py:313
  5.7 10.5 %collective-permute-start.18 = (f32[2,8,2560]{2,1,0:T(8,128)S(1)}, f32[2,8,2560]{2,1,0:T(8,128)S(1)}, u32[]{:S(2)}, u32[]{:S(2)}) collective-permute-start(f32[2,8,2560]{2,1,0:T(8,128)S(1)} %get-tuple-element.104.refs_0_), channel_id=1, source_target_pairs={{0,4},{1,5},{2,6},{3,7},{4,0},{5,1},{6,2},{7,3},{8,12},{9,13},{10,... | collective-permute-start | bytes 491528 | tf_op jit(solution)/shard_map/ppermute | solution.py:313
  6.2 10.0 %collective-permute-start.17 = (f32[2,8,2560]{2,1,0:T(8,128)S(1)}, f32[2,8,2560]{2,1,0:T(8,128)S(1)}, u32[]{:S(2)}, u32[]{:S(2)}) collective-permute-start(f32[2,8,2560]{2,1,0:T(8,128)S(1)} %get-tuple-element.104.refs_0_), channel_id=1, source_target_pairs={{0,2},{1,3},{2,0},{3,1},{4,6},{5,7},{6,4},{7,5},{8,10},{9,11},{10,... | collective-permute-start | bytes 491528 | tf_op jit(solution)/shard_map/ppermute | solution.py:313
  6.3 16.8 %collective-permute-start.2 = (f32[2,8,2560]{2,1,0:T(8,128)S(1)}, f32[2,8,2560]{2,1,0:T(8,128)S(1)}, u32[]{:S(2)}, u32[]{:S(2)}) collective-permute-start(f32[2,8,2560]{2,1,0:T(8,128)S(1)} %get-tuple-element.105.refs_0_), channel_id=1, source_target_pairs={{0,6},{1,7},{2,4},{3,5},{4,2},{5,3},{6,0},{7,1},{8,14},{9,15},{10,... | collective-permute-start | bytes 491528 | tf_op jit(solution)/shard_map/ppermute | solution.py:313
  13.2 10.0 %collective-permute-start.1 = (f32[2,8,2560]{2,1,0:T(8,128)S(1)}, f32[2,8,2560]{2,1,0:T(8,128)S(1)}, u32[]{:S(2)}, u32[]{:S(2)}) collective-permute-start(f32[2,8,2560]{2,1,0:T(8,128)S(1)} %get-tuple-element.105.refs_0_), channel_id=1, source_target_pairs={{0,4},{1,5},{2,6},{3,7},{4,0},{5,1},{6,2},{7,3},{8,12},{9,13},{10,... | collective-permute-start | bytes 491528 | tf_op jit(solution)/shard_map/ppermute | solution.py:313
  15.9 7.3 %collective-permute-start = (f32[2,8,2560]{2,1,0:T(8,128)S(1)}, f32[2,8,2560]{2,1,0:T(8,128)S(1)}, u32[]{:S(2)}, u32[]{:S(2)}) collective-permute-start(f32[2,8,2560]{2,1,0:T(8,128)S(1)} %get-tuple-element.105.refs_0_), channel_id=1, source_target_pairs={{0,2},{1,3},{2,0},{3,1},{4,6},{5,7},{6,4},{7,5},{8,10},{9,11},{10,... | collective-permute-start | bytes 491528 | tf_op jit(solution)/shard_map/ppermute | solution.py:313
  18.8 7.5 %collective-permute-start.23 = (f32[32,1408]{1,0:T(8,128)S(1)}, f32[32,1408]{1,0:T(8,128)S(1)}, u32[]{:S(2)}, u32[]{:S(2)}) collective-permute-start(f32[32,1408]{1,0:T(8,128)S(1)} %get-tuple-element.88), channel_id=1, source_target_pairs={{0,4},{1,5},{2,6},{3,7},{4,0},{5,1},{6,2},{7,3},{8,12},{9,13},{10,... | collective-permute-start | bytes 540680 | tf_op jit(solution)/shard_map/ppermute | solution.py:310
  21.6 7.9 %collective-permute-start.20 = (f32[32,1280]{1,0:T(8,128)S(1)}, f32[32,1280]{1,0:T(8,128)S(1)}, u32[]{:S(2)}, u32[]{:S(2)}) collective-permute-start(f32[32,1280]{1,0:T(8,128)S(1)} %get-tuple-element.86), channel_id=1, source_target_pairs={{0,2},{1,3},{2,0},{3,1},{4,6},{5,7},{6,4},{7,5},{8,10},{9,11},{10,... | collective-permute-start | bytes 491528 | tf_op jit(solution)/shard_map/ppermute | solution.py:310
  25.8 7.0 %collective-permute-start.7 = (f32[32,1408]{1,0:T(8,128)S(1)}, f32[32,1408]{1,0:T(8,128)S(1)}, u32[]{:S(2)}, u32[]{:S(2)}) collective-permute-start(f32[32,1408]{1,0:T(8,128)S(1)} %get-tuple-element.67), channel_id=1, source_target_pairs={{0,2},{1,3},{2,0},{3,1},{4,6},{5,7},{6,4},{7,5},{8,10},{9,11},{10,... | collective-permute-start | bytes 540680 | tf_op jit(solution)/shard_map/ppermute | solution.py:310
  26.4 8.3 %collective-permute-start.24 = (f32[32,1408]{1,0:T(8,128)S(1)}, f32[32,1408]{1,0:T(8,128)S(1)}, u32[]{:S(2)}, u32[]{:S(2)}) collective-permute-start(f32[32,1408]{1,0:T(8,128)S(1)} %add.58), channel_id=1, source_target_pairs={{0,2},{1,3},{2,0},{3,1},{4,6},{5,7},{6,4},{7,5},{8,10},{9,11},{10,... | collective-permute-start | bytes 540680 | tf_op jit(solution)/shard_map/ppermute | solution.py:310
  28.9 7.2 %collective-permute-start.4 = (f32[32,1280]{1,0:T(8,128)S(1)}, f32[32,1280]{1,0:T(8,128)S(1)}, u32[]{:S(2)}, u32[]{:S(2)}) collective-permute-start(f32[32,1280]{1,0:T(8,128)S(1)} %get-tuple-element.65), channel_id=1, source_target_pairs={{0,4},{1,5},{2,6},{3,7},{4,0},{5,1},{6,2},{7,3},{8,12},{9,13},{10,... | collective-permute-start | bytes 491528 | tf_op jit(solution)/shard_map/ppermute | solution.py:310
  29.5 10.1 %collective-permute-start.21 = (f32[32,1280]{1,0:T(8,128)S(1)}, f32[32,1280]{1,0:T(8,128)S(1)}, u32[]{:S(2)}, u32[]{:S(2)}) collective-permute-start(f32[32,1280]{1,0:T(8,128)S(1)} %add.56), channel_id=1, source_target_pairs={{0,4},{1,5},{2,6},{3,7},{4,0},{5,1},{6,2},{7,3},{8,12},{9,13},{10,... | collective-permute-start | bytes 491528 | tf_op jit(solution)/shard_map/ppermute | solution.py:310
  32.8 10.3 %collective-permute-start.8 = (f32[32,1408]{1,0:T(8,128)S(1)}, f32[32,1408]{1,0:T(8,128)S(1)}, u32[]{:S(2)}, u32[]{:S(2)}) collective-permute-start(f32[32,1408]{1,0:T(8,128)S(1)} %add.50), channel_id=1, source_target_pairs={{0,4},{1,5},{2,6},{3,7},{4,0},{5,1},{6,2},{7,3},{8,12},{9,13},{10,... | collective-permute-start | bytes 540680 | tf_op jit(solution)/shard_map/ppermute | solution.py:310
  34.7 11.0 %collective-permute-start.25 = (f32[32,1408]{1,0:T(8,128)S(1)}, f32[32,1408]{1,0:T(8,128)S(1)}, u32[]{:S(2)}, u32[]{:S(2)}) collective-permute-start(f32[32,1408]{1,0:T(8,128)S(1)} %add.59.refs_0_), channel_id=1, source_target_pairs={{0,4},{1,5},{2,6},{3,7},{4,0},{5,1},{6,2},{7,3},{8,12},{9,13},{10,... | collective-permute-start | bytes 540680 | tf_op jit(solution)/shard_map/ppermute | solution.py:310
  36.1 5.5 %collective-permute-start.5 = (f32[32,1280]{1,0:T(8,128)S(1)}, f32[32,1280]{1,0:T(8,128)S(1)}, u32[]{:S(2)}, u32[]{:S(2)}) collective-permute-start(f32[32,1280]{1,0:T(8,128)S(1)} %add.48), channel_id=1, source_target_pairs={{0,2},{1,3},{2,0},{3,1},{4,6},{5,7},{6,4},{7,5},{8,10},{9,11},{10,... | collective-permute-start | bytes 491528 | tf_op jit(solution)/shard_map/ppermute | solution.py:310
  39.6 7.0 %collective-permute-start.22 = (f32[32,1280]{1,0:T(8,128)S(1)}, f32[32,1280]{1,0:T(8,128)S(1)}, u32[]{:S(2)}, u32[]{:S(2)}) collective-permute-start(f32[32,1280]{1,0:T(8,128)S(1)} %add.57.refs_0_), channel_id=1, source_target_pairs={{0,2},{1,3},{2,0},{3,1},{4,6},{5,7},{6,4},{7,5},{8,10},{9,11},{10,... | collective-permute-start | bytes 491528 | tf_op jit(solution)/shard_map/ppermute | solution.py:310
  41.6 10.9 %collective-permute-start.6 = (f32[32,1280]{1,0:T(8,128)S(1)}, f32[32,1280]{1,0:T(8,128)S(1)}, u32[]{:S(2)}, u32[]{:S(2)}) collective-permute-start(f32[32,1280]{1,0:T(8,128)S(1)} %add.49.refs_0_), channel_id=1, source_target_pairs={{0,4},{1,5},{2,6},{3,7},{4,0},{5,1},{6,2},{7,3},{8,12},{9,13},{10,... | collective-permute-start | bytes 491528 | tf_op jit(solution)/shard_map/ppermute | solution.py:310
  43.2 8.4 %collective-permute-start.9 = (f32[32,1408]{1,0:T(8,128)S(1)}, f32[32,1408]{1,0:T(8,128)S(1)}, u32[]{:S(2)}, u32[]{:S(2)}) collective-permute-start(f32[32,1408]{1,0:T(8,128)S(1)} %add.51.refs_0_), channel_id=1, source_target_pairs={{0,2},{1,3},{2,0},{3,1},{4,6},{5,7},{6,4},{7,5},{8,10},{9,11},{10,... | collective-permute-start | bytes 540680 | tf_op jit(solution)/shard_map/ppermute | solution.py:310
  48.5 9.2 %collective-permute-start.29 = (f32[32,1408]{1,0:T(8,128)S(1)}, f32[32,1408]{1,0:T(8,128)S(1)}, u32[]{:S(2)}, u32[]{:S(2)}) collective-permute-start(f32[32,1408]{1,0:T(8,128)S(1)} %get-tuple-element.97), channel_id=1, source_target_pairs={{0,4},{1,5},{2,6},{3,7},{4,0},{5,1},{6,2},{7,3},{8,12},{9,13},{10,... | collective-permute-start | bytes 540680 | tf_op jit(solution)/shard_map/ppermute | solution.py:310
  50.8 8.2 %collective-permute-start.26 = (f32[32,1280]{1,0:T(8,128)S(1)}, f32[32,1280]{1,0:T(8,128)S(1)}, u32[]{:S(2)}, u32[]{:S(2)}) collective-permute-start(f32[32,1280]{1,0:T(8,128)S(1)} %get-tuple-element.94), channel_id=1, source_target_pairs={{0,2},{1,3},{2,0},{3,1},{4,6},{5,7},{6,4},{7,5},{8,10},{9,11},{10,... | collective-permute-start | bytes 491528 | tf_op jit(solution)/shard_map/ppermute | solution.py:310
  54.4 7.4 %collective-permute-start.13 = (f32[32,1408]{1,0:T(8,128)S(1)}, f32[32,1408]{1,0:T(8,128)S(1)}, u32[]{:S(2)}, u32[]{:S(2)}) collective-permute-start(f32[32,1408]{1,0:T(8,128)S(1)} %get-tuple-element.75), channel_id=1, source_target_pairs={{0,2},{1,3},{2,0},{3,1},{4,6},{5,7},{6,4},{7,5},{8,10},{9,11},{10,... | collective-permute-start | bytes 540680 | tf_op jit(solution)/shard_map/ppermute | solution.py:310
  56.9 6.2 %collective-permute-start.10 = (f32[32,1280]{1,0:T(8,128)S(1)}, f32[32,1280]{1,0:T(8,128)S(1)}, u32[]{:S(2)}, u32[]{:S(2)}) collective-permute-start(f32[32,1280]{1,0:T(8,128)S(1)} %get-tuple-element.73), channel_id=1, source_target_pairs={{0,4},{1,5},{2,6},{3,7},{4,0},{5,1},{6,2},{7,3},{8,12},{9,13},{10,... | collective-permute-start | bytes 491528 | tf_op jit(solution)/shard_map/ppermute | solution.py:310
  57.7 7.9 %collective-permute-start.30 = (f32[32,1408]{1,0:T(8,128)S(1)}, f32[32,1408]{1,0:T(8,128)S(1)}, u32[]{:S(2)}, u32[]{:S(2)}) collective-permute-start(f32[32,1408]{1,0:T(8,128)S(1)} %add.62), channel_id=1, source_target_pairs={{0,2},{1,3},{2,0},{3,1},{4,6},{5,7},{6,4},{7,5},{8,10},{9,11},{10,... | collective-permute-start | bytes 540680 | tf_op jit(solution)/shard_map/ppermute | solution.py:310
  59.1 7.8 %collective-permute-start.27 = (f32[32,1280]{1,0:T(8,128)S(1)}, f32[32,1280]{1,0:T(8,128)S(1)}, u32[]{:S(2)}, u32[]{:S(2)}) collective-permute-start(f32[32,1280]{1,0:T(8,128)S(1)} %add.60), channel_id=1, source_target_pairs={{0,4},{1,5},{2,6},{3,7},{4,0},{5,1},{6,2},{7,3},{8,12},{9,13},{10,... | collective-permute-start | bytes 491528 | tf_op jit(solution)/shard_map/ppermute | solution.py:310
  61.8 7.8 %collective-permute-start.14 = (f32[32,1408]{1,0:T(8,128)S(1)}, f32[32,1408]{1,0:T(8,128)S(1)}, u32[]{:S(2)}, u32[]{:S(2)}) collective-permute-start(f32[32,1408]{1,0:T(8,128)S(1)} %add.54), channel_id=1, source_target_pairs={{0,4},{1,5},{2,6},{3,7},{4,0},{5,1},{6,2},{7,3},{8,12},{9,13},{10,... | collective-permute-start | bytes 540680 | tf_op jit(solution)/shard_map/ppermute | solution.py:310
  63.1 7.4 %collective-permute-start.11 = (f32[32,1280]{1,0:T(8,128)S(1)}, f32[32,1280]{1,0:T(8,128)S(1)}, u32[]{:S(2)}, u32[]{:S(2)}) collective-permute-start(f32[32,1280]{1,0:T(8,128)S(1)} %add.52), channel_id=1, source_target_pairs={{0,2},{1,3},{2,0},{3,1},{4,6},{5,7},{6,4},{7,5},{8,10},{9,11},{10,... | collective-permute-start | bytes 491528 | tf_op jit(solution)/shard_map/ppermute | solution.py:310
  65.7 6.2 %collective-permute-start.31 = (f32[32,1408]{1,0:T(8,128)S(1)}, f32[32,1408]{1,0:T(8,128)S(1)}, u32[]{:S(2)}, u32[]{:S(2)}) collective-permute-start(f32[32,1408]{1,0:T(8,128)S(1)} %add.63.refs_0_), channel_id=1, source_target_pairs={{0,4},{1,5},{2,6},{3,7},{4,0},{5,1},{6,2},{7,3},{8,12},{9,13},{10,... | collective-permute-start | bytes 540680 | tf_op jit(solution)/shard_map/ppermute | solution.py:310
  66.9 5.8 %collective-permute-start.28 = (f32[32,1280]{1,0:T(8,128)S(1)}, f32[32,1280]{1,0:T(8,128)S(1)}, u32[]{:S(2)}, u32[]{:S(2)}) collective-permute-start(f32[32,1280]{1,0:T(8,128)S(1)} %add.61.refs_0_), channel_id=1, source_target_pairs={{0,2},{1,3},{2,0},{3,1},{4,6},{5,7},{6,4},{7,5},{8,10},{9,11},{10,... | collective-permute-start | bytes 491528 | tf_op jit(solution)/shard_map/ppermute | solution.py:310
  69.7 5.6 %collective-permute-start.15 = (f32[32,1408]{1,0:T(8,128)S(1)}, f32[32,1408]{1,0:T(8,128)S(1)}, u32[]{:S(2)}, u32[]{:S(2)}) collective-permute-start(f32[32,1408]{1,0:T(8,128)S(1)} %add.55.refs_0_), channel_id=1, source_target_pairs={{0,2},{1,3},{2,0},{3,1},{4,6},{5,7},{6,4},{7,5},{8,10},{9,11},{10,... | collective-permute-start | bytes 540680 | tf_op jit(solution)/shard_map/ppermute | solution.py:310
  70.5 5.7 %collective-permute-start.12 = (f32[32,1280]{1,0:T(8,128)S(1)}, f32[32,1280]{1,0:T(8,128)S(1)}, u32[]{:S(2)}, u32[]{:S(2)}) collective-permute-start(f32[32,1280]{1,0:T(8,128)S(1)} %add.53.refs_0_), channel_id=1, source_target_pairs={{0,4},{1,5},{2,6},{3,7},{4,0},{5,1},{6,2},{7,3},{8,12},{9,13},{10,... | collective-permute-start | bytes 491528 | tf_op jit(solution)/shard_map/ppermute | solution.py:310
  73.4 4.5 %collective-permute-start.32 = (f32[2,64,256]{2,1,0:T(8,128)S(1)}, f32[2,64,256]{2,1,0:T(8,128)S(1)}, u32[]{:S(2)}, u32[]{:S(2)}) collective-permute-start(f32[2,64,256]{2,1,0:T(8,128)S(1)} %shard_map.57), channel_id=1, source_target_pairs={{0,1},{1,0},{2,3},{3,2},{4,5},{5,4},{6,7},{7,6},{8,9},{9,8},{10,11... | collective-permute-start | bytes 393224 | tf_op jit(solution)/shard_map/ppermute | solution.py:310
  77.1 1.4 %collective-permute-start.16 = (f32[2,64,256]{2,1,0:T(8,128)S(1)}, f32[2,64,256]{2,1,0:T(8,128)S(1)}, u32[]{:S(2)}, u32[]{:S(2)}) collective-permute-start(f32[2,64,256]{2,1,0:T(8,128)S(1)} %get-tuple-element.83), channel_id=1, source_target_pairs={{0,1},{1,0},{2,3},{3,2},{4,5},{5,4},{6,7},{7,6},{8,9},{9,8},{10,11... | collective-permute-start | bytes 393224 | tf_op jit(solution)/shard_map/ppermute | solution.py:310

commit v11 on v10

--- a/solution.py
+++ b/solution.py
@@ -9,8 +9,8 @@
 damping_ratio = 0.1
 LANES = 128
 GROUPS = 2
-ORDER = {'bE': ['a1.2']}
-COST = {'bC.': 0.3, 'aL.': 0, 'aR': 30, 'bM': 10, 'bL.': 0, 'bC': 0, 'aC': 0.3, 'aC.': 3, 'aL': 0}
+ORDER = {"b02": ["aC"]}
+COST = {"aR": 30, "aC": 0.3, "bC": 3, "aL": 0, "aM": 30, "aC.": 3, "bC.": 0.3, "aL.": 0, "bL.": 0}
 f32 = jnp.float32
 bf16 = jnp.bfloat16
 

time: 79.7 us -> 79.2 us (level)
  waiting for transfers between devices: 16 us -> 14.9 us
    ppermute x27, waiting for transfers between devices: 16 us -> 14.8 us  [swap(): lax.ppermute(value, 'rcv', [(at, at ^ 1 << bit) for at in range(count)])]
  transfers between devices with their start and end apart: 33 -> 33, of which waited for: 12 -> 11; matrix products, arithmetic and copies ran while one was open for 2% -> 2% of each run, Pallas kernels for 31% -> 31%
where the time goes in v11:
time: 79.2 us; the launch traced here: 79 us
  starting transfers between devices  36.3 us (46%)
  Pallas kernels  25.5 us (32%)
  waiting for transfers between devices  14.9 us (19%)
  local copies, waits for them, and re-layouts  1.02 us (1%)
  between operations  0.91 us (1%)
    ppermute x27, starting transfers between devices, swap(): lax.ppermute(value, 'rcv', [(at, at ^ 1 << bit) for at in range(count)])  28.4 us
    pallas_call x18, Pallas kernels, call(): pl.pallas_call(kernel, out_shape=[jax.ShapeDtypeStruct(shape, dtype) for...  25.5 us
    ppermute x27, waiting for transfers between devices, swap(): lax.ppermute(value, 'rcv', [(at, at ^ 1 << bit) for at in range(count)])  14.8 us
    ppermute x6, starting transfers between devices, jump(): lax.ppermute(value, 'rcv', [(at, at ^ mask << 1) for at in range(count)])  7.87 us
  transfers between devices with their start and end apart: 33, of which 11 were waited for; matrix products, arithmetic and copies ran while one was open for 2% of the time, Pallas kernels for 31%

profile of v11, /device:TPU:0, one launch (start us, length us, event | category | flops | bytes accessed | tf_op | source)
XLA Modules:
  0.0 79.0 jit_solution(11182756383735030283)
XLA Ops:
  0.6 0.5 collective-permute-start.3
  1.1 1.0 %fusion = (f32[2,8,2560]{2,1,0:T(8,128)S(1)}, f32[2,8,2560]{2,1,0:T(8,128)S(1)}) fusion(f32[2,16,2560]{2,1,0:T(8,128)} %param.3), kind=kLoop, calls=%fused_computation | loop fusion | bytes 655360 | tf_op jit(solution)/shard_map/slice | solution.py:319
  2.2 2.6 %collective-permute-start.17 = (f32[2,8,2560]{2,1,0:T(8,128)S(1)}, f32[2,8,2560]{2,1,0:T(8,128)S(1)}, u32[]{:S(2)}, u32[]{:S(2)}) collective-permute-start(f32[2,8,2560]{2,1,0:T(8,128)S(1)} %get-tuple-element.104.refs_0_), channel_id=1, source_target_pairs={{0,2},{1,3},{2,0},{3,1},{4,6},{5,7},{6,4},{7,5},{8,10},{9,11},{10,... | collective-permute-start | bytes 491528 | tf_op jit(solution)/shard_map/ppermute | solution.py:313
  4.7 1.5 %collective-permute-start.18 = (f32[2,8,2560]{2,1,0:T(8,128)S(1)}, f32[2,8,2560]{2,1,0:T(8,128)S(1)}, u32[]{:S(2)}, u32[]{:S(2)}) collective-permute-start(f32[2,8,2560]{2,1,0:T(8,128)S(1)} %get-tuple-element.104.refs_0_), channel_id=1, source_target_pairs={{0,4},{1,5},{2,6},{3,7},{4,0},{5,1},{6,2},{7,3},{8,12},{9,13},{10,... | collective-permute-start | bytes 491528 | tf_op jit(solution)/shard_map/ppermute | solution.py:313
  6.3 0.0 collective-permute-start.19
  6.3 1.9 %collective-permute-start = (f32[2,8,2560]{2,1,0:T(8,128)S(1)}, f32[2,8,2560]{2,1,0:T(8,128)S(1)}, u32[]{:S(2)}, u32[]{:S(2)}) collective-permute-start(f32[2,8,2560]{2,1,0:T(8,128)S(1)} %get-tuple-element.105.refs_0_), channel_id=1, source_target_pairs={{0,2},{1,3},{2,0},{3,1},{4,6},{5,7},{6,4},{7,5},{8,10},{9,11},{10,... | collective-permute-start | bytes 491528 | tf_op jit(solution)/shard_map/ppermute | solution.py:313
  8.2 4.0 %shard_map.41 = (bf16[2,256,2560]{2,1,0:T(8,128)(2,1)S(1)}, bf16[2,256,2560]{2,1,0:T(8,128)(2,1)S(1)}, bf16[2,2560,256]{2,1,0:T(8,128)(2,1)S(1)}, bf16[2,2560,256]{2,1,0:T(8,128)(2,1)S(1)}, f32[8,128]{1,0:T(8,128)S(1)}) custom-call(f32[2,256,2560]{2,1,0:T(8,128)} %imag_ref.1, f32[2,256,2560]{2,1,0:T(8,128)} %imag_ref.1), custom_call_target="tpu_custom_call" | custom-call | bytes 10485760 | tf_op jit(solution)/shard_map/pallas_call | solution.py:30
  12.2 1.6 %collective-permute-start.1 = (f32[2,8,2560]{2,1,0:T(8,128)S(1)}, f32[2,8,2560]{2,1,0:T(8,128)S(1)}, u32[]{:S(2)}, u32[]{:S(2)}) collective-permute-start(f32[2,8,2560]{2,1,0:T(8,128)S(1)} %get-tuple-element.105.refs_0_), channel_id=1, source_target_pairs={{0,4},{1,5},{2,6},{3,7},{4,0},{5,1},{6,2},{7,3},{8,12},{9,13},{10,... | collective-permute-start | bytes 491528 | tf_op jit(solution)/shard_map/ppermute | solution.py:313
  13.8 2.1 %shard_map.42 = (bf16[2,256,2560]{2,1,0:T(8,128)(2,1)S(1)}, bf16[2,256,2560]{2,1,0:T(8,128)(2,1)S(1)}, bf16[2,2560,256]{2,1,0:T(8,128)(2,1)S(1)}, bf16[2,2560,256]{2,1,0:T(8,128)(2,1)S(1)}, f32[8,128]{1,0:T(8,128)S(1)}) custom-call(f32[2,256,2560]{2,1,0:T(8,128)S(1)} %collective-permute-done.3.real_ref.imag_ref, ...), custom_call_target="tpu_custom_call" | custom-call | bytes 10485760 | tf_op jit(solution)/shard_map/pallas_call | solution.py:30
  15.9 0.2 collective-permute-start.2
  16.2 2.6 %shard_map.50 = (f32[64,512]{1,0:T(8,128)S(1)}, f32[32,1408]{1,0:T(8,128)S(1)}, f32[32,1408]{1,0:T(8,128)S(1)}) custom-call(f32[2,8,2560]{2,1,0:T(8,128)S(1)} %get-tuple-element.104.refs_0_, f32[2,8,2560]{2,1,0:T(8,128)S(1)} %collective-permute-done.17.refs_1_, f32[2,8,2560]{2,1,0:T(8,128)S(1)} %collective-permute-done.18.refs_2_, ...), custom_call_target="tpu_custom_call" | custom-call | flops 3019898880 | bytes 21635072 | tf_op jit(solution)/shard_map/pallas_call | solution.py:30
  18.8 1.9 %collective-permute-start.23 = (f32[32,1408]{1,0:T(8,128)S(1)}, f32[32,1408]{1,0:T(8,128)S(1)}, u32[]{:S(2)}, u32[]{:S(2)}) collective-permute-start(f32[32,1408]{1,0:T(8,128)S(1)} %get-tuple-element.89), channel_id=1, source_target_pairs={{0,4},{1,5},{2,6},{3,7},{4,0},{5,1},{6,2},{7,3},{8,12},{9,13},{10,... | collective-permute-start | bytes 540680 | tf_op jit(solution)/shard_map/ppermute | solution.py:310
  20.7 0.9 %shard_map.51 = (f32[32,1280]{1,0:T(8,128)S(1)}, f32[32,1280]{1,0:T(8,128)S(1)}) custom-call(f32[64,512]{1,0:T(8,128)S(1)} %get-tuple-element.84.refs_0_.refs_5_, bf16[2,256,2560]{2,1,0:T(8,128)(2,1)S(1)} %get-tuple-element.53.refs_4_.refs_1_.refs_6_, bf16[2,256,2560]{2,1,0:T(8,128)(2,1)S(1)} %get-tuple-element.54.refs_5_.refs_2_.refs_7_, ...), custom_call_target="tpu_custom_call" | custom-call | flops 3019898880 | bytes 10616832 | tf_op jit(solution)/shard_map/pallas_call | solution.py:30
  21.6 1.5 %collective-permute-start.20 = (f32[32,1280]{1,0:T(8,128)S(1)}, f32[32,1280]{1,0:T(8,128)S(1)}, u32[]{:S(2)}, u32[]{:S(2)}) collective-permute-start(f32[32,1280]{1,0:T(8,128)S(1)} %get-tuple-element.86), channel_id=1, source_target_pairs={{0,2},{1,3},{2,0},{3,1},{4,6},{5,7},{6,4},{7,5},{8,10},{9,11},{10,... | collective-permute-start | bytes 491528 | tf_op jit(solution)/shard_map/ppermute | solution.py:310
  23.2 2.6 %shard_map.43 = (f32[64,512]{1,0:T(8,128)S(1)}, f32[32,1408]{1,0:T(8,128)S(1)}, f32[32,1408]{1,0:T(8,128)S(1)}) custom-call(f32[2,8,2560]{2,1,0:T(8,128)S(1)} %get-tuple-element.105.refs_0_, f32[2,8,2560]{2,1,0:T(8,128)S(1)} %collective-permute-done.refs_1_, f32[2,8,2560]{2,1,0:T(8,128)S(1)} %collective-permute-done.1.refs_2_, ...), custom_call_target="tpu_custom_call" | custom-call | flops 90596966400 | bytes 21635072 | tf_op jit(solution)/shard_map/pallas_call | solution.py:30
  25.8 0.9 %shard_map.44 = (f32[32,1280]{1,0:T(8,128)S(1)}, f32[32,1280]{1,0:T(8,128)S(1)}) custom-call(f32[64,512]{1,0:T(8,128)S(1)} %get-tuple-element.63.refs_0_.refs_5_, bf16[2,256,2560]{2,1,0:T(8,128)(2,1)S(1)} %get-tuple-element.53.refs_4_.refs_1_.refs_6_, bf16[2,256,2560]{2,1,0:T(8,128)(2,1)S(1)} %get-tuple-element.54.refs_5_.refs_2_.refs_7_, ...), custom_call_target="tpu_custom_call" | custom-call | flops 301989888 | bytes 10616832 | tf_op jit(solution)/shard_map/pallas_call | solution.py:30
  26.7 0.6 collective-permute-start.7
  27.4 1.5 %collective-permute-start.24 = (f32[32,1408]{1,0:T(8,128)S(1)}, f32[32,1408]{1,0:T(8,128)S(1)}, u32[]{:S(2)}, u32[]{:S(2)}) collective-permute-start(f32[32,1408]{1,0:T(8,128)S(1)} %add.58), channel_id=1, source_target_pairs={{0,2},{1,3},{2,0},{3,1},{4,6},{5,7},{6,4},{7,5},{8,10},{9,11},{10,... | collective-permute-start | bytes 540680 | tf_op jit(solution)/shard_map/ppermute | solution.py:310
  28.9 0.5 collective-permute-start.4
  29.5 1.6 %collective-permute-start.21 = (f32[32,1280]{1,0:T(8,128)S(1)}, f32[32,1280]{1,0:T(8,128)S(1)}, u32[]{:S(2)}, u32[]{:S(2)}) collective-permute-start(f32[32,1280]{1,0:T(8,128)S(1)} %add.56), channel_id=1, source_target_pairs={{0,4},{1,5},{2,6},{3,7},{4,0},{5,1},{6,2},{7,3},{8,12},{9,13},{10,... | collective-permute-start | bytes 491528 | tf_op jit(solution)/shard_map/ppermute | solution.py:310
  31.0 2.4 %collective-permute-done.7 = f32[32,1408]{1,0:T(8,128)S(1)} collective-permute-done((f32[32,1408]{1,0:T(8,128)S(1)}, f32[32,1408]{1,0:T(8,128)S(1)}, u32[]{:S(2)}, u32[]{:S(2)}) %collective-permute-start.7) | collective-permute-done | bytes 180256 | tf_op jit(solution)/shard_map/ppermute | solution.py:310
  33.5 0.6 collective-permute-start.8
  34.0 1.3 %collective-permute-done.24 = f32[32,1408]{1,0:T(8,128)S(1)} collective-permute-done((f32[32,1408]{1,0:T(8,128)S(1)}, f32[32,1408]{1,0:T(8,128)S(1)}, u32[]{:S(2)}, u32[]{:S(2)}) %collective-permute-start.24) | collective-permute-done | bytes 180256 | tf_op jit(solution)/shard_map/ppermute | solution.py:310
  35.4 0.6 collective-permute-start.25
  35.9 0.1 collective-permute-done.4
  36.1 1.0 %collective-permute-start.5 = (f32[32,1280]{1,0:T(8,128)S(1)}, f32[32,1280]{1,0:T(8,128)S(1)}, u32[]{:S(2)}, u32[]{:S(2)}) collective-permute-start(f32[32,1280]{1,0:T(8,128)S(1)} %add.48), channel_id=1, source_target_pairs={{0,2},{1,3},{2,0},{3,1},{4,6},{5,7},{6,4},{7,5},{8,10},{9,11},{10,... | collective-permute-start | bytes 491528 | tf_op jit(solution)/shard_map/ppermute | solution.py:310
  37.0 2.5 %collective-permute-done.21 = f32[32,1280]{1,0:T(8,128)S(1)} collective-permute-done((f32[32,1280]{1,0:T(8,128)S(1)}, f32[32,1280]{1,0:T(8,128)S(1)}, u32[]{:S(2)}, u32[]{:S(2)}) %collective-permute-start.21) | collective-permute-done | bytes 163872 | tf_op jit(solution)/shard_map/ppermute | solution.py:310
  39.6 0.6 collective-permute-start.22
  40.2 1.3 %collective-permute-done.5 = f32[32,1280]{1,0:T(8,128)S(1)} collective-permute-done((f32[32,1280]{1,0:T(8,128)S(1)}, f32[32,1280]{1,0:T(8,128)S(1)}, u32[]{:S(2)}, u32[]{:S(2)}) %collective-permute-start.5) | collective-permute-done | bytes 163872 | tf_op jit(solution)/shard_map/ppermute | solution.py:310
  41.5 2.3 %collective-permute-start.6 = (f32[32,1280]{1,0:T(8,128)S(1)}, f32[32,1280]{1,0:T(8,128)S(1)}, u32[]{:S(2)}, u32[]{:S(2)}) collective-permute-start(f32[32,1280]{1,0:T(8,128)S(1)} %add.49.refs_0_), channel_id=1, source_target_pairs={{0,4},{1,5},{2,6},{3,7},{4,0},{5,1},{6,2},{7,3},{8,12},{9,13},{10,... | collective-permute-start | bytes 491528 | tf_op jit(solution)/shard_map/ppermute | solution.py:310
  43.8 0.2 collective-permute-start.9
  44.1 1.6 %collective-permute-done.25.refs_1_ = f32[32,1408]{1,0:T(8,128)S(1)} collective-permute-done((f32[32,1408]{1,0:T(8,128)S(1)}, f32[32,1408]{1,0:T(8,128)S(1)}, u32[]{:S(2)}, u32[]{:S(2)}) %collective-permute-start.25) | collective-permute-done | bytes 180256 | tf_op jit(solution)/shard_map/ppermute | solution.py:310
  45.7 0.9 %shard_map.52 = (f32[64,1280]{1,0:T(8,128)S(1)}, f32[64,128]{1,0:T(8,128)S(1)}, f32[64,512]{1,0:T(8,128)S(1)}) custom-call(f32[32,1408]{1,0:T(8,128)S(1)} %add.59.refs_0_, f32[32,1408]{1,0:T(8,128)S(1)} %collective-permute-done.25.refs_1_, bf16[2,2560,256]{2,1,0:T(8,128)(2,1)S(1)} %get-tuple-element.57.refs_8_.refs_2_.refs_10_.refs_11_, ...), custom_call_target="tpu_custom_call" | custom-call | flops 1006632960 | bytes 10846208 | tf_op jit(solution)/shard_map/pallas_call | solution.py:30
  46.6 1.8 %shard_map.53 = (f32[64,1280]{1,0:T(8,128)S(1)}, f32[64,128]{1,0:T(8,128)S(1)}, f32[64,512]{1,0:T(8,128)S(1)}, f32[64,512]{1,0:T(8,128)S(1)}, f32[32,1408]{1,0:T(8,128)S(1)}, /*index=5*/f32[32,1408]{1,0:T(8,128)S(1)}) custom-call(f32[32,1280]{1,0:T(8,128)S(1)} %add.57.refs_0_, f32[32,1280]{1,0:T(8,128)S(1)} %collective-permute-done.22.refs_1_, ...), custom_call_target="tpu_custom_call" | custom-call | flops 2013265920 | bytes 21921792 | tf_op jit(solution)/shard_map/pallas_call | solution.py:30
  48.5 0.6 collective-permute-start.29
  49.0 0.9 %shard_map.54 = (f32[32,1280]{1,0:T(8,128)S(1)}, f32[32,1280]{1,0:T(8,128)S(1)}) custom-call(f32[64,512]{1,0:T(8,128)S(1)} %get-tuple-element.93.refs_0_.refs_10_, bf16[2,256,2560]{2,1,0:T(8,128)(2,1)S(1)} %get-tuple-element.53.refs_4_.refs_1_.refs_6_, bf16[2,256,2560]{2,1,0:T(8,128)(2,1)S(1)} %get-tuple-element.54.refs_5_.refs_2_.refs_7_, ...), custom_call_target="tpu_custom_call" | custom-call | flops 301989888 | bytes 10616832 | tf_op jit(solution)/shard_map/pallas_call | solution.py:30
  50.0 1.1 %collective-permute-start.26 = (f32[32,1280]{1,0:T(8,128)S(1)}, f32[32,1280]{1,0:T(8,128)S(1)}, u32[]{:S(2)}, u32[]{:S(2)}) collective-permute-start(f32[32,1280]{1,0:T(8,128)S(1)} %get-tuple-element.95), channel_id=1, source_target_pairs={{0,2},{1,3},{2,0},{3,1},{4,6},{5,7},{6,4},{7,5},{8,10},{9,11},{10,... | collective-permute-start | bytes 491528 | tf_op jit(solution)/shard_map/ppermute | solution.py:310
  51.1 0.0 collective-permute-done.9.refs_1_
  51.1 0.9 %shard_map.45 = (f32[64,1280]{1,0:T(8,128)S(1)}, f32[64,128]{1,0:T(8,128)S(1)}, f32[64,512]{1,0:T(8,128)S(1)}) custom-call(f32[32,1408]{1,0:T(8,128)S(1)} %add.51.refs_0_, f32[32,1408]{1,0:T(8,128)S(1)} %collective-permute-done.9.refs_1_, bf16[2,2560,256]{2,1,0:T(8,128)(2,1)S(1)} %get-tuple-element.57.refs_8_.refs_2_.refs_10_.refs_11_, ...), custom_call_target="tpu_custom_call" | custom-call | bytes 10846208 | tf_op jit(solution)/shard_map/pallas_call | solution.py:30
  52.1 1.8 %shard_map.46 = (f32[64,1280]{1,0:T(8,128)S(1)}, f32[64,128]{1,0:T(8,128)S(1)}, f32[64,512]{1,0:T(8,128)S(1)}, f32[64,512]{1,0:T(8,128)S(1)}, f32[32,1408]{1,0:T(8,128)S(1)}, /*index=5*/f32[32,1408]{1,0:T(8,128)S(1)}) custom-call(f32[32,1280]{1,0:T(8,128)S(1)} %add.49.refs_0_, f32[32,1280]{1,0:T(8,128)S(1)} %collective-permute-done.6.refs_1_, ...), custom_call_target="tpu_custom_call" | custom-call | flops 60397977600 | bytes 21921792 | tf_op jit(solution)/shard_map/pallas_call | solution.py:30
  53.9 1.2 %collective-permute-start.13 = (f32[32,1408]{1,0:T(8,128)S(1)}, f32[32,1408]{1,0:T(8,128)S(1)}, u32[]{:S(2)}, u32[]{:S(2)}) collective-permute-start(f32[32,1408]{1,0:T(8,128)S(1)} %get-tuple-element.75), channel_id=1, source_target_pairs={{0,2},{1,3},{2,0},{3,1},{4,6},{5,7},{6,4},{7,5},{8,10},{9,11},{10,... | collective-permute-start | bytes 540680 | tf_op jit(solution)/shard_map/ppermute | solution.py:310
  55.1 0.9 %shard_map.47 = (f32[32,1280]{1,0:T(8,128)S(1)}, f32[32,1280]{1,0:T(8,128)S(1)}) custom-call(f32[64,512]{1,0:T(8,128)S(1)} %get-tuple-element.71.refs_0_.refs_10_, bf16[2,256,2560]{2,1,0:T(8,128)(2,1)S(1)} %get-tuple-element.53.refs_4_.refs_1_.refs_6_, bf16[2,256,2560]{2,1,0:T(8,128)(2,1)S(1)} %get-tuple-element.54.refs_5_.refs_2_.refs_7_, ...), custom_call_target="tpu_custom_call" | custom-call | flops 3019898880 | bytes 10616832 | tf_op jit(solution)/shard_map/pallas_call | solution.py:30
  56.0 1.6 %collective-permute-start.10 = (f32[32,1280]{1,0:T(8,128)S(1)}, f32[32,1280]{1,0:T(8,128)S(1)}, u32[]{:S(2)}, u32[]{:S(2)}) collective-permute-start(f32[32,1280]{1,0:T(8,128)S(1)} %get-tuple-element.73), channel_id=1, source_target_pairs={{0,4},{1,5},{2,6},{3,7},{4,0},{5,1},{6,2},{7,3},{8,12},{9,13},{10,... | collective-permute-start | bytes 491528 | tf_op jit(solution)/shard_map/ppermute | solution.py:310
  57.7 1.3 %collective-permute-start.30 = (f32[32,1408]{1,0:T(8,128)S(1)}, f32[32,1408]{1,0:T(8,128)S(1)}, u32[]{:S(2)}, u32[]{:S(2)}) collective-permute-start(f32[32,1408]{1,0:T(8,128)S(1)} %add.62), channel_id=1, source_target_pairs={{0,2},{1,3},{2,0},{3,1},{4,6},{5,7},{6,4},{7,5},{8,10},{9,11},{10,... | collective-permute-start | bytes 540680 | tf_op jit(solution)/shard_map/ppermute | solution.py:310
  59.0 0.4 collective-permute-start.27
  59.4 1.3 %collective-permute-done.13 = f32[32,1408]{1,0:T(8,128)S(1)} collective-permute-done((f32[32,1408]{1,0:T(8,128)S(1)}, f32[32,1408]{1,0:T(8,128)S(1)}, u32[]{:S(2)}, u32[]{:S(2)}) %collective-permute-start.13) | collective-permute-done | bytes 180256 | tf_op jit(solution)/shard_map/ppermute | solution.py:310
  60.8 2.7 %collective-permute-start.14 = (f32[32,1408]{1,0:T(8,128)S(1)}, f32[32,1408]{1,0:T(8,128)S(1)}, u32[]{:S(2)}, u32[]{:S(2)}) collective-permute-start(f32[32,1408]{1,0:T(8,128)S(1)} %add.54), channel_id=1, source_target_pairs={{0,4},{1,5},{2,6},{3,7},{4,0},{5,1},{6,2},{7,3},{8,12},{9,13},{10,... | collective-permute-start | bytes 540680 | tf_op jit(solution)/shard_map/ppermute | solution.py:310
  63.5 0.8 collective-permute-start.11
  64.3 0.8 %collective-permute-done.30 = f32[32,1408]{1,0:T(8,128)S(1)} collective-permute-done((f32[32,1408]{1,0:T(8,128)S(1)}, f32[32,1408]{1,0:T(8,128)S(1)}, u32[]{:S(2)}, u32[]{:S(2)}) %collective-permute-start.30) | collective-permute-done | bytes 180256 | tf_op jit(solution)/shard_map/ppermute | solution.py:310
  65.1 2.2 %collective-permute-start.31 = (f32[32,1408]{1,0:T(8,128)S(1)}, f32[32,1408]{1,0:T(8,128)S(1)}, u32[]{:S(2)}, u32[]{:S(2)}) collective-permute-start(f32[32,1408]{1,0:T(8,128)S(1)} %add.63.refs_0_), channel_id=1, source_target_pairs={{0,4},{1,5},{2,6},{3,7},{4,0},{5,1},{6,2},{7,3},{8,12},{9,13},{10,... | collective-permute-start | bytes 540680 | tf_op jit(solution)/shard_map/ppermute | solution.py:310
  67.4 0.1 collective-permute-start.28
  67.4 1.4 %collective-permute-done.14 = f32[32,1408]{1,0:T(8,128)S(1)} collective-permute-done((f32[32,1408]{1,0:T(8,128)S(1)}, f32[32,1408]{1,0:T(8,128)S(1)}, u32[]{:S(2)}, u32[]{:S(2)}) %collective-permute-start.14) | collective-permute-done | bytes 180256 | tf_op jit(solution)/shard_map/ppermute | solution.py:310
  68.9 1.1 %collective-permute-start.15 = (f32[32,1408]{1,0:T(8,128)S(1)}, f32[32,1408]{1,0:T(8,128)S(1)}, u32[]{:S(2)}, u32[]{:S(2)}) collective-permute-start(f32[32,1408]{1,0:T(8,128)S(1)} %add.55.refs_0_), channel_id=1, source_target_pairs={{0,2},{1,3},{2,0},{3,1},{4,6},{5,7},{6,4},{7,5},{8,10},{9,11},{10,... | collective-permute-start | bytes 540680 | tf_op jit(solution)/shard_map/ppermute | solution.py:310
  70.0 1.8 %collective-permute-start.12 = (f32[32,1280]{1,0:T(8,128)S(1)}, f32[32,1280]{1,0:T(8,128)S(1)}, u32[]{:S(2)}, u32[]{:S(2)}) collective-permute-start(f32[32,1280]{1,0:T(8,128)S(1)} %add.53.refs_0_), channel_id=1, source_target_pairs={{0,4},{1,5},{2,6},{3,7},{4,0},{5,1},{6,2},{7,3},{8,12},{9,13},{10,... | collective-permute-start | bytes 491528 | tf_op jit(solution)/shard_map/ppermute | solution.py:310
  71.8 0.9 %shard_map.55 = (f32[64,1280]{1,0:T(8,128)S(1)}, f32[64,128]{1,0:T(8,128)S(1)}, f32[64,512]{1,0:T(8,128)S(1)}) custom-call(f32[32,1408]{1,0:T(8,128)S(1)} %add.63.refs_0_, f32[32,1408]{1,0:T(8,128)S(1)} %collective-permute-done.31.refs_1_, bf16[2,2560,256]{2,1,0:T(8,128)(2,1)S(1)} %get-tuple-element.57.refs_8_.refs_2_.refs_10_.refs_11_, ...), custom_call_target="tpu_custom_call" | custom-call | bytes 10846208 | tf_op jit(solution)/shard_map/pallas_call | solution.py:30
  72.8 0.6 shard_map.57
  73.4 0.1 collective-permute-start.32
  73.5 1.2 %collective-permute-done.15.refs_1_ = f32[32,1408]{1,0:T(8,128)S(1)} collective-permute-done((f32[32,1408]{1,0:T(8,128)S(1)}, f32[32,1408]{1,0:T(8,128)S(1)}, u32[]{:S(2)}, u32[]{:S(2)}) %collective-permute-start.15) | collective-permute-done | bytes 180256 | tf_op jit(solution)/shard_map/ppermute | solution.py:310
  74.7 0.9 %shard_map.48 = (f32[64,1280]{1,0:T(8,128)S(1)}, f32[64,128]{1,0:T(8,128)S(1)}, f32[64,512]{1,0:T(8,128)S(1)}) custom-call(f32[32,1408]{1,0:T(8,128)S(1)} %add.55.refs_0_, f32[32,1408]{1,0:T(8,128)S(1)} %collective-permute-done.15.refs_1_, bf16[2,2560,256]{2,1,0:T(8,128)(2,1)S(1)} %get-tuple-element.57.refs_8_.refs_2_.refs_10_.refs_11_, ...), custom_call_target="tpu_custom_call" | custom-call | bytes 10846208 | tf_op jit(solution)/shard_map/pallas_call | solution.py:30
  75.6 1.0 %shard_map.49 = (f32[2,64,256]{2,1,0:T(8,128)S(1)}, f32[2,64,256]{2,1,0:T(8,128)S(1)}) custom-call(f32[32,1280]{1,0:T(8,128)S(1)} %add.53.refs_0_, f32[32,1280]{1,0:T(8,128)S(1)} %collective-permute-done.12.refs_1_, f32[64,1280]{1,0:T(8,128)S(1)} %get-tuple-element.76.refs_2_, f32[64,128]{1,0:T(8,128)S(1)} %get-tuple-element.77.refs_3_, ...), custom_call_target="tpu_custom_call" | custom-call | flops 1006632960 | bytes 12386304 | tf_op jit(solution)/shard_map/pallas_call | solution.py:30
  76.6 0.1 collective-permute-start.16
  76.7 0.6 shard_map.56.refs_2_
  77.3 0.7 collective-permute-done.16.refs_1_
  78.0 0.9 %shard_map.58 = (f32[2,256,128]{2,1,0:T(8,128)}, f32[2,256,128]{2,1,0:T(8,128)}) custom-call(f32[2,64,256]{2,1,0:T(8,128)S(1)} %get-tuple-element.82.refs_0_, f32[2,64,256]{2,1,0:T(8,128)S(1)} %collective-permute-done.16.refs_1_, f32[2,64,256]{2,1,0:T(8,128)S(1)} %shard_map.56.refs_2_, f32[2,64,256]{2,1,0:T(8,128)S(1)} %collective-permute-done.32.refs_3_), custom_call_target="tpu_custom_call" | custom-call | bytes 524288 | tf_op jit(solution)/shard_map/pallas_call | solution.py:30
  (37 shorter events, 0.4 us)
Async XLA Ops:
  0.6 11.6 %collective-permute-start.3 = (f32[2,256,2560]{2,1,0:T(8,128)}, f32[2,256,2560]{2,1,0:T(8,128)S(1)}, u32[]{:S(2)}, u32[]{:S(2)}) collective-permute-start(f32[2,256,2560]{2,1,0:T(8,128)} %imag_ref.1), channel_id=1, source_target_pairs={{0,1},{1,0},{2,3},{3,2},{4,5},{5,4},{6,7},{7,6},{8,9},{9,8},{10,11... | collective-permute-start | bytes 15728648 | tf_op jit(solution)/shard_map/ppermute | solution.py:310
  2.2 13.8 %collective-permute-start.17 = (f32[2,8,2560]{2,1,0:T(8,128)S(1)}, f32[2,8,2560]{2,1,0:T(8,128)S(1)}, u32[]{:S(2)}, u32[]{:S(2)}) collective-permute-start(f32[2,8,2560]{2,1,0:T(8,128)S(1)} %get-tuple-element.104.refs_0_), channel_id=1, source_target_pairs={{0,2},{1,3},{2,0},{3,1},{4,6},{5,7},{6,4},{7,5},{8,10},{9,11},{10,... | collective-permute-start | bytes 491528 | tf_op jit(solution)/shard_map/ppermute | solution.py:313
  4.7 11.4 %collective-permute-start.18 = (f32[2,8,2560]{2,1,0:T(8,128)S(1)}, f32[2,8,2560]{2,1,0:T(8,128)S(1)}, u32[]{:S(2)}, u32[]{:S(2)}) collective-permute-start(f32[2,8,2560]{2,1,0:T(8,128)S(1)} %get-tuple-element.104.refs_0_), channel_id=1, source_target_pairs={{0,4},{1,5},{2,6},{3,7},{4,0},{5,1},{6,2},{7,3},{8,12},{9,13},{10,... | collective-permute-start | bytes 491528 | tf_op jit(solution)/shard_map/ppermute | solution.py:313
  6.3 9.9 %collective-permute-start.19 = (f32[2,8,2560]{2,1,0:T(8,128)S(1)}, f32[2,8,2560]{2,1,0:T(8,128)S(1)}, u32[]{:S(2)}, u32[]{:S(2)}) collective-permute-start(f32[2,8,2560]{2,1,0:T(8,128)S(1)} %get-tuple-element.104.refs_0_), channel_id=1, source_target_pairs={{0,6},{1,7},{2,4},{3,5},{4,2},{5,3},{6,0},{7,1},{8,14},{9,15},{10,... | collective-permute-start | bytes 491528 | tf_op jit(solution)/shard_map/ppermute | solution.py:313
  6.3 16.9 %collective-permute-start = (f32[2,8,2560]{2,1,0:T(8,128)S(1)}, f32[2,8,2560]{2,1,0:T(8,128)S(1)}, u32[]{:S(2)}, u32[]{:S(2)}) collective-permute-start(f32[2,8,2560]{2,1,0:T(8,128)S(1)} %get-tuple-element.105.refs_0_), channel_id=1, source_target_pairs={{0,2},{1,3},{2,0},{3,1},{4,6},{5,7},{6,4},{7,5},{8,10},{9,11},{10,... | collective-permute-start | bytes 491528 | tf_op jit(solution)/shard_map/ppermute | solution.py:313
  12.2 10.9 %collective-permute-start.1 = (f32[2,8,2560]{2,1,0:T(8,128)S(1)}, f32[2,8,2560]{2,1,0:T(8,128)S(1)}, u32[]{:S(2)}, u32[]{:S(2)}) collective-permute-start(f32[2,8,2560]{2,1,0:T(8,128)S(1)} %get-tuple-element.105.refs_0_), channel_id=1, source_target_pairs={{0,4},{1,5},{2,6},{3,7},{4,0},{5,1},{6,2},{7,3},{8,12},{9,13},{10,... | collective-permute-start | bytes 491528 | tf_op jit(solution)/shard_map/ppermute | solution.py:313
  15.9 7.2 %collective-permute-start.2 = (f32[2,8,2560]{2,1,0:T(8,128)S(1)}, f32[2,8,2560]{2,1,0:T(8,128)S(1)}, u32[]{:S(2)}, u32[]{:S(2)}) collective-permute-start(f32[2,8,2560]{2,1,0:T(8,128)S(1)} %get-tuple-element.105.refs_0_), channel_id=1, source_target_pairs={{0,6},{1,7},{2,4},{3,5},{4,2},{5,3},{6,0},{7,1},{8,14},{9,15},{10,... | collective-permute-start | bytes 491528 | tf_op jit(solution)/shard_map/ppermute | solution.py:313
  18.8 8.6 %collective-permute-start.23 = (f32[32,1408]{1,0:T(8,128)S(1)}, f32[32,1408]{1,0:T(8,128)S(1)}, u32[]{:S(2)}, u32[]{:S(2)}) collective-permute-start(f32[32,1408]{1,0:T(8,128)S(1)} %get-tuple-element.89), channel_id=1, source_target_pairs={{0,4},{1,5},{2,6},{3,7},{4,0},{5,1},{6,2},{7,3},{8,12},{9,13},{10,... | collective-permute-start | bytes 540680 | tf_op jit(solution)/shard_map/ppermute | solution.py:310
  21.6 7.8 %collective-permute-start.20 = (f32[32,1280]{1,0:T(8,128)S(1)}, f32[32,1280]{1,0:T(8,128)S(1)}, u32[]{:S(2)}, u32[]{:S(2)}) collective-permute-start(f32[32,1280]{1,0:T(8,128)S(1)} %get-tuple-element.86), channel_id=1, source_target_pairs={{0,2},{1,3},{2,0},{3,1},{4,6},{5,7},{6,4},{7,5},{8,10},{9,11},{10,... | collective-permute-start | bytes 491528 | tf_op jit(solution)/shard_map/ppermute | solution.py:310
  26.7 6.7 %collective-permute-start.7 = (f32[32,1408]{1,0:T(8,128)S(1)}, f32[32,1408]{1,0:T(8,128)S(1)}, u32[]{:S(2)}, u32[]{:S(2)}) collective-permute-start(f32[32,1408]{1,0:T(8,128)S(1)} %get-tuple-element.67), channel_id=1, source_target_pairs={{0,2},{1,3},{2,0},{3,1},{4,6},{5,7},{6,4},{7,5},{8,10},{9,11},{10,... | collective-permute-start | bytes 540680 | tf_op jit(solution)/shard_map/ppermute | solution.py:310
  27.4 8.0 %collective-permute-start.24 = (f32[32,1408]{1,0:T(8,128)S(1)}, f32[32,1408]{1,0:T(8,128)S(1)}, u32[]{:S(2)}, u32[]{:S(2)}) collective-permute-start(f32[32,1408]{1,0:T(8,128)S(1)} %add.58), channel_id=1, source_target_pairs={{0,2},{1,3},{2,0},{3,1},{4,6},{5,7},{6,4},{7,5},{8,10},{9,11},{10,... | collective-permute-start | bytes 540680 | tf_op jit(solution)/shard_map/ppermute | solution.py:310
  28.9 7.1 %collective-permute-start.4 = (f32[32,1280]{1,0:T(8,128)S(1)}, f32[32,1280]{1,0:T(8,128)S(1)}, u32[]{:S(2)}, u32[]{:S(2)}) collective-permute-start(f32[32,1280]{1,0:T(8,128)S(1)} %get-tuple-element.65), channel_id=1, source_target_pairs={{0,4},{1,5},{2,6},{3,7},{4,0},{5,1},{6,2},{7,3},{8,12},{9,13},{10,... | collective-permute-start | bytes 491528 | tf_op jit(solution)/shard_map/ppermute | solution.py:310
  29.5 10.1 %collective-permute-start.21 = (f32[32,1280]{1,0:T(8,128)S(1)}, f32[32,1280]{1,0:T(8,128)S(1)}, u32[]{:S(2)}, u32[]{:S(2)}) collective-permute-start(f32[32,1280]{1,0:T(8,128)S(1)} %add.56), channel_id=1, source_target_pairs={{0,4},{1,5},{2,6},{3,7},{4,0},{5,1},{6,2},{7,3},{8,12},{9,13},{10,... | collective-permute-start | bytes 491528 | tf_op jit(solution)/shard_map/ppermute | solution.py:310
  33.5 10.4 %collective-permute-start.8 = (f32[32,1408]{1,0:T(8,128)S(1)}, f32[32,1408]{1,0:T(8,128)S(1)}, u32[]{:S(2)}, u32[]{:S(2)}) collective-permute-start(f32[32,1408]{1,0:T(8,128)S(1)} %add.50), channel_id=1, source_target_pairs={{0,4},{1,5},{2,6},{3,7},{4,0},{5,1},{6,2},{7,3},{8,12},{9,13},{10,... | collective-permute-start | bytes 540680 | tf_op jit(solution)/shard_map/ppermute | solution.py:310
  35.4 10.3 %collective-permute-start.25 = (f32[32,1408]{1,0:T(8,128)S(1)}, f32[32,1408]{1,0:T(8,128)S(1)}, u32[]{:S(2)}, u32[]{:S(2)}) collective-permute-start(f32[32,1408]{1,0:T(8,128)S(1)} %add.59.refs_0_), channel_id=1, source_target_pairs={{0,4},{1,5},{2,6},{3,7},{4,0},{5,1},{6,2},{7,3},{8,12},{9,13},{10,... | collective-permute-start | bytes 540680 | tf_op jit(solution)/shard_map/ppermute | solution.py:310
  36.1 5.4 %collective-permute-start.5 = (f32[32,1280]{1,0:T(8,128)S(1)}, f32[32,1280]{1,0:T(8,128)S(1)}, u32[]{:S(2)}, u32[]{:S(2)}) collective-permute-start(f32[32,1280]{1,0:T(8,128)S(1)} %add.48), channel_id=1, source_target_pairs={{0,2},{1,3},{2,0},{3,1},{4,6},{5,7},{6,4},{7,5},{8,10},{9,11},{10,... | collective-permute-start | bytes 491528 | tf_op jit(solution)/shard_map/ppermute | solution.py:310
  39.6 7.1 %collective-permute-start.22 = (f32[32,1280]{1,0:T(8,128)S(1)}, f32[32,1280]{1,0:T(8,128)S(1)}, u32[]{:S(2)}, u32[]{:S(2)}) collective-permute-start(f32[32,1280]{1,0:T(8,128)S(1)} %add.57.refs_0_), channel_id=1, source_target_pairs={{0,2},{1,3},{2,0},{3,1},{4,6},{5,7},{6,4},{7,5},{8,10},{9,11},{10,... | collective-permute-start | bytes 491528 | tf_op jit(solution)/shard_map/ppermute | solution.py:310
  41.5 10.6 %collective-permute-start.6 = (f32[32,1280]{1,0:T(8,128)S(1)}, f32[32,1280]{1,0:T(8,128)S(1)}, u32[]{:S(2)}, u32[]{:S(2)}) collective-permute-start(f32[32,1280]{1,0:T(8,128)S(1)} %add.49.refs_0_), channel_id=1, source_target_pairs={{0,4},{1,5},{2,6},{3,7},{4,0},{5,1},{6,2},{7,3},{8,12},{9,13},{10,... | collective-permute-start | bytes 491528 | tf_op jit(solution)/shard_map/ppermute | solution.py:310
  43.8 7.3 %collective-permute-start.9 = (f32[32,1408]{1,0:T(8,128)S(1)}, f32[32,1408]{1,0:T(8,128)S(1)}, u32[]{:S(2)}, u32[]{:S(2)}) collective-permute-start(f32[32,1408]{1,0:T(8,128)S(1)} %add.51.refs_0_), channel_id=1, source_target_pairs={{0,2},{1,3},{2,0},{3,1},{4,6},{5,7},{6,4},{7,5},{8,10},{9,11},{10,... | collective-permute-start | bytes 540680 | tf_op jit(solution)/shard_map/ppermute | solution.py:310
  48.5 9.2 %collective-permute-start.29 = (f32[32,1408]{1,0:T(8,128)S(1)}, f32[32,1408]{1,0:T(8,128)S(1)}, u32[]{:S(2)}, u32[]{:S(2)}) collective-permute-start(f32[32,1408]{1,0:T(8,128)S(1)} %get-tuple-element.97), channel_id=1, source_target_pairs={{0,4},{1,5},{2,6},{3,7},{4,0},{5,1},{6,2},{7,3},{8,12},{9,13},{10,... | collective-permute-start | bytes 540680 | tf_op jit(solution)/shard_map/ppermute | solution.py:310
  50.0 9.0 %collective-permute-start.26 = (f32[32,1280]{1,0:T(8,128)S(1)}, f32[32,1280]{1,0:T(8,128)S(1)}, u32[]{:S(2)}, u32[]{:S(2)}) collective-permute-start(f32[32,1280]{1,0:T(8,128)S(1)} %get-tuple-element.95), channel_id=1, source_target_pairs={{0,2},{1,3},{2,0},{3,1},{4,6},{5,7},{6,4},{7,5},{8,10},{9,11},{10,... | collective-permute-start | bytes 491528 | tf_op jit(solution)/shard_map/ppermute | solution.py:310
  53.9 6.8 %collective-permute-start.13 = (f32[32,1408]{1,0:T(8,128)S(1)}, f32[32,1408]{1,0:T(8,128)S(1)}, u32[]{:S(2)}, u32[]{:S(2)}) collective-permute-start(f32[32,1408]{1,0:T(8,128)S(1)} %get-tuple-element.75), channel_id=1, source_target_pairs={{0,2},{1,3},{2,0},{3,1},{4,6},{5,7},{6,4},{7,5},{8,10},{9,11},{10,... | collective-permute-start | bytes 540680 | tf_op jit(solution)/shard_map/ppermute | solution.py:310
  56.0 7.4 %collective-permute-start.10 = (f32[32,1280]{1,0:T(8,128)S(1)}, f32[32,1280]{1,0:T(8,128)S(1)}, u32[]{:S(2)}, u32[]{:S(2)}) collective-permute-start(f32[32,1280]{1,0:T(8,128)S(1)} %get-tuple-element.73), channel_id=1, source_target_pairs={{0,4},{1,5},{2,6},{3,7},{4,0},{5,1},{6,2},{7,3},{8,12},{9,13},{10,... | collective-permute-start | bytes 491528 | tf_op jit(solution)/shard_map/ppermute | solution.py:310
  57.7 7.4 %collective-permute-start.30 = (f32[32,1408]{1,0:T(8,128)S(1)}, f32[32,1408]{1,0:T(8,128)S(1)}, u32[]{:S(2)}, u32[]{:S(2)}) collective-permute-start(f32[32,1408]{1,0:T(8,128)S(1)} %add.62), channel_id=1, source_target_pairs={{0,2},{1,3},{2,0},{3,1},{4,6},{5,7},{6,4},{7,5},{8,10},{9,11},{10,... | collective-permute-start | bytes 540680 | tf_op jit(solution)/shard_map/ppermute | solution.py:310
  59.0 8.3 %collective-permute-start.27 = (f32[32,1280]{1,0:T(8,128)S(1)}, f32[32,1280]{1,0:T(8,128)S(1)}, u32[]{:S(2)}, u32[]{:S(2)}) collective-permute-start(f32[32,1280]{1,0:T(8,128)S(1)} %add.60), channel_id=1, source_target_pairs={{0,4},{1,5},{2,6},{3,7},{4,0},{5,1},{6,2},{7,3},{8,12},{9,13},{10,... | collective-permute-start | bytes 491528 | tf_op jit(solution)/shard_map/ppermute | solution.py:310
  60.8 8.1 %collective-permute-start.14 = (f32[32,1408]{1,0:T(8,128)S(1)}, f32[32,1408]{1,0:T(8,128)S(1)}, u32[]{:S(2)}, u32[]{:S(2)}) collective-permute-start(f32[32,1408]{1,0:T(8,128)S(1)} %add.54), channel_id=1, source_target_pairs={{0,4},{1,5},{2,6},{3,7},{4,0},{5,1},{6,2},{7,3},{8,12},{9,13},{10,... | collective-permute-start | bytes 540680 | tf_op jit(solution)/shard_map/ppermute | solution.py:310
  63.5 6.5 %collective-permute-start.11 = (f32[32,1280]{1,0:T(8,128)S(1)}, f32[32,1280]{1,0:T(8,128)S(1)}, u32[]{:S(2)}, u32[]{:S(2)}) collective-permute-start(f32[32,1280]{1,0:T(8,128)S(1)} %add.52), channel_id=1, source_target_pairs={{0,2},{1,3},{2,0},{3,1},{4,6},{5,7},{6,4},{7,5},{8,10},{9,11},{10,... | collective-permute-start | bytes 491528 | tf_op jit(solution)/shard_map/ppermute | solution.py:310
  65.1 6.7 %collective-permute-start.31 = (f32[32,1408]{1,0:T(8,128)S(1)}, f32[32,1408]{1,0:T(8,128)S(1)}, u32[]{:S(2)}, u32[]{:S(2)}) collective-permute-start(f32[32,1408]{1,0:T(8,128)S(1)} %add.63.refs_0_), channel_id=1, source_target_pairs={{0,4},{1,5},{2,6},{3,7},{4,0},{5,1},{6,2},{7,3},{8,12},{9,13},{10,... | collective-permute-start | bytes 540680 | tf_op jit(solution)/shard_map/ppermute | solution.py:310
  67.4 5.4 %collective-permute-start.28 = (f32[32,1280]{1,0:T(8,128)S(1)}, f32[32,1280]{1,0:T(8,128)S(1)}, u32[]{:S(2)}, u32[]{:S(2)}) collective-permute-start(f32[32,1280]{1,0:T(8,128)S(1)} %add.61.refs_0_), channel_id=1, source_target_pairs={{0,2},{1,3},{2,0},{3,1},{4,6},{5,7},{6,4},{7,5},{8,10},{9,11},{10,... | collective-permute-start | bytes 491528 | tf_op jit(solution)/shard_map/ppermute | solution.py:310
  68.9 5.8 %collective-permute-start.15 = (f32[32,1408]{1,0:T(8,128)S(1)}, f32[32,1408]{1,0:T(8,128)S(1)}, u32[]{:S(2)}, u32[]{:S(2)}) collective-permute-start(f32[32,1408]{1,0:T(8,128)S(1)} %add.55.refs_0_), channel_id=1, source_target_pairs={{0,2},{1,3},{2,0},{3,1},{4,6},{5,7},{6,4},{7,5},{8,10},{9,11},{10,... | collective-permute-start | bytes 540680 | tf_op jit(solution)/shard_map/ppermute | solution.py:310
  70.0 5.6 %collective-permute-start.12 = (f32[32,1280]{1,0:T(8,128)S(1)}, f32[32,1280]{1,0:T(8,128)S(1)}, u32[]{:S(2)}, u32[]{:S(2)}) collective-permute-start(f32[32,1280]{1,0:T(8,128)S(1)} %add.53.refs_0_), channel_id=1, source_target_pairs={{0,4},{1,5},{2,6},{3,7},{4,0},{5,1},{6,2},{7,3},{8,12},{9,13},{10,... | collective-permute-start | bytes 491528 | tf_op jit(solution)/shard_map/ppermute | solution.py:310
  73.4 4.0 %collective-permute-start.32 = (f32[2,64,256]{2,1,0:T(8,128)S(1)}, f32[2,64,256]{2,1,0:T(8,128)S(1)}, u32[]{:S(2)}, u32[]{:S(2)}) collective-permute-start(f32[2,64,256]{2,1,0:T(8,128)S(1)} %shard_map.57), channel_id=1, source_target_pairs={{0,1},{1,0},{2,3},{3,2},{4,5},{5,4},{6,7},{7,6},{8,9},{9,8},{10,11... | collective-permute-start | bytes 393224 | tf_op jit(solution)/shard_map/ppermute | solution.py:310
  76.6 1.4 %collective-permute-start.16 = (f32[2,64,256]{2,1,0:T(8,128)S(1)}, f32[2,64,256]{2,1,0:T(8,128)S(1)}, u32[]{:S(2)}, u32[]{:S(2)}) collective-permute-start(f32[2,64,256]{2,1,0:T(8,128)S(1)} %get-tuple-element.83), channel_id=1, source_target_pairs={{0,1},{1,0},{2,3},{3,2},{4,5},{5,4},{6,7},{7,6},{8,9},{9,8},{10,11... | collective-permute-start | bytes 393224 | tf_op jit(solution)/shard_map/ppermute | solution.py:310
